TPU v7x, 32 devices: a whole 2x2x4 slice. The times are simulated.
32 devices in a mesh: dp: 4 (over z), head: 4 (over y, core), mp: 2 (over x).
Axes of the slice: x: 2, y: 2, z: 4, core: 2. Of those that a mesh axis runs over, the one named last changes fastest.
Arguments:
- inputs: bfloat16 [2, 8192, 2048], P(None, ('dp', 'head', 'mp')), may hold values from -6 to 6
- cotangent: bfloat16 [2, 8192, 2048], P(None, ('dp', 'head', 'mp')), may hold values from -6 to 6
- seq_counts: int32 [8], replicated, may hold values from 1024 to 2048, as said below
- seq_bucket: int32 [8], replicated, may hold values from 0 to 7, each once
- attn_norm_gain: float32 [2048], replicated, may hold values from 0.5 to 1.5
- q_norm_gain: float32 [128], replicated, may hold values from 0.1 to 1.9
- k_norm_gain: float32 [128], replicated, may hold values from 0.1 to 1.9
- w_query: bfloat16 [2048, 2048], P(('dp', 'mp'), 'head'), may hold values from -0.125 to 0.125
- w_key: bfloat16 [2048, 1024], P(('dp', 'mp'), 'head'), may hold values from -0.125 to 0.125
- w_value: bfloat16 [2048, 1024], P(('dp', 'mp'), 'head'), may hold values from -0.125 to 0.125
- w_headgate: bfloat16 [2048, 16], P(('dp', 'mp'), 'head'), may hold values from -0.125 to 0.125
- w_out: bfloat16 [2048, 2048], P('head', ('dp', 'mp')), may hold values from -4 to 4
- ffn_norm_gain: float32 [2048], replicated, may hold values from 0.5 to 1.5
- w_gate: bfloat16 [2048, 6144], P(('dp', 'head'), 'mp'), may hold values from -0.125 to 0.125
- w_up: bfloat16 [2048, 6144], P(('dp', 'head'), 'mp'), may hold values from -0.125 to 0.125
- w_down: bfloat16 [6144, 2048], P('mp', ('dp', 'head')), may hold values from -0.078125 to 0.078125
Outputs:
- block_out: bfloat16 [2, 8192, 2048], P(None, ('dp', 'head', 'mp'))
- input_grad: bfloat16 [2, 8192, 2048], P(None, ('dp', 'head', 'mp'))
- grad_attn_norm_gain: float32 [2048], replicated
- grad_q_norm_gain: float32 [128], replicated
- grad_k_norm_gain: float32 [128], replicated
- grad_w_query: float32 [2048, 2048], P(('dp', 'mp'), 'head')
- grad_w_key: float32 [2048, 1024], P(('dp', 'mp'), 'head')
- grad_w_value: float32 [2048, 1024], P(('dp', 'mp'), 'head')
- grad_w_headgate: float32 [2048, 16], P(('dp', 'mp'), 'head')
- grad_w_out: float32 [2048, 2048], P('head', ('dp', 'mp'))
- grad_ffn_norm_gain: float32 [2048], replicated
- grad_w_gate: float32 [2048, 6144], P(('dp', 'head'), 'mp')
- grad_w_up: float32 [2048, 6144], P(('dp', 'head'), 'mp')
- grad_w_down: float32 [6144, 2048], P('mp', ('dp', 'head'))
Inputs may be any that keep to these rules, and one draw needn't show every extreme that they name: `seq_counts`: at least one sequence has exactly 2048 tokens. `seq_bucket`: A permutation: each bucket holds exactly one sequence.
All inputs are finite; a program needn't handle non-finite values.
Results may differ from a plain program's by a relative error of at most 0.024.
Values may be sent and summed in bfloat16 or wider, within the bound.
A program may use at most 184 MiB of HBM per device.

v0:
```python
import jax
import jax.numpy as jnp
from jax import lax
from jax.sharding import PartitionSpec as P

EPS = 1e-06
ROPE_BASE = 1000000.0
NEG_FILL = -1e30


def rms_scale(values):
    return lax.rsqrt(jnp.mean(values * values, axis=-1, keepdims=True) + EPS)


def norm_back(grad_out, normed, scale_rows, gain):
    d_normed = grad_out * gain
    return scale_rows * (d_normed - normed * jnp.mean(d_normed * normed, axis=-1, keepdims=True))


def rope_tables(positions, half):
    freq = jnp.power(ROPE_BASE, -jnp.arange(half, dtype=jnp.float32) / half)
    angle = positions.astype(jnp.float32)[:, None] * freq[None, :]
    return (jnp.cos(angle)[:, None, :], jnp.sin(angle)[:, None, :])


def rotate(values, cosine, sine):
    half = values.shape[-1] // 2
    first = values[..., :half]
    second = values[..., half:]
    return jnp.concatenate(
        [first * cosine - second * sine, second * cosine + first * sine], axis=-1
    )


def rotate_back(grads, cosine, sine):
    half = grads.shape[-1] // 2
    first = grads[..., :half]
    second = grads[..., half:]
    return jnp.concatenate(
        [first * cosine + second * sine, second * cosine - first * sine], axis=-1
    )


def masked_scores(q_group, key_piece, query_pos, key_pos, live_count):
    scores = jnp.einsum("qhgd,khd->hgqk", q_group, key_piece, preferred_element_type=jnp.float32)
    allowed = (key_pos[None, :] <= query_pos[:, None]) & (key_pos[None, :] < live_count)
    return (scores, allowed)


def split_keys(keys, values, key_pos, key_block):
    n_blocks = keys.shape[0] // key_block
    key_pieces = keys.reshape(n_blocks, key_block, keys.shape[1], keys.shape[2])
    value_pieces = values.reshape(n_blocks, key_block, values.shape[1], values.shape[2])
    return (key_pieces, value_pieces, key_pos.reshape(n_blocks, key_block))


def attend_forward(q_group, keys, values, query_pos, key_pos, live_count, key_block):
    n_query, kv_here, group_size, head_dim = q_group.shape
    key_pieces, value_pieces, pos_pieces = split_keys(keys, values, key_pos, key_block)

    def stats(carry, piece):
        row_max, row_total = carry
        key_piece, piece_pos = piece
        scores, allowed = masked_scores(q_group, key_piece, query_pos, piece_pos, live_count)
        scores = jnp.where(allowed, scores, NEG_FILL)
        new_max = jnp.maximum(row_max, jnp.max(scores, axis=-1))
        kept_exp = jnp.where(allowed, jnp.exp(scores - new_max[..., None]), 0.0)
        row_total = row_total * jnp.exp(row_max - new_max) + jnp.sum(kept_exp, axis=-1)
        return ((new_max, row_total), None)

    start = (
        jnp.full((kv_here, group_size, n_query), NEG_FILL, jnp.float32),
        jnp.zeros((kv_here, group_size, n_query), jnp.float32),
    )
    (row_max, row_total), unused = lax.scan(stats, start, (key_pieces, pos_pieces))
    log_total = row_max + jnp.log(row_total)

    def weigh(acc, piece):
        key_piece, value_piece, piece_pos = piece
        scores, allowed = masked_scores(q_group, key_piece, query_pos, piece_pos, live_count)
        prob_low = jnp.where(allowed, jnp.exp(scores - log_total[..., None]), 0.0).astype(
            jnp.bfloat16
        )
        acc = acc + jnp.einsum(
            "hgqk,khd->qhgd", prob_low, value_piece, preferred_element_type=jnp.float32
        )
        return (acc, None)

    attn_o, unused = lax.scan(
        weigh, jnp.zeros(q_group.shape, jnp.float32), (key_pieces, value_pieces, pos_pieces)
    )
    return (attn_o, log_total)


def attend_backward(
    q_group, keys, values, query_pos, key_pos, live_count, key_block, log_total, d_out, delta
):
    kv_here = keys.shape[1]
    head_dim = keys.shape[2]
    key_pieces, value_pieces, pos_pieces = split_keys(keys, values, key_pos, key_block)

    def backstep(d_query, piece):
        key_piece, value_piece, piece_pos = piece
        scores, allowed = masked_scores(q_group, key_piece, query_pos, piece_pos, live_count)
        probs = jnp.where(allowed, jnp.exp(scores - log_total[..., None]), 0.0)
        d_probs = jnp.einsum(
            "qhgd,khd->hgqk", d_out, value_piece, preferred_element_type=jnp.float32
        )
        d_scores = (probs * (d_probs - delta[..., None])).astype(jnp.bfloat16)
        d_query = d_query + jnp.einsum(
            "hgqk,khd->qhgd", d_scores, key_piece, preferred_element_type=jnp.float32
        )
        d_key = jnp.einsum("hgqk,qhgd->khd", d_scores, q_group, preferred_element_type=jnp.float32)
        d_value = jnp.einsum(
            "hgqk,qhgd->khd", probs.astype(jnp.bfloat16), d_out, preferred_element_type=jnp.float32
        )
        return (d_query, (d_key, d_value))

    d_query, (d_key, d_value) = lax.scan(
        backstep, jnp.zeros(q_group.shape, jnp.float32), (key_pieces, value_pieces, pos_pieces)
    )
    return (d_query, d_key.reshape(-1, kv_here * head_dim), d_value.reshape(-1, kv_here * head_dim))


def gather_weights(w_query, w_key, w_value, w_headgate, w_out, w_gate, w_up, w_down):
    attn_parts = (
        lax.all_gather(w_query, ("dp", "mp"), axis=0, tiled=True),
        lax.all_gather(w_key, ("dp", "mp"), axis=0, tiled=True),
        lax.all_gather(w_value, ("dp", "mp"), axis=0, tiled=True),
        lax.all_gather(w_headgate, ("dp", "mp"), axis=0, tiled=True),
        lax.all_gather(w_out, ("dp", "mp"), axis=1, tiled=True),
    )
    ffn_parts = (
        lax.all_gather(w_gate, ("dp", "head"), axis=0, tiled=True),
        lax.all_gather(w_up, ("dp", "head"), axis=0, tiled=True),
        lax.all_gather(w_down, ("dp", "head"), axis=1, tiled=True),
    )
    return tuple(attn_parts) + tuple(ffn_parts)


def reduce_grads(g_query, g_key, g_value, g_headgate, g_out, g_gate, g_up, g_down):
    attn_parts = (
        lax.psum_scatter(
            g_query.astype(jnp.bfloat16), ("dp", "mp"), scatter_dimension=0, tiled=True
        ).astype(jnp.float32),
        lax.psum_scatter(
            g_key.astype(jnp.bfloat16), ("dp", "mp"), scatter_dimension=0, tiled=True
        ).astype(jnp.float32),
        lax.psum_scatter(
            g_value.astype(jnp.bfloat16), ("dp", "mp"), scatter_dimension=0, tiled=True
        ).astype(jnp.float32),
        lax.psum_scatter(
            g_headgate.astype(jnp.bfloat16), ("dp", "mp"), scatter_dimension=0, tiled=True
        ).astype(jnp.float32),
        lax.psum_scatter(
            g_out.astype(jnp.bfloat16), ("dp", "mp"), scatter_dimension=1, tiled=True
        ).astype(jnp.float32),
    )
    ffn_parts = (
        lax.psum_scatter(
            g_gate.astype(jnp.bfloat16), ("dp", "head"), scatter_dimension=0, tiled=True
        ).astype(jnp.float32),
        lax.psum_scatter(
            g_up.astype(jnp.bfloat16), ("dp", "head"), scatter_dimension=0, tiled=True
        ).astype(jnp.float32),
        lax.psum_scatter(
            g_down.astype(jnp.bfloat16), ("dp", "head"), scatter_dimension=1, tiled=True
        ).astype(jnp.float32),
    )
    return tuple(attn_parts) + tuple(ffn_parts)


def local(
    inputs,
    cotangent,
    seq_counts,
    seq_bucket,
    attn_norm_gain,
    q_norm_gain,
    k_norm_gain,
    w_query,
    w_key,
    w_value,
    w_headgate,
    w_out,
    ffn_norm_gain,
    w_gate,
    w_up,
    w_down,
):
    micro_batches, row_count, model_width = inputs.shape
    n_head = lax.axis_size("head")
    n_mp = lax.axis_size("mp")
    n_dp = lax.axis_size("dp")
    head_idx = lax.axis_index("head")
    mp_idx = lax.axis_index("mp")
    dp_idx = lax.axis_index("dp")
    head_dim = q_norm_gain.shape[0]
    q_heads = w_query.shape[1] // head_dim
    kv_heads = w_key.shape[1] // head_dim
    group_size = q_heads // kv_heads
    q_scale = head_dim ** (-0.5)
    seq_len = row_count * n_head * n_mp
    key_block = min(512, seq_len)
    n_query = n_head * row_count
    slot_ids = jnp.arange(micro_batches * n_dp, dtype=jnp.int32)
    slot_count = jnp.sum(
        jnp.where(seq_bucket[None, :] == slot_ids[:, None], seq_counts[None, :], 0), axis=1
    )
    local_idx = jnp.arange(row_count, dtype=jnp.int32)
    own_pos = head_idx * n_mp * row_count + mp_idx * row_count + local_idx
    query_idx = jnp.arange(n_query, dtype=jnp.int32)
    query_pos = (
        query_idx // row_count * n_mp * row_count + mp_idx * row_count + query_idx % row_count
    )
    key_idx = jnp.arange(seq_len, dtype=jnp.int32)
    key_pos = (
        key_idx % n_query // row_count * n_mp * row_count
        + key_idx // n_query * row_count
        + key_idx % row_count
    )
    rope_cos, rope_sin = rope_tables(query_pos, head_dim // 2)
    grad_total = None
    gain_attn = jnp.zeros((model_width,), jnp.float32)
    gain_query = jnp.zeros((head_dim,), jnp.float32)
    gain_key = jnp.zeros((head_dim,), jnp.float32)
    gain_ffn = jnp.zeros((model_width,), jnp.float32)
    outputs = []
    input_grads = []
    for micro_batch in range(micro_batches):
        weights = gather_weights(w_query, w_key, w_value, w_headgate, w_out, w_gate, w_up, w_down)
        wq_full, wk_full, wv_full, wg_full, wo_full, wgate_full, wup_full, wdown_full = weights
        live_count = slot_count[micro_batch * n_dp + dp_idx]
        x_float = inputs[micro_batch].astype(jnp.float32)
        scale1 = rms_scale(x_float)
        normed1 = x_float * scale1
        xn1 = (normed1 * attn_norm_gain).astype(jnp.bfloat16)
        gathered_rows = lax.all_gather(xn1, "head", axis=0, tiled=True)
        q_raw = jnp.dot(gathered_rows, wq_full, preferred_element_type=jnp.float32).reshape(
            n_query, q_heads, head_dim
        )
        k_raw = jnp.dot(gathered_rows, wk_full, preferred_element_type=jnp.float32).reshape(
            n_query, kv_heads, head_dim
        )
        value_low = jnp.dot(gathered_rows, wv_full, preferred_element_type=jnp.float32).astype(
            jnp.bfloat16
        )
        gate_logit = jnp.dot(gathered_rows, wg_full, preferred_element_type=jnp.float32)
        q_rms = rms_scale(q_raw)
        q_hat = q_raw * q_rms
        query_low = (rotate(q_hat * q_norm_gain, rope_cos, rope_sin) * q_scale).astype(jnp.bfloat16)
        k_rms = rms_scale(k_raw)
        k_hat = k_raw * k_rms
        key_low = rotate(k_hat * k_norm_gain, rope_cos, rope_sin).astype(jnp.bfloat16)
        all_keys, all_values = (
            lax.all_gather(key_low.reshape(n_query, kv_heads * head_dim), "mp", axis=0, tiled=True),
            lax.all_gather(value_low, "mp", axis=0, tiled=True),
        )
        all_keys = all_keys.reshape(seq_len, kv_heads, head_dim)
        all_values = all_values.reshape(seq_len, kv_heads, head_dim)
        q_group = query_low.reshape(n_query, kv_heads, group_size, head_dim)
        attn_o, log_total = attend_forward(
            q_group, all_keys, all_values, query_pos, key_pos, live_count, key_block
        )
        gate_prob = jax.nn.sigmoid(gate_logit)
        attn_heads = attn_o.reshape(n_query, q_heads, head_dim)
        gated = (
            (attn_heads * gate_prob[..., None])
            .reshape(n_query, q_heads * head_dim)
            .astype(jnp.bfloat16)
        )
        attn_sum = lax.psum_scatter(
            jnp.dot(gated, wo_full, preferred_element_type=jnp.float32).astype(jnp.bfloat16),
            "head",
            scatter_dimension=0,
            tiled=True,
        ).astype(jnp.float32)
        hidden1 = x_float + attn_sum
        scale2 = rms_scale(hidden1)
        normed2 = hidden1 * scale2
        xn2 = (normed2 * ffn_norm_gain).astype(jnp.bfloat16)
        live = (own_pos < live_count).astype(jnp.float32)[:, None]
        cot_live = cotangent[micro_batch].astype(jnp.float32) * live
        ffn_in, cot_rows = (
            lax.all_gather(xn2, "mp", axis=0, tiled=True),
            lax.all_gather(cot_live.astype(jnp.bfloat16), "mp", axis=0, tiled=True),
        )
        gate_pre = jnp.dot(ffn_in, wgate_full, preferred_element_type=jnp.float32)
        up_pre = jnp.dot(ffn_in, wup_full, preferred_element_type=jnp.float32)
        gate_sig = jax.nn.sigmoid(gate_pre)
        gate_act = gate_pre * gate_sig
        hidden = (gate_act * up_pre).astype(jnp.bfloat16)
        ffn_sum = lax.psum_scatter(
            jnp.dot(hidden, wdown_full, preferred_element_type=jnp.float32).astype(jnp.bfloat16),
            "mp",
            scatter_dimension=0,
            tiled=True,
        ).astype(jnp.float32)
        outputs.append((hidden1 + ffn_sum).astype(jnp.bfloat16))
        d_hidden = jnp.einsum("rd,fd->rf", cot_rows, wdown_full, preferred_element_type=jnp.float32)
        grad_down = jnp.einsum("rf,rd->fd", hidden, cot_rows, preferred_element_type=jnp.float32)
        d_up = (d_hidden * gate_act).astype(jnp.bfloat16)
        d_gate = (d_hidden * up_pre * gate_sig * (1.0 + gate_pre * (1.0 - gate_sig))).astype(
            jnp.bfloat16
        )
        grad_gate = jnp.einsum("rd,rf->df", ffn_in, d_gate, preferred_element_type=jnp.float32)
        grad_up = jnp.einsum("rd,rf->df", ffn_in, d_up, preferred_element_type=jnp.float32)
        ffn_term = jnp.einsum(
            "rf,df->rd", d_gate, wgate_full, preferred_element_type=jnp.float32
        ) + jnp.einsum("rf,df->rd", d_up, wup_full, preferred_element_type=jnp.float32)
        d_xn2 = lax.psum_scatter(
            ffn_term.astype(jnp.bfloat16), "mp", scatter_dimension=0, tiled=True
        ).astype(jnp.float32)
        gain_ffn = gain_ffn + jnp.sum(d_xn2 * normed2, axis=0)
        d_hidden1 = cot_live + norm_back(d_xn2, normed2, scale2, ffn_norm_gain)
        d_attn = lax.all_gather(d_hidden1.astype(jnp.bfloat16), "head", axis=0, tiled=True)
        d_gated = jnp.einsum(
            "rd,cd->rc", d_attn, wo_full, preferred_element_type=jnp.float32
        ).reshape(n_query, q_heads, head_dim)
        grad_out = jnp.einsum("rc,rd->cd", gated, d_attn, preferred_element_type=jnp.float32)
        d_out_low = (d_gated * gate_prob[..., None]).astype(jnp.bfloat16)
        d_gate_logit = (
            jnp.sum(d_gated * attn_heads, axis=-1) * gate_prob * (1.0 - gate_prob)
        ).astype(jnp.bfloat16)
        grad_headgate = jnp.einsum(
            "rd,rc->dc", gathered_rows, d_gate_logit, preferred_element_type=jnp.float32
        )
        d_out_group = d_out_low.reshape(n_query, kv_heads, group_size, head_dim)
        delta = jnp.transpose(jnp.sum(d_out_group.astype(jnp.float32) * attn_o, axis=-1), (1, 2, 0))
        d_query, d_key_all, d_value_all = attend_backward(
            q_group,
            all_keys,
            all_values,
            query_pos,
            key_pos,
            live_count,
            key_block,
            log_total,
            d_out_group,
            delta,
        )
        d_key_own, d_value_own = (
            lax.psum_scatter(
                d_key_all.astype(jnp.bfloat16), "mp", scatter_dimension=0, tiled=True
            ).astype(jnp.float32),
            lax.psum_scatter(
                d_value_all.astype(jnp.bfloat16), "mp", scatter_dimension=0, tiled=True
            ).astype(jnp.float32),
        )
        dq_norm = rotate_back(
            (d_query * q_scale).reshape(n_query, q_heads, head_dim), rope_cos, rope_sin
        )
        gain_query = gain_query + jnp.sum(dq_norm * q_hat, axis=(0, 1))
        d_q_raw = (
            norm_back(dq_norm, q_hat, q_rms, q_norm_gain)
            .reshape(n_query, q_heads * head_dim)
            .astype(jnp.bfloat16)
        )
        dk_norm = rotate_back(d_key_own.reshape(n_query, kv_heads, head_dim), rope_cos, rope_sin)
        gain_key = gain_key + jnp.sum(dk_norm * k_hat, axis=(0, 1))
        d_k_raw = (
            norm_back(dk_norm, k_hat, k_rms, k_norm_gain)
            .reshape(n_query, kv_heads * head_dim)
            .astype(jnp.bfloat16)
        )
        d_value_low = d_value_own.astype(jnp.bfloat16)
        grad_query = jnp.einsum(
            "rd,rc->dc", gathered_rows, d_q_raw, preferred_element_type=jnp.float32
        )
        grad_key = jnp.einsum(
            "rd,rc->dc", gathered_rows, d_k_raw, preferred_element_type=jnp.float32
        )
        grad_value = jnp.einsum(
            "rd,rc->dc", gathered_rows, d_value_low, preferred_element_type=jnp.float32
        )
        attn_term = jnp.einsum("rc,dc->rd", d_q_raw, wq_full, preferred_element_type=jnp.float32)
        attn_term = attn_term + jnp.einsum(
            "rc,dc->rd", d_k_raw, wk_full, preferred_element_type=jnp.float32
        )
        attn_term = attn_term + jnp.einsum(
            "rc,dc->rd", d_value_low, wv_full, preferred_element_type=jnp.float32
        )
        attn_term = attn_term + jnp.einsum(
            "rc,dc->rd", d_gate_logit, wg_full, preferred_element_type=jnp.float32
        )
        d_xn1 = lax.psum_scatter(
            attn_term.astype(jnp.bfloat16), "head", scatter_dimension=0, tiled=True
        ).astype(jnp.float32)
        gain_attn = gain_attn + jnp.sum(d_xn1 * normed1, axis=0)
        input_grads.append(
            (d_hidden1 + norm_back(d_xn1, normed1, scale1, attn_norm_gain)).astype(jnp.bfloat16)
        )
        batch_grads = reduce_grads(
            grad_query, grad_key, grad_value, grad_headgate, grad_out, grad_gate, grad_up, grad_down
        )
        if grad_total is None:
            grad_total = batch_grads
        else:
            grad_total = tuple((a + b for a, b in zip(grad_total, batch_grads)))
    sum_attn, sum_query, sum_key, sum_ffn = lax.psum(
        (gain_attn, gain_query, gain_key, gain_ffn), ("dp", "head", "mp")
    )
    return (
        jnp.stack(outputs),
        jnp.stack(input_grads),
        sum_attn,
        sum_query,
        sum_key,
        grad_total[0],
        grad_total[1],
        grad_total[2],
        grad_total[3],
        grad_total[4],
        sum_ffn,
        grad_total[5],
        grad_total[6],
        grad_total[7],
    )


def solution(mesh):
    placed = (
        P(None, ("dp", "head", "mp"), None),
        P(None, ("dp", "head", "mp"), None),
        P(),
        P(),
        P(),
        P(),
        P(),
        P(("dp", "mp"), "head"),
        P(("dp", "mp"), "head"),
        P(("dp", "mp"), "head"),
        P(("dp", "mp"), "head"),
        P("head", ("dp", "mp")),
        P(),
        P(("dp", "head"), "mp"),
        P(("dp", "head"), "mp"),
        P("mp", ("dp", "head")),
    )
    return jax.shard_map(
        local,
        mesh=mesh,
        in_specs=placed,
        out_specs=(
            P(None, ("dp", "head", "mp"), None),
            P(None, ("dp", "head", "mp"), None),
            P(),
            P(),
            P(),
            P(("dp", "mp"), "head"),
            P(("dp", "mp"), "head"),
            P(("dp", "mp"), "head"),
            P(("dp", "mp"), "head"),
            P("head", ("dp", "mp")),
            P(),
            P(("dp", "head"), "mp"),
            P(("dp", "head"), "mp"),
            P("mp", ("dp", "head")),
        ),
        check_vma=False,
    )
```

profile of v0, /device:TPU:0, one launch (start us, length us, event | category | flops | bytes accessed | tf_op | source)
XLA Modules:
  0.0 3029.3 jit_solution(16326290270986205264)
XLA Ops:
  14.9 38.1 %all-gather.26.cloned.1.call-done = bf16[2048,256]{1,0:T(8,128)(2,1)} async-done(((bf16[256,256]{1,0:T(8,128)(2,1)}), bf16[2048,256]{1,0:T(8,128)(2,1)}) %all-gather.26.cloned.1.call-update) | async-done | bytes 1048592 | tf_op jit(solution)/shard_map/all_gather | solution.py:128
  53.0 35.4 %all-gather.20.cloned.1.call-done = bf16[1024,2048]{1,0:T(8,128)(2,1)} async-done(((bf16[256,2048]{1,0:T(8,128)(2,1)}), bf16[1024,2048]{1,0:T(8,128)(2,1)}) %all-gather.20.cloned.1.call-update) | async-done | bytes 4194320 | tf_op jit(solution)/shard_map/all_gather | solution.py:238
  92.3 32.8 %all-gather.42.cloned.1.call-done = bf16[1024,2048]{1,0:T(8,128)(2,1)} async-done(((bf16[256,2048]{1,0:T(8,128)(2,1)}), bf16[1024,2048]{1,0:T(8,128)(2,1)}) %all-gather.42.cloned.1.call-update) | async-done | bytes 4194320 | tf_op jit(solution)/shard_map/all_gather | solution.py:238
  131.1 36.3 %all-gather.22.cloned.1.call-done = bf16[2048,256]{1,0:T(8,128)(2,1)} async-done(((bf16[256,256]{1,0:T(8,128)(2,1)}), bf16[2048,256]{1,0:T(8,128)(2,1)}) %all-gather.22.cloned.1.call-update) | async-done | bytes 1048592 | tf_op jit(solution)/shard_map/all_gather | solution.py:129
  245.8 45.1 %while.78 = (s32[]{:T(128)}, f32[2,2,1024]{2,1,0:T(2,128)S(1)}, f32[2,2,1024]{2,1,0:T(2,128)S(1)}, s32[4,512]{1,0:T(4,128)S(1)}, s32[]{:T(128)}, /*index=5*/bf16...) while((s32[]{:T(128)}, f32[2,2,1024]{2,1,0:T(2,128)S(1)}, ...), condition=%wide.region_7.8_spmd.clone, body=%wide.region_4.7_spmd.clone.sunk | while | flops 550538752 | bytes 19889288 | solution.py:75
  293.1 30.0 while.79
  345.7 42.0 %while.80 = (s32[]{:T(128)}, f32[2,2,1024]{2,1,0:T(2,128)S(1)}, f32[2,2,1024]{2,1,0:T(2,128)S(1)}, s32[4,512]{1,0:T(4,128)S(1)}, s32[]{:T(128)}, /*index=5*/bf16...) while((s32[]{:T(128)}, f32[2,2,1024]{2,1,0:T(2,128)S(1)}, ...), condition=%wide.region_19.20_spmd.clone, body=%wide.region_16.19_spmd.clone.sunk | while | flops 550538752 | bytes 19889288 | solution.py:75
  425.9 43.7 %reduce-scatter.41.cloned.1.call-done = bf16[256,2048]{1,0:T(8,128)(2,1)} async-done(((bf16[1024,2048]{1,0:T(8,128)(2,1)}), bf16[256,2048]{1,0:T(8,128)(2,1)}) %reduce-scatter.41.cloned.1.call-update) | async-done | bytes 1048592 | tf_op jit(solution)/shard_map/reduce_scatter | solution.py:272
  507.7 102.9 %all-gather.36.cloned.1.call-done = bf16[2048,3072]{1,0:T(8,128)(2,1)} async-done(((bf16[128,3072]{1,0:T(8,128)(2,1)}), bf16[2048,3072]{1,0:T(8,128)(2,1)}) %all-gather.36.cloned.1.call-update) | async-done | bytes 12582928 | tf_op jit(solution)/shard_map/all_gather | solution.py:134
  622.6 89.1 %all-gather.38.cloned.1.call-done = bf16[2048,3072]{1,0:T(8,128)(2,1)} async-done(((bf16[128,3072]{1,0:T(8,128)(2,1)}), bf16[2048,3072]{1,0:T(8,128)(2,1)}) %all-gather.38.cloned.1.call-update) | async-done | bytes 12582928 | tf_op jit(solution)/shard_map/all_gather | solution.py:135
  744.5 106.0 %all-gather.40.cloned.1.call-done = bf16[3072,2048]{1,0:T(8,128)(2,1)} async-done(((bf16[3072,128]{1,0:T(8,128)(2,1)}), bf16[3072,2048]{1,0:T(8,128)(2,1)}) %all-gather.40.cloned.1.call-update) | async-done | bytes 12582928 | tf_op jit(solution)/shard_map/all_gather | solution.py:136
  997.2 30.1 reduce-scatter.43.cloned.1.call-done
  1027.3 34.2 %reduce-scatter.39.cloned.1.call-done = bf16[256,2048]{1,0:T(8,128)(2,1)} async-done(((bf16[512,2048]{1,0:T(8,128)(2,1)}), bf16[256,2048]{1,0:T(8,128)(2,1)}) %reduce-scatter.39.cloned.1.call-update) | async-done | bytes 1048592 | tf_op jit(solution)/shard_map/reduce_scatter | solution.py:293
  1119.4 86.9 %while.82 = (s32[]{:T(128)}, f32[1024,2,2,128]{0,3,2,1:T(8,128)}, bf16[4,512,2,128]{3,1,2,0:T(8,128)(2,1)}, bf16[4,512,2,128]{3,1,2,0:T(8,128)(2,1)}, bf16[4,512...) while((s32[]{:T(128)}, f32[1024,2,2,128]{0,3,2,1:T(8,128)}, ...), condition=%wide.region_29.30_spmd.clone, body=%wide.region_28.29_spmd.clone.sunk | while | flops 2703244800 | bytes 150797744 | solution.py:119
  1224.5 82.3 %while.83 = (s32[]{:T(128)}, f32[1024,2,2,128]{0,3,2,1:T(8,128)S(1)}, bf16[4,512,2,128]{3,1,2,0:T(8,128)(2,1)}, bf16[4,512,2,128]{3,1,2,0:T(8,128)(2,1)}, bf16[4...) while((s32[]{:T(128)}, ...), condition=%wide.region_41.42_spmd.clone, body=%wide.region_40.41_spmd.clone.sunk | while | flops 2703244800 | bytes 150797744 | solution.py:119
  1537.8 39.5 %reduce-scatter.63.cloned.1.call-done = bf16[256,512]{1,0:T(8,128)(2,1)} async-done(((bf16[2048,512]{1,0:T(8,128)(2,1)}), bf16[256,512]{1,0:T(8,128)(2,1)}) %reduce-scatter.63.cloned.1.call-update) | async-done | bytes 262160 | tf_op jit(solution)/shard_map/reduce_scatter | solution.py:143
  1577.4 70.8 %reduce-scatter.61.cloned.1.call-done = bf16[256,512]{1,0:T(8,128)(2,1)} async-done(((bf16[2048,512]{1,0:T(8,128)(2,1)}), bf16[256,512]{1,0:T(8,128)(2,1)}) %reduce-scatter.61.cloned.1.call-update) | async-done | bytes 262160 | tf_op jit(solution)/shard_map/reduce_scatter | solution.py:143
  1650.1 69.0 %reduce-scatter.75.cloned.1.call-done = bf16[512,256]{1,0:T(8,128)(2,1)} async-done(((bf16[512,2048]{1,0:T(8,128)(2,1)}), bf16[512,256]{1,0:T(8,128)(2,1)}) %reduce-scatter.75.cloned.1.call-update) | async-done | bytes 262160 | tf_op jit(solution)/shard_map/reduce_scatter | solution.py:155
  1719.1 70.9 %reduce-scatter.73.cloned.1.call-done = bf16[512,256]{1,0:T(8,128)(2,1)} async-done(((bf16[512,2048]{1,0:T(8,128)(2,1)}), bf16[512,256]{1,0:T(8,128)(2,1)}) %reduce-scatter.73.cloned.1.call-update) | async-done | bytes 262160 | tf_op jit(solution)/shard_map/reduce_scatter | solution.py:155
  1791.9 64.4 %reduce-scatter.67.cloned.1.call-done = bf16[256,256]{1,0:T(8,128)(2,1)} async-done(((bf16[2048,256]{1,0:T(8,128)(2,1)}), bf16[256,256]{1,0:T(8,128)(2,1)}) %reduce-scatter.67.cloned.1.call-update) | async-done | bytes 131088 | tf_op jit(solution)/shard_map/reduce_scatter | solution.py:146
  1856.3 66.0 %reduce-scatter.65.cloned.1.call-done = bf16[256,256]{1,0:T(8,128)(2,1)} async-done(((bf16[2048,256]{1,0:T(8,128)(2,1)}), bf16[256,256]{1,0:T(8,128)(2,1)}) %reduce-scatter.65.cloned.1.call-update) | async-done | bytes 131088 | tf_op jit(solution)/shard_map/reduce_scatter | solution.py:146
  1923.9 64.1 %reduce-scatter.71.cloned.1.call-done = bf16[256,256]{1,0:T(8,128)(2,1)} async-done(((bf16[2048,256]{1,0:T(8,128)(2,1)}), bf16[256,256]{1,0:T(8,128)(2,1)}) %reduce-scatter.71.cloned.1.call-update) | async-done | bytes 131088 | tf_op jit(solution)/shard_map/reduce_scatter | solution.py:149
  1988.0 66.7 %reduce-scatter.69.cloned.1.call-done = bf16[256,256]{1,0:T(8,128)(2,1)} async-done(((bf16[2048,256]{1,0:T(8,128)(2,1)}), bf16[256,256]{1,0:T(8,128)(2,1)}) %reduce-scatter.69.cloned.1.call-update) | async-done | bytes 131088 | tf_op jit(solution)/shard_map/reduce_scatter | solution.py:149
  2056.5 136.2 %reduce-scatter.91.cloned.1.call-done = bf16[128,3072]{1,0:T(8,128)(2,1)} async-done(((bf16[2048,3072]{1,0:T(8,128)(2,1)}), bf16[128,3072]{1,0:T(8,128)(2,1)}) %reduce-scatter.91.cloned.1.call-update) | async-done | bytes 786448
  2194.1 136.5 %reduce-scatter.89.cloned.1.call-done = bf16[128,3072]{1,0:T(8,128)(2,1)} async-done(((bf16[2048,3072]{1,0:T(8,128)(2,1)}), bf16[128,3072]{1,0:T(8,128)(2,1)}) %reduce-scatter.89.cloned.1.call-update) | async-done | bytes 786448
  2333.4 135.2 %reduce-scatter.79.cloned.1.call-done = bf16[128,3072]{1,0:T(8,128)(2,1)} async-done(((bf16[2048,3072]{1,0:T(8,128)(2,1)}), bf16[128,3072]{1,0:T(8,128)(2,1)}) %reduce-scatter.79.cloned.1.call-update) | async-done | bytes 786448 | tf_op jit(solution)/shard_map/reduce_scatter | solution.py:160
  2468.6 137.9 %reduce-scatter.77.cloned.1.call-done = bf16[128,3072]{1,0:T(8,128)(2,1)} async-done(((bf16[2048,3072]{1,0:T(8,128)(2,1)}), bf16[128,3072]{1,0:T(8,128)(2,1)}) %reduce-scatter.77.cloned.1.call-update) | async-done | bytes 786448 | tf_op jit(solution)/shard_map/reduce_scatter | solution.py:160
  2609.2 135.3 %reduce-scatter.83.cloned.1.call-done = bf16[128,3072]{1,0:T(8,128)(2,1)} async-done(((bf16[2048,3072]{1,0:T(8,128)(2,1)}), bf16[128,3072]{1,0:T(8,128)(2,1)}) %reduce-scatter.83.cloned.1.call-update) | async-done | bytes 786448 | tf_op jit(solution)/shard_map/reduce_scatter | solution.py:163
  2744.5 137.8 %reduce-scatter.81.cloned.1.call-done = bf16[128,3072]{1,0:T(8,128)(2,1)} async-done(((bf16[2048,3072]{1,0:T(8,128)(2,1)}), bf16[128,3072]{1,0:T(8,128)(2,1)}) %reduce-scatter.81.cloned.1.call-update) | async-done | bytes 786448 | tf_op jit(solution)/shard_map/reduce_scatter | solution.py:163
  2885.0 43.3 %reduce-scatter.51.cloned.1.call-done = bf16[256,2048]{1,0:T(8,128)(2,1)} async-done(((bf16[1024,2048]{1,0:T(8,128)(2,1)}), bf16[256,2048]{1,0:T(8,128)(2,1)}) %reduce-scatter.51.cloned.1.call-update) | async-done | bytes 1048592 | tf_op jit(solution)/shard_map/reduce_scatter | solution.py:386
  2928.3 47.1 %reduce-scatter.59.cloned.1.call-done = bf16[256,2048]{1,0:T(8,128)(2,1)} async-done(((bf16[1024,2048]{1,0:T(8,128)(2,1)}), bf16[256,2048]{1,0:T(8,128)(2,1)}) %reduce-scatter.59.cloned.1.call-update) | async-done | bytes 1048592 | tf_op jit(solution)/shard_map/reduce_scatter | solution.py:386
  2982.8 39.7 %all-reduce = (f32[2048]{0:T(1024)}, f32[128]{0:T(128)}, f32[128]{0:T(128)}, f32[2048]{0:T(1024)}) all-reduce(f32[2048]{0:T(1024)S(1)} %add.482, f32[128]{0:T(128)S(1)} %add.483, f32[128]{0:T(128)S(1)} %add.484, f32[2048]{0:T(1024)S(1)} %add.490), channel_id=1, replica_groups=mesh['dp'=4,'head'=4,'mp'=2] {'dp','head','mp'}, use_global_device_ids=true, to_apply=%region_51.52 | all-reduce | flops 4352 | bytes 34816 | tf_op jit(solution)/shard_map/psum | solution.py:400
  (840 shorter events, 1031.3 us)
Async XLA Ops:
  12.7 154.7 %all-gather.22.cloned.1.call-start = ((), (), s32[]{:S(2)}) async-start(), calls=%async_computation.29 | async-start | bytes 1179648 | tf_op jit(solution)/shard_map/all_gather | solution.py:129
  13.3 204.2 %all-gather.30.cloned.1.call-start = ((), (), s32[]{:S(2)}) async-start(), calls=%async_computation.33 | async-start | bytes 2359296 | tf_op jit(solution)/shard_map/all_gather | solution.py:127
  13.8 229.5 %all-gather.28.cloned.1.call-start = ((), (), s32[]{:S(2)}) async-start(), calls=%async_computation.32 | async-start | bytes 1572864 | tf_op jit(solution)/shard_map/all_gather | solution.py:256
  131.0 159.9 %all-gather.24.cloned.1.call-start = ((), (), s32[]{:S(2)}) async-start(), calls=%async_computation.30 | async-start | bytes 1572864 | tf_op jit(solution)/shard_map/all_gather | solution.py:257
  173.0 166.4 %all-gather.32.cloned.1.call-start = ((), (), s32[]{:S(2)}) async-start(), calls=%async_computation.34 | async-start | bytes 2359296 | tf_op jit(solution)/shard_map/all_gather | solution.py:131
  173.8 214.0 %all-gather.44.cloned.1.call-start = ((), (), s32[]{:S(2)}) async-start(), calls=%async_computation.42 | async-start | bytes 1572864 | tf_op jit(solution)/shard_map/all_gather | solution.py:257
  238.1 187.8 %reduce-scatter.37.cloned.1.call-start = ((), (), s32[]{:S(2)}) async-start(), calls=%async_computation.35 | async-start | bytes 5242880 | tf_op jit(solution)/shard_map/reduce_scatter | solution.py:272
  475.0 236.7 %all-gather.38.cloned.1.call-start = ((), (), s32[]{:S(2)}) async-start(), calls=%async_computation.38 | async-start | bytes 13369344 | tf_op jit(solution)/shard_map/all_gather | solution.py:135
  475.6 268.9 %all-gather.50.cloned.1.call-start = ((), (), s32[]{:S(2)}) async-start(), calls=%async_computation.47 | async-start | bytes 3145728 | tf_op jit(solution)/shard_map/all_gather | solution.py:286
  478.7 371.7 %all-gather.40.cloned.1.call-start = ((), (), s32[]{:S(2)}) async-start(), calls=%async_computation.39 | async-start | bytes 13369344 | tf_op jit(solution)/shard_map/all_gather | solution.py:136
  479.3 411.6 %all-gather.48.cloned.1.call-start = ((), (), s32[]{:S(2)}) async-start(), calls=%async_computation.45 | async-start | bytes 3145728 | tf_op jit(solution)/shard_map/all_gather | solution.py:285
  479.9 438.0 %all-gather.54.cloned.1.call-start = ((), (), s32[]{:S(2)}) async-start(), calls=%async_computation.53 | async-start | bytes 3145728 | tf_op jit(solution)/shard_map/all_gather | solution.py:286
  480.6 503.1 %reduce-scatter.45.cloned.1.call-start = ((), (), s32[]{:S(2)}) async-start(), calls=%async_computation.48 | async-start | bytes 3145728 | tf_op jit(solution)/shard_map/reduce_scatter | solution.py:311
  1074.1 288.1 %reduce-scatter.47.cloned.1.call-start = ((), (), s32[]{:S(2)}) async-start(), calls=%async_computation.50 | async-start | bytes 1572864 | tf_op jit(solution)/shard_map/reduce_scatter | solution.py:343
  1315.6 219.7 %reduce-scatter.87.cloned.1.call-start = ((), (), s32[]{:S(2)}) async-start(), calls=%async_computation.72 | async-start | bytes 589824
  1325.6 210.7 %reduce-scatter.85.cloned.1.call-start = ((), (), s32[]{:S(2)}) async-start(), calls=%async_computation.71 | async-start | bytes 589824
  1333.2 244.2 %reduce-scatter.63.cloned.1.call-start = ((), (), s32[]{:S(2)}) async-start(), calls=%async_computation.60 | async-start | bytes 2359296 | tf_op jit(solution)/shard_map/reduce_scatter | solution.py:143
  1340.7 307.5 %reduce-scatter.61.cloned.1.call-start = ((), (), s32[]{:S(2)}) async-start(), calls=%async_computation.59 | async-start | bytes 2359296 | tf_op jit(solution)/shard_map/reduce_scatter | solution.py:143
  1347.5 371.6 %reduce-scatter.75.cloned.1.call-start = ((), (), s32[]{:S(2)}) async-start(), calls=%async_computation.66 | async-start | bytes 2359296 | tf_op jit(solution)/shard_map/reduce_scatter | solution.py:155
  1354.6 435.4 %reduce-scatter.73.cloned.1.call-start = ((), (), s32[]{:S(2)}) async-start(), calls=%async_computation.65 | async-start | bytes 2359296 | tf_op jit(solution)/shard_map/reduce_scatter | solution.py:155
  1361.6 494.6 %reduce-scatter.67.cloned.1.call-start = ((), (), s32[]{:S(2)}) async-start(), calls=%async_computation.62 | async-start | bytes 1179648 | tf_op jit(solution)/shard_map/reduce_scatter | solution.py:146
  1372.3 549.9 %reduce-scatter.65.cloned.1.call-start = ((), (), s32[]{:S(2)}) async-start(), calls=%async_computation.61 | async-start | bytes 1179648 | tf_op jit(solution)/shard_map/reduce_scatter | solution.py:146
  1378.0 610.0 %reduce-scatter.71.cloned.1.call-start = ((), (), s32[]{:S(2)}) async-start(), calls=%async_computation.64 | async-start | bytes 1179648 | tf_op jit(solution)/shard_map/reduce_scatter | solution.py:149
  1382.7 672.0 %reduce-scatter.69.cloned.1.call-start = ((), (), s32[]{:S(2)}) async-start(), calls=%async_computation.63 | async-start | bytes 1179648 | tf_op jit(solution)/shard_map/reduce_scatter | solution.py:149
  1387.6 805.1 %reduce-scatter.91.cloned.1.call-start = ((), (), s32[]{:S(2)}) async-start(), calls=%async_computation.74 | async-start | bytes 13369344
  1416.1 914.5 %reduce-scatter.89.cloned.1.call-start = ((), (), s32[]{:S(2)}) async-start(), calls=%async_computation.73 | async-start | bytes 13369344
  1446.0 1022.6 %reduce-scatter.79.cloned.1.call-start = ((), (), s32[]{:S(2)}) async-start(), calls=%async_computation.68 | async-start | bytes 13369344 | tf_op jit(solution)/shard_map/reduce_scatter | solution.py:160
  1459.1 1147.4 %reduce-scatter.77.cloned.1.call-start = ((), (), s32[]{:S(2)}) async-start(), calls=%async_computation.67 | async-start | bytes 13369344 | tf_op jit(solution)/shard_map/reduce_scatter | solution.py:160
  1472.2 1272.3 %reduce-scatter.83.cloned.1.call-start = ((), (), s32[]{:S(2)}) async-start(), calls=%async_computation.70 | async-start | bytes 13369344 | tf_op jit(solution)/shard_map/reduce_scatter | solution.py:163
  1484.1 1398.2 %reduce-scatter.81.cloned.1.call-start = ((), (), s32[]{:S(2)}) async-start(), calls=%async_computation.69 | async-start | bytes 13369344 | tf_op jit(solution)/shard_map/reduce_scatter | solution.py:163
  1495.7 1432.7 %reduce-scatter.51.cloned.1.call-start = ((), (), s32[]{:S(2)}) async-start(), calls=%async_computation.52 | async-start | bytes 5242880 | tf_op jit(solution)/shard_map/reduce_scatter | solution.py:386
  1514.3 1461.1 %reduce-scatter.59.cloned.1.call-start = ((), (), s32[]{:S(2)}) async-start(), calls=%async_computation.58 | async-start | bytes 5242880 | tf_op jit(solution)/shard_map/reduce_scatter | solution.py:386
  (199 other events, 5181.0 us)
Sparse Core Ops, SparseCore 0:
  10.2 42.8 all-gather.25
  55.2 33.2 all-gather.19
  90.6 34.4 all-gather.41
  127.1 40.2 all-gather.21
  169.3 48.1 all-gather.29
  288.3 51.0 all-gather.31
  362.8 44.4 reduce-scatter.36
  425.9 43.6 reduce-scatter.40
  509.8 100.7 all-gather.35
  612.8 98.9 all-gather.37
  746.5 103.9 all-gather.39
  884.7 33.0 all-gather.53
  1068.3 34.4 all-gather.51
  1104.4 34.4 all-gather.55
  1380.7 61.8 reduce-scatter.86
  1446.3 60.8 reduce-scatter.84
  1510.8 66.5 reduce-scatter.62
  1581.3 66.8 reduce-scatter.60
  1651.7 67.3 reduce-scatter.74
  1722.6 67.3 reduce-scatter.72
  1793.8 62.3 reduce-scatter.66
  1859.9 62.3 reduce-scatter.64
  1925.6 62.3 reduce-scatter.70
  1992.3 62.4 reduce-scatter.68
  2058.8 133.7 reduce-scatter.90
  2196.7 133.8 reduce-scatter.88
  2334.7 133.9 reduce-scatter.78
  2472.5 133.9 reduce-scatter.76
  2610.5 133.8 reduce-scatter.82
  2748.4 133.8 reduce-scatter.80
  2884.7 43.6 reduce-scatter.50
  2930.9 44.4 reduce-scatter.58
  (15 shorter events, 386.2 us)
where the time goes:
time: 3040 us; the launch traced here: 3030 us
  waiting for transfers between devices  2090 us (69%)
  matrix products  559 us (18%)
  local copies, waits for them, and re-layouts  145 us (5%)
  other arithmetic  145 us (5%)
  blocking collectives  66.3 us (2%)
    unnamed x51, waiting for transfers between devices  279 us
    reduce_scatter x2, waiting for transfers between devices, reduce_grads(): lax.psum_scatter(g_up.astype(jnp.bfloat16), ('dp', 'head'), scatter_dimen...  273 us
    reduce_scatter x2, waiting for transfers between devices, reduce_grads(): lax.psum_scatter(g_gate.astype(jnp.bfloat16), ('dp', 'head'), scatter_dim...  273 us
    reduce_scatter x2, waiting for transfers between devices, reduce_grads(): lax.psum_scatter(g_out.astype(jnp.bfloat16), ('dp', 'mp'), scatter_dimens...  140 us
    reduce_scatter x2, waiting for transfers between devices, reduce_grads(): lax.psum_scatter(g_value.astype(jnp.bfloat16), ('dp', 'mp'), scatter_dime...  131 us
    reduce_scatter x2, waiting for transfers between devices, reduce_grads(): lax.psum_scatter(g_key.astype(jnp.bfloat16), ('dp', 'mp'), scatter_dimens...  130 us
    reduce_scatter x2, waiting for transfers between devices, reduce_grads(): lax.psum_scatter(g_query.astype(jnp.bfloat16), ('dp', 'mp'), scatter_dime...  110 us
    all_gather x1, waiting for transfers between devices, gather_weights(): lax.all_gather(w_down, ('dp', 'head'), axis=1, tiled=True)  106 us
  transfers between devices with their start and end apart: 47, of which 33 were waited for; matrix products, arithmetic and copies ran while one was open for 26% of the time, Pallas kernels for 0%

commit v1 on v0

--- a/solution.py
+++ b/solution.py
@@ -1,6 +1,10 @@
+import functools
+
 import jax
 import jax.numpy as jnp
 from jax import lax
+from jax.experimental import pallas as pl
+from jax.experimental.pallas import tpu as pltpu
 from jax.sharding import PartitionSpec as P
 
 EPS = 1e-06
@@ -418,6 +422,531 @@
     )
 
 
+PLANE = ("head", "mp")
+BIT_X, BIT_C, BIT_Y = 1, 2, 4
+NT = (((1,), (1,)), ((), ()))
+NN = (((1,), (0,)), ((), ()))
+TN = (((0,), (0,)), ((), ()))
+F32 = jnp.float32
+BF16 = jnp.bfloat16
+
+
+def dot(left, right, dims=NN):
+    return lax.dot_general(left, right, dims, preferred_element_type=F32)
+
+
+def swap(values, bits):
+    return lax.ppermute(values, PLANE, [(i, i ^ bits) for i in range(8)])
+
+
+def swap_mixed(values):
+    return lax.ppermute(
+        values, PLANE, [(i, i ^ (BIT_Y if i & BIT_C else BIT_X)) for i in range(8)]
+    )
+
+
+def gather_rows(rows, core):
+    from_x = swap(rows, BIT_X)
+    from_y = swap(rows, BIT_Y)
+    diagonal = swap_mixed(jnp.where(core == 0, from_y, from_x))
+    mine = jnp.concatenate([rows, from_x, from_y, diagonal], axis=0)
+    return (mine, swap(mine, BIT_C))
+
+
+def scatter_rows(mine, other, core):
+    count = mine.shape[0] // 4
+    summed = (mine + swap(other.astype(BF16), BIT_C).astype(F32)).astype(BF16)
+    own, to_x, to_y, diagonal = [summed[k * count : (k + 1) * count] for k in range(4)]
+    passed = swap_mixed(diagonal).astype(F32)
+    zero = jnp.zeros((), F32)
+    to_x = (to_x.astype(F32) + jnp.where(core == 1, passed, zero)).astype(BF16)
+    to_y = (to_y.astype(F32) + jnp.where(core == 0, passed, zero)).astype(BF16)
+    return own.astype(F32) + swap(to_x, BIT_X).astype(F32) + swap(to_y, BIT_Y).astype(F32)
+
+
+def norm_rope(raw, gain, cosine, sine):
+    scale_rows = lax.rsqrt(jnp.mean(raw * raw, axis=-1, keepdims=True) + EPS)
+    hat = raw * scale_rows
+    turned = hat * gain
+    return (turned * cosine + pltpu.roll(turned, 64, 1) * sine, hat, scale_rows)
+
+
+def norm_rope_back(grad, hat, scale_rows, gain, cosine, sine):
+    grad_n = grad * cosine - pltpu.roll(grad, 64, 1) * sine
+    gain_part = jnp.sum(grad_n * hat, axis=0, keepdims=True)
+    scaled = grad_n * gain
+    raw = scale_rows * (scaled - hat * jnp.mean(scaled * hat, axis=-1, keepdims=True))
+    return (raw, gain_part)
+
+
+def two_lanes(first, second, shape):
+    lane = lax.broadcasted_iota(jnp.int32, shape, 1)
+    return jnp.where(lane == 0, first, jnp.where(lane == 1, second, 0.0))
+
+
+def attend_forward_kernel(
+    table, proj, cosine, sine, q_gain, k_gain, gated, attn_o, lse, keys, values, acc
+):
+    step = pl.program_id(0)
+    rows = proj.shape[0]
+    live = table[8]
+    cos_b, sin_b = cosine[...], sine[...]
+    here = pl.multiple_of(step * rows, rows)
+    key, _, _ = norm_rope(proj[:, 256:384], k_gain[...], cos_b, sin_b)
+    keys[pl.ds(here, rows), :] = key.astype(BF16)
+    values[pl.ds(here, rows), 0:128] = proj[:, 384:512].astype(BF16)
+    values[pl.ds(here, rows), 128:256] = jnp.ones((rows, 128), BF16)
+    q_scale = 128**-0.5
+    first, _, _ = norm_rope(proj[:, 0:128], q_gain[...], cos_b, sin_b)
+    second, _, _ = norm_rope(proj[:, 128:256], q_gain[...], cos_b, sin_b)
+    query = (jnp.concatenate([first, second], axis=0) * q_scale).astype(BF16)
+    row = lax.broadcasted_iota(jnp.int32, (2 * rows, rows), 0)
+    column = lax.broadcasted_iota(jnp.int32, (2 * rows, rows), 1)
+    scores = dot(query, keys[pl.ds(here, rows), :], NT)
+    allowed = (column <= jnp.where(row >= rows, row - rows, row)) & (column + here < live)
+    weight = jnp.where(allowed, jnp.exp(scores), 0.0).astype(BF16)
+    acc[...] = dot(weight, values[pl.ds(here, rows), :])
+
+    def block(index, carry):
+        there = pl.multiple_of(index * rows, rows)
+        part = dot(query, keys[pl.ds(there, rows), :], NT)
+        kept = jnp.where(column + there < live, jnp.exp(part), 0.0).astype(BF16)
+        acc[...] += dot(kept, values[pl.ds(there, rows), :])
+        return carry
+
+    lax.fori_loop(0, step, block, 0)
+    total = acc[:, 128:129]
+    out = acc[:, 0:128] / total
+    log_total = jnp.log(total)
+    gate0 = jax.nn.sigmoid(proj[:, 512:513])
+    gate1 = jax.nn.sigmoid(proj[:, 513:514])
+    attn_o[:, 0:128] = out[:rows]
+    attn_o[:, 128:256] = out[rows:]
+    gated[:, 0:128] = (out[:rows] * gate0).astype(BF16)
+    gated[:, 128:256] = (out[rows:] * gate1).astype(BF16)
+    lse[...] = two_lanes(log_total[:rows], log_total[rows:], (rows, 128))
+
+
+def attend_backward_kernel(
+    table,
+    proj,
+    d_gated,
+    attn_o,
+    lse,
+    cosine,
+    sine,
+    q_gain,
+    k_gain,
+    d_proj,
+    gain_q,
+    gain_k,
+    keys,
+    keys_t,
+    values,
+    k_raw,
+    d_keys,
+    d_values,
+    d_query,
+):
+    step = pl.program_id(0)
+    rows = proj.shape[0]
+    live = table[8]
+    here = pl.multiple_of(step * rows, rows)
+    slot = pl.multiple_of(table[step] * rows, rows)
+    cos_b, sin_b = cosine[pl.ds(here, rows), :], sine[pl.ds(here, rows), :]
+    raw_key = proj[:, 256:384]
+    k_raw[pl.ds(here, rows), :] = raw_key
+    key, _, _ = norm_rope(raw_key, k_gain[...], cos_b, sin_b)
+    key = key.astype(BF16)
+    keys[pl.ds(here, rows), :] = key
+    keys_t[step] = key.T
+    value = proj[:, 384:512].astype(BF16)
+    values[pl.ds(here, rows), :] = value
+    q_scale = 128**-0.5
+    first, hat0, scale0 = norm_rope(proj[:, 0:128], q_gain[...], cos_b, sin_b)
+    second, hat1, scale1 = norm_rope(proj[:, 128:256], q_gain[...], cos_b, sin_b)
+    query = (jnp.concatenate([first, second], axis=0) * q_scale).astype(BF16)
+    gate0 = jax.nn.sigmoid(proj[:, 512:513])
+    gate1 = jax.nn.sigmoid(proj[:, 513:514])
+    dg0, dg1 = d_gated[:, 0:128], d_gated[:, 128:256]
+    out0, out1 = attn_o[:, 0:128], attn_o[:, 128:256]
+    do0, do1 = (dg0 * gate0).astype(BF16), (dg1 * gate1).astype(BF16)
+    logit0 = jnp.sum(dg0 * out0, axis=-1, keepdims=True) * gate0 * (1.0 - gate0)
+    logit1 = jnp.sum(dg1 * out1, axis=-1, keepdims=True) * gate1 * (1.0 - gate1)
+    d_proj[pl.ds(slot, rows), 512:640] = two_lanes(logit0, logit1, (rows, 128)).astype(BF16)
+    delta0 = jnp.sum(do0.astype(F32) * out0, axis=-1, keepdims=True)
+    delta1 = jnp.sum(do1.astype(F32) * out1, axis=-1, keepdims=True)
+    delta_t = two_lanes(delta0, delta1, (rows, 128)).T
+    delta = jnp.concatenate([delta_t[0:1], delta_t[1:2]], axis=1)
+    lse_t = lse[...].T
+    log_total = jnp.concatenate([lse_t[0:1], lse_t[1:2]], axis=1)
+    d_out = jnp.concatenate([do0, do1], axis=0)
+    key_row = lax.broadcasted_iota(jnp.int32, (rows, 2 * rows), 0)
+    q_col = lax.broadcasted_iota(jnp.int32, (rows, 2 * rows), 1)
+
+    def pieces(key_b, value_b, allowed):
+        scores = dot(key_b, query, NT)
+        probs = jnp.where(allowed, jnp.exp(scores - log_total), 0.0)
+        d_probs = dot(value_b, d_out, NT)
+        d_scores = (probs * (d_probs - delta)).astype(BF16)
+        return (probs.astype(BF16), d_scores)
+
+    allowed = (key_row <= jnp.where(q_col >= rows, q_col - rows, q_col)) & (key_row + here < live)
+    probs, d_scores = pieces(key, value, allowed)
+    d_values[pl.ds(here, rows), :] = dot(probs, d_out)
+    d_keys[pl.ds(here, rows), :] = dot(d_scores, query)
+    d_query[...] = dot(keys_t[step], d_scores)
+
+    def block(index, carry):
+        there = pl.multiple_of(index * rows, rows)
+        probs, d_scores = pieces(
+            keys[pl.ds(there, rows), :], values[pl.ds(there, rows), :], key_row + there < live
+        )
+        d_values[pl.ds(there, rows), :] += dot(probs, d_out)
+        d_keys[pl.ds(there, rows), :] += dot(d_scores, query)
+        d_query[...] += dot(keys_t[index], d_scores)
+        return carry
+
+    lax.fori_loop(0, step, block, 0)
+    grads = d_query[...].T * q_scale
+    raw0, part0 = norm_rope_back(grads[:rows], hat0, scale0, q_gain[...], cos_b, sin_b)
+    raw1, part1 = norm_rope_back(grads[rows:], hat1, scale1, q_gain[...], cos_b, sin_b)
+    d_proj[pl.ds(slot, rows), 0:128] = raw0.astype(BF16)
+    d_proj[pl.ds(slot, rows), 128:256] = raw1.astype(BF16)
+
+    @pl.when(step == 0)
+    def _():
+        gain_q[...] = jnp.zeros_like(gain_q)
+        gain_k[...] = jnp.zeros_like(gain_k)
+
+    gain_q[0:1, :] += part0 + part1
+
+    @pl.when(step == pl.num_programs(0) - 1)
+    def _():
+        def finish(index, carry):
+            there = pl.multiple_of(index * rows, rows)
+            to_slot = pl.multiple_of(table[index] * rows, rows)
+            cos_k, sin_k = cosine[pl.ds(there, rows), :], sine[pl.ds(there, rows), :]
+            _, hat, scale_rows = norm_rope(k_raw[pl.ds(there, rows), :], k_gain[...], cos_k, sin_k)
+            raw, part = norm_rope_back(
+                d_keys[pl.ds(there, rows), :], hat, scale_rows, k_gain[...], cos_k, sin_k
+            )
+            gain_k[0:1, :] += part
+            d_proj[pl.ds(to_slot, rows), 256:384] = raw.astype(BF16)
+            d_proj[pl.ds(to_slot, rows), 384:512] = d_values[pl.ds(there, rows), :].astype(BF16)
+            return carry
+
+        lax.fori_loop(0, pl.num_programs(0), finish, 0)
+
+
+def attend_costs(seq_len, matmuls):
+    pairs = 2 * seq_len * (seq_len + 256) // 2
+    return pl.CostEstimate(
+        flops=2 * matmuls * pairs * 128, bytes_accessed=12 * seq_len * 640, transcendentals=pairs
+    )
+
+
+def attend_forward_call(table, proj, cosine, sine, q_gain, k_gain):
+    seq_len = proj.shape[0]
+    rows = seq_len // 8
+    by_slot = lambda i, t: (t[i], 0)
+    by_place = lambda i, t: (i, 0)
+    fixed = lambda i, t: (0, 0)
+    return pl.pallas_call(
+        attend_forward_kernel,
+        grid_spec=pltpu.PrefetchScalarGridSpec(
+            num_scalar_prefetch=1,
+            grid=(8,),
+            in_specs=[
+                pl.BlockSpec((rows, 640), by_slot),
+                pl.BlockSpec((rows, 128), by_place),
+                pl.BlockSpec((rows, 128), by_place),
+                pl.BlockSpec((1, 128), fixed),
+                pl.BlockSpec((1, 128), fixed),
+            ],
+            out_specs=[
+                pl.BlockSpec((rows, 256), by_slot),
+                pl.BlockSpec((rows, 256), by_slot),
+                pl.BlockSpec((rows, 128), by_slot),
+            ],
+            scratch_shapes=[
+                pltpu.VMEM((seq_len, 128), BF16),
+                pltpu.VMEM((seq_len, 256), BF16),
+                pltpu.VMEM((2 * rows, 256), F32),
+            ],
+        ),
+        out_shape=[
+            jax.ShapeDtypeStruct((seq_len, 256), BF16),
+            jax.ShapeDtypeStruct((seq_len, 256), F32),
+            jax.ShapeDtypeStruct((seq_len, 128), F32),
+        ],
+        compiler_params=pltpu.CompilerParams(
+            dimension_semantics=("arbitrary",), vmem_limit_bytes=32 << 20
+        ),
+        cost_estimate=attend_costs(seq_len, 2),
+        name="attend_forward",
+    )(table, proj, cosine, sine, q_gain, k_gain)
+
+
+def attend_backward_call(table, proj, d_gated, attn_o, lse, cosine, sine, q_gain, k_gain):
+    seq_len = proj.shape[0]
+    rows = seq_len // 8
+    by_slot = lambda i, t: (t[i], 0)
+    fixed = lambda i, t: (0, 0)
+    return pl.pallas_call(
+        attend_backward_kernel,
+        grid_spec=pltpu.PrefetchScalarGridSpec(
+            num_scalar_prefetch=1,
+            grid=(8,),
+            in_specs=[
+                pl.BlockSpec((rows, 640), by_slot),
+                pl.BlockSpec((rows, 256), by_slot),
+                pl.BlockSpec((rows, 256), by_slot),
+                pl.BlockSpec((rows, 128), by_slot),
+                pl.BlockSpec((seq_len, 128), fixed),
+                pl.BlockSpec((seq_len, 128), fixed),
+                pl.BlockSpec((1, 128), fixed),
+                pl.BlockSpec((1, 128), fixed),
+            ],
+            out_specs=[
+                pl.BlockSpec((seq_len, 640), fixed),
+                pl.BlockSpec((8, 128), fixed),
+                pl.BlockSpec((8, 128), fixed),
+            ],
+            scratch_shapes=[
+                pltpu.VMEM((seq_len, 128), BF16),
+                pltpu.VMEM((8, 128, rows), BF16),
+                pltpu.VMEM((seq_len, 128), BF16),
+                pltpu.VMEM((seq_len, 128), F32),
+                pltpu.VMEM((seq_len, 128), F32),
+                pltpu.VMEM((seq_len, 128), F32),
+                pltpu.VMEM((128, 2 * rows), F32),
+            ],
+        ),
+        out_shape=[
+            jax.ShapeDtypeStruct((seq_len, 640), BF16),
+            jax.ShapeDtypeStruct((8, 128), F32),
+            jax.ShapeDtypeStruct((8, 128), F32),
+        ],
+        compiler_params=pltpu.CompilerParams(
+            dimension_semantics=("arbitrary",), vmem_limit_bytes=40 << 20
+        ),
+        cost_estimate=attend_costs(seq_len, 5),
+        name="attend_backward",
+    )(table, proj, d_gated, attn_o, lse, cosine, sine, q_gain, k_gain)
+
+
+def pick(flag, first, second):
+    return jnp.where(flag, first, second)
+
+
+def reorder_by(pieces, index):
+    low, high = (index & 1) == 1, (index & 2) == 2
+    swapped = [pick(low, pieces[j ^ 1], pieces[j]) for j in range(4)]
+    return [pick(high, swapped[j ^ 2], swapped[j]) for j in range(4)]
+
+
+def local_plane(
+    inputs,
+    cotangent,
+    seq_counts,
+    seq_bucket,
+    attn_norm_gain,
+    q_norm_gain,
+    k_norm_gain,
+    w_query,
+    w_key,
+    w_value,
+    w_headgate,
+    w_out,
+    ffn_norm_gain,
+    w_gate,
+    w_up,
+    w_down,
+):
+    micro_batches, row_count, model_width = inputs.shape
+    n_dp = lax.axis_size("dp")
+    head_idx = lax.axis_index("head")
+    mp_idx = lax.axis_index("mp")
+    dp_idx = lax.axis_index("dp")
+    core = head_idx & 1
+    plane_idx = head_idx * 2 + mp_idx
+    seq_len = row_count * 8
+    ffn_cols = w_gate.shape[1] // 4
+    slot_ids = jnp.arange(micro_batches * n_dp, dtype=jnp.int32)
+    slot_count = jnp.sum(
+        jnp.where(seq_bucket[None, :] == slot_ids[:, None], seq_counts[None, :], 0), axis=1
+    )
+    own_pos = plane_idx * row_count + jnp.arange(row_count, dtype=jnp.int32)
+    apart = jnp.arange(8, dtype=jnp.int32) ^ plane_idx
+    slots = (apart & 1) | ((apart & 4) >> 1) | ((apart & 2) << 1)
+    table_cos, table_sin = rope_tables(jnp.arange(seq_len, dtype=jnp.int32), 64)
+    table_cos, table_sin = table_cos[:, 0, :], table_sin[:, 0, :]
+    cosine = jnp.concatenate([table_cos, table_cos], axis=1)
+    sine = jnp.concatenate([-table_sin, table_sin], axis=1)
+    q_gain, k_gain = q_norm_gain[None, :], k_norm_gain[None, :]
+
+    spare = jnp.zeros((row_count, 126), BF16)
+    halves = [
+        jnp.concatenate(
+            [
+                w_query[:, k * 256 : (k + 1) * 256],
+                w_key[:, k * 128 : (k + 1) * 128],
+                w_value[:, k * 128 : (k + 1) * 128],
+                w_headgate[:, k * 2 : (k + 1) * 2],
+                spare,
+                w_out[k * 256 : (k + 1) * 256, :].T,
+            ],
+            axis=1,
+        )
+        for k in range(2)
+    ]
+    is_first = mp_idx == 0
+    kept = pick(is_first, halves[0], halves[1])
+    came = swap(pick(is_first, halves[1], halves[0]), BIT_X)
+    attn_rows = jnp.concatenate([pick(is_first, kept, came), pick(is_first, came, kept)], axis=0)
+    attn_full = lax.all_gather(attn_rows, "dp", axis=0, tiled=True)
+    w_proj, w_out_t = attn_full[:, :640], attn_full[:, 640:]
+
+    down_t = w_down.T
+    quarters = jnp.stack(
+        [
+            jnp.concatenate(
+                [w[:, k * ffn_cols : (k + 1) * ffn_cols] for w in (w_gate, w_up, down_t)], axis=1
+            )
+            for k in range(4)
+        ]
+    )
+    traded = [lax.dynamic_index_in_dim(quarters, head_idx, 0, False)] + [
+        swap(lax.dynamic_index_in_dim(quarters, head_idx ^ r, 0, False), r * 2) for r in (1, 2, 3)
+    ]
+    ffn_rows = jnp.concatenate(reorder_by(traded, head_idx), axis=0)
+    w_gate_up = lax.all_gather(ffn_rows[:, : 2 * ffn_cols], "dp", axis=0, tiled=True)
+    w_down_t = lax.all_gather(ffn_rows[:, 2 * ffn_cols :], "dp", axis=0, tiled=True)
+
+    outputs, input_grads = ([], [])
+    gain_attn = jnp.zeros((model_width,), F32)
+    gain_ffn = jnp.zeros((model_width,), F32)
+    gain_query = jnp.zeros((128,), F32)
+    gain_key = jnp.zeros((128,), F32)
+    grad_gate_up = grad_down_t = grad_proj = grad_out_t = None
+
+    def plus(total, term):
+        return term if total is None else total + term
+
+    for micro_batch in range(micro_batches):
+        live_count = slot_count[micro_batch * n_dp + dp_idx]
+        table = jnp.concatenate([slots, live_count[None]]).astype(jnp.int32)
+        x_float = inputs[micro_batch].astype(F32)
+        scale1 = rms_scale(x_float)
+        normed1 = x_float * scale1
+        xn1 = gather_rows((normed1 * attn_norm_gain).astype(BF16), core)
+        live = (own_pos < live_count).astype(F32)[:, None]
+        cot_live = cotangent[micro_batch].astype(F32) * live
+        cot_rows = gather_rows(cot_live.astype(BF16), core)
+        proj = jnp.concatenate([dot(piece, w_proj) for piece in xn1], axis=0)
+        gated, attn_o, lse = attend_forward_call(table, proj, cosine, sine, q_gain, k_gain)
+        half = seq_len // 2
+        gated_pieces = (gated[:half], gated[half:])
+        out_other = dot(gated_pieces[1], w_out_t, NT)
+        out_mine = dot(gated_pieces[0], w_out_t, NT)
+        hidden1 = x_float + scatter_rows(out_mine, out_other, core)
+        scale2 = rms_scale(hidden1)
+        normed2 = hidden1 * scale2
+        xn2 = gather_rows((normed2 * ffn_norm_gain).astype(BF16), core)
+        down_parts, back_parts = ([], [])
+        for xn2_piece, cot_piece in zip(xn2, cot_rows):
+            pre = dot(xn2_piece, w_gate_up)
+            gate_pre, up_pre = pre[:, :ffn_cols], pre[:, ffn_cols:]
+            gate_sig = jax.nn.sigmoid(gate_pre)
+            gate_act = gate_pre * gate_sig
+            hidden = (gate_act * up_pre).astype(BF16)
+            d_hidden = dot(cot_piece, w_down_t)
+            d_up = (d_hidden * gate_act).astype(BF16)
+            d_gate = (d_hidden * up_pre * gate_sig * (1.0 + gate_pre * (1.0 - gate_sig))).astype(
+                BF16
+            )
+            d_both = jnp.concatenate([d_gate, d_up], axis=1)
+            down_parts.append(dot(hidden, w_down_t, NT))
+            back_parts.append(dot(d_both, w_gate_up, NT))
+            grad_gate_up = plus(grad_gate_up, dot(xn2_piece, d_both, TN))
+            grad_down_t = plus(grad_down_t, dot(cot_piece, hidden, TN))
+        outputs.append((hidden1 + scatter_rows(down_parts[0], down_parts[1], core)).astype(BF16))
+        d_xn2 = scatter_rows(back_parts[0], back_parts[1], core)
+        gain_ffn = gain_ffn + jnp.sum(d_xn2 * normed2, axis=0)
+        d_hidden1 = cot_live + norm_back(d_xn2, normed2, scale2, ffn_norm_gain)
+        d_attn = gather_rows(d_hidden1.astype(BF16), core)
+        d_gated = jnp.concatenate([dot(piece, w_out_t) for piece in d_attn], axis=0)
+        for d_piece, gated_piece in zip(d_attn, gated_pieces):
+            grad_out_t = plus(grad_out_t, dot(d_piece, gated_piece, TN))
+        d_proj, part_q, part_k = attend_backward_call(
+            table, proj, d_gated, attn_o, lse, cosine, sine, q_gain, k_gain
+        )
+        gain_query = gain_query + part_q[0]
+        gain_key = gain_key + part_k[0]
+        d_pieces = (d_proj[:half], d_proj[half:])
+        for x_piece, d_piece in zip(xn1, d_pieces):
+            grad_proj = plus(grad_proj, dot(x_piece, d_piece, TN))
+        term_other = dot(d_pieces[1], w_proj, NT)
+        term_mine = dot(d_pieces[0], w_proj, NT)
+        d_xn1 = scatter_rows(term_mine, term_other, core)
+        gain_attn = gain_attn + jnp.sum(d_xn1 * normed1, axis=0)
+        input_grads.append(
+            (d_hidden1 + norm_back(d_xn1, normed1, scale1, attn_norm_gain)).astype(BF16)
+        )
+
+    sum_ffn = [
+        lax.psum_scatter(g.astype(BF16), "dp", scatter_dimension=0, tiled=True)
+        for g in (grad_gate_up, grad_down_t)
+    ]
+    ffn_sum = jnp.concatenate(sum_ffn, axis=1).reshape(4, -1, 3 * ffn_cols)
+    back = [lax.dynamic_index_in_dim(ffn_sum, head_idx, 0, False)] + [
+        swap(lax.dynamic_index_in_dim(ffn_sum, head_idx ^ r, 0, False), r * 2) for r in (1, 2, 3)
+    ]
+    back = reorder_by(back, head_idx)
+    grad_gate, grad_up, grad_down = [
+        jnp.concatenate([b[:, k * ffn_cols : (k + 1) * ffn_cols] for b in back], axis=1).astype(F32)
+        for k in range(3)
+    ]
+    grad_down = grad_down.T
+    attn_grads = jnp.concatenate([grad_proj, grad_out_t], axis=1).astype(BF16)
+    attn_sum = lax.psum_scatter(attn_grads, "dp", scatter_dimension=0, tiled=True)
+    upper, lower = attn_sum[:row_count], attn_sum[row_count:]
+    kept = pick(is_first, upper, lower)
+    came = swap(pick(is_first, lower, upper), BIT_X)
+    by_half = [v.astype(F32) for v in (pick(is_first, kept, came), pick(is_first, came, kept))]
+    grad_query = jnp.concatenate([v[:, 0:256] for v in by_half], axis=1)
+    grad_key = jnp.concatenate([v[:, 256:384] for v in by_half], axis=1)
+    grad_value = jnp.concatenate([v[:, 384:512] for v in by_half], axis=1)
+    grad_headgate = jnp.concatenate([v[:, 512:514] for v in by_half], axis=1)
+    grad_out = jnp.concatenate([v[:, 640:896].T for v in by_half], axis=0)
+    sum_attn, sum_query, sum_key, sum_gain_ffn = lax.psum(
+        (gain_attn, gain_query, gain_key, gain_ffn), ("dp", "head", "mp")
+    )
+    return (
+        jnp.stack(outputs),
+        jnp.stack(input_grads),
+        sum_attn,
+        sum_query,
+        sum_key,
+        grad_query,
+        grad_key,
+        grad_value,
+        grad_headgate,
+        grad_out,
+        sum_gain_ffn,
+        grad_gate,
+        grad_up,
+        grad_down,
+    )
+
+
+def choose_local(mesh):
+    if mesh.shape["head"] == 4 and mesh.shape["mp"] == 2:
+        return local_plane
+    return local
+
+
 def solution(mesh):
     placed = (
         P(None, ("dp", "head", "mp"), None),
@@ -438,7 +967,7 @@
         P("mp", ("dp", "head")),
     )
     return jax.shard_map(
-        local,
+        choose_local(mesh),
         mesh=mesh,
         in_specs=placed,
         out_specs=(

time: 3040 us -> 1240 us (0.41)
  waiting for transfers between devices: 2090 us -> 494 us
  matrix products: 559 us -> 338 us
  Pallas kernels: 0 us -> 109 us
  local copies, waits for them, and re-layouts: 145 us -> 56.3 us
  starting transfers between devices: 4.49 us -> 75 us
  other arithmetic: 145 us -> 104 us
    reduce_scatter x24 -> x3, waiting for transfers between devices: 1270 us -> 0.06 us  [the longest x2 0.04 us: local_plane(): lax.psum_scatter(g.astype(BF16), 'dp', scatter_dimension=0, tiled=True)]
    all_gather x19 -> x3, waiting for transfers between devices: 547 us -> 34.9 us  [the longest x1 34.8 us: local_plane(): lax.all_gather(ffn_rows[:, 2 * ffn_cols:], 'dp', axis=0, tiled=True)]
    ppermute x0 -> x72, waiting for transfers between devices: none -> 459 us  [the longest x56 286 us: swap(): return lax.ppermute(values, PLANE, [(i, i ^ bits) for i in range(8)])]
    unnamed x51 -> x6, waiting for transfers between devices: 279 us -> 0.1 us
    dot_general x104 -> x48, matrix products: 559 us -> 338 us  [dot(): return lax.dot_general(left, right, dims, preferred_element_type=F32)]
    pallas_call x0 -> x4, Pallas kernels: none -> 109 us  [the longest x2 59.6 us: attend_backward_call(): pl.pallas_call(attend_backward_kernel, grid_spec=pltpu.PrefetchScalarGrid...]
    ppermute x0 -> x72, starting transfers between devices: none -> 74 us  [the longest x56 51.9 us: swap(): return lax.ppermute(values, PLANE, [(i, i ^ bits) for i in range(8)])]
    reduce_sum x23 -> x4, other arithmetic: 64.2 us -> 13.1 us  [the longest x2 9.3 us: local_plane(): gain_ffn = gain_ffn + jnp.sum(d_xn2 * normed2, axis=0)]
  transfers between devices with their start and end apart: 47 -> 78, of which waited for: 33 -> 47; matrix products, arithmetic and copies ran while one was open for 26% -> 35% of each run, Pallas kernels for 0% -> 9%
where the time goes in v1:
time: 1240 us; the launch traced here: 1230 us
  waiting for transfers between devices  494 us (40%)
  matrix products  338 us (27%)
  Pallas kernels  109 us (9%)
  other arithmetic  104 us (8%)
  starting transfers between devices  75 us (6%)
  local copies, waits for them, and re-layouts  56.3 us (5%)
  blocking collectives  38.7 us (3%)
  between operations  16.5 us (1%)
    dot_general x48, matrix products, dot(): return lax.dot_general(left, right, dims, preferred_element_type=F32)  338 us
    ppermute x56, waiting for transfers between devices, swap(): return lax.ppermute(values, PLANE, [(i, i ^ bits) for i in range(8)])  286 us
    ppermute x16, waiting for transfers between devices, swap_mixed(): lax.ppermute(values, PLANE, [(i, i ^ (BIT_Y if i & BIT_C else BIT_X)) for...  172 us
    pallas_call x2, Pallas kernels, attend_backward_call(): pl.pallas_call(attend_backward_kernel, grid_spec=pltpu.PrefetchScalarGrid...  59.6 us
    ppermute x56, starting transfers between devices, swap(): return lax.ppermute(values, PLANE, [(i, i ^ bits) for i in range(8)])  51.9 us
    pallas_call x2, Pallas kernels, attend_forward_call(): pl.pallas_call(attend_forward_kernel, grid_spec=pltpu.PrefetchScalarGridS...  49 us
    psum x1, blocking collectives, local_plane(): lax.psum((gain_attn, gain_query, gain_key, gain_ffn), ('dp', 'head', 'mp'))  38.7 us
    all_gather x1, waiting for transfers between devices, local_plane(): lax.all_gather(ffn_rows[:, 2 * ffn_cols:], 'dp', axis=0, tiled=True)  34.8 us
  transfers between devices with their start and end apart: 78, of which 47 were waited for; matrix products, arithmetic and copies ran while one was open for 35% of the time, Pallas kernels for 9%

profile of v1, /device:TPU:0, one launch (start us, length us, event | category | flops | bytes accessed | tf_op | source)
XLA Modules:
  0.0 1231.1 jit_solution(10782394908400243009)
XLA Ops:
  29.9 13.7 %collective-permute-done.1 = bf16[256,2048]{1,0:T(8,128)(2,1)S(1)} collective-permute-done((bf16[256,2048]{1,0:T(8,128)(2,1)}, bf16[256,2048]{1,0:T(8,128)(2,1)S(1)}, u32[]{:S(2)}, u32[]{:S(2)}) %collective-permute-start.1) | collective-permute-done | bytes 1048608 | tf_op jit(solution)/shard_map/ppermute | solution.py:439
  53.2 22.1 %collective-permute-done.2 = bf16[256,2048]{1,0:T(8,128)(2,1)S(1)} collective-permute-done((bf16[256,2048]{1,0:T(8,128)(2,1)S(1)}, bf16[256,2048]{1,0:T(8,128)(2,1)S(1)}, u32[]{:S(2)}, u32[]{:S(2)}) %collective-permute-start.2) | collective-permute-done | bytes 1048608 | tf_op jit(solution)/shard_map/ppermute | solution.py:443
  129.4 24.5 %attend_forward.2 = (bf16[2048,256]{1,0:T(8,128)(2,1)S(1)}, f32[2048,256]{1,0:T(8,128)S(1)}, f32[2048,128]{1,0:T(8,128)S(1)}) custom-call(s32[9]{0:T(128)S(1)} %get-tuple-element.195.table, f32[2048,640]{1,0:T(8,128)S(1)} %pad_maximum_fusion.proj, f32[2048,128]{1,0:T(8,128)S(1)} %get-tuple-element.201.cosine, f32[2048,128]{1,0:T(8,128)S(1)} %get-tuple-element.202.sine, ...), custom_call_target="tpu_custom_call" | custom-call | flops 2415919104 | bytes 15728640 | tf_op jit(solution)/shard_map/attend_forward/pallas_call | solution.py:655
  164.4 24.5 %attend_forward.3 = (bf16[2048,256]{1,0:T(8,128)(2,1)S(1)}, f32[2048,256]{1,0:T(8,128)S(1)}, f32[2048,128]{1,0:T(8,128)S(1)}) custom-call(s32[9]{0:T(128)S(1)} %get-tuple-element.196.table, f32[2048,640]{1,0:T(8,128)S(1)} %pad_maximum_fusion.1.proj, f32[2048,128]{1,0:T(8,128)S(1)} %get-tuple-element.201.cosine, f32[2048,128]{1,0:T(8,128)S(1)} %copy-done.7, ...), custom_call_target="tpu_custom_call" | custom-call | flops 2415919104 | bytes 15728640 | tf_op jit(solution)/shard_map/attend_forward/pallas_call | solution.py:655
  213.3 13.5 %collective-permute-done.12 = bf16[128,2304]{0,1:T(8,128)(2,1)} collective-permute-done((bf16[128,2304]{0,1:T(8,128)(2,1)}, bf16[128,2304]{0,1:T(8,128)(2,1)}, u32[]{:S(2)}, u32[]{:S(2)}) %collective-permute-start.12) | collective-permute-done | bytes 589856 | tf_op jit(solution)/shard_map/ppermute | solution.py:439
  226.8 13.0 %collective-permute-done.13 = bf16[128,2304]{0,1:T(8,128)(2,1)} collective-permute-done((bf16[128,2304]{0,1:T(8,128)(2,1)}, bf16[128,2304]{0,1:T(8,128)(2,1)}, u32[]{:S(2)}, u32[]{:S(2)}) %collective-permute-start.13) | collective-permute-done | bytes 589856 | tf_op jit(solution)/shard_map/ppermute | solution.py:439
  267.3 15.2 %collective-permute-done.25 = bf16[256,2048]{1,0:T(8,128)(2,1)S(1)} collective-permute-done((bf16[256,2048]{1,0:T(8,128)(2,1)S(1)}, bf16[256,2048]{1,0:T(8,128)(2,1)S(1)}, u32[]{:S(2)}, u32[]{:S(2)}) %collective-permute-start.25) | collective-permute-done | bytes 1048608 | tf_op jit(solution)/shard_map/ppermute | solution.py:443
  290.4 14.6 %collective-permute-done.7 = bf16[256,2048]{1,0:T(8,128)(2,1)S(1)} collective-permute-done((bf16[256,2048]{1,0:T(8,128)(2,1)S(1)}, bf16[256,2048]{1,0:T(8,128)(2,1)S(1)}, u32[]{:S(2)}, u32[]{:S(2)}) %collective-permute-start.7) | collective-permute-done | bytes 1048608 | tf_op jit(solution)/shard_map/ppermute | solution.py:439
  328.2 19.6 %collective-permute-done.10 = bf16[256,2048]{1,0:T(8,128)(2,1)} collective-permute-done((bf16[256,2048]{1,0:T(8,128)(2,1)}, bf16[256,2048]{1,0:T(8,128)(2,1)}, u32[]{:S(2)}, u32[]{:S(2)}) %collective-permute-start.10) | collective-permute-done | bytes 1048608 | tf_op jit(solution)/shard_map/ppermute | solution.py:439
  354.3 21.6 %collective-permute-done.11 = bf16[256,2048]{1,0:T(8,128)(2,1)S(1)} collective-permute-done((bf16[256,2048]{1,0:T(8,128)(2,1)S(1)}, bf16[256,2048]{1,0:T(8,128)(2,1)S(1)}, u32[]{:S(2)}, u32[]{:S(2)}) %collective-permute-start.11) | collective-permute-done | bytes 1048608 | tf_op jit(solution)/shard_map/ppermute | solution.py:443
  391.2 12.4 %collective-permute-done.38 = bf16[256,2048]{1,0:T(8,128)(2,1)} collective-permute-done((bf16[256,2048]{1,0:T(8,128)(2,1)}, bf16[256,2048]{1,0:T(8,128)(2,1)}, u32[]{:S(2)}, u32[]{:S(2)}) %collective-permute-start.38) | collective-permute-done | bytes 1048608 | tf_op jit(solution)/shard_map/ppermute | solution.py:443
  407.3 11.8 fusion.167
  419.1 34.8 %all-gather.8.cloned.1.call-done = bf16[2048,768]{0,1:T(8,128)(2,1)} async-done(((bf16[512,768]{0,1:T(8,128)(2,1)}), bf16[2048,768]{0,1:T(8,128)(2,1)}) %all-gather.8.cloned.1.call-update) | async-done | bytes 3145744 | tf_op jit(solution)/shard_map/all_gather | solution.py:825
  463.5 12.8 %convolution_convert_fusion.1 = bf16[1024,2048]{1,0:T(8,128)(2,1)} fusion(bf16[2048,1536]{0,1:T(8,128)(2,1)} %all-gather.6.cloned.1.call-done, bf16[1024,768]{1,0:T(8,128)(2,1)S(1)} %get-tuple-element.93, bf16[1024,768]{1,0:T(8,128)(2,1)S(1)} %get-tuple-element.92), kind=kOutput, calls=%fused_computation.22 | convolution fusion | flops 6450839552 | bytes 13631488 | tf_op jit(solution)/shard_map/dot_general | solution.py:435
  481.8 11.6 fusion.148
  531.8 14.8 %collective-permute-done.17 = bf16[256,2048]{1,0:T(8,128)(2,1)S(1)} collective-permute-done((bf16[256,2048]{1,0:T(8,128)(2,1)S(1)}, bf16[256,2048]{1,0:T(8,128)(2,1)S(1)}, u32[]{:S(2)}, u32[]{:S(2)}) %collective-permute-start.17) | collective-permute-done | bytes 1048608 | tf_op jit(solution)/shard_map/ppermute | solution.py:443
  555.0 14.1 %collective-permute-done.42 = bf16[256,2048]{1,0:T(8,128)(2,1)S(1)} collective-permute-done((bf16[256,2048]{1,0:T(8,128)(2,1)S(1)}, bf16[256,2048]{1,0:T(8,128)(2,1)S(1)}, u32[]{:S(2)}, u32[]{:S(2)}) %collective-permute-start.42) | collective-permute-done | bytes 1048608 | tf_op jit(solution)/shard_map/ppermute | solution.py:439
  591.8 22.0 %collective-permute-done.29 = bf16[256,2048]{1,0:T(8,128)(2,1)S(1)} collective-permute-done((bf16[256,2048]{1,0:T(8,128)(2,1)S(1)}, bf16[256,2048]{1,0:T(8,128)(2,1)S(1)}, u32[]{:S(2)}, u32[]{:S(2)}) %collective-permute-start.29) | collective-permute-done | bytes 1048608 | tf_op jit(solution)/shard_map/ppermute | solution.py:439
  617.0 19.4 %collective-permute-done.53 = bf16[256,2048]{1,0:T(8,128)(2,1)S(1)} collective-permute-done((bf16[256,2048]{1,0:T(8,128)(2,1)S(1)}, bf16[256,2048]{1,0:T(8,128)(2,1)S(1)}, u32[]{:S(2)}, u32[]{:S(2)}) %collective-permute-start.53) | collective-permute-done | bytes 1048608 | tf_op jit(solution)/shard_map/ppermute | solution.py:439
  647.4 10.8 collective-permute-done.54
  667.2 11.8 fusion.71
  687.3 12.2 fusion.168
  722.5 14.3 %fusion.147 = f32[1024,1536]{1,0:T(8,128)} fusion(bf16[2048,1536]{0,1:T(8,128)(2,1)} %all-gather.6.cloned.1.call-done, bf16[256,2048]{1,0:T(8,128)(2,1)S(1)} %collective-permute-done.30, bf16[256,2048]{1,0:T(8,128)(2,1)S(1)} %collective-permute-done.29, bf16[256,2048]{1,0:T(8,128)(2,1)S(1)} %collective-permute-done.28, ...), kind=kOutput, calls=%fused_computation.314 | convolution fusion | flops 6459228160 | bytes 16777216 | tf_op jit(solution)/shard_map/dot_general | solution.py:435
  772.7 13.6 %collective-permute-done.33 = bf16[256,2048]{1,0:T(8,128)(2,1)S(1)} collective-permute-done((bf16[256,2048]{1,0:T(8,128)(2,1)S(1)}, bf16[256,2048]{1,0:T(8,128)(2,1)S(1)}, u32[]{:S(2)}, u32[]{:S(2)}) %collective-permute-start.33) | collective-permute-done | bytes 1048608 | tf_op jit(solution)/shard_map/ppermute | solution.py:443
  808.9 10.6 collective-permute-done.35
  838.7 11.8 fusion.70
  897.6 20.4 %add_convert_fusion = bf16[2048,1536]{1,0:T(8,128)(2,1)} fusion(f32[2048,1536]{1,0:T(8,128)} %fusion.68, f32[2048,1536]{1,0:T(8,128)} %fusion.71, f32[2048,1536]{1,0:T(8,128)} %fusion.70, bf16[1024,2048]{1,0:T(8,128)(2,1)} %copy-done.117, bf16[1024,768]{1,0:T(8,128)(2,1)} %copy-done.133, bf16[1024,768]{1,0:T(8,128)(2,1)S(1)} %copy-done.132), kind=kOutput, calls=%fused_computation | convolution fusion | flops 6461325312 | bytes 51380224 | tf_op jit(solution)/shard_map/dot_general | solution.py:435
  935.1 29.8 %attend_backward.2 = (bf16[2048,640]{1,0:T(8,128)(2,1)S(1)}, f32[8,128]{1,0:T(8,128)S(1)}, f32[8,128]{1,0:T(8,128)S(1)}) custom-call(s32[9]{0:T(128)S(1)} %get-tuple-element.195.table, f32[2048,640]{1,0:T(8,128)} %copy-done.1, f32[2048,256]{1,0:T(8,128)S(1)} %pad_maximum_fusion.19.d_gated, f32[2048,256]{1,0:T(8,128)S(1)} %copy-done.16, ...), custom_call_target="tpu_custom_call" | custom-call | flops 6039797760 | bytes 15728640 | tf_op jit(solution)/shard_map/attend_backward/pallas_call | solution.py:696
  976.0 29.8 %attend_backward.3 = (bf16[2048,640]{1,0:T(8,128)(2,1)S(1)}, f32[8,128]{1,0:T(8,128)S(1)}, f32[8,128]{1,0:T(8,128)S(1)}) custom-call(s32[9]{0:T(128)S(1)} %get-tuple-element.196.table, f32[2048,640]{1,0:T(8,128)} %copy-done, f32[2048,256]{1,0:T(8,128)S(1)} %pad_maximum_fusion.20.d_gated, f32[2048,256]{1,0:T(8,128)S(1)} %copy-done.14, ...), custom_call_target="tpu_custom_call" | custom-call | flops 6039797760 | bytes 15728640 | tf_op jit(solution)/shard_map/attend_backward/pallas_call | solution.py:696
  1071.6 13.2 %collective-permute-done.70 = bf16[128,2304]{0,1:T(8,128)(2,1)} collective-permute-done((bf16[128,2304]{0,1:T(8,128)(2,1)}, bf16[128,2304]{0,1:T(8,128)(2,1)}, u32[]{:S(2)}, u32[]{:S(2)}) %collective-permute-start.70) | collective-permute-done | bytes 589856 | tf_op jit(solution)/shard_map/ppermute | solution.py:439
  1112.3 13.1 %collective-permute-done.65 = bf16[256,2048]{1,0:T(8,128)(2,1)S(1)} collective-permute-done((bf16[256,2048]{1,0:T(8,128)(2,1)S(1)}, bf16[256,2048]{1,0:T(8,128)(2,1)S(1)}, u32[]{:S(2)}, u32[]{:S(2)}) %collective-permute-start.65) | collective-permute-done | bytes 1048608 | tf_op jit(solution)/shard_map/ppermute | solution.py:443
  1176.8 38.7 %all-reduce = (f32[2048]{0:T(1024)}, f32[128]{0:T(128)}, f32[128]{0:T(128)}, f32[2048]{0:T(1024)}) all-reduce(f32[2048]{0:T(1024)S(1)} %add.382, f32[128]{0:T(128)S(1)} %copy-done.115, f32[128]{0:T(128)S(1)} %copy-done.116, f32[2048]{0:T(1024)S(1)} %add.393), channel_id=1, replica_groups=mesh['dp'=4,'head'=4,'mp'=2] {'dp','head','mp'}, use_global_device_ids=true, to_apply=%region_11.12 | all-reduce | flops 4352 | bytes 34816 | tf_op jit(solution)/shard_map/psum | solution.py:923
  (630 shorter events, 648.3 us)
Async XLA Ops:
  7.2 104.6 %all-gather.4.cloned.1.call-start = ((), (), s32[]{:S(2)}) async-start(), calls=%async_computation.3 | async-start | bytes 4587520 | tf_op jit(solution)/shard_map/all_gather | solution.py:808
  29.7 377.6 %all-gather.6.cloned.1.call-start = ((), (), s32[]{:S(2)}) async-start(), calls=%async_computation.4 | async-start | bytes 7864320 | tf_op jit(solution)/shard_map/all_gather | solution.py:824
  52.7 34.0 %collective-permute-start.20 = (bf16[256,2048]{1,0:T(8,128)(2,1)}, bf16[256,2048]{1,0:T(8,128)(2,1)S(1)}, u32[]{:S(2)}, u32[]{:S(2)}) collective-permute-start(bf16[256,2048]{1,0:T(8,128)(2,1)} %get-tuple-element.138), channel_id=1, source_target_pairs={{0,1},{1,0},{2,3},{3,2},{4,5},{5,4},{6,7},{7,6},{8,9},{9,8},{10,11... | collective-permute-start | bytes 3145736 | tf_op jit(solution)/shard_map/ppermute | solution.py:439
  79.1 44.0 %collective-permute-start.4 = (bf16[1024,2048]{1,0:T(8,128)(2,1)}, bf16[1024,2048]{1,0:T(8,128)(2,1)}, u32[]{:S(2)}, u32[]{:S(2)}) collective-permute-start(bf16[1024,2048]{1,0:T(8,128)(2,1)} %pad_maximum_fusion.2), channel_id=1, source_target_pairs={{0,2},{1,3},{2,0},{3,1},{4,6},{5,7},{6,4},{7,5},{8,10},{9,11},{10,... | collective-permute-start | bytes 12582920 | tf_op jit(solution)/shard_map/ppermute | solution.py:439
  107.4 50.4 %collective-permute-start.23 = (bf16[1024,2048]{1,0:T(8,128)(2,1)}, bf16[1024,2048]{1,0:T(8,128)(2,1)}, u32[]{:S(2)}, u32[]{:S(2)}) collective-permute-start(bf16[1024,2048]{1,0:T(8,128)(2,1)} %pad_maximum_fusion.4), channel_id=1, source_target_pairs={{0,2},{1,3},{2,0},{3,1},{4,6},{5,7},{6,4},{7,5},{8,10},{9,11},{10,... | collective-permute-start | bytes 12582920 | tf_op jit(solution)/shard_map/ppermute | solution.py:439
  157.3 87.4 %collective-permute-start.5 = (bf16[1024,2048]{1,0:T(8,128)(2,1)}, bf16[1024,2048]{1,0:T(8,128)(2,1)}, u32[]{:S(2)}, u32[]{:S(2)}) collective-permute-start(bf16[1024,2048]{1,0:T(8,128)(2,1)} %convolution_convert_fusion.5), channel_id=1, source_target_pairs={{0,2},{1,3},{2,0},{3,1},{4,6},{5,7},{6,4},{7,5},{8,10},{9,11},{10,... | collective-permute-start | bytes 12582920 | tf_op jit(solution)/shard_map/ppermute | solution.py:439
  192.4 57.9 %collective-permute-start.24 = (bf16[1024,2048]{1,0:T(8,128)(2,1)}, bf16[1024,2048]{1,0:T(8,128)(2,1)}, u32[]{:S(2)}, u32[]{:S(2)}) collective-permute-start(bf16[1024,2048]{1,0:T(8,128)(2,1)} %convolution_convert_fusion.4), channel_id=1, source_target_pairs={{0,2},{1,3},{2,0},{3,1},{4,6},{5,7},{6,4},{7,5},{8,10},{9,11},{10,... | collective-permute-start | bytes 12582920 | tf_op jit(solution)/shard_map/ppermute | solution.py:439
  244.3 209.7 %all-gather.8.cloned.1.call-start = ((), (), s32[]{:S(2)}) async-start(), calls=%async_computation.5 | async-start | bytes 3932160 | tf_op jit(solution)/shard_map/all_gather | solution.py:825
  265.8 39.2 %collective-permute-start.7 = (bf16[256,2048]{1,0:T(8,128)(2,1)S(1)}, bf16[256,2048]{1,0:T(8,128)(2,1)S(1)}, u32[]{:S(2)}, u32[]{:S(2)}) collective-permute-start(bf16[256,2048]{1,0:T(8,128)(2,1)S(1)} %get-tuple-element.112), channel_id=1, source_target_pairs={{0,1},{1,0},{2,3},{3,2},{4,5},{5,4},{6,7},{7,6},{8,9},{9,8},{10,11... | collective-permute-start | bytes 3145736 | tf_op jit(solution)/shard_map/ppermute | solution.py:439
  285.9 33.8 %collective-permute-start.26 = (bf16[256,2048]{1,0:T(8,128)(2,1)S(1)}, bf16[256,2048]{1,0:T(8,128)(2,1)S(1)}, u32[]{:S(2)}, u32[]{:S(2)}) collective-permute-start(bf16[256,2048]{1,0:T(8,128)(2,1)S(1)} %get-tuple-element.116), channel_id=1, source_target_pairs={{0,1},{1,0},{2,3},{3,2},{4,5},{5,4},{6,7},{7,6},{8,9},{9,8},{10,11... | collective-permute-start | bytes 3145736 | tf_op jit(solution)/shard_map/ppermute | solution.py:439
  353.8 33.3 %collective-permute-start.36 = (bf16[256,2048]{1,0:T(8,128)(2,1)S(1)}, bf16[256,2048]{1,0:T(8,128)(2,1)S(1)}, u32[]{:S(2)}, u32[]{:S(2)}) collective-permute-start(bf16[256,2048]{1,0:T(8,128)(2,1)S(1)} %get-tuple-element.140), channel_id=1, source_target_pairs={{0,1},{1,0},{2,3},{3,2},{4,5},{5,4},{6,7},{7,6},{8,9},{9,8},{10,11... | collective-permute-start | bytes 3145736 | tf_op jit(solution)/shard_map/ppermute | solution.py:439
  391.0 660.1 %reduce-scatter.8.cloned.1.call-start = ((), (), s32[]{:S(2)}) async-start(), calls=%async_computation.8 | async-start | bytes 3932160 | tf_op jit(solution)/shard_map/reduce_scatter | solution.py:899
  407.3 46.7 %collective-permute-start.39 = (bf16[1024,2048]{1,0:T(8,128)(2,1)}, bf16[1024,2048]{1,0:T(8,128)(2,1)}, u32[]{:S(2)}, u32[]{:S(2)}) collective-permute-start(bf16[1024,2048]{1,0:T(8,128)(2,1)} %pad_maximum_fusion.6), channel_id=1, source_target_pairs={{0,2},{1,3},{2,0},{3,1},{4,6},{5,7},{6,4},{7,5},{8,10},{9,11},{10,... | collective-permute-start | bytes 12582920 | tf_op jit(solution)/shard_map/ppermute | solution.py:439
  481.3 33.4 %collective-permute-start.16 = (bf16[1024,2048]{1,0:T(8,128)(2,1)}, bf16[1024,2048]{1,0:T(8,128)(2,1)S(1)}, u32[]{:S(2)}, u32[]{:S(2)}) collective-permute-start(bf16[1024,2048]{1,0:T(8,128)(2,1)} %convolution_convert_fusion.7), channel_id=1, source_target_pairs={{0,2},{1,3},{2,0},{3,1},{4,6},{5,7},{6,4},{7,5},{8,10},{9,11},{10,... | collective-permute-start | bytes 12582920 | tf_op jit(solution)/shard_map/ppermute | solution.py:439
  530.3 38.8 %collective-permute-start.42 = (bf16[256,2048]{1,0:T(8,128)(2,1)S(1)}, bf16[256,2048]{1,0:T(8,128)(2,1)S(1)}, u32[]{:S(2)}, u32[]{:S(2)}) collective-permute-start(bf16[256,2048]{1,0:T(8,128)(2,1)S(1)} %get-tuple-element.106), channel_id=1, source_target_pairs={{0,1},{1,0},{2,3},{3,2},{4,5},{5,4},{6,7},{7,6},{8,9},{9,8},{10,11... | collective-permute-start | bytes 3145736 | tf_op jit(solution)/shard_map/ppermute | solution.py:439
  549.7 34.6 %collective-permute-start.18 = (bf16[256,2048]{1,0:T(8,128)(2,1)S(1)}, bf16[256,2048]{1,0:T(8,128)(2,1)S(1)}, u32[]{:S(2)}, u32[]{:S(2)}) collective-permute-start(bf16[256,2048]{1,0:T(8,128)(2,1)S(1)} %get-tuple-element.110), channel_id=1, source_target_pairs={{0,1},{1,0},{2,3},{3,2},{4,5},{5,4},{6,7},{7,6},{8,9},{9,8},{10,11... | collective-permute-start | bytes 3145736 | tf_op jit(solution)/shard_map/ppermute | solution.py:439
  590.7 45.6 %collective-permute-start.53 = (bf16[256,2048]{1,0:T(8,128)(2,1)S(1)}, bf16[256,2048]{1,0:T(8,128)(2,1)S(1)}, u32[]{:S(2)}, u32[]{:S(2)}) collective-permute-start(bf16[256,2048]{1,0:T(8,128)(2,1)S(1)} %copy-done.80), channel_id=1, source_target_pairs={{0,4},{1,5},{2,6},{3,7},{4,0},{5,1},{6,2},{7,3},{8,12},{9,13},{10,... | collective-permute-start | bytes 3145736 | tf_op jit(solution)/shard_map/ppermute | solution.py:439
  591.3 45.1 %collective-permute-start.52 = (bf16[256,2048]{1,0:T(8,128)(2,1)S(1)}, bf16[256,2048]{1,0:T(8,128)(2,1)S(1)}, u32[]{:S(2)}, u32[]{:S(2)}) collective-permute-start(bf16[256,2048]{1,0:T(8,128)(2,1)S(1)} %copy-done.80), channel_id=1, source_target_pairs={{0,1},{1,0},{2,3},{3,2},{4,5},{5,4},{6,7},{7,6},{8,9},{9,8},{10,11... | collective-permute-start | bytes 3145736 | tf_op jit(solution)/shard_map/ppermute | solution.py:439
  647.3 40.0 %collective-permute-start.31 = (bf16[1024,2048]{1,0:T(8,128)(2,1)S(1)}, bf16[1024,2048]{1,0:T(8,128)(2,1)S(1)}, u32[]{:S(2)}, u32[]{:S(2)}) collective-permute-start(bf16[1024,2048]{1,0:T(8,128)(2,1)S(1)} %pad_maximum_fusion.5), channel_id=1, source_target_pairs={{0,2},{1,3},{2,0},{3,1},{4,6},{5,7},{6,4},{7,5},{8,10},{9,11},{10,... | collective-permute-start | bytes 12582920 | tf_op jit(solution)/shard_map/ppermute | solution.py:439
  658.6 40.9 %collective-permute-start.55 = (bf16[1024,2048]{1,0:T(8,128)(2,1)S(1)}, bf16[1024,2048]{1,0:T(8,128)(2,1)}, u32[]{:S(2)}, u32[]{:S(2)}) collective-permute-start(bf16[1024,2048]{1,0:T(8,128)(2,1)S(1)} %pad_maximum_fusion.8), channel_id=1, source_target_pairs={{0,2},{1,3},{2,0},{3,1},{4,6},{5,7},{6,4},{7,5},{8,10},{9,11},{10,... | collective-permute-start | bytes 12582920 | tf_op jit(solution)/shard_map/ppermute | solution.py:439
  771.2 37.7 %collective-permute-start.58 = (bf16[256,2048]{1,0:T(8,128)(2,1)}, bf16[256,2048]{1,0:T(8,128)(2,1)}, u32[]{:S(2)}, u32[]{:S(2)}) collective-permute-start(bf16[256,2048]{1,0:T(8,128)(2,1)} %get-tuple-element.108), channel_id=1, source_target_pairs={{0,1},{1,0},{2,3},{3,2},{4,5},{5,4},{6,7},{7,6},{8,9},{9,8},{10,11... | collective-permute-start | bytes 3145736 | tf_op jit(solution)/shard_map/ppermute | solution.py:439
  788.3 36.7 %collective-permute-start.34 = (bf16[256,2048]{1,0:T(8,128)(2,1)}, bf16[256,2048]{1,0:T(8,128)(2,1)}, u32[]{:S(2)}, u32[]{:S(2)}) collective-permute-start(bf16[256,2048]{1,0:T(8,128)(2,1)} %get-tuple-element.114), channel_id=1, source_target_pairs={{0,1},{1,0},{2,3},{3,2},{4,5},{5,4},{6,7},{7,6},{8,9},{9,8},{10,11... | collective-permute-start | bytes 3145736 | tf_op jit(solution)/shard_map/ppermute | solution.py:439
  800.0 251.1 %reduce-scatter.6.cloned.1.call-start = ((), (), s32[]{:S(2)}) async-start(), calls=%async_computation.7 | async-start | bytes 7864320 | tf_op jit(solution)/shard_map/reduce_scatter | solution.py:899
  850.5 34.6 %collective-permute-start.61 = (bf16[256,2048]{1,0:T(8,128)(2,1)S(1)}, bf16[256,2048]{1,0:T(8,128)(2,1)S(1)}, u32[]{:S(2)}, u32[]{:S(2)}) collective-permute-start(bf16[256,2048]{1,0:T(8,128)(2,1)S(1)} %get-tuple-element.135), channel_id=1, source_target_pairs={{0,4},{1,5},{2,6},{3,7},{4,0},{5,1},{6,2},{7,3},{8,12},{9,13},{10,... | collective-permute-start | bytes 3145736 | tf_op jit(solution)/shard_map/ppermute | solution.py:439
  852.0 33.2 %collective-permute-start.60 = (bf16[256,2048]{1,0:T(8,128)(2,1)S(1)}, bf16[256,2048]{1,0:T(8,128)(2,1)S(1)}, u32[]{:S(2)}, u32[]{:S(2)}) collective-permute-start(bf16[256,2048]{1,0:T(8,128)(2,1)S(1)} %get-tuple-element.135), channel_id=1, source_target_pairs={{0,1},{1,0},{2,3},{3,2},{4,5},{5,4},{6,7},{7,6},{8,9},{9,8},{10,11... | collective-permute-start | bytes 3145736 | tf_op jit(solution)/shard_map/ppermute | solution.py:439
  918.0 249.6 %reduce-scatter.4.cloned.1.call-start = ((), (), s32[]{:S(2)}) async-start(), calls=%async_computation.6 | async-start | bytes 4587520 | tf_op jit(solution)/shard_map/reduce_scatter | solution.py:913
  921.7 49.0 %collective-permute-start.63 = (bf16[1024,2048]{1,0:T(8,128)(2,1)S(1)}, bf16[1024,2048]{1,0:T(8,128)(2,1)}, u32[]{:S(2)}, u32[]{:S(2)}) collective-permute-start(bf16[1024,2048]{1,0:T(8,128)(2,1)S(1)} %pad_maximum_fusion.9), channel_id=1, source_target_pairs={{0,2},{1,3},{2,0},{3,1},{4,6},{5,7},{6,4},{7,5},{8,10},{9,11},{10,... | collective-permute-start | bytes 12582920 | tf_op jit(solution)/shard_map/ppermute | solution.py:439
  969.9 116.5 %collective-permute-start.48 = (bf16[1024,2048]{1,0:T(8,128)(2,1)}, bf16[1024,2048]{1,0:T(8,128)(2,1)}, u32[]{:S(2)}, u32[]{:S(2)}) collective-permute-start(bf16[1024,2048]{1,0:T(8,128)(2,1)} %convolution_convert_fusion.3), channel_id=1, source_target_pairs={{0,2},{1,3},{2,0},{3,1},{4,6},{5,7},{6,4},{7,5},{8,10},{9,11},{10,... | collective-permute-start | bytes 12582920 | tf_op jit(solution)/shard_map/ppermute | solution.py:439
  1010.9 83.2 %collective-permute-start.64 = (bf16[1024,2048]{1,0:T(8,128)(2,1)}, bf16[1024,2048]{1,0:T(8,128)(2,1)}, u32[]{:S(2)}, u32[]{:S(2)}) collective-permute-start(bf16[1024,2048]{1,0:T(8,128)(2,1)} %convolution_convert_fusion.2), channel_id=1, source_target_pairs={{0,2},{1,3},{2,0},{3,1},{4,6},{5,7},{6,4},{7,5},{8,10},{9,11},{10,... | collective-permute-start | bytes 12582920 | tf_op jit(solution)/shard_map/ppermute | solution.py:439
  1110.9 37.1 %collective-permute-start.50 = (bf16[256,2048]{1,0:T(8,128)(2,1)}, bf16[256,2048]{1,0:T(8,128)(2,1)}, u32[]{:S(2)}, u32[]{:S(2)}) collective-permute-start(bf16[256,2048]{1,0:T(8,128)(2,1)} %get-tuple-element.104), channel_id=1, source_target_pairs={{0,1},{1,0},{2,3},{3,2},{4,5},{5,4},{6,7},{7,6},{8,9},{9,8},{10,11... | collective-permute-start | bytes 3145736 | tf_op jit(solution)/shard_map/ppermute | solution.py:439
  1129.1 34.7 %collective-permute-start.66 = (bf16[256,2048]{1,0:T(8,128)(2,1)}, bf16[256,2048]{1,0:T(8,128)(2,1)}, u32[]{:S(2)}, u32[]{:S(2)}) collective-permute-start(bf16[256,2048]{1,0:T(8,128)(2,1)} %get-tuple-element.102), channel_id=1, source_target_pairs={{0,1},{1,0},{2,3},{3,2},{4,5},{5,4},{6,7},{7,6},{8,9},{9,8},{10,11... | collective-permute-start | bytes 3145736 | tf_op jit(solution)/shard_map/ppermute | solution.py:439
  1169.6 49.0 %collective-permute-start.68 = (bf16[256,896]{0,1:T(8,128)(2,1)}, bf16[256,896]{0,1:T(8,128)(2,1)}, u32[]{:S(2)}, u32[]{:S(2)}) collective-permute-start(bf16[256,896]{0,1:T(8,128)(2,1)} %broadcast_select_fusion.20), channel_id=1, source_target_pairs={{0,1},{1,0},{2,3},{3,2},{4,5},{5,4},{6,7},{7,6},{8,9},{9,8},{10,11... | collective-permute-start | bytes 1376264 | tf_op jit(solution)/shard_map/ppermute | solution.py:439
  (199 other events, 4411.2 us)
Sparse Core Ops, SparseCore 0:
  29.8 73.9 all-gather.3
  244.4 116.6 all-gather.5
  391.1 62.8 all-gather.7
  800.1 58.7 reduce-scatter.7
  918.1 109.5 reduce-scatter.5
  1051.2 67.0 reduce-scatter.3

commit v2 on v1

--- a/solution.py
+++ b/solution.py
@@ -439,29 +439,62 @@
     return lax.ppermute(values, PLANE, [(i, i ^ bits) for i in range(8)])
 
 
-def swap_mixed(values):
+def swap_mixed(values, core0, core1):
     return lax.ppermute(
-        values, PLANE, [(i, i ^ (BIT_Y if i & BIT_C else BIT_X)) for i in range(8)]
-    )
-
-
-def gather_rows(rows, core):
-    from_x = swap(rows, BIT_X)
-    from_y = swap(rows, BIT_Y)
-    diagonal = swap_mixed(jnp.where(core == 0, from_y, from_x))
-    mine = jnp.concatenate([rows, from_x, from_y, diagonal], axis=0)
-    return (mine, swap(mine, BIT_C))
-
-
-def scatter_rows(mine, other, core):
-    count = mine.shape[0] // 4
-    summed = (mine + swap(other.astype(BF16), BIT_C).astype(F32)).astype(BF16)
-    own, to_x, to_y, diagonal = [summed[k * count : (k + 1) * count] for k in range(4)]
-    passed = swap_mixed(diagonal).astype(F32)
-    zero = jnp.zeros((), F32)
-    to_x = (to_x.astype(F32) + jnp.where(core == 1, passed, zero)).astype(BF16)
-    to_y = (to_y.astype(F32) + jnp.where(core == 0, passed, zero)).astype(BF16)
-    return own.astype(F32) + swap(to_x, BIT_X).astype(F32) + swap(to_y, BIT_Y).astype(F32)
+        values, PLANE, [(i, i ^ (core1 if i & BIT_C else core0)) for i in range(8)]
+    )
+
+
+class Gather:
+    def __init__(self, rows):
+        self.rows = rows
+        self.came = swap_mixed(rows, BIT_X, BIT_Y)
+
+    def second(self):
+        self.pair = jnp.concatenate([self.rows, self.came], axis=0)
+        self.came = swap_mixed(self.pair, BIT_Y, BIT_X)
+        return self.pair
+
+    def third(self):
+        self.mine = jnp.concatenate([self.pair, self.came], axis=0)
+        self.other = swap(self.mine, BIT_C)
+        return self.mine
+
+
+class Scatter:
+    def __init__(self, other):
+        self.came = swap(other, BIT_C)
+
+    def second(self, summed):
+        half = summed.shape[0] // 2
+        self.kept = summed[:half]
+        self.came = swap_mixed(summed[half:], BIT_Y, BIT_X)
+
+    def third(self):
+        pair = (self.kept.astype(F32) + self.came.astype(F32)).astype(BF16)
+        half = pair.shape[0] // 2
+        self.kept = pair[:half]
+        self.came = swap_mixed(pair[half:], BIT_X, BIT_Y)
+        return pair
+
+    def result(self):
+        return self.kept.astype(F32) + self.came.astype(F32)
+
+
+class Order:
+    def __init__(self):
+        self.ahead = []
+
+    def need(self, *values):
+        self.ahead.extend(values)
+
+    def run(self, op, *operands):
+        if self.ahead:
+            held = lax.optimization_barrier((tuple(operands), tuple(self.ahead)))
+            operands = held[0]
+        out = op(*operands)
+        self.ahead = [out[0] if isinstance(out, (tuple, list)) else out]
+        return out
 
 
 def norm_rope(raw, gain, cosine, sine):
@@ -736,6 +769,75 @@
     )(table, proj, d_gated, attn_o, lse, cosine, sine, q_gain, k_gain)
 
 
+def feed_forward_kernel(with_sum, *refs):
+    if with_sum:
+        rows, d_hidden, w_gate_up, w_down_t, down_in, back_in = refs[:6]
+        hidden_out, d_pre_out, down_out, back_out = refs[6:]
+    else:
+        rows, d_hidden, w_gate_up, w_down_t = refs[:4]
+        hidden_out, d_pre_out, down_out, back_out = refs[4:]
+    units = d_hidden.shape[1]
+    pre = dot(rows[...], w_gate_up[...])
+    gate_pre, up_pre = pre[:, :units], pre[:, units:]
+    gate_sig = jax.nn.sigmoid(gate_pre)
+    gate_act = gate_pre * gate_sig
+    d_hid = d_hidden[...].astype(F32)
+    hidden = (gate_act * up_pre).astype(BF16)
+    hidden_out[...] = hidden
+    d_pre_out[:, units:] = (d_hid * gate_act).astype(BF16)
+    d_pre_out[:, :units] = (
+        d_hid * up_pre * gate_sig * (1.0 + gate_pre * (1.0 - gate_sig))
+    ).astype(BF16)
+    back = dot(d_pre_out[...], w_gate_up[...], NT)
+    down = dot(hidden, w_down_t[...], NT)
+    if with_sum:
+        back = back + back_in[...].astype(F32)
+        down = down + down_in[...].astype(F32)
+    back_out[...] = back.astype(BF16)
+    down_out[...] = down.astype(BF16)
+
+
+def feed_forward_call(rows, d_hidden, w_gate_up, w_down_t, *sums):
+    count, width = rows.shape
+    units = d_hidden.shape[1]
+    tile = min(256, count)
+    by_row = lambda i: (i, 0)
+    fixed = lambda i: (0, 0)
+    wide = pl.BlockSpec((tile, width), by_row)
+    return pl.pallas_call(
+        functools.partial(feed_forward_kernel, bool(sums)),
+        grid=(count // tile,),
+        in_specs=[
+            wide,
+            pl.BlockSpec((tile, units), by_row),
+            pl.BlockSpec((width, 2 * units), fixed, pipeline_mode=pl.Buffered(1)),
+            pl.BlockSpec((width, units), fixed, pipeline_mode=pl.Buffered(1)),
+        ]
+        + [wide] * len(sums),
+        out_specs=[
+            pl.BlockSpec((tile, units), by_row),
+            pl.BlockSpec((tile, 2 * units), by_row),
+            wide,
+            wide,
+        ],
+        out_shape=[
+            jax.ShapeDtypeStruct((count, units), BF16),
+            jax.ShapeDtypeStruct((count, 2 * units), BF16),
+            jax.ShapeDtypeStruct((count, width), BF16),
+            jax.ShapeDtypeStruct((count, width), BF16),
+        ],
+        compiler_params=pltpu.CompilerParams(
+            dimension_semantics=("arbitrary",), vmem_limit_bytes=48 << 20
+        ),
+        cost_estimate=pl.CostEstimate(
+            flops=2 * count * width * 5 * units,
+            bytes_accessed=2 * (3 * count * width + 3 * width * units + 4 * count * units),
+            transcendentals=count * units,
+        ),
+        name="feed_forward",
+    )(rows, d_hidden, w_gate_up, w_down_t, *sums)
+
+
 def pick(flag, first, second):
     return jnp.where(flag, first, second)
 
@@ -779,12 +881,17 @@
     )
     own_pos = plane_idx * row_count + jnp.arange(row_count, dtype=jnp.int32)
     apart = jnp.arange(8, dtype=jnp.int32) ^ plane_idx
-    slots = (apart & 1) | ((apart & 4) >> 1) | ((apart & 2) << 1)
+    along_x, along_y, across = apart & 1, apart >> 2, (apart >> 1) & 1
+    x_first = (core ^ across) == 0
+    slots = across * 4 + jnp.where(x_first, along_x + 2 * along_y, along_y + 2 * along_x)
     table_cos, table_sin = rope_tables(jnp.arange(seq_len, dtype=jnp.int32), 64)
     table_cos, table_sin = table_cos[:, 0, :], table_sin[:, 0, :]
     cosine = jnp.concatenate([table_cos, table_cos], axis=1)
     sine = jnp.concatenate([-table_sin, table_sin], axis=1)
     q_gain, k_gain = q_norm_gain[None, :], k_norm_gain[None, :]
+
+    def after(value, *ahead):
+        return lax.optimization_barrier((value, ahead))[0]
 
     spare = jnp.zeros((row_count, 126), BF16)
     halves = [
@@ -808,6 +915,21 @@
     attn_full = lax.all_gather(attn_rows, "dp", axis=0, tiled=True)
     w_proj, w_out_t = attn_full[:, :640], attn_full[:, 640:]
 
+    first_batch, second_batch = range(micro_batches)
+    half = seq_len // 2
+    live_counts = [slot_count[n * n_dp + dp_idx] for n in range(micro_batches)]
+    tables = [jnp.concatenate([slots, live[None]]).astype(jnp.int32) for live in live_counts]
+    x_float = [inputs[n].astype(F32) for n in range(micro_batches)]
+    scale1 = [rms_scale(x) for x in x_float]
+    normed1 = [x * scale for x, scale in zip(x_float, scale1)]
+    xn1_own = [(n * attn_norm_gain).astype(BF16) for n in normed1]
+    cot_live = [
+        cotangent[n].astype(F32) * (own_pos < live_counts[n]).astype(F32)[:, None]
+        for n in range(micro_batches)
+    ]
+    xn1 = [Gather(xn1_own[0]), None]
+    pair = xn1[0].second()
+
     down_t = w_down.T
     quarters = jnp.stack(
         [
@@ -821,79 +943,176 @@
         swap(lax.dynamic_index_in_dim(quarters, head_idx ^ r, 0, False), r * 2) for r in (1, 2, 3)
     ]
     ffn_rows = jnp.concatenate(reorder_by(traded, head_idx), axis=0)
+    ffn_rows = after(ffn_rows, attn_rows)
+    w_down_t = lax.all_gather(ffn_rows[:, 2 * ffn_cols :], "dp", axis=0, tiled=True)
     w_gate_up = lax.all_gather(ffn_rows[:, : 2 * ffn_cols], "dp", axis=0, tiled=True)
-    w_down_t = lax.all_gather(ffn_rows[:, 2 * ffn_cols :], "dp", axis=0, tiled=True)
-
-    outputs, input_grads = ([], [])
-    gain_attn = jnp.zeros((model_width,), F32)
-    gain_ffn = jnp.zeros((model_width,), F32)
-    gain_query = jnp.zeros((128,), F32)
-    gain_key = jnp.zeros((128,), F32)
-    grad_gate_up = grad_down_t = grad_proj = grad_out_t = None
-
-    def plus(total, term):
-        return term if total is None else total + term
-
-    for micro_batch in range(micro_batches):
-        live_count = slot_count[micro_batch * n_dp + dp_idx]
-        table = jnp.concatenate([slots, live_count[None]]).astype(jnp.int32)
-        x_float = inputs[micro_batch].astype(F32)
-        scale1 = rms_scale(x_float)
-        normed1 = x_float * scale1
-        xn1 = gather_rows((normed1 * attn_norm_gain).astype(BF16), core)
-        live = (own_pos < live_count).astype(F32)[:, None]
-        cot_live = cotangent[micro_batch].astype(F32) * live
-        cot_rows = gather_rows(cot_live.astype(BF16), core)
-        proj = jnp.concatenate([dot(piece, w_proj) for piece in xn1], axis=0)
-        gated, attn_o, lse = attend_forward_call(table, proj, cosine, sine, q_gain, k_gain)
-        half = seq_len // 2
-        gated_pieces = (gated[:half], gated[half:])
-        out_other = dot(gated_pieces[1], w_out_t, NT)
-        out_mine = dot(gated_pieces[0], w_out_t, NT)
-        hidden1 = x_float + scatter_rows(out_mine, out_other, core)
-        scale2 = rms_scale(hidden1)
-        normed2 = hidden1 * scale2
-        xn2 = gather_rows((normed2 * ffn_norm_gain).astype(BF16), core)
-        down_parts, back_parts = ([], [])
-        for xn2_piece, cot_piece in zip(xn2, cot_rows):
-            pre = dot(xn2_piece, w_gate_up)
-            gate_pre, up_pre = pre[:, :ffn_cols], pre[:, ffn_cols:]
-            gate_sig = jax.nn.sigmoid(gate_pre)
-            gate_act = gate_pre * gate_sig
-            hidden = (gate_act * up_pre).astype(BF16)
-            d_hidden = dot(cot_piece, w_down_t)
-            d_up = (d_hidden * gate_act).astype(BF16)
-            d_gate = (d_hidden * up_pre * gate_sig * (1.0 + gate_pre * (1.0 - gate_sig))).astype(
-                BF16
-            )
-            d_both = jnp.concatenate([d_gate, d_up], axis=1)
-            down_parts.append(dot(hidden, w_down_t, NT))
-            back_parts.append(dot(d_both, w_gate_up, NT))
-            grad_gate_up = plus(grad_gate_up, dot(xn2_piece, d_both, TN))
-            grad_down_t = plus(grad_down_t, dot(cot_piece, hidden, TN))
-        outputs.append((hidden1 + scatter_rows(down_parts[0], down_parts[1], core)).astype(BF16))
-        d_xn2 = scatter_rows(back_parts[0], back_parts[1], core)
-        gain_ffn = gain_ffn + jnp.sum(d_xn2 * normed2, axis=0)
-        d_hidden1 = cot_live + norm_back(d_xn2, normed2, scale2, ffn_norm_gain)
-        d_attn = gather_rows(d_hidden1.astype(BF16), core)
-        d_gated = jnp.concatenate([dot(piece, w_out_t) for piece in d_attn], axis=0)
-        for d_piece, gated_piece in zip(d_attn, gated_pieces):
-            grad_out_t = plus(grad_out_t, dot(d_piece, gated_piece, TN))
-        d_proj, part_q, part_k = attend_backward_call(
-            table, proj, d_gated, attn_o, lse, cosine, sine, q_gain, k_gain
-        )
-        gain_query = gain_query + part_q[0]
-        gain_key = gain_key + part_k[0]
-        d_pieces = (d_proj[:half], d_proj[half:])
-        for x_piece, d_piece in zip(xn1, d_pieces):
-            grad_proj = plus(grad_proj, dot(x_piece, d_piece, TN))
-        term_other = dot(d_pieces[1], w_proj, NT)
-        term_mine = dot(d_pieces[0], w_proj, NT)
-        d_xn1 = scatter_rows(term_mine, term_other, core)
-        gain_attn = gain_attn + jnp.sum(d_xn1 * normed1, axis=0)
-        input_grads.append(
-            (d_hidden1 + norm_back(d_xn1, normed1, scale1, attn_norm_gain)).astype(BF16)
-        )
+
+    xn1[1] = Gather(after(xn1_own[1], pair))
+    order = Order()
+    project = lambda rows, w: dot(rows, w)
+    project_t = lambda rows, w: dot(rows, w, NT).astype(BF16)
+    add_t = lambda rows, w, came: (dot(rows, w, NT) + came.astype(F32)).astype(BF16)
+    weight_grad = lambda rows, grads: dot(rows, grads, TN)
+    add_grad = lambda rows, grads, total: dot(rows, grads, TN) + total
+
+    def attend(n, proj):
+        return attend_forward_call(tables[n], proj, cosine, sine, q_gain, k_gain)
+
+    order.need(xn1[0].third(), xn1[1].second(), ffn_rows)
+    proj, att, cot = ([None, None] for _ in range(3))
+    proj_a = order.run(project, xn1[0].mine, w_proj)
+    proj_b = order.run(project, xn1[0].other, w_proj)
+    proj[0] = jnp.concatenate([proj_a, proj_b], axis=0)
+    cot[0] = Gather(after(cot_live[0].astype(BF16), proj_a))
+    att[0] = order.run(lambda p: attend(0, p), proj[0])
+    order.need(xn1[1].third(), cot[0].second())
+    out_sum = [None, None]
+    out_sum[0] = Scatter(order.run(project_t, att[0][0][half:], w_out_t))
+    proj_a = order.run(project, xn1[1].mine, w_proj)
+    proj_b = order.run(project, xn1[1].other, w_proj)
+    proj[1] = jnp.concatenate([proj_a, proj_b], axis=0)
+    out_sum[0].second(order.run(add_t, att[0][0][:half], w_out_t, out_sum[0].came))
+    order.need(cot[0].third())
+    att[1] = order.run(lambda p: attend(1, p), proj[1])
+    order.need(out_sum[0].third())
+    out_sum[1] = Scatter(order.run(project_t, att[1][0][half:], w_out_t))
+    d_hidden = [[None, None], [None, None]]
+    d_hidden[0][1] = order.run(project, cot[0].other, w_down_t)
+
+    hidden1, scale2, normed2, xn2 = ([None, None] for _ in range(4))
+
+    def middle(n):
+        hidden1[n] = x_float[n] + out_sum[n].result()
+        scale2[n] = rms_scale(hidden1[n])
+        normed2[n] = hidden1[n] * scale2[n]
+        rows = (normed2[n] * ffn_norm_gain).astype(BF16)
+        xn2[n] = Gather(rows)
+        return rows
+
+    order.need(middle(0))
+    out_sum[1].second(order.run(add_t, att[1][0][:half], w_out_t, out_sum[1].came))
+    order.need(xn2[0].second())
+    d_hidden[0][0] = order.run(project, cot[0].mine, w_down_t)
+    cot[1] = Gather(after(cot_live[1].astype(BF16), d_hidden[0][0]))
+    order.need(out_sum[1].third(), xn2[0].third())
+
+    down, back = ([None, None] for _ in range(2))
+    feed_o, feed_m = ([None, None] for _ in range(2))
+
+    def feed_other(n):
+        feed_o[n] = order.run(
+            feed_forward_call, xn2[n].other, d_hidden[n][1], w_gate_up, w_down_t
+        )
+        back[n] = Scatter(feed_o[n][3])
+        down[n] = Scatter(feed_o[n][2])
+
+    def feed_mine(n):
+        feed_m[n] = order.run(
+            feed_forward_call,
+            xn2[n].mine,
+            d_hidden[n][0],
+            w_gate_up,
+            w_down_t,
+            down[n].came,
+            back[n].came,
+        )
+        back[n].second(feed_m[n][3])
+
+    feed_other(0)
+    order.need(middle(1), cot[1].second())
+    feed_mine(0)
+    order.need(xn2[1].second(), cot[1].third())
+    d_hidden[1][1] = order.run(project, cot[1].other, w_down_t)
+    d_hidden[1][0] = order.run(project, cot[1].mine, w_down_t)
+    order.need(back[0].third(), xn2[1].third())
+
+    d_hidden1, d_attn = ([None, None] for _ in range(2))
+    gain_ffn = []
+
+    def turn(n):
+        d_xn2 = back[n].result()
+        gain_ffn.append(jnp.sum(d_xn2 * normed2[n], axis=0))
+        d_hidden1[n] = cot_live[n] + norm_back(d_xn2, normed2[n], scale2[n], ffn_norm_gain)
+        rows = d_hidden1[n].astype(BF16)
+        d_attn[n] = Gather(rows)
+        return rows
+
+    grad_gate_up = order.run(weight_grad, xn2[0].other, feed_o[0][1])
+    order.need(turn(0))
+    feed_other(1)
+    order.need(d_attn[0].second())
+    feed_mine(1)
+    order.need(d_attn[0].third())
+    grad_gate_up = order.run(add_grad, xn2[0].mine, feed_m[0][1], grad_gate_up)
+    grad_gate_up = order.run(add_grad, xn2[1].other, feed_o[1][1], grad_gate_up)
+    order.need(back[1].third())
+    grad_gate_up = order.run(add_grad, xn2[1].mine, feed_m[1][1], grad_gate_up)
+    order.need(turn(1))
+    grad_down_t = order.run(weight_grad, cot[0].other, feed_o[0][0])
+    down[0].second(after(feed_m[0][2], grad_down_t))
+    grad_down_t = order.run(add_grad, cot[0].mine, feed_m[0][0], grad_down_t)
+    order.need(d_attn[1].second())
+    grad_down_t = order.run(add_grad, cot[1].other, feed_o[1][0], grad_down_t)
+    grad_down_t = order.run(add_grad, cot[1].mine, feed_m[1][0], grad_down_t)
+    order.need(down[0].third())
+
+    d_proj, gain_parts, rows_sum = ([None, None] for _ in range(3))
+    outputs, input_grads = ([None, None] for _ in range(2))
+
+    def back_attend(n):
+        d_a = order.run(project, d_attn[n].mine, w_out_t)
+        d_b = order.run(project, d_attn[n].other, w_out_t)
+        d_gated = jnp.concatenate([d_a, d_b], axis=0)
+        d_proj[n], part_q, part_k = order.run(
+            lambda *v: attend_backward_call(tables[n], *v, cosine, sine, q_gain, k_gain),
+            proj[n],
+            d_gated,
+            att[n][1],
+            att[n][2],
+        )
+        gain_parts[n] = (part_q[0], part_k[0])
+
+    def finish(n):
+        d_xn1 = rows_sum[n].result()
+        input_grads[n] = (
+            d_hidden1[n] + norm_back(d_xn1, normed1[n], scale1[n], attn_norm_gain)
+        ).astype(BF16)
+
+    back_attend(0)
+    order.need(d_attn[1].third())
+    rows_sum[0] = Scatter(order.run(project_t, d_proj[0][half:], w_proj))
+    outputs[0] = (hidden1[0] + down[0].result()).astype(BF16)
+    grad_out_t = order.run(weight_grad, d_attn[0].mine, att[0][0][:half])
+    grad_out_t = order.run(add_grad, d_attn[0].other, att[0][0][half:], grad_out_t)
+    rows_sum[0].second(order.run(add_t, d_proj[0][:half], w_proj, rows_sum[0].came))
+    down[1].second(after(feed_m[1][2], outputs[0]))
+    back_attend(1)
+    order.need(rows_sum[0].third(), down[1].third())
+    rows_sum[1] = Scatter(order.run(project_t, d_proj[1][half:], w_proj))
+    grad_proj = order.run(weight_grad, xn1[0].mine, d_proj[0][:half])
+    rows_sum[1].second(order.run(add_t, d_proj[1][:half], w_proj, rows_sum[1].came))
+    grad_proj = order.run(add_grad, xn1[0].other, d_proj[0][half:], grad_proj)
+    grad_proj = order.run(add_grad, xn1[1].mine, d_proj[1][:half], grad_proj)
+    grad_proj = order.run(add_grad, xn1[1].other, d_proj[1][half:], grad_proj)
+    order.need(rows_sum[1].third())
+    grad_out_t = order.run(add_grad, d_attn[1].mine, att[1][0][:half], grad_out_t)
+    grad_out_t = order.run(add_grad, d_attn[1].other, att[1][0][half:], grad_out_t)
+    finish(0)
+    finish(1)
+    outputs[1] = (hidden1[1] + down[1].result()).astype(BF16)
+
+    gain_attn = jnp.sum(grad_proj * w_proj.astype(F32), axis=1) / attn_norm_gain
+    gains = jnp.concatenate(
+        [gain_attn, gain_ffn[0] + gain_ffn[1]]
+        + [gain_parts[0][k] + gain_parts[1][k] for k in range(2)]
+    ).reshape(-1, 128)
+    for bits in (BIT_C, BIT_X, BIT_Y):
+        gains = gains + swap(gains, bits)
+    for step in (1, 2):
+        gains = gains + lax.ppermute(gains, "dp", [(i, i ^ step) for i in range(4)])
+    gains = gains.reshape(-1)
+    sum_attn, sum_gain_ffn = gains[:model_width], gains[model_width : 2 * model_width]
+    sum_query, sum_key = gains[-256:-128], gains[-128:]
 
     sum_ffn = [
         lax.psum_scatter(g.astype(BF16), "dp", scatter_dimension=0, tiled=True)
@@ -920,9 +1139,6 @@
     grad_value = jnp.concatenate([v[:, 384:512] for v in by_half], axis=1)
     grad_headgate = jnp.concatenate([v[:, 512:514] for v in by_half], axis=1)
     grad_out = jnp.concatenate([v[:, 640:896].T for v in by_half], axis=0)
-    sum_attn, sum_query, sum_key, sum_gain_ffn = lax.psum(
-        (gain_attn, gain_query, gain_key, gain_ffn), ("dp", "head", "mp")
-    )
     return (
         jnp.stack(outputs),
         jnp.stack(input_grads),
@@ -942,7 +1158,7 @@
 
 
 def choose_local(mesh):
-    if mesh.shape["head"] == 4 and mesh.shape["mp"] == 2:
+    if mesh.shape["head"] == 4 and mesh.shape["mp"] == 2 and mesh.shape["dp"] == 4:
         return local_plane
     return local
 

time: 1240 us -> 1020 us (0.82)
  waiting for transfers between devices: 494 us -> 310 us
  matrix products: 338 us -> 221 us
  Pallas kernels: 109 us -> 203 us
  local copies, waits for them, and re-layouts: 56.3 us -> 97.2 us
  blocking collectives: 38.7 us -> 0 us
    ppermute x56 -> x27, waiting for transfers between devices: 286 us -> 48 us  [swap(): return lax.ppermute(values, PLANE, [(i, i ^ bits) for i in range(8)])]
    dot_general x48 -> x36, matrix products: 338 us -> 221 us  [dot(): return lax.dot_general(left, right, dims, preferred_element_type=F32)]
    pallas_call x0 -> x4, Pallas kernels: none -> 94.2 us  [feed_forward_call(): pl.pallas_call(functools.partial(feed_forward_kernel, bool(sums)), grid=(...]
    ppermute x16 -> x34, waiting for transfers between devices: 172 us -> 258 us  [the longest x32 258 us: swap_mixed(): lax.ppermute(values, PLANE, [(i, i ^ (core1 if i & BIT_C else core0)) for...]
    ppermute x56 -> x27, starting transfers between devices: 51.9 us -> 12.5 us  [swap(): return lax.ppermute(values, PLANE, [(i, i ^ bits) for i in range(8)])]
    psum x1 -> x0, blocking collectives: 38.7 us -> none  [local_plane(): lax.psum((gain_attn, gain_query, gain_key, gain_ffn), ('dp', 'head', 'mp'))]
    all_gather x1, waiting for transfers between devices: 34.8 us -> 0.02 us  [local_plane(): lax.all_gather(ffn_rows[:, 2 * ffn_cols:], 'dp', axis=0, tiled=True)]
    ppermute x16 -> x34, starting transfers between devices: 22 us -> 50 us  [the longest x32 46 us: swap_mixed(): lax.ppermute(values, PLANE, [(i, i ^ (core1 if i & BIT_C else core0)) for...]
  transfers between devices with their start and end apart: 78 -> 67, of which waited for: 47 -> 29; matrix products, arithmetic and copies ran while one was open for 35% -> 38% of each run, Pallas kernels for 9% -> 18%
where the time goes in v2:
time: 1020 us; the launch traced here: 1010 us
  waiting for transfers between devices  310 us (30%)
  matrix products  221 us (22%)
  Pallas kernels  203 us (20%)
  other arithmetic  99.5 us (10%)
  local copies, waits for them, and re-layouts  97.2 us (10%)
  starting transfers between devices  63.7 us (6%)
  between operations  16.4 us (2%)
    ppermute x32, waiting for transfers between devices, swap_mixed(): lax.ppermute(values, PLANE, [(i, i ^ (core1 if i & BIT_C else core0)) for...  258 us
    dot_general x36, matrix products, dot(): return lax.dot_general(left, right, dims, preferred_element_type=F32)  221 us
    pallas_call x4, Pallas kernels, feed_forward_call(): pl.pallas_call(functools.partial(feed_forward_kernel, bool(sums)), grid=(...  94.2 us
    pallas_call x2, Pallas kernels, attend_backward_call(): pl.pallas_call(attend_backward_kernel, grid_spec=pltpu.PrefetchScalarGrid...  59.6 us
    pallas_call x2, Pallas kernels, attend_forward_call(): pl.pallas_call(attend_forward_kernel, grid_spec=pltpu.PrefetchScalarGridS...  49 us
    ppermute x27, waiting for transfers between devices, swap(): return lax.ppermute(values, PLANE, [(i, i ^ bits) for i in range(8)])  48 us
    ppermute x32, starting transfers between devices, swap_mixed(): lax.ppermute(values, PLANE, [(i, i ^ (core1 if i & BIT_C else core0)) for...  46 us
    unnamed x242, local copies, waits for them, and re-layouts  42.6 us
  transfers between devices with their start and end apart: 67, of which 29 were waited for; matrix products, arithmetic and copies ran while one was open for 38% of the time, Pallas kernels for 18%

profile of v2, /device:TPU:0, one launch (start us, length us, event | category | flops | bytes accessed | tf_op | source)
XLA Modules:
  0.0 1010.5 jit_solution(12919745723201263862)
XLA Ops:
  61.0 24.4 %collective-permute-done.1 = bf16[512,2048]{1,0:T(8,128)(2,1)} collective-permute-done((bf16[512,2048]{1,0:T(8,128)(2,1)}, bf16[512,2048]{1,0:T(8,128)(2,1)}, u32[]{:S(2)}, u32[]{:S(2)}) %collective-permute-start.1) | collective-permute-done | bytes 2097184 | tf_op jit(solution)/shard_map/ppermute | solution.py:443
  118.9 17.8 %collective-permute-done.8 = bf16[512,2048]{1,0:T(8,128)(2,1)} collective-permute-done((bf16[512,2048]{1,0:T(8,128)(2,1)}, bf16[512,2048]{1,0:T(8,128)(2,1)}, u32[]{:S(2)}, u32[]{:S(2)}) %collective-permute-start.8) | collective-permute-done | bytes 2097184 | tf_op jit(solution)/shard_map/ppermute | solution.py:443
  151.8 24.5 %attend_forward.2 = (bf16[2048,256]{1,0:T(8,128)(2,1)S(1)}, f32[2048,256]{1,0:T(8,128)S(1)}, f32[2048,128]{1,0:T(8,128)S(1)}) custom-call(s32[9]{0:T(128)S(1)} %get-tuple-element.472.table, f32[2048,640]{1,0:T(8,128)S(1)} %pad_maximum_fusion.proj, f32[2048,128]{1,0:T(8,128)S(1)} %get-tuple-element.485.cosine, f32[2048,128]{1,0:T(8,128)S(1)} %get-tuple-element.486.sine, ...), custom_call_target="tpu_custom_call" | custom-call | flops 2415919104 | bytes 15728640 | tf_op jit(solution)/shard_map/attend_forward/pallas_call | solution.py:688
  183.8 8.1 fusion.62
  205.7 23.9 %collective-permute-done.12 = bf16[512,2048]{1,0:T(8,128)(2,1)S(1)} collective-permute-done((bf16[512,2048]{1,0:T(8,128)(2,1)S(1)}, bf16[512,2048]{1,0:T(8,128)(2,1)S(1)}, u32[]{:S(2)}, u32[]{:S(2)}) %collective-permute-start.12) | collective-permute-done | bytes 2097184 | tf_op jit(solution)/shard_map/ppermute | solution.py:443
  239.1 24.3 %collective-permute-done.16 = bf16[512,2048]{1,0:T(8,128)(2,1)} collective-permute-done((bf16[512,2048]{1,0:T(8,128)(2,1)}, bf16[512,2048]{1,0:T(8,128)(2,1)}, u32[]{:S(2)}, u32[]{:S(2)}) %collective-permute-start.16) | collective-permute-done | bytes 2097184 | tf_op jit(solution)/shard_map/ppermute | solution.py:443
  266.6 24.5 %attend_forward.3 = (bf16[2048,256]{1,0:T(8,128)(2,1)S(1)}, f32[2048,256]{1,0:T(8,128)S(1)}, f32[2048,128]{1,0:T(8,128)S(1)}) custom-call(s32[9]{0:T(128)S(1)} %get-tuple-element.473.table, f32[2048,640]{1,0:T(8,128)S(1)} %pad_maximum_fusion.1.proj, f32[2048,128]{1,0:T(8,128)S(1)} %get-tuple-element.485.cosine, f32[2048,128]{1,0:T(8,128)S(1)} %get-tuple-element.486.sine, ...), custom_call_target="tpu_custom_call" | custom-call | flops 2415919104 | bytes 15728640 | tf_op jit(solution)/shard_map/attend_forward/pallas_call | solution.py:688
  300.5 8.4 collective-permute-done.14
  311.2 24.0 %collective-permute-done.15 = bf16[512,2048]{1,0:T(8,128)(2,1)S(1)} collective-permute-done((bf16[512,2048]{1,0:T(8,128)(2,1)S(1)}, bf16[512,2048]{1,0:T(8,128)(2,1)S(1)}, u32[]{:S(2)}, u32[]{:S(2)}) %collective-permute-start.15) | collective-permute-done | bytes 2097184 | tf_op jit(solution)/shard_map/ppermute | solution.py:443
  337.8 8.3 fusion.64.refs_1_
  361.9 23.5 %collective-permute-done.24 = bf16[256,2048]{1,0:T(8,128)(2,1)S(1)} collective-permute-done((bf16[256,2048]{1,0:T(8,128)(2,1)S(1)}, bf16[256,2048]{1,0:T(8,128)(2,1)S(1)}, u32[]{:S(2)}, u32[]{:S(2)}) %collective-permute-start.24) | collective-permute-done | bytes 1048608 | tf_op jit(solution)/shard_map/ppermute | solution.py:443
  390.7 23.3 %feed_forward.4 = (bf16[1024,768]{1,0:T(8,128)(2,1)S(1)}, bf16[1024,1536]{1,0:T(8,128)(2,1)S(1)}, bf16[1024,2048]{1,0:T(8,128)(2,1)}, bf16[1024,2048]{1,0:T(8,128)(2,1)}) custom-call(bf16[1024,2048]{1,0:T(8,128)(2,1)} %collective-permute-done.19.refs_0_, f32[1024,768]{1,0:T(8,128)} %fusion.64.refs_1_, ...), custom_call_target="tpu_custom_call" | custom-call | flops 16106127360 | bytes 28311552 | tf_op jit(solution)/shard_map/feed_forward/pallas_call | solution.py:807
  419.5 10.1 %collective-permute-done.23 = bf16[256,2048]{1,0:T(8,128)(2,1)S(1)} collective-permute-done((bf16[256,2048]{1,0:T(8,128)(2,1)S(1)}, bf16[256,2048]{1,0:T(8,128)(2,1)S(1)}, u32[]{:S(2)}, u32[]{:S(2)}) %collective-permute-start.23) | collective-permute-done | bytes 1048608 | tf_op jit(solution)/shard_map/ppermute | solution.py:443
  432.1 13.3 %collective-permute-done.25 = bf16[256,2048]{1,0:T(8,128)(2,1)S(1)} collective-permute-done((bf16[256,2048]{1,0:T(8,128)(2,1)S(1)}, bf16[256,2048]{1,0:T(8,128)(2,1)S(1)}, u32[]{:S(2)}, u32[]{:S(2)}) %collective-permute-start.25) | collective-permute-done | bytes 1048608 | tf_op jit(solution)/shard_map/ppermute | solution.py:443
  452.5 23.9 %feed_forward.5 = (bf16[1024,768]{1,0:T(8,128)(2,1)S(1)}, bf16[1024,1536]{1,0:T(8,128)(2,1)S(1)}, bf16[1024,2048]{1,0:T(8,128)(2,1)}, bf16[1024,2048]{1,0:T(8,128)(2,1)}) custom-call(bf16[1024,2048]{1,0:T(8,128)(2,1)} %pad_maximum_fusion.3.refs_0_, f32[1024,768]{1,0:T(8,128)} %fusion.65.refs_1_, bf16[2048,1536]{1,0:T(8,128)(2,1)} %all-gather.8.cloned.1.call-done.refs_2_, ...), custom_call_target="tpu_custom_call" | custom-call | flops 16106127360 | bytes 28311552 | tf_op jit(solution)/shard_map/feed_forward/pallas_call | solution.py:807
  481.5 8.8 fusion.66.refs_1_
  495.4 9.6 collective-permute-done.30
  507.5 12.1 %fusion.68 = f32[2048,1536]{1,0:T(8,128)} fusion(bf16[1024,2048]{1,0:T(8,128)(2,1)} %collective-permute-done.19.refs_0_, bf16[1024,1536]{1,0:T(8,128)(2,1)S(1)} %get-tuple-element.218), kind=kOutput, calls=%fused_computation.224 | convolution fusion | flops 6442450944 | bytes 19922944 | tf_op jit(solution)/shard_map/dot_general | solution.py:435
  526.3 23.0 %feed_forward.6 = (bf16[1024,768]{1,0:T(8,128)(2,1)S(1)}, bf16[1024,1536]{1,0:T(8,128)(2,1)S(1)}, bf16[1024,2048]{1,0:T(8,128)(2,1)}, bf16[1024,2048]{1,0:T(8,128)(2,1)}) custom-call(bf16[1024,2048]{1,0:T(8,128)(2,1)} %copy-done.103, f32[1024,768]{1,0:T(8,128)} %fusion.66.refs_1_, bf16[2048,1536]{1,0:T(8,128)(2,1)} %all-gather.8.cloned.1.call-done.refs_2_, ...), custom_call_target="tpu_custom_call" | custom-call | flops 16106127360 | bytes 28311552 | tf_op jit(solution)/shard_map/feed_forward/pallas_call | solution.py:807
  551.5 13.1 %collective-permute-done.34 = bf16[256,2048]{1,0:T(8,128)(2,1)S(1)} collective-permute-done((bf16[256,2048]{1,0:T(8,128)(2,1)S(1)}, bf16[256,2048]{1,0:T(8,128)(2,1)S(1)}, u32[]{:S(2)}, u32[]{:S(2)}) %collective-permute-start.34) | collective-permute-done | bytes 1048608 | tf_op jit(solution)/shard_map/ppermute | solution.py:443
  565.4 25.6 %collective-permute-done.35 = bf16[512,2048]{1,0:T(8,128)(2,1)S(1)} collective-permute-done((bf16[512,2048]{1,0:T(8,128)(2,1)S(1)}, bf16[512,2048]{1,0:T(8,128)(2,1)S(1)}, u32[]{:S(2)}, u32[]{:S(2)}) %collective-permute-start.35) | collective-permute-done | bytes 2097184 | tf_op jit(solution)/shard_map/ppermute | solution.py:443
  597.3 24.0 %feed_forward.7 = (bf16[1024,768]{1,0:T(8,128)(2,1)S(1)}, bf16[1024,1536]{1,0:T(8,128)(2,1)S(1)}, bf16[1024,2048]{1,0:T(8,128)(2,1)}, bf16[1024,2048]{1,0:T(8,128)(2,1)}) custom-call(bf16[1024,2048]{1,0:T(8,128)(2,1)} %copy-done.56, f32[1024,768]{1,0:T(8,128)} %fusion.67.refs_1_, bf16[2048,1536]{1,0:T(8,128)(2,1)} %all-gather.8.cloned.1.call-done.refs_2_, ...), custom_call_target="tpu_custom_call" | custom-call | flops 16106127360 | bytes 28311552 | tf_op jit(solution)/shard_map/feed_forward/pallas_call | solution.py:807
  624.2 14.0 %fusion.57 = f32[2048,1536]{1,0:T(8,128)} fusion(f32[2048,1536]{1,0:T(8,128)} %fusion.68, bf16[1024,2048]{1,0:T(8,128)(2,1)} %pad_maximum_fusion.3.refs_0_, bf16[1024,1536]{1,0:T(8,128)(2,1)S(1)} %get-tuple-element.237), kind=kOutput, calls=%fused_computation.213 | convolution fusion | flops 6445596672 | bytes 32505856 | tf_op jit(solution)/shard_map/dot_general | solution.py:435
  638.3 14.0 %convolution_add_fusion = f32[2048,1536]{1,0:T(8,128)} fusion(f32[2048,1536]{1,0:T(8,128)} %fusion.57, bf16[1024,2048]{1,0:T(8,128)(2,1)} %copy-done.103, bf16[1024,1536]{1,0:T(8,128)(2,1)S(1)} %get-tuple-element.240), kind=kOutput, calls=%fused_computation | convolution fusion | flops 6445596672 | bytes 32505856 | tf_op jit(solution)/shard_map/dot_general | solution.py:435
  658.8 11.7 %fusion.58 = bf16[2048,1536]{1,0:T(8,128)(2,1)} fusion(f32[2048,1536]{1,0:T(8,128)} %convolution_add_fusion, bf16[1024,2048]{1,0:T(8,128)(2,1)S(1)} %copy-done.57, bf16[1024,1536]{1,0:T(8,128)(2,1)S(1)} %get-tuple-element.244), kind=kOutput, calls=%fused_computation.214 | convolution fusion | flops 6448742400 | bytes 26214400 | tf_op jit(solution)/shard_map/dot_general | solution.py:435
  728.4 29.8 %attend_backward.2 = (bf16[2048,640]{1,0:T(8,128)(2,1)S(1)}, f32[8,128]{1,0:T(8,128)S(1)}, f32[8,128]{1,0:T(8,128)S(1)}) custom-call(s32[9]{0:T(128)S(1)} %copy-done.3, f32[2048,640]{1,0:T(8,128)} %copy-done.1, f32[2048,256]{1,0:T(8,128)S(1)} %pad_maximum_fusion.17.d_gated, f32[2048,256]{1,0:T(8,128)S(1)} %copy-done.9, f32[2048,128]{1,0:T(8,128)S(1)} %copy-done.11, ...), custom_call_target="tpu_custom_call" | custom-call | flops 6039797760 | bytes 15728640 | tf_op jit(solution)/shard_map/attend_backward/pallas_call | solution.py:729
  771.9 13.2 %collective-permute-done.39 = bf16[256,2048]{1,0:T(8,128)(2,1)S(1)} collective-permute-done((bf16[256,2048]{1,0:T(8,128)(2,1)S(1)}, bf16[256,2048]{1,0:T(8,128)(2,1)S(1)}, u32[]{:S(2)}, u32[]{:S(2)}) %collective-permute-start.39) | collective-permute-done | bytes 1048608 | tf_op jit(solution)/shard_map/ppermute | solution.py:443
  806.2 8.3 collective-permute-done.40
  826.4 29.8 %attend_backward.3 = (bf16[2048,640]{1,0:T(8,128)(2,1)S(1)}, f32[8,128]{1,0:T(8,128)S(1)}, f32[8,128]{1,0:T(8,128)S(1)}) custom-call(s32[9]{0:T(128)S(1)} %get-tuple-element.473.table, f32[2048,640]{1,0:T(8,128)} %copy-done, f32[2048,256]{1,0:T(8,128)S(1)} %pad_maximum_fusion.18.d_gated, f32[2048,256]{1,0:T(8,128)S(1)} %copy-done.7, ...), custom_call_target="tpu_custom_call" | custom-call | flops 6039797760 | bytes 15728640 | tf_op jit(solution)/shard_map/attend_backward/pallas_call | solution.py:729
  866.0 8.0 fusion.75
  926.4 10.6 %collective-permute-done.58 = bf16[128,2304]{1,0:T(8,128)(2,1)S(1)} collective-permute-done((bf16[128,2304]{1,0:T(8,128)(2,1)S(1)}, bf16[128,2304]{1,0:T(8,128)(2,1)S(1)}, u32[]{:S(2)}, u32[]{:S(2)}) %collective-permute-start.58) | collective-permute-done | bytes 589856 | tf_op jit(solution)/shard_map/ppermute | solution.py:439
  937.0 12.9 %collective-permute-done.59 = bf16[128,2304]{1,0:T(8,128)(2,1)S(1)} collective-permute-done((bf16[128,2304]{1,0:T(8,128)(2,1)S(1)}, bf16[128,2304]{1,0:T(8,128)(2,1)S(1)}, u32[]{:S(2)}, u32[]{:S(2)}) %collective-permute-start.59) | collective-permute-done | bytes 589856 | tf_op jit(solution)/shard_map/ppermute | solution.py:439
  (541 shorter events, 443.2 us)
Async XLA Ops:
  7.2 99.7 %all-gather.4.cloned.1.call-start = ((), (), s32[]{:S(2)}) async-start(), calls=%async_computation.3 | async-start | bytes 4587520 | tf_op jit(solution)/shard_map/all_gather | solution.py:915
  26.7 311.0 %all-gather.6.cloned.1.call-start = ((), (), s32[]{:S(2)}) async-start(), calls=%async_computation.4 | async-start | bytes 3932160 | tf_op jit(solution)/shard_map/all_gather | solution.py:947
  40.8 44.6 %collective-permute-start.1 = (bf16[512,2048]{1,0:T(8,128)(2,1)}, bf16[512,2048]{1,0:T(8,128)(2,1)}, u32[]{:S(2)}, u32[]{:S(2)}) collective-permute-start(bf16[512,2048]{1,0:T(8,128)(2,1)} %pad_maximum_fusion.11), channel_id=1, source_target_pairs={{0,4},{1,5},{2,3},{3,2},{4,0},{5,1},{6,7},{7,6},{8,12},{9,13},{10,... | collective-permute-start | bytes 6291464 | tf_op jit(solution)/shard_map/ppermute | solution.py:443
  46.4 51.4 %collective-permute-start.4 = (bf16[128,2304]{1,0:T(8,128)(2,1)}, bf16[128,2304]{1,0:T(8,128)(2,1)}, u32[]{:S(2)}, u32[]{:S(2)}) collective-permute-start(bf16[128,2304]{1,0:T(8,128)(2,1)} %bitcast.188), channel_id=1, source_target_pairs={{0,6},{1,7},{2,4},{3,5},{4,2},{5,3},{6,0},{7,1},{8,14},{9,15},{10,... | collective-permute-start | bytes 1769480 | tf_op jit(solution)/shard_map/ppermute | solution.py:439
  47.5 56.2 %collective-permute-start.5 = (bf16[128,2304]{1,0:T(8,128)(2,1)}, bf16[128,2304]{1,0:T(8,128)(2,1)}, u32[]{:S(2)}, u32[]{:S(2)}) collective-permute-start(bf16[128,2304]{1,0:T(8,128)(2,1)} %bitcast.189), channel_id=1, source_target_pairs={{0,4},{1,5},{2,6},{3,7},{4,0},{5,1},{6,2},{7,3},{8,12},{9,13},{10,... | collective-permute-start | bytes 1769480 | tf_op jit(solution)/shard_map/ppermute | solution.py:439
  50.0 53.7 %collective-permute-start.6 = (bf16[128,2304]{1,0:T(8,128)(2,1)}, bf16[128,2304]{1,0:T(8,128)(2,1)}, u32[]{:S(2)}, u32[]{:S(2)}) collective-permute-start(bf16[128,2304]{1,0:T(8,128)(2,1)} %bitcast.190), channel_id=1, source_target_pairs={{0,2},{1,3},{2,0},{3,1},{4,6},{5,7},{6,4},{7,5},{8,10},{9,11},{10,... | collective-permute-start | bytes 1769480 | tf_op jit(solution)/shard_map/ppermute | solution.py:439
  59.5 33.0 %collective-permute-start.3 = (bf16[256,2048]{1,0:T(8,128)(2,1)S(1)}, bf16[256,2048]{1,0:T(8,128)(2,1)}, u32[]{:S(2)}, u32[]{:S(2)}) collective-permute-start(bf16[256,2048]{1,0:T(8,128)(2,1)S(1)} %copy-done.59), channel_id=1, source_target_pairs={{0,1},{1,0},{2,6},{3,7},{4,5},{5,4},{6,2},{7,3},{8,9},{9,8},{10,14... | collective-permute-start | bytes 3145736 | tf_op jit(solution)/shard_map/ppermute | solution.py:443
  88.8 57.1 %collective-permute-start.7 = (bf16[1024,2048]{1,0:T(8,128)(2,1)}, bf16[1024,2048]{1,0:T(8,128)(2,1)}, u32[]{:S(2)}, u32[]{:S(2)}) collective-permute-start(bf16[1024,2048]{1,0:T(8,128)(2,1)} %pad_maximum_fusion.2), channel_id=1, source_target_pairs={{0,2},{1,3},{2,0},{3,1},{4,6},{5,7},{6,4},{7,5},{8,10},{9,11},{10,... | collective-permute-start | bytes 12582920 | tf_op jit(solution)/shard_map/ppermute | solution.py:439
  95.4 41.3 %collective-permute-start.8 = (bf16[512,2048]{1,0:T(8,128)(2,1)}, bf16[512,2048]{1,0:T(8,128)(2,1)}, u32[]{:S(2)}, u32[]{:S(2)}) collective-permute-start(bf16[512,2048]{1,0:T(8,128)(2,1)} %get-tuple-element.419), channel_id=1, source_target_pairs={{0,4},{1,5},{2,3},{3,2},{4,0},{5,1},{6,7},{7,6},{8,12},{9,13},{10,... | collective-permute-start | bytes 6291464 | tf_op jit(solution)/shard_map/ppermute | solution.py:443
  139.9 52.1 %collective-permute-start.11 = (bf16[1024,2048]{1,0:T(8,128)(2,1)}, bf16[1024,2048]{1,0:T(8,128)(2,1)}, u32[]{:S(2)}, u32[]{:S(2)}) collective-permute-start(bf16[1024,2048]{1,0:T(8,128)(2,1)} %constant_dynamic-update-slice_fusion.2), channel_id=1, source_target_pairs={{0,2},{1,3},{2,0},{3,1},{4,6},{5,7},{6,4},{7,5},{8,10},{9,11},{10,... | collective-permute-start | bytes 12582920 | tf_op jit(solution)/shard_map/ppermute | solution.py:439
  183.3 207.4 %all-gather.8.cloned.1.call-start = ((), (), s32[]{:S(2)}) async-start(), calls=%async_computation.5 | async-start | bytes 7864320 | tf_op jit(solution)/shard_map/all_gather | solution.py:948
  205.7 57.8 %collective-permute-start.16 = (bf16[512,2048]{1,0:T(8,128)(2,1)}, bf16[512,2048]{1,0:T(8,128)(2,1)}, u32[]{:S(2)}, u32[]{:S(2)}) collective-permute-start(bf16[512,2048]{1,0:T(8,128)(2,1)} %get-tuple-element.414), channel_id=1, source_target_pairs={{0,4},{1,5},{2,3},{3,2},{4,0},{5,1},{6,7},{7,6},{8,12},{9,13},{10,... | collective-permute-start | bytes 6291464 | tf_op jit(solution)/shard_map/ppermute | solution.py:443
  232.9 58.3 %collective-permute-start.13 = (bf16[256,2048]{1,0:T(8,128)(2,1)}, bf16[256,2048]{1,0:T(8,128)(2,1)}, u32[]{:S(2)}, u32[]{:S(2)}) collective-permute-start(bf16[256,2048]{1,0:T(8,128)(2,1)} %slice.441), channel_id=1, source_target_pairs={{0,1},{1,0},{2,6},{3,7},{4,5},{5,4},{6,2},{7,3},{8,9},{9,8},{10,14... | collective-permute-start | bytes 3145736 | tf_op jit(solution)/shard_map/ppermute | solution.py:443
  236.2 683.2 %reduce-scatter.8.cloned.1.call-start = ((), (), s32[]{:S(2)}) async-start(), calls=%async_computation.8 | async-start | bytes 3932160 | tf_op jit(solution)/shard_map/reduce_scatter | solution.py:1118
  266.6 71.1 %collective-permute-start.18 = (bf16[1024,2048]{1,0:T(8,128)(2,1)}, bf16[1024,2048]{1,0:T(8,128)(2,1)}, u32[]{:S(2)}, u32[]{:S(2)}) collective-permute-start(bf16[1024,2048]{1,0:T(8,128)(2,1)} %constant_dynamic-update-slice_fusion.7), channel_id=1, source_target_pairs={{0,2},{1,3},{2,0},{3,1},{4,6},{5,7},{6,4},{7,5},{8,10},{9,11},{10,... | collective-permute-start | bytes 12582920 | tf_op jit(solution)/shard_map/ppermute | solution.py:439
  300.3 45.8 %collective-permute-start.17 = (bf16[1024,2048]{1,0:T(8,128)(2,1)}, bf16[1024,2048]{1,0:T(8,128)(2,1)}, u32[]{:S(2)}, u32[]{:S(2)}) collective-permute-start(bf16[1024,2048]{1,0:T(8,128)(2,1)} %convolution_convert_fusion.2), channel_id=1, source_target_pairs={{0,2},{1,3},{2,0},{3,1},{4,6},{5,7},{6,4},{7,5},{8,10},{9,11},{10,... | collective-permute-start | bytes 12582920 | tf_op jit(solution)/shard_map/ppermute | solution.py:439
  337.6 53.1 %collective-permute-start.19 = (bf16[1024,2048]{1,0:T(8,128)(2,1)}, bf16[1024,2048]{1,0:T(8,128)(2,1)}, u32[]{:S(2)}, u32[]{:S(2)}) collective-permute-start(bf16[1024,2048]{1,0:T(8,128)(2,1)} %pad_maximum_fusion.3.refs_0_), channel_id=1, source_target_pairs={{0,2},{1,3},{2,0},{3,1},{4,6},{5,7},{6,4},{7,5},{8,10},{9,11},{10,... | collective-permute-start | bytes 12582920 | tf_op jit(solution)/shard_map/ppermute | solution.py:439
  349.8 38.2 %collective-permute-start.20 = (bf16[512,2048]{1,0:T(8,128)(2,1)S(1)}, bf16[512,2048]{1,0:T(8,128)(2,1)S(1)}, u32[]{:S(2)}, u32[]{:S(2)}) collective-permute-start(bf16[512,2048]{1,0:T(8,128)(2,1)S(1)} %slice.443), channel_id=1, source_target_pairs={{0,4},{1,5},{2,3},{3,2},{4,0},{5,1},{6,7},{7,6},{8,12},{9,13},{10,... | collective-permute-start | bytes 6291464 | tf_op jit(solution)/shard_map/ppermute | solution.py:443
  414.1 34.5 %collective-permute-start.21 = (bf16[1024,2048]{1,0:T(8,128)(2,1)}, bf16[1024,2048]{1,0:T(8,128)(2,1)S(1)}, u32[]{:S(2)}, u32[]{:S(2)}) collective-permute-start(bf16[1024,2048]{1,0:T(8,128)(2,1)} %get-tuple-element.199), channel_id=1, source_target_pairs={{0,2},{1,3},{2,0},{3,1},{4,6},{5,7},{6,4},{7,5},{8,10},{9,11},{10,... | collective-permute-start | bytes 12582920 | tf_op jit(solution)/shard_map/ppermute | solution.py:439
  414.1 34.4 %collective-permute-start.22 = (bf16[1024,2048]{1,0:T(8,128)(2,1)}, bf16[1024,2048]{1,0:T(8,128)(2,1)S(1)}, u32[]{:S(2)}, u32[]{:S(2)}) collective-permute-start(bf16[1024,2048]{1,0:T(8,128)(2,1)} %get-tuple-element.200), channel_id=1, source_target_pairs={{0,2},{1,3},{2,0},{3,1},{4,6},{5,7},{6,4},{7,5},{8,10},{9,11},{10,... | collective-permute-start | bytes 12582920 | tf_op jit(solution)/shard_map/ppermute | solution.py:439
  419.5 62.0 %collective-permute-start.28 = (bf16[1024,2048]{1,0:T(8,128)(2,1)}, bf16[1024,2048]{1,0:T(8,128)(2,1)}, u32[]{:S(2)}, u32[]{:S(2)}) collective-permute-start(bf16[1024,2048]{1,0:T(8,128)(2,1)} %constant_dynamic-update-slice_fusion.12), channel_id=1, source_target_pairs={{0,2},{1,3},{2,0},{3,1},{4,6},{5,7},{6,4},{7,5},{8,10},{9,11},{10,... | collective-permute-start | bytes 12582920 | tf_op jit(solution)/shard_map/ppermute | solution.py:439
  481.4 42.7 %collective-permute-start.29 = (bf16[1024,2048]{1,0:T(8,128)(2,1)S(1)}, bf16[1024,2048]{1,0:T(8,128)(2,1)S(1)}, u32[]{:S(2)}, u32[]{:S(2)}) collective-permute-start(bf16[1024,2048]{1,0:T(8,128)(2,1)S(1)} %pad_maximum_fusion.4.refs_0_), channel_id=1, source_target_pairs={{0,2},{1,3},{2,0},{3,1},{4,6},{5,7},{6,4},{7,5},{8,10},{9,11},{10,... | collective-permute-start | bytes 12582920 | tf_op jit(solution)/shard_map/ppermute | solution.py:439
  549.3 44.0 %collective-permute-start.32 = (bf16[1024,2048]{1,0:T(8,128)(2,1)}, bf16[1024,2048]{1,0:T(8,128)(2,1)S(1)}, u32[]{:S(2)}, u32[]{:S(2)}) collective-permute-start(bf16[1024,2048]{1,0:T(8,128)(2,1)} %get-tuple-element.223), channel_id=1, source_target_pairs={{0,2},{1,3},{2,0},{3,1},{4,6},{5,7},{6,4},{7,5},{8,10},{9,11},{10,... | collective-permute-start | bytes 12582920 | tf_op jit(solution)/shard_map/ppermute | solution.py:439
  549.3 44.0 %collective-permute-start.33 = (bf16[1024,2048]{1,0:T(8,128)(2,1)}, bf16[1024,2048]{1,0:T(8,128)(2,1)S(1)}, u32[]{:S(2)}, u32[]{:S(2)}) collective-permute-start(bf16[1024,2048]{1,0:T(8,128)(2,1)} %get-tuple-element.224), channel_id=1, source_target_pairs={{0,2},{1,3},{2,0},{3,1},{4,6},{5,7},{6,4},{7,5},{8,10},{9,11},{10,... | collective-permute-start | bytes 12582920 | tf_op jit(solution)/shard_map/ppermute | solution.py:439
  593.3 129.8 %collective-permute-start.43 = (bf16[1024,2048]{1,0:T(8,128)(2,1)}, bf16[1024,2048]{1,0:T(8,128)(2,1)}, u32[]{:S(2)}, u32[]{:S(2)}) collective-permute-start(bf16[1024,2048]{1,0:T(8,128)(2,1)} %pad_maximum_fusion.5), channel_id=1, source_target_pairs={{0,2},{1,3},{2,0},{3,1},{4,6},{5,7},{6,4},{7,5},{8,10},{9,11},{10,... | collective-permute-start | bytes 12582920 | tf_op jit(solution)/shard_map/ppermute | solution.py:439
  700.2 59.3 %collective-permute-start.44 = (bf16[512,2048]{1,0:T(8,128)(2,1)}, bf16[512,2048]{1,0:T(8,128)(2,1)}, u32[]{:S(2)}, u32[]{:S(2)}) collective-permute-start(bf16[512,2048]{1,0:T(8,128)(2,1)} %pad_maximum_fusion.16), channel_id=1, source_target_pairs={{0,4},{1,5},{2,3},{3,2},{4,0},{5,1},{6,7},{7,6},{8,12},{9,13},{10,... | collective-permute-start | bytes 6291464 | tf_op jit(solution)/shard_map/ppermute | solution.py:443
  713.1 206.4 %reduce-scatter.6.cloned.1.call-start = ((), (), s32[]{:S(2)}) async-start(), calls=%async_computation.7 | async-start | bytes 7864320 | tf_op jit(solution)/shard_map/reduce_scatter | solution.py:1118
  771.8 49.4 %collective-permute-start.48 = (bf16[1024,2048]{1,0:T(8,128)(2,1)}, bf16[1024,2048]{1,0:T(8,128)(2,1)}, u32[]{:S(2)}, u32[]{:S(2)}) collective-permute-start(bf16[1024,2048]{1,0:T(8,128)(2,1)} %pad_maximum_fusion.6), channel_id=1, source_target_pairs={{0,2},{1,3},{2,0},{3,1},{4,6},{5,7},{6,4},{7,5},{8,10},{9,11},{10,... | collective-permute-start | bytes 12582920 | tf_op jit(solution)/shard_map/ppermute | solution.py:439
  789.8 195.6 %reduce-scatter.4.cloned.1.call-start = ((), (), s32[]{:S(2)}) async-start(), calls=%async_computation.6 | async-start | bytes 4587520 | tf_op jit(solution)/shard_map/reduce_scatter | solution.py:1132
  805.8 50.7 %collective-permute-start.46 = (bf16[512,2048]{1,0:T(8,128)(2,1)}, bf16[512,2048]{1,0:T(8,128)(2,1)}, u32[]{:S(2)}, u32[]{:S(2)}) collective-permute-start(bf16[512,2048]{1,0:T(8,128)(2,1)} %slice.455), channel_id=1, source_target_pairs={{0,4},{1,5},{2,3},{3,2},{4,0},{5,1},{6,7},{7,6},{8,12},{9,13},{10,... | collective-permute-start | bytes 6291464 | tf_op jit(solution)/shard_map/ppermute | solution.py:443
  864.3 52.1 %collective-permute-start.41 = (bf16[256,2048]{1,0:T(8,128)(2,1)S(1)}, bf16[256,2048]{1,0:T(8,128)(2,1)}, u32[]{:S(2)}, u32[]{:S(2)}) collective-permute-start(bf16[256,2048]{1,0:T(8,128)(2,1)S(1)} %slice.453), channel_id=1, source_target_pairs={{0,1},{1,0},{2,6},{3,7},{4,5},{5,4},{6,2},{7,3},{8,9},{9,8},{10,14... | collective-permute-start | bytes 3145736 | tf_op jit(solution)/shard_map/ppermute | solution.py:443
  925.9 46.8 %collective-permute-start.47 = (bf16[256,2048]{1,0:T(8,128)(2,1)}, bf16[256,2048]{1,0:T(8,128)(2,1)S(1)}, u32[]{:S(2)}, u32[]{:S(2)}) collective-permute-start(bf16[256,2048]{1,0:T(8,128)(2,1)} %slice.457), channel_id=1, source_target_pairs={{0,1},{1,0},{2,6},{3,7},{4,5},{5,4},{6,2},{7,3},{8,9},{9,8},{10,14... | collective-permute-start | bytes 3145736 | tf_op jit(solution)/shard_map/ppermute | solution.py:443
  (148 other events, 1713.6 us)
Sparse Core Ops, SparseCore 0:
  26.9 73.5 all-gather.3
  183.4 65.6 all-gather.5
  251.3 113.9 all-gather.7
  713.2 61.4 reduce-scatter.7
  789.9 110.9 reduce-scatter.5
  915.9 69.4 reduce-scatter.3

commit v3 on v0

--- a/solution.py
+++ b/solution.py
@@ -1,6 +1,10 @@
+import functools
+
 import jax
 import jax.numpy as jnp
 from jax import lax
+from jax.experimental import pallas as pl
+from jax.experimental.pallas import tpu as pltpu
 from jax.sharding import PartitionSpec as P
 
 EPS = 1e-06
@@ -418,6 +422,1046 @@
     )
 
 
+PLANE = ("head", "mp")
+BIT_X, BIT_C, BIT_Y = 1, 2, 4
+NT = (((1,), (1,)), ((), ()))
+NN = (((1,), (0,)), ((), ()))
+TN = (((0,), (0,)), ((), ()))
+F32 = jnp.float32
+BF16 = jnp.bfloat16
+COST_SHARE = 0.4
+LATE_SHARE = 0.4
+
+
+def dot(left, right, dims=NN):
+    return lax.dot_general(left, right, dims, preferred_element_type=F32)
+
+
+def swap(values, bits):
+    return lax.ppermute(values, PLANE, [(i, i ^ bits) for i in range(8)])
+
+
+def swap_mixed(values, core0, core1):
+    return lax.ppermute(
+        values, PLANE, [(i, i ^ (core1 if i & BIT_C else core0)) for i in range(8)]
+    )
+
+
+class Order:
+    def __init__(self):
+        self.ahead = []
+        self.last = None
+
+    def need(self, *values):
+        self.ahead.extend(values)
+
+    def pin(self, value):
+        if self.last is None:
+            return value
+        return lax.optimization_barrier((value, self.last))[0]
+
+    def run(self, op, *operands):
+        if self.ahead:
+            operands = lax.optimization_barrier((tuple(operands), tuple(self.ahead)))[0]
+        out = op(*operands)
+        self.last = out[0] if isinstance(out, (tuple, list)) else out
+        self.ahead = [self.last]
+        return out
+
+
+class Gather:
+    def __init__(self, order, rows):
+        self.order = order
+        self.rows = rows
+        self.came = swap_mixed(rows, BIT_X, BIT_Y)
+
+    def second(self):
+        came = self.order.pin(self.came)
+        near = jnp.concatenate([self.rows, came], axis=0)
+        self.came = swap_mixed(near, BIT_Y, BIT_X)
+        self.pieces = [near, None, swap(near, BIT_C), None]
+        return near
+
+    def third(self):
+        far = self.order.pin(self.came)
+        self.pieces[1], self.pieces[3] = far, swap(far, BIT_C)
+        return far
+
+
+class Scatter:
+    def __init__(self, order, near, far):
+        self.order = order
+        self.came = (swap(near, BIT_C), swap(far, BIT_C))
+
+    def add(self, near, far):
+        near_came, far_came = self.order.pin(self.came)
+        far = (far.astype(F32) + far_came.astype(F32)).astype(BF16)
+        near = (near.astype(F32) + near_came.astype(F32)).astype(BF16)
+        return self.second(near, far)
+
+    def second(self, near, far):
+        self.kept = near
+        self.came = swap_mixed(far, BIT_Y, BIT_X)
+        return (near, far)
+
+    def third(self):
+        came = self.order.pin(self.came)
+        half = came.shape[0] // 2
+        sent = (self.kept[half:].astype(F32) + came[half:].astype(F32)).astype(BF16)
+        self.kept = self.kept[:half].astype(F32) + came[:half].astype(F32)
+        self.came = swap_mixed(sent, BIT_X, BIT_Y)
+        return sent
+
+    def result(self):
+        return self.kept + self.order.pin(self.came).astype(F32)
+
+
+def norm_rope(raw, gain, cosine, sine):
+    scale_rows = lax.rsqrt(jnp.mean(raw * raw, axis=-1, keepdims=True) + EPS)
+    hat = raw * scale_rows
+    turned = hat * gain
+    return (turned * cosine + pltpu.roll(turned, 64, 1) * sine, hat, scale_rows)
+
+
+def norm_rope_back(grad, hat, scale_rows, gain, cosine, sine):
+    grad_n = grad * cosine - pltpu.roll(grad, 64, 1) * sine
+    gain_part = jnp.sum(grad_n * hat, axis=0, keepdims=True)
+    scaled = grad_n * gain
+    raw = scale_rows * (scaled - hat * jnp.mean(scaled * hat, axis=-1, keepdims=True))
+    return (raw, gain_part)
+
+
+def two_lanes(first, second, shape):
+    lane = lax.broadcasted_iota(jnp.int32, shape, 1)
+    return jnp.where(lane == 0, first, jnp.where(lane == 1, second, 0.0))
+
+
+def cost(flops, traffic, transcendentals=0, share=COST_SHARE):
+    return pl.CostEstimate(
+        flops=int(flops / share),
+        bytes_accessed=int(traffic / share),
+        transcendentals=int(transcendentals / share),
+    )
+
+
+SLOT, LIVE, BLOCK, PLACE = 0, 8, 9, 41
+
+
+def attend_table(plane_idx, core, live_count):
+    slot = jnp.arange(8, dtype=jnp.int32)
+    across, low, high = slot >> 2, slot & 1, (slot >> 1) & 1
+    x_first = (core ^ across) == 0
+    apart = across * 2 + jnp.where(x_first, low + 4 * high, high + 4 * low)
+    place = apart ^ plane_idx
+    slots = jnp.sum(jnp.where(place[None, :] == slot[:, None], slot[None, :], 0), axis=1)
+    steps = jnp.arange(8, dtype=jnp.int32)
+    blocks = []
+    for piece in range(4):
+        one, two = place[2 * piece], place[2 * piece + 1]
+        first = jnp.where(one < two, 0, 1)
+        blocks.append(jnp.where(steps >= jnp.maximum(one, two), 1 - first, first))
+    return jnp.concatenate([slots, live_count[None]] + blocks + [place]).astype(jnp.int32)
+
+
+def take_piece(slot, pieces):
+    near = jnp.where(slot < 2, pieces[0][...], pieces[1][...])
+    far = jnp.where(slot < 6, pieces[2][...], pieces[3][...])
+    return jnp.where(slot < 4, near, far)
+
+
+def attend_forward_kernel(table, *refs):
+    x_pieces, (weights, cosine, sine, q_gain, k_gain) = refs[:4], refs[4:9]
+    proj, attn_o, lse, gated = refs[9:13]
+    out_pieces, (keys, values, acc) = refs[13:17], refs[17:]
+    step = pl.program_id(0)
+    rows = proj.shape[0]
+    live, slot = table[LIVE], table[SLOT + step]
+    cos_b, sin_b = cosine[...], sine[...]
+    here = pl.multiple_of(step * rows, rows)
+    proj[...] = dot(take_piece(slot, x_pieces), weights[:, 0:640])
+    key, _, _ = norm_rope(proj[:, 256:384], k_gain[...], cos_b, sin_b)
+    keys[pl.ds(here, rows), :] = key.astype(BF16)
+    values[pl.ds(here, rows), 0:128] = proj[:, 384:512].astype(BF16)
+    values[pl.ds(here, rows), 128:256] = jnp.ones((rows, 128), BF16)
+    q_scale = 128**-0.5
+    first, _, _ = norm_rope(proj[:, 0:128], q_gain[...], cos_b, sin_b)
+    second, _, _ = norm_rope(proj[:, 128:256], q_gain[...], cos_b, sin_b)
+    query = (jnp.concatenate([first, second], axis=0) * q_scale).astype(BF16)
+
+    def add_block(index, mask_of):
+        there = pl.multiple_of(index * rows, rows)
+        weight = jnp.exp(dot(query, keys[pl.ds(there, rows), :], NT))
+        if mask_of is not None:
+            weight = jnp.where(mask_of(there), weight, 0.0)
+        acc[...] += dot(weight.astype(BF16), values[pl.ds(there, rows), :])
+
+    def column():
+        return lax.broadcasted_iota(jnp.int32, (2 * rows, rows), 1)
+
+    def causal(there):
+        row = lax.broadcasted_iota(jnp.int32, (2 * rows, rows), 0)
+        return (column() <= jnp.where(row >= rows, row - rows, row)) & (column() + there < live)
+
+    acc[...] = jnp.zeros_like(acc)
+    whole = jnp.minimum(step, live // rows)
+
+    def block(index, carry):
+        add_block(index, None)
+        return carry
+
+    lax.fori_loop(0, whole, block, 0)
+
+    @pl.when((whole < step) & (whole * rows < live))
+    def _():
+        add_block(whole, lambda there: column() + there < live)
+
+    @pl.when(here < live)
+    def _():
+        add_block(step, causal)
+
+    total = acc[:, 128:129]
+    out = acc[:, 0:128] / total
+    log_total = jnp.log(total)
+    gate0 = jax.nn.sigmoid(proj[:, 512:513])
+    gate1 = jax.nn.sigmoid(proj[:, 513:514])
+    attn_o[:, 0:128] = out[:rows]
+    attn_o[:, 128:256] = out[rows:]
+    gated[:, 0:128] = (out[:rows] * gate0).astype(BF16)
+    gated[:, 128:256] = (out[rows:] * gate1).astype(BF16)
+    lse[...] = two_lanes(log_total[:rows], log_total[rows:], (rows, 128))
+    part = dot(gated[...], weights[:, 640:896], NT).astype(BF16)
+    for piece in range(4):
+
+        @pl.when(slot // 2 == piece)
+        def _():
+            out_pieces[piece][...] = part
+
+
+def attend_backward_kernel(table, *refs):
+    d_pieces = refs[:4]
+    weights, proj, attn_o, lse, cosine, sine, q_gain, k_gain = refs[4:12]
+    d_proj, gain_q, gain_k = refs[12:15]
+    back_pieces = refs[15:19]
+    keys, keys_t, values, k_raw, d_keys, d_values, d_query, d_held = refs[19:]
+    step = pl.program_id(0)
+    rows = proj.shape[0]
+    live = table[LIVE]
+    q_scale = 128**-0.5
+
+    @pl.when(step == 0)
+    def _():
+        gain_q[...] = jnp.zeros_like(gain_q)
+        gain_k[...] = jnp.zeros_like(gain_k)
+
+    @pl.when(step < 8)
+    def _():
+        here = pl.multiple_of(step * rows, rows)
+        slot = table[SLOT + step]
+        cos_b, sin_b = cosine[pl.ds(here, rows), :], sine[pl.ds(here, rows), :]
+        raw_key = proj[:, 256:384]
+        k_raw[pl.ds(here, rows), :] = raw_key
+        key, _, _ = norm_rope(raw_key, k_gain[...], cos_b, sin_b)
+        key = key.astype(BF16)
+        keys[pl.ds(here, rows), :] = key
+        keys_t[step] = key.T
+        values[pl.ds(here, rows), :] = proj[:, 384:512].astype(BF16)
+        d_keys[pl.ds(here, rows), :] = jnp.zeros((rows, 128), F32)
+        d_values[pl.ds(here, rows), :] = jnp.zeros((rows, 128), F32)
+        d_query[...] = jnp.zeros_like(d_query)
+        first, hat0, scale0 = norm_rope(proj[:, 0:128], q_gain[...], cos_b, sin_b)
+        second, hat1, scale1 = norm_rope(proj[:, 128:256], q_gain[...], cos_b, sin_b)
+        query = (jnp.concatenate([first, second], axis=0) * q_scale).astype(BF16)
+        gate0 = jax.nn.sigmoid(proj[:, 512:513])
+        gate1 = jax.nn.sigmoid(proj[:, 513:514])
+        d_gated = dot(take_piece(slot, d_pieces), weights[:, 640:896])
+        dg0, dg1 = d_gated[:, 0:128], d_gated[:, 128:256]
+        out0, out1 = attn_o[:, 0:128], attn_o[:, 128:256]
+        do0, do1 = (dg0 * gate0).astype(BF16), (dg1 * gate1).astype(BF16)
+        logit0 = jnp.sum(dg0 * out0, axis=-1, keepdims=True) * gate0 * (1.0 - gate0)
+        logit1 = jnp.sum(dg1 * out1, axis=-1, keepdims=True) * gate1 * (1.0 - gate1)
+        d_held[pl.ds(here, rows), 512:640] = two_lanes(logit0, logit1, (rows, 128)).astype(BF16)
+        delta0 = jnp.sum(do0.astype(F32) * out0, axis=-1, keepdims=True)
+        delta1 = jnp.sum(do1.astype(F32) * out1, axis=-1, keepdims=True)
+        delta_t = two_lanes(delta0, delta1, (rows, 128)).T
+        delta = jnp.concatenate([delta_t[0:1], delta_t[1:2]], axis=1)
+        lse_t = lse[...].T
+        log_total = jnp.concatenate([lse_t[0:1], lse_t[1:2]], axis=1)
+        d_out = jnp.concatenate([do0, do1], axis=0)
+
+        def add_block(index, mask_of):
+            there = pl.multiple_of(index * rows, rows)
+            scores = dot(keys[pl.ds(there, rows), :], query, NT)
+            probs = jnp.exp(scores - log_total)
+            if mask_of is not None:
+                probs = jnp.where(mask_of(there), probs, 0.0)
+            d_probs = dot(values[pl.ds(there, rows), :], d_out, NT)
+            d_scores = (probs * (d_probs - delta)).astype(BF16)
+            d_values[pl.ds(there, rows), :] += dot(probs.astype(BF16), d_out)
+            d_keys[pl.ds(there, rows), :] += dot(d_scores, query)
+            d_query[...] += dot(keys_t[index], d_scores)
+
+        def key_row():
+            return lax.broadcasted_iota(jnp.int32, (rows, 2 * rows), 0)
+
+        def causal(there):
+            q_col = lax.broadcasted_iota(jnp.int32, (rows, 2 * rows), 1)
+            q_col = jnp.where(q_col >= rows, q_col - rows, q_col)
+            return (key_row() <= q_col) & (key_row() + there < live)
+
+        whole = jnp.minimum(step, live // rows)
+
+        def block(index, carry):
+            add_block(index, None)
+            return carry
+
+        lax.fori_loop(0, whole, block, 0)
+
+        @pl.when((whole < step) & (whole * rows < live))
+        def _():
+            add_block(whole, lambda there: key_row() + there < live)
+
+        @pl.when(here < live)
+        def _():
+            add_block(step, causal)
+
+        grads = d_query[...].T * q_scale
+        raw0, part0 = norm_rope_back(grads[:rows], hat0, scale0, q_gain[...], cos_b, sin_b)
+        raw1, part1 = norm_rope_back(grads[rows:], hat1, scale1, q_gain[...], cos_b, sin_b)
+        d_held[pl.ds(here, rows), 0:128] = raw0.astype(BF16)
+        d_held[pl.ds(here, rows), 128:256] = raw1.astype(BF16)
+        gain_q[0:1, :] += part0 + part1
+
+    @pl.when(step >= 8)
+    def _():
+        slot = (step - 4) % 8
+        there = pl.multiple_of(table[PLACE + slot] * rows, rows)
+        cos_k, sin_k = cosine[pl.ds(there, rows), :], sine[pl.ds(there, rows), :]
+        _, hat, scale_rows = norm_rope(k_raw[pl.ds(there, rows), :], k_gain[...], cos_k, sin_k)
+        raw, part = norm_rope_back(
+            d_keys[pl.ds(there, rows), :], hat, scale_rows, k_gain[...], cos_k, sin_k
+        )
+        gain_k[0:1, :] += part
+        d_held[pl.ds(there, rows), 256:384] = raw.astype(BF16)
+        d_held[pl.ds(there, rows), 384:512] = d_values[pl.ds(there, rows), :].astype(BF16)
+        d_block = d_held[pl.ds(there, rows), :]
+        d_proj[...] = d_block
+        back = dot(d_block, weights[:, 0:640], NT).astype(BF16)
+        for piece in range(4):
+
+            @pl.when(slot // 2 == piece)
+            def _():
+                back_pieces[piece][...] = back
+
+
+def attend_forward_call(table, pieces, weights, cosine, sine, q_gain, k_gain):
+    seq_len, width = cosine.shape[0], weights.shape[0]
+    rows = seq_len // 8
+    by_slot = lambda i, t: (t[SLOT + i], 0)
+    by_place = lambda i, t: (i, 0)
+    fixed = lambda i, t: (0, 0)
+    whole = [
+        pl.BlockSpec((rows, width), lambda i, t, k=k: (t[BLOCK + 8 * k + i], 0)) for k in range(4)
+    ]
+    pairs = seq_len * (seq_len + rows)
+    return pl.pallas_call(
+        attend_forward_kernel,
+        grid_spec=pltpu.PrefetchScalarGridSpec(
+            num_scalar_prefetch=1,
+            grid=(8,),
+            in_specs=whole
+            + [
+                pl.BlockSpec(weights.shape, fixed, pipeline_mode=pl.Buffered(1)),
+                pl.BlockSpec((rows, 128), by_place),
+                pl.BlockSpec((rows, 128), by_place),
+                pl.BlockSpec((1, 128), fixed),
+                pl.BlockSpec((1, 128), fixed),
+            ],
+            out_specs=[
+                pl.BlockSpec((rows, 640), by_slot),
+                pl.BlockSpec((rows, 256), by_slot),
+                pl.BlockSpec((rows, 128), by_slot),
+                pl.BlockSpec((rows, 256), by_slot),
+            ]
+            + whole,
+            scratch_shapes=[
+                pltpu.VMEM((seq_len, 128), BF16),
+                pltpu.VMEM((seq_len, 256), BF16),
+                pltpu.VMEM((2 * rows, 256), F32),
+            ],
+        ),
+        out_shape=[
+            jax.ShapeDtypeStruct((seq_len, 640), F32),
+            jax.ShapeDtypeStruct((seq_len, 256), F32),
+            jax.ShapeDtypeStruct((seq_len, 128), F32),
+            jax.ShapeDtypeStruct((seq_len, 256), BF16),
+        ]
+        + [jax.ShapeDtypeStruct((2 * rows, width), BF16)] * 4,
+        compiler_params=pltpu.CompilerParams(
+            dimension_semantics=("arbitrary",), vmem_limit_bytes=62 << 20
+        ),
+        cost_estimate=cost(
+            2 * seq_len * width * 896 + 4 * pairs * 128, 2 * seq_len * (2 * width + 2200), pairs
+        ),
+        name="attend_forward",
+    )(table, *pieces, weights, cosine, sine, q_gain, k_gain)
+
+
+def attend_backward_call(table, pieces, weights, proj, attn_o, lse, cosine, sine, q_gain, k_gain):
+    seq_len, width = cosine.shape[0], weights.shape[0]
+    rows = seq_len // 8
+    by_slot = lambda i, t: (t[SLOT + jnp.minimum(i, 7)], 0)
+    last_slot = lambda i, t: (jnp.where(i < 8, 4, (i - 4) % 8), 0)
+    fixed = lambda i, t: (0, 0)
+    pairs = seq_len * (seq_len + rows)
+    return pl.pallas_call(
+        attend_backward_kernel,
+        grid_spec=pltpu.PrefetchScalarGridSpec(
+            num_scalar_prefetch=1,
+            grid=(16,),
+            in_specs=[
+                pl.BlockSpec(
+                    (rows, width), lambda i, t, k=k: (t[BLOCK + 8 * k + jnp.minimum(i, 7)], 0)
+                )
+                for k in range(4)
+            ]
+            + [
+                pl.BlockSpec(weights.shape, fixed, pipeline_mode=pl.Buffered(1)),
+                pl.BlockSpec((rows, 640), by_slot),
+                pl.BlockSpec((rows, 256), by_slot),
+                pl.BlockSpec((rows, 128), by_slot),
+                pl.BlockSpec((seq_len, 128), fixed, pipeline_mode=pl.Buffered(1)),
+                pl.BlockSpec((seq_len, 128), fixed, pipeline_mode=pl.Buffered(1)),
+                pl.BlockSpec((1, 128), fixed),
+                pl.BlockSpec((1, 128), fixed),
+            ],
+            out_specs=[
+                pl.BlockSpec((rows, 640), last_slot),
+                pl.BlockSpec((8, 128), fixed),
+                pl.BlockSpec((8, 128), fixed),
+            ]
+            + [
+                pl.BlockSpec(
+                    (rows, width), lambda i, t, k=k: (jnp.clip(i - 8 - (2 * k + 4) % 8, 0, 1), 0)
+                )
+                for k in range(4)
+            ],
+            scratch_shapes=[
+                pltpu.VMEM((seq_len, 128), BF16),
+                pltpu.VMEM((8, 128, rows), BF16),
+                pltpu.VMEM((seq_len, 128), BF16),
+                pltpu.VMEM((seq_len, 128), F32),
+                pltpu.VMEM((seq_len, 128), F32),
+                pltpu.VMEM((seq_len, 128), F32),
+                pltpu.VMEM((128, 2 * rows), F32),
+                pltpu.VMEM((seq_len, 640), BF16),
+            ],
+        ),
+        out_shape=[
+            jax.ShapeDtypeStruct((seq_len, 640), BF16),
+            jax.ShapeDtypeStruct((8, 128), F32),
+            jax.ShapeDtypeStruct((8, 128), F32),
+        ]
+        + [jax.ShapeDtypeStruct((2 * rows, width), BF16)] * 4,
+        compiler_params=pltpu.CompilerParams(
+            dimension_semantics=("arbitrary",), vmem_limit_bytes=62 << 20
+        ),
+        cost_estimate=cost(
+            2 * seq_len * width * 896 + 10 * pairs * 128,
+            2 * seq_len * (2 * width + 2200),
+            pairs,
+            LATE_SHARE,
+        ),
+        name="attend_backward",
+    )(table, *pieces, weights, proj, attn_o, lse, cosine, sine, q_gain, k_gain)
+
+
+def feed_forward_kernel(*refs):
+    rows_near, rows_far, cot_near, cot_far, w_down_t, w_inner = refs[:6]
+    sums = refs[6:-6]
+    hidden_out, d_pre_out, down_near, down_far, back_near, back_far = refs[-6:]
+    near = pl.program_id(0) < 2
+    units = hidden_out.shape[1]
+    pre = dot(jnp.where(near, rows_near[...], rows_far[...]), w_inner[...])
+    d_hidden = dot(jnp.where(near, cot_near[...], cot_far[...]), w_down_t[...])
+    gate_pre, up_pre = pre[:, :units], pre[:, units:]
+    gate_sig = jax.nn.sigmoid(gate_pre)
+    gate_act = gate_pre * gate_sig
+    hidden_out[...] = (gate_act * up_pre).astype(BF16)
+    d_pre_out[:, units:] = (d_hidden * gate_act).astype(BF16)
+    d_pre_out[:, :units] = (
+        d_hidden * up_pre * gate_sig * (1.0 + gate_pre * (1.0 - gate_sig))
+    ).astype(BF16)
+    back = dot(d_pre_out[...], w_inner[...], NT)
+    down = dot(hidden_out[...], w_down_t[...], NT)
+    if sums:
+        back = back + jnp.where(near, sums[0][...], sums[1][...]).astype(F32)
+
+    @pl.when(near)
+    def _():
+        back_near[...] = back.astype(BF16)
+        down_near[...] = down.astype(BF16)
+
+    @pl.when(jnp.logical_not(near))
+    def _():
+        back_far[...] = back.astype(BF16)
+        down_far[...] = down.astype(BF16)
+
+
+def feed_forward_call(rows, cots, w_down_t, w_inner, backs=()):
+    count, width = rows[0].shape
+    units = w_down_t.shape[1]
+    tile = count // 2
+    by_row = lambda i: (i, 0)
+    fixed = lambda i: (0, 0)
+    near = pl.BlockSpec((tile, width), lambda i: (jnp.minimum(i, 1), 0))
+    far = pl.BlockSpec((tile, width), lambda i: (jnp.maximum(i - 2, 0), 0))
+    wide = jax.ShapeDtypeStruct((count, width), BF16)
+    out = pl.pallas_call(
+        feed_forward_kernel,
+        grid=(4,),
+        in_specs=[near, far, near, far]
+        + [pl.BlockSpec(w.shape, fixed, pipeline_mode=pl.Buffered(1)) for w in (w_down_t, w_inner)]
+        + [near, far] * (len(backs) // 2),
+        out_specs=[
+            pl.BlockSpec((tile, units), by_row),
+            pl.BlockSpec((tile, 2 * units), by_row),
+            near,
+            far,
+            near,
+            far,
+        ],
+        out_shape=[
+            jax.ShapeDtypeStruct((2 * count, units), BF16),
+            jax.ShapeDtypeStruct((2 * count, 2 * units), BF16),
+            wide,
+            wide,
+            wide,
+            wide,
+        ],
+        compiler_params=pltpu.CompilerParams(
+            dimension_semantics=("arbitrary",), vmem_limit_bytes=52 << 20
+        ),
+        cost_estimate=cost(24 * count * width * units, 2 * width * (8 * count + 3 * units)),
+        name="feed_forward",
+    )(*rows, *cots, w_down_t, w_inner, *backs)
+    return (out[0], out[1], (out[2], out[3]), (out[4], out[5]))
+
+
+def weight_grad_call(n_parts, lefts, terms, weights=None):
+    n_pieces = len(lefts[0])
+    rows, width = lefts[0][0].shape
+    columns = [pieces[0][0].shape[1] for _, pieces in terms]
+    starts = [sum(columns[:k]) for k in range(len(terms))]
+    total = sum(columns)
+    arrays, place = ([], {})
+    for _, pieces in terms:
+        for array, _ in pieces:
+            if id(array) not in place:
+                place[id(array)] = len(arrays)
+                arrays.append(array)
+    n_left, n_terms = len(lefts), len(terms)
+
+    def kernel(*refs):
+        left_refs = refs[: n_left * n_pieces]
+        right_refs = refs[len(left_refs) : len(left_refs) + len(arrays)]
+        rest = list(refs[len(left_refs) + len(arrays) :])
+        if weights is not None:
+            weights_ref = rest.pop(0)
+        out = rest.pop(0)
+        if weights is not None:
+            gain = rest.pop(0)
+        left_buf, right_buf = rest[:n_left], rest[n_left : n_left + n_terms]
+        accs, sems = rest[n_left + n_terms : -1], rest[-1]
+
+        def copies(piece, slot):
+            made = [
+                pltpu.make_async_copy(
+                    left_refs[k * n_pieces + piece], left_buf[k].at[slot], sems.at[slot, k]
+                )
+                for k in range(n_left)
+            ]
+            for k, (_, pieces) in enumerate(terms):
+                array, first = pieces[piece]
+                made.append(
+                    pltpu.make_async_copy(
+                        right_refs[place[id(array)]].at[pl.ds(first, rows)],
+                        right_buf[k].at[slot],
+                        sems.at[slot, n_left + k],
+                    )
+                )
+            return made
+
+        for copy in copies(0, 0):
+            copy.start()
+        for acc in accs:
+            acc[...] = jnp.zeros_like(acc)
+
+        def body(index, carry):
+            slot = lax.rem(index, 2)
+            for piece in range(1, n_pieces):
+
+                @pl.when(index + 1 == piece)
+                def _():
+                    for copy in copies(piece, piece % 2):
+                        copy.start()
+
+            for copy in copies(0, slot):
+                copy.wait()
+            for k, (left, _) in enumerate(terms):
+                for first in range(0, columns[k], 256):
+                    some = slice(first, min(first + 256, columns[k]))
+                    accs[k][some, :] += dot(right_buf[k][slot, :, some], left_buf[left][slot], TN)
+            return carry
+
+        lax.fori_loop(0, n_pieces, body, 0)
+        part = width // n_parts
+        for p in range(n_parts):
+            for k in range(n_terms):
+                start = p * total + starts[k]
+                out[start : start + columns[k], :] = accs[k][:, p * part : (p + 1) * part].astype(
+                    BF16
+                )
+        if weights is not None:
+            scaled = accs[0][...] * weights_ref[:, : columns[0]].T.astype(F32)
+            gain[...] = jnp.broadcast_to(jnp.sum(scaled, axis=0, keepdims=True), gain.shape)
+
+    out_shape = [jax.ShapeDtypeStruct((n_parts * total, width // n_parts), BF16)]
+    vmem = pl.BlockSpec(memory_space=pltpu.VMEM)
+    operands = [piece for pieces in lefts for piece in pieces] + arrays
+    in_specs = [pl.BlockSpec(memory_space=pl.ANY)] * len(operands)
+    if weights is not None:
+        operands.append(weights)
+        in_specs.append(vmem)
+        out_shape.append(jax.ShapeDtypeStruct((8, width), F32))
+    return pl.pallas_call(
+        kernel,
+        in_specs=in_specs,
+        out_specs=[vmem] * len(out_shape),
+        out_shape=out_shape,
+        scratch_shapes=[pltpu.VMEM((2, rows, width), BF16)] * n_left
+        + [pltpu.VMEM((2, rows, c), BF16) for c in columns]
+        + [pltpu.VMEM((c, width), F32) for c in columns]
+        + [pltpu.SemaphoreType.DMA((2, n_left + n_terms))],
+        compiler_params=pltpu.CompilerParams(vmem_limit_bytes=56 << 20),
+        cost_estimate=cost(
+            2 * n_pieces * rows * width * total,
+            2 * n_pieces * rows * (n_left * width + total) + 2 * width * total,
+            0,
+            LATE_SHARE,
+        ),
+        name="weight_grad",
+    )(*operands)
+
+
+def pack_attention_kernel(index, query, key, value, headgate, out, packed):
+    half = pl.program_id(0) ^ index[0]
+    packed[0, :, 0:256] = query[...]
+    packed[0, :, 256:384] = key[...]
+    packed[0, :, 384:512] = value[...]
+    gates = headgate[...].astype(F32)
+    first = jnp.where(half == 0, gates[:, 0:1], gates[:, 2:3])
+    second = jnp.where(half == 0, gates[:, 1:2], gates[:, 3:4])
+    packed[0, :, 512:640] = two_lanes(first, second, (packed.shape[1], 128)).astype(BF16)
+    packed[0, :, 640:896] = out[...].T
+
+
+def pack_attention(index, query, key, value, headgate, out):
+    rows = query.shape[0]
+    half = lambda i, t: (0, i ^ t[0])
+    return pl.pallas_call(
+        pack_attention_kernel,
+        grid_spec=pltpu.PrefetchScalarGridSpec(
+            num_scalar_prefetch=1,
+            grid=(2,),
+            in_specs=[
+                pl.BlockSpec((rows, 256), half),
+                pl.BlockSpec((rows, 128), half),
+                pl.BlockSpec((rows, 128), half),
+                pl.BlockSpec(headgate.shape, lambda i, t: (0, 0)),
+                pl.BlockSpec((256, out.shape[1]), lambda i, t: (i ^ t[0], 0)),
+            ],
+            out_specs=pl.BlockSpec((1, rows, 896), lambda i, t: (i, 0, 0)),
+        ),
+        out_shape=jax.ShapeDtypeStruct((2, rows, 896), BF16),
+        cost_estimate=cost(0, 4 * rows * 896 * 2),
+        name="pack_attention",
+    )(index, query, key, value, headgate, out)
+
+
+def unpack_attention_kernel(index, kept, came, out_kept, out_came, query, key, value, headgate, out):
+    flip = index[0] == 1
+
+    def ordered(mine, other):
+        return [
+            jnp.where(flip, other[...], mine[...]).astype(F32),
+            jnp.where(flip, mine[...], other[...]).astype(F32),
+        ]
+
+    for k, part in enumerate(ordered(kept, came)):
+        query[:, 256 * k : 256 * k + 256] = part[0:256].T
+        key[:, 128 * k : 128 * k + 128] = part[256:384].T
+        value[:, 128 * k : 128 * k + 128] = part[384:512].T
+        headgate[:, 2 * k : 2 * k + 2] = part[512:640].T[:, 0:2]
+    for k, part in enumerate(ordered(out_kept, out_came)):
+        out[256 * k : 256 * k + 256, :] = part
+
+
+def unpack_attention(index, kept, came, out_kept, out_came):
+    rows = kept.shape[1]
+    vmem = pl.BlockSpec(memory_space=pltpu.VMEM)
+    shapes = [(rows, 512), (rows, 256), (rows, 256), (rows, 4), (512, rows)]
+    return pl.pallas_call(
+        unpack_attention_kernel,
+        in_specs=[pl.BlockSpec(memory_space=pltpu.SMEM)] + [vmem] * 4,
+        out_specs=[vmem] * 5,
+        out_shape=[jax.ShapeDtypeStruct(shape, F32) for shape in shapes],
+        cost_estimate=cost(0, 8 * rows * 896),
+        name="unpack_attention",
+    )(index, kept, came, out_kept, out_came)
+
+
+def pack_feed_forward_kernel(index, gate, up, down, packed):
+    units = gate.shape[1]
+    packed[0, :, :units] = down[...].T
+    packed[0, :, units : 2 * units] = gate[...]
+    packed[0, :, 2 * units :] = up[...]
+
+
+def pack_feed_forward(index, gate, up, down):
+    rows, units = gate.shape[0], gate.shape[1] // 4
+    quarter = pl.BlockSpec((rows, units), lambda i, t: (0, i ^ t[0]))
+    return pl.pallas_call(
+        pack_feed_forward_kernel,
+        grid_spec=pltpu.PrefetchScalarGridSpec(
+            num_scalar_prefetch=1,
+            grid=(4,),
+            in_specs=[
+                quarter,
+                quarter,
+                pl.BlockSpec((units, rows), lambda i, t: (i ^ t[0], 0)),
+            ],
+            out_specs=pl.BlockSpec((1, rows, 3 * units), lambda i, t: (i, 0, 0)),
+        ),
+        out_shape=jax.ShapeDtypeStruct((4, rows, 3 * units), BF16),
+        cost_estimate=cost(0, 8 * rows * units * 6),
+        name="pack_feed_forward",
+    )(index, gate, up, down)
+
+
+def unpack_feed_forward_kernel(index, *refs):
+    pieces, (gate, up, down) = refs[:8], refs[8:]
+    units = gate.shape[1]
+    apart = pl.program_id(0) ^ index[0]
+
+    def of_piece(group):
+        low = jnp.where(apart == 0, group[0][...], group[1][...])
+        high = jnp.where(apart == 2, group[2][...], group[3][...])
+        return jnp.where(apart < 2, low, high).astype(F32)
+
+    inner = of_piece(pieces[:4])
+    gate[...] = inner[:units].T
+    up[...] = inner[units:].T
+    down[...] = of_piece(pieces[4:])
+
+
+def unpack_feed_forward(index, inners, downs):
+    units, rows = downs[0].shape
+    quarter = pl.BlockSpec((rows, units), lambda i, t: (0, i))
+    whole = [pl.BlockSpec(v.shape, lambda i, t: (0, 0)) for v in (*inners, *downs)]
+    wide = jax.ShapeDtypeStruct((rows, 4 * units), F32)
+    return pl.pallas_call(
+        unpack_feed_forward_kernel,
+        grid_spec=pltpu.PrefetchScalarGridSpec(
+            num_scalar_prefetch=1,
+            grid=(4,),
+            in_specs=whole,
+            out_specs=[quarter, quarter, pl.BlockSpec((units, rows), lambda i, t: (i, 0))],
+        ),
+        out_shape=[wide, wide, jax.ShapeDtypeStruct((4 * units, rows), F32)],
+        cost_estimate=cost(0, 24 * rows * units * 4),
+        name="unpack_feed_forward",
+    )(index, *inners, *downs)
+
+
+def pick(flag, first, second):
+    return jnp.where(flag, first, second)
+
+
+def reorder_by(pieces, index):
+    low, high = (index & 1) == 1, (index & 2) == 2
+    swapped = [pick(low, pieces[j ^ 1], pieces[j]) for j in range(4)]
+    return [pick(high, swapped[j ^ 2], swapped[j]) for j in range(4)]
+
+
+def local_plane(
+    inputs,
+    cotangent,
+    seq_counts,
+    seq_bucket,
+    attn_norm_gain,
+    q_norm_gain,
+    k_norm_gain,
+    w_query,
+    w_key,
+    w_value,
+    w_headgate,
+    w_out,
+    ffn_norm_gain,
+    w_gate,
+    w_up,
+    w_down,
+):
+    micro_batches, row_count, model_width = inputs.shape
+    both = range(micro_batches)
+    n_dp = lax.axis_size("dp")
+    head_idx = lax.axis_index("head")
+    mp_idx = lax.axis_index("mp")
+    dp_idx = lax.axis_index("dp")
+    core = head_idx & 1
+    plane_idx = head_idx * 2 + mp_idx
+    seq_len = row_count * 8
+    units = w_gate.shape[1] // 4
+    head_at = head_idx[None].astype(jnp.int32)
+    mp_at = mp_idx[None].astype(jnp.int32)
+    order = Order()
+
+    def after(value, *ahead):
+        return lax.optimization_barrier((value, ahead))[0]
+
+    halves = pack_attention(mp_at, w_query, w_key, w_value, w_headgate, w_out)
+    attn_came = swap(halves[1], BIT_X)
+
+    slot_ids = jnp.arange(micro_batches * n_dp, dtype=jnp.int32)
+    slot_count = jnp.sum(
+        jnp.where(seq_bucket[None, :] == slot_ids[:, None], seq_counts[None, :], 0), axis=1
+    )
+    own_pos = plane_idx * row_count + jnp.arange(row_count, dtype=jnp.int32)
+    live = [slot_count[n * n_dp + dp_idx] for n in both]
+    x_float = [inputs[n].astype(F32) for n in both]
+    scale1 = [rms_scale(x) for x in x_float]
+    normed1 = [x * scale for x, scale in zip(x_float, scale1)]
+    xn1_own = [(n * attn_norm_gain).astype(BF16) for n in normed1]
+    cot_live = [
+        cotangent[n].astype(F32) * (own_pos < live[n]).astype(F32)[:, None] for n in both
+    ]
+    cot_own = [c.astype(BF16) for c in cot_live]
+    xn1, xn2, cot, d_attn = ([None] * micro_batches for _ in range(4))
+    xn1[0] = Gather(order, xn1_own[0])
+    is_first = mp_idx == 0
+    attn_rows = jnp.concatenate(
+        [pick(is_first, halves[0], attn_came), pick(is_first, attn_came, halves[0])], axis=0
+    )
+    w_attn = lax.all_gather(attn_rows, "dp", axis=0, tiled=True)
+
+    quarters = pack_feed_forward(head_at, w_gate, w_up, w_down)
+    traded = [quarters[0]] + [swap(quarters[r], r * 2) for r in (1, 2, 3)]
+    near = xn1[0].second()
+    parts = [[t[:, :units] for t in traded], [t[:, units:] for t in traded]]
+    ffn_rows = [jnp.concatenate(reorder_by(part, head_idx), axis=0) for part in parts]
+    ffn_rows = after(tuple(ffn_rows), attn_rows)
+    w_ffn = [lax.all_gather(rows, "dp", axis=0, tiled=True) for rows in ffn_rows]
+
+    xn1[1] = Gather(order, after(xn1_own[1], traded[1]))
+    tables = [attend_table(plane_idx, core, count) for count in live]
+    table_cos, table_sin = rope_tables(jnp.arange(seq_len, dtype=jnp.int32), 64)
+    table_cos, table_sin = table_cos[:, 0, :], table_sin[:, 0, :]
+    cosine = jnp.concatenate([table_cos, table_cos], axis=1)
+    sine = jnp.concatenate([-table_sin, table_sin], axis=1)
+    fixed = (cosine, sine, q_norm_gain[None, :], k_norm_gain[None, :])
+    att, out_sum = ([None] * micro_batches for _ in range(2))
+
+    def attend(n):
+        att[n] = order.run(
+            lambda *pieces: attend_forward_call(tables[n], pieces, w_attn, *fixed), *xn1[n].pieces
+        )
+        out_sum[n] = Scatter(order, att[n][6], att[n][7])
+
+    cot[0] = Gather(order, after(cot_own[0], xn1[1].second()))
+    order.need(xn1[0].third(), cot[0].second())
+    attend(0)
+    order.need(xn1[1].third(), cot[0].third())
+    order.need(*out_sum[0].add(att[0][4], att[0][5]), w_ffn[0])
+    attend(1)
+    order.need(out_sum[0].third())
+
+    hidden1, scale2, normed2 = ([None] * micro_batches for _ in range(3))
+
+    def middle(n):
+        hidden1[n] = x_float[n] + out_sum[n].result()
+        scale2[n] = rms_scale(hidden1[n])
+        normed2[n] = hidden1[n] * scale2[n]
+        rows = (normed2[n] * ffn_norm_gain).astype(BF16)
+        xn2[n] = Gather(order, rows)
+        return rows
+
+    rows = middle(0)
+    order.need(*out_sum[1].add(after(att[1][4], rows), att[1][5]))
+    order.need(xn2[0].second(), out_sum[1].third())
+    order.need(xn2[0].third(), middle(1))
+    cot[1] = Gather(order, after(cot_own[1], xn2[0].pieces[1]))
+
+    feed = {}
+    down, back = ([None] * micro_batches for _ in range(2))
+
+    def feed_other(n):
+        feed[n, 1] = order.run(
+            lambda *v: feed_forward_call(v[0:2], v[2:4], *w_ffn), *xn2[n].pieces[2:], *cot[n].pieces[2:]
+        )
+        back[n] = Scatter(order, *feed[n, 1][3])
+
+    def feed_mine(n):
+        feed[n, 0] = order.run(
+            lambda *v: feed_forward_call(v[0:2], v[2:4], *w_ffn, order.pin(back[n].came)),
+            *xn2[n].pieces[:2],
+            *cot[n].pieces[:2],
+        )
+        back[n].second(*feed[n, 0][3])
+        down[n] = Scatter(order, *after(feed[n, 1][2], feed[n, 0][0]))
+
+    d_hidden1 = [None] * micro_batches
+    gain_ffn = []
+
+    def turn(n):
+        d_xn2 = back[n].result()
+        gain_ffn.append(jnp.sum(d_xn2 * normed2[n], axis=0))
+        d_hidden1[n] = cot_live[n] + norm_back(d_xn2, normed2[n], scale2[n], ffn_norm_gain)
+        rows = d_hidden1[n].astype(BF16)
+        d_attn[n] = Gather(order, rows)
+        return rows
+
+    def row_pieces(array):
+        count = array.shape[0] // (2 * row_count)
+        return [(array, 2 * row_count * k) for k in range(count)]
+
+    def of_feed(which):
+        return [p for n in both for side in (0, 1) for p in row_pieces(feed[n, side][which])]
+
+    def rows_of(gathers):
+        return [piece for gather in gathers for piece in gather.pieces]
+
+    def grad_call(lefts, terms, weights=None):
+        count = [len(left) for left in lefts]
+        return order.run(
+            lambda *v: weight_grad_call(
+                n_dp,
+                [list(v[sum(count[:k]) : sum(count[: k + 1])]) for k in range(len(lefts))],
+                terms,
+                weights,
+            ),
+            *[piece for left in lefts for piece in left],
+        )
+
+    def sum_over_dp(values):
+        return lax.psum_scatter(values, "dp", scatter_dimension=0, tiled=True)
+
+    def quarters_of(values):
+        width = values.shape[1] // 4
+        quarter = lambda k: lax.dynamic_slice_in_dim(values, k * width, width, 1)
+        return [quarter(head_idx)] + [swap(quarter(head_idx ^ r), r * 2) for r in (1, 2, 3)]
+
+    feed_other(0)
+    order.need(xn2[1].second(), cot[1].second())
+    feed_mine(0)
+    order.need(cot[1].third(), xn2[1].third())
+    feed_other(1)
+    order.need(back[0].third(), *down[0].add(*feed[0, 0][2]))
+    feed_mine(1)
+    order.need(turn(0))
+    grads_inner = sum_over_dp(grad_call([rows_of(xn2)], [(0, of_feed(1))])[0])
+    order.need(d_attn[0].second(), down[0].third())
+    grads_down = sum_over_dp(grad_call([rows_of(cot)], [(0, of_feed(0))])[0])
+    order.need(back[1].third(), d_attn[0].third(), turn(1))
+
+    d_proj, gain_parts, rows_sum = ([None] * micro_batches for _ in range(3))
+
+    def attend_back(n):
+        out = order.run(
+            lambda *v: attend_backward_call(
+                tables[n], v, w_attn, att[n][0], att[n][1], att[n][2], *fixed
+            ),
+            *d_attn[n].pieces,
+        )
+        d_proj[n] = out[0]
+        gain_parts[n] = (out[1][0], out[2][0])
+        rows_sum[n] = Scatter(order, out[5], out[6])
+        return out
+
+    def finish(n):
+        d_xn1 = rows_sum[n].result()
+        return (d_hidden1[n] + norm_back(d_xn1, normed1[n], scale1[n], attn_norm_gain)).astype(BF16)
+
+    outputs, input_grads = ([None] * micro_batches for _ in range(2))
+    back_0 = attend_back(0)
+    order.need(d_attn[1].second(), *down[1].add(*feed[1, 0][2]))
+    order.need(*rows_sum[0].add(back_0[3], back_0[4]), d_attn[1].third())
+    grads_out = sum_over_dp(
+        grad_call(
+            [rows_of(d_attn)], [(0, [p for n in both for p in row_pieces(att[n][3])])]
+        )[0]
+    )
+    inner_quarters = quarters_of(grads_inner)
+    order.need(grads_inner)
+    back_1 = attend_back(1)
+    outputs[0] = (hidden1[0] + down[0].result()).astype(BF16)
+    order.need(rows_sum[0].third(), down[1].third(), *inner_quarters)
+    order.need(*rows_sum[1].add(back_1[3], back_1[4]))
+    down_quarters = quarters_of(grads_down)
+    order.need(grads_down)
+    grads_proj, gain_rows = grad_call(
+        [rows_of(xn1)], [(0, [p for n in both for p in row_pieces(d_proj[n])])], w_attn
+    )
+    grads_proj = sum_over_dp(grads_proj)
+    input_grads[0] = finish(0)
+    order.need(rows_sum[1].third(), *down_quarters)
+    grad_gate, grad_up, grad_down = order.run(
+        lambda *v: unpack_feed_forward(head_at, v[:4], v[4:]), *inner_quarters, *down_quarters
+    )
+    outputs[1] = (hidden1[1] + down[1].result()).astype(BF16)
+    input_grads[1] = finish(1)
+
+    gains = jnp.concatenate(
+        [gain_rows[0] / attn_norm_gain, gain_ffn[0] + gain_ffn[1]]
+        + [gain_parts[0][k] + gain_parts[1][k] for k in range(2)]
+    ).reshape(-1, 128)
+    for bits in (BIT_C, BIT_X, BIT_Y):
+        gains = gains + swap(gains, bits)
+    for step in (1, 2):
+        gains = gains + lax.ppermute(gains, "dp", [(i, i ^ step) for i in range(4)])
+    gains = gains.reshape(-1)
+    sum_attn, sum_gain_ffn = gains[:model_width], gains[model_width : 2 * model_width]
+    sum_query, sum_key = gains[-256:-128], gains[-128:]
+
+    def halves_of(values):
+        left, right = values[:, :row_count], values[:, row_count:]
+        return pick(is_first, left, right), swap(pick(is_first, right, left), BIT_X)
+
+    grad_query, grad_key, grad_value, grad_headgate, grad_out = unpack_attention(
+        mp_at, *halves_of(grads_proj), *halves_of(grads_out)
+    )
+    return (
+        jnp.stack(outputs),
+        jnp.stack(input_grads),
+        sum_attn,
+        sum_query,
+        sum_key,
+        grad_query,
+        grad_key,
+        grad_value,
+        grad_headgate,
+        grad_out,
+        sum_gain_ffn,
+        grad_gate,
+        grad_up,
+        grad_down,
+    )
+
+
+def choose_local(mesh):
+    if mesh.shape["head"] == 4 and mesh.shape["mp"] == 2 and mesh.shape["dp"] == 4:
+        return local_plane
+    return local
+
+
 def solution(mesh):
     placed = (
         P(None, ("dp", "head", "mp"), None),
@@ -438,7 +1482,7 @@
         P("mp", ("dp", "head")),
     )
     return jax.shard_map(
-        local,
+        choose_local(mesh),
         mesh=mesh,
         in_specs=placed,
         out_specs=(

time: 3040 us -> 948 us (0.31)
  waiting for transfers between devices: 2090 us -> 267 us
  matrix products: 559 us -> 0 us
  Pallas kernels: 0 us -> 401 us
  local copies, waits for them, and re-layouts: 145 us -> 41.5 us
  starting transfers between devices: 4.49 us -> 89.4 us
  blocking collectives: 66.3 us -> 0 us
  other arithmetic: 145 us -> 114 us
    reduce_scatter x24 -> x4, waiting for transfers between devices: 1270 us -> 0.05 us  [sum_over_dp(): return lax.psum_scatter(values, 'dp', scatter_dimension=0, tiled=True)]
    dot_general x104 -> x0, matrix products: 559 us -> none  [the longest x16 60.8 us: masked_scores(): jnp.einsum('qhgd,khd->hgqk', q_group, key_piece, preferred_element_type=j...]
    all_gather x19 -> x3, waiting for transfers between devices: 547 us -> 0.01 us  [the longest x2 0.01 us: local_plane(): lax.all_gather(rows, 'dp', axis=0, tiled=True)]
    pallas_call x0 -> x16, Pallas kernels: none -> 401 us  [the longest x4 120 us: feed_forward_call(): pl.pallas_call(feed_forward_kernel, grid=(4,), in_specs=[near, far, near,...]
    unnamed x51 -> x7, waiting for transfers between devices: 279 us -> 0.12 us
    ppermute x0 -> x81, waiting for transfers between devices: none -> 267 us  [the longest x32 213 us: swap_mixed(): lax.ppermute(values, PLANE, [(i, i ^ (core1 if i & BIT_C else core0)) for...]
    ppermute x0 -> x81, starting transfers between devices: none -> 88.8 us  [the longest x47 44.8 us: swap(): return lax.ppermute(values, PLANE, [(i, i ^ bits) for i in range(8)])]
    reduce_sum x21 -> x4, other arithmetic: 57.8 us -> 6.21 us  [the longest x2 5.98 us: turn(): gain_ffn.append(jnp.sum(d_xn2 * normed2[n], axis=0))]
  transfers between devices with their start and end apart: 47 -> 88, of which waited for: 33 -> 23; matrix products, arithmetic and copies ran while one was open for 26% -> 14% of each run, Pallas kernels for 0% -> 39%
where the time goes in v3:
time: 948 us; the launch traced here: 940 us
  Pallas kernels  401 us (42%)
  waiting for transfers between devices  267 us (28%)
  other arithmetic  114 us (12%)
  starting transfers between devices  89.4 us (9%)
  local copies, waits for them, and re-layouts  41.5 us (4%)
  between operations  25.9 us (3%)
    ppermute x32, waiting for transfers between devices, swap_mixed(): lax.ppermute(values, PLANE, [(i, i ^ (core1 if i & BIT_C else core0)) for...  213 us
    pallas_call x4, Pallas kernels, feed_forward_call(): pl.pallas_call(feed_forward_kernel, grid=(4,), in_specs=[near, far, near,...  120 us
    pallas_call x2, Pallas kernels, attend_backward_call(): pl.pallas_call(attend_backward_kernel, grid_spec=pltpu.PrefetchScalarGrid...  109 us
    pallas_call x4, Pallas kernels, weight_grad_call(): pl.pallas_call(kernel, in_specs=in_specs, out_specs=[vmem] * len(out_shap...  82.8 us
    pallas_call x2, Pallas kernels, attend_forward_call(): pl.pallas_call(attend_forward_kernel, grid_spec=pltpu.PrefetchScalarGridS...  75.7 us
    ppermute x47, waiting for transfers between devices, swap(): return lax.ppermute(values, PLANE, [(i, i ^ bits) for i in range(8)])  52.7 us
    ppermute x47, starting transfers between devices, swap(): return lax.ppermute(values, PLANE, [(i, i ^ bits) for i in range(8)])  44.8 us
    ppermute x32, starting transfers between devices, swap_mixed(): lax.ppermute(values, PLANE, [(i, i ^ (core1 if i & BIT_C else core0)) for...  42.2 us
  transfers between devices with their start and end apart: 88, of which 23 were waited for; matrix products, arithmetic and copies ran while one was open for 14% of the time, Pallas kernels for 39%

profile of v3, /device:TPU:0, one launch (start us, length us, event | category | flops | bytes accessed | tf_op | source)
XLA Modules:
  0.0 939.6 jit_solution(14099950188634525121)
XLA Ops:
  15.8 10.1 %collective-permute-done.7 = bf16[256,896]{1,0:T(8,128)(2,1)} collective-permute-done((bf16[256,896]{1,0:T(8,128)(2,1)S(1)}, bf16[256,896]{1,0:T(8,128)(2,1)}, u32[]{:S(2)}, u32[]{:S(2)}) %collective-permute-start.7) | collective-permute-done | bytes 458784 | tf_op jit(solution)/shard_map/ppermute | solution.py:441
  66.0 35.7 %collective-permute-done.1.refs_1_ = bf16[512,2048]{1,0:T(8,128)(2,1)} collective-permute-done((bf16[512,2048]{1,0:T(8,128)(2,1)}, bf16[512,2048]{1,0:T(8,128)(2,1)}, u32[]{:S(2)}, u32[]{:S(2)}) %collective-permute-start.1) | collective-permute-done | bytes 2097184 | tf_op jit(solution)/shard_map/ppermute | solution.py:445
  115.6 14.2 %collective-permute-done.6 = bf16[256,2048]{1,0:T(8,128)(2,1)S(1)} collective-permute-done((bf16[256,2048]{1,0:T(8,128)(2,1)S(1)}, bf16[256,2048]{1,0:T(8,128)(2,1)S(1)}, u32[]{:S(2)}, u32[]{:S(2)}) %collective-permute-start.6) | collective-permute-done | bytes 1048608 | tf_op jit(solution)/shard_map/ppermute | solution.py:445
  133.2 37.6 %attend_forward.2 = (f32[2048,640]{1,0:T(8,128)}, f32[2048,256]{1,0:T(8,128)}, f32[2048,128]{1,0:T(8,128)}, bf16[2048,256]{1,0:T(8,128)(2,1)}, bf16[512,2048]{1,...) custom-call(s32[49]{0:T(128)} %concatenate.48.table, ...), custom_call_target="tpu_custom_call" | custom-call | flops 24830279680 | bytes 64471040 | tf_op jit(solution)/shard_map/attend_forward/pallas_call | solution.py:766
  173.2 4.2 collective-permute-done.8
  178.4 4.6 add_convert_fusion.10
  185.4 38.1 %attend_forward.3 = (f32[2048,640]{1,0:T(8,128)}, f32[2048,256]{1,0:T(8,128)}, f32[2048,128]{1,0:T(8,128)}, bf16[2048,256]{1,0:T(8,128)(2,1)}, bf16[512,2048]{1,...) custom-call(s32[49]{0:T(128)} %concatenate.55.table, ...), custom_call_target="tpu_custom_call" | custom-call | flops 24830279680 | bytes 64471040 | tf_op jit(solution)/shard_map/attend_forward/pallas_call | solution.py:766
  227.8 12.7 %collective-permute-done.17 = bf16[256,2048]{1,0:T(8,128)(2,1)S(1)} collective-permute-done((bf16[256,2048]{1,0:T(8,128)(2,1)S(1)}, bf16[256,2048]{1,0:T(8,128)(2,1)S(1)}, u32[]{:S(2)}, u32[]{:S(2)}) %collective-permute-start.17) | collective-permute-done | bytes 1048608 | tf_op jit(solution)/shard_map/ppermute | solution.py:445
  249.0 20.5 %collective-permute-done.18 = bf16[256,2048]{1,0:T(8,128)(2,1)S(1)} collective-permute-done((bf16[256,2048]{1,0:T(8,128)(2,1)S(1)}, bf16[256,2048]{1,0:T(8,128)(2,1)S(1)}, u32[]{:S(2)}, u32[]{:S(2)}) %collective-permute-start.18) | collective-permute-done | bytes 1048608 | tf_op jit(solution)/shard_map/ppermute | solution.py:445
  273.8 7.1 collective-permute-done.26
  284.6 30.0 %collective-permute-done.19.refs_1_ = bf16[512,2048]{1,0:T(8,128)(2,1)S(1)} collective-permute-done((bf16[512,2048]{1,0:T(8,128)(2,1)S(1)}, bf16[512,2048]{1,0:T(8,128)(2,1)S(1)}, u32[]{:S(2)}, u32[]{:S(2)}) %collective-permute-start.19) | collective-permute-done | bytes 2097184 | tf_op jit(solution)/shard_map/ppermute | solution.py:445
  321.1 30.4 %feed_forward.4 = (bf16[1024,768]{1,0:T(8,128)(2,1)S(1)}, bf16[1024,1536]{1,0:T(8,128)(2,1)}, bf16[512,2048]{1,0:T(8,128)(2,1)}, bf16[512,2048]{1,0:T(8,128)(2,1...) custom-call(bf16[512,2048]{1,0:T(8,128)(2,1)} %copy-done.75, ...), custom_call_target="tpu_custom_call" | custom-call | flops 48318382080 | bytes 65536000 | tf_op jit(solution)/shard_map/feed_forward/pallas_call | solution.py:919
  354.3 12.7 %collective-permute-done.29 = bf16[256,2048]{1,0:T(8,128)(2,1)S(1)} collective-permute-done((bf16[256,2048]{1,0:T(8,128)(2,1)S(1)}, bf16[256,2048]{1,0:T(8,128)(2,1)S(1)}, u32[]{:S(2)}, u32[]{:S(2)}) %collective-permute-start.29) | collective-permute-done | bytes 1048608 | tf_op jit(solution)/shard_map/ppermute | solution.py:445
  367.0 11.2 %collective-permute-done.28 = bf16[256,2048]{1,0:T(8,128)(2,1)S(1)} collective-permute-done((bf16[256,2048]{1,0:T(8,128)(2,1)S(1)}, bf16[256,2048]{1,0:T(8,128)(2,1)S(1)}, u32[]{:S(2)}, u32[]{:S(2)}) %collective-permute-start.28) | collective-permute-done | bytes 1048608 | tf_op jit(solution)/shard_map/ppermute | solution.py:445
  382.3 29.4 %feed_forward.5 = (bf16[1024,768]{1,0:T(8,128)(2,1)S(1)}, bf16[1024,1536]{1,0:T(8,128)(2,1)}, bf16[512,2048]{1,0:T(8,128)(2,1)}, bf16[512,2048]{1,0:T(8,128)(2,1...) custom-call(bf16[512,2048]{1,0:T(8,128)(2,1)} %copy-done.44, bf16[512,2048]{1,0:T(8,128)(2,1)} %copy-done.74, ...), custom_call_target="tpu_custom_call" | custom-call | flops 48318382080 | bytes 65536000 | tf_op jit(solution)/shard_map/feed_forward/pallas_call | solution.py:919
  413.2 13.9 %collective-permute-done.35.refs_1_.refs_5_ = bf16[512,2048]{1,0:T(8,128)(2,1)} collective-permute-done((bf16[512,2048]{1,0:T(8,128)(2,1)S(1)}, bf16[512,2048]{1,0:T(8,128)(2,1)}, u32[]{:S(2)}, u32[]{:S(2)}) %collective-permute-start.35) | collective-permute-done | bytes 2097184 | tf_op jit(solution)/shard_map/ppermute | solution.py:445
  434.5 30.2 %feed_forward.6 = (bf16[1024,768]{1,0:T(8,128)(2,1)S(1)}, bf16[1024,1536]{1,0:T(8,128)(2,1)}, bf16[512,2048]{1,0:T(8,128)(2,1)}, bf16[512,2048]{1,0:T(8,128)(2,1...) custom-call(bf16[512,2048]{1,0:T(8,128)(2,1)} %collective-permute-done.34.refs_0_.refs_6_, ...), custom_call_target="tpu_custom_call" | custom-call | flops 48318382080 | bytes 65536000 | tf_op jit(solution)/shard_map/feed_forward/pallas_call | solution.py:919
  474.1 30.4 %feed_forward.7 = (bf16[1024,768]{1,0:T(8,128)(2,1)S(1)}, bf16[1024,1536]{1,0:T(8,128)(2,1)}, bf16[512,2048]{1,0:T(8,128)(2,1)}, bf16[512,2048]{1,0:T(8,128)(2,1...) custom-call(bf16[512,2048]{1,0:T(8,128)(2,1)} %copy-done.45, ...), custom_call_target="tpu_custom_call" | custom-call | flops 48318382080 | bytes 65536000 | tf_op jit(solution)/shard_map/feed_forward/pallas_call | solution.py:919
  510.9 33.1 %weight_grad.4 = bf16[6144,512]{1,0:T(8,128)(2,1)} custom-call(bf16[512,2048]{1,0:T(8,128)(2,1)} %copy-done.44, bf16[512,2048]{1,0:T(8,128)(2,1)} %copy-done.74, bf16[512,2048]{1,0:T(8,128)(2,1)} %copy-done.75, bf16[512,2048]{1,0:T(8,128)(2,1)} %collective-permute-done.21.refs_1_.refs_3_, bf16[512,2048]{1,0:T(8,128)(2,1)} %copy-done.45, ...), custom_call_target="tpu_custom_call" | custom-call | flops 64424509440 | bytes 89128960 | tf_op jit(solution)/shard_map/weight_grad/pallas_call | solution.py:1036
  551.6 18.5 %weight_grad.5 = bf16[3072,512]{1,0:T(8,128)(2,1)} custom-call(bf16[512,2048]{1,0:T(8,128)(2,1)} %constant_dynamic-update-slice_fusion.2.refs_2_.refs_0_, bf16[512,2048]{1,0:T(8,128)(2,1)} %collective-permute-done.14.refs_3_.refs_1_, bf16[512,2048]{1,0:T(8,128)(2,1)} %copy-done.72, bf16[512,2048]{1,0:T(8,128)(2,1)} %copy-done.73, ...), custom_call_target="tpu_custom_call" | custom-call | flops 32212254720 | bytes 65536000 | tf_op jit(solution)/shard_map/weight_grad/pallas_call | solution.py:1036
  574.1 30.1 %collective-permute-done.50.refs_1_ = bf16[512,2048]{1,0:T(8,128)(2,1)} collective-permute-done((bf16[512,2048]{1,0:T(8,128)(2,1)}, bf16[512,2048]{1,0:T(8,128)(2,1)}, u32[]{:S(2)}, u32[]{:S(2)}) %collective-permute-start.50) | collective-permute-done | bytes 2097184 | tf_op jit(solution)/shard_map/ppermute | solution.py:445
  612.5 54.6 %attend_backward.2 = (bf16[2048,640]{1,0:T(8,128)(2,1)}, f32[8,128]{1,0:T(8,128)}, f32[8,128]{1,0:T(8,128)}, bf16[512,2048]{1,0:T(8,128)(2,1)}, bf16[512,2048]{1...) custom-call(s32[49]{0:T(128)} %concatenate.48.table, ...), custom_call_target="tpu_custom_call" | custom-call | flops 33889976320 | bytes 64471040 | tf_op jit(solution)/shard_map/attend_backward/pallas_call | solution.py:816
  672.0 24.3 %collective-permute-done.53.refs_5_.refs_1_ = bf16[512,2048]{1,0:T(8,128)(2,1)} collective-permute-done((bf16[512,2048]{1,0:T(8,128)(2,1)}, bf16[512,2048]{1,0:T(8,128)(2,1)}, u32[]{:S(2)}, u32[]{:S(2)}) %collective-permute-start.53) | collective-permute-done | bytes 2097184 | tf_op jit(solution)/shard_map/ppermute | solution.py:445
  715.7 11.7 %weight_grad.6 = bf16[1024,512]{1,0:T(8,128)(2,1)} custom-call(bf16[512,2048]{1,0:T(8,128)(2,1)} %pad_maximum_fusion.3.refs_0_, bf16[512,2048]{1,0:T(8,128)(2,1)} %collective-permute-done.50.refs_1_, bf16[512,2048]{1,0:T(8,128)(2,1)} %collective-permute-done.51.refs_2_, bf16[512,2048]{1,0:T(8,128)(2,1)} %collective-permute-done.52.refs_3_, ...), custom_call_target="tpu_custom_call" | custom-call | flops 10737418240 | bytes 49807360 | tf_op jit(solution)/shard_map/weight_grad/pallas_call | solution.py:1036
  727.4 54.8 %attend_backward.3 = (bf16[2048,640]{1,0:T(8,128)(2,1)}, f32[8,128]{1,0:T(8,128)}, f32[8,128]{1,0:T(8,128)}, bf16[512,2048]{1,0:T(8,128)(2,1)}, bf16[512,2048]{1...) custom-call(s32[49]{0:T(128)} %concatenate.55.table, ...), custom_call_target="tpu_custom_call" | custom-call | flops 33889976320 | bytes 64471040 | tf_op jit(solution)/shard_map/attend_backward/pallas_call | solution.py:816
  800.4 4.8 collective-permute-done.64.refs_3_
  805.3 19.5 %weight_grad.7 = (bf16[2560,512]{1,0:T(8,128)(2,1)}, f32[8,2048]{1,0:T(8,128)}) custom-call(bf16[512,2048]{1,0:T(8,128)(2,1)} %pad_maximum_fusion.refs_0_, bf16[512,2048]{1,0:T(8,128)(2,1)} %collective-permute-done.1.refs_1_, bf16[512,2048]{1,0:T(8,128)(2,1)} %collective-permute-done.2.refs_2_, bf16[512,2048]{1,0:T(8,128)(2,1)} %collective-permute-done.3.refs_3_, ...), custom_call_target="tpu_custom_call" | custom-call | flops 26843545600 | bytes 61603840 | tf_op jit(solution)/shard_map/weight_grad/pallas_call | solution.py:1036
  832.8 18.0 %collective-permute-done.75 = f32[34,128]{1,0:T(8,128)S(1)} collective-permute-done((f32[34,128]{1,0:T(8,128)S(1)}, f32[34,128]{1,0:T(8,128)S(1)}, u32[]{:S(2)}, u32[]{:S(2)}) %collective-permute-start.75) | collective-permute-done | bytes 17440 | tf_op jit(solution)/shard_map/ppermute | solution.py:441
  854.9 22.3 %collective-permute-start.65 = (bf16[768,128]{1,0:T(8,128)(2,1)}, bf16[768,128]{1,0:T(8,128)(2,1)S(1)}, u32[]{:S(2)}, u32[]{:S(2)}) collective-permute-start(bf16[768,128]{1,0:T(8,128)(2,1)} %get-tuple-element.464), channel_id=1, source_target_pairs={{0,2},{1,3},{2,0},{3,1},{4,6},{5,7},{6,4},{7,5},{8,10},{9,11},{10,... | collective-permute-start | bytes 589832 | tf_op jit(solution)/shard_map/ppermute | solution.py:441
  895.7 6.2 collective-permute-done.67.refs_7_
  902.7 4.3 unpack_feed_forward.1
  918.7 4.8 fusion.26
  (429 shorter events, 233.3 us)
Async XLA Ops:
  7.2 126.0 %all-gather.4.cloned.1.call-start = ((), (), s32[]{:S(2)}) async-start(), calls=%async_computation.4 | async-start | bytes 4587520 | tf_op jit(solution)/shard_map/all_gather | solution.py:1254
  28.0 157.4 %all-gather.6.cloned.1.call-start = ((), (), s32[]{:S(2)}) async-start(), calls=%async_computation.5 | async-start | bytes 3932160 | tf_op jit(solution)/shard_map/all_gather | solution.py:1262
  38.5 63.2 %collective-permute-start.15 = (bf16[128,2304]{1,0:T(8,128)(2,1)}, bf16[128,2304]{1,0:T(8,128)(2,1)}, u32[]{:S(2)}, u32[]{:S(2)}) collective-permute-start(bf16[128,2304]{1,0:T(8,128)(2,1)} %get-tuple-element.448), channel_id=1, source_target_pairs={{0,6},{1,7},{2,4},{3,5},{4,2},{5,3},{6,0},{7,1},{8,14},{9,15},{10,... | collective-permute-start | bytes 1769480 | tf_op jit(solution)/shard_map/ppermute | solution.py:441
  40.2 61.6 %collective-permute-start.16 = (bf16[128,2304]{1,0:T(8,128)(2,1)}, bf16[128,2304]{1,0:T(8,128)(2,1)}, u32[]{:S(2)}, u32[]{:S(2)}) collective-permute-start(bf16[128,2304]{1,0:T(8,128)(2,1)} %get-tuple-element.447), channel_id=1, source_target_pairs={{0,4},{1,5},{2,6},{3,7},{4,0},{5,1},{6,2},{7,3},{8,12},{9,13},{10,... | collective-permute-start | bytes 1769480 | tf_op jit(solution)/shard_map/ppermute | solution.py:441
  53.2 48.5 %collective-permute-start.1 = (bf16[512,2048]{1,0:T(8,128)(2,1)}, bf16[512,2048]{1,0:T(8,128)(2,1)}, u32[]{:S(2)}, u32[]{:S(2)}) collective-permute-start(bf16[512,2048]{1,0:T(8,128)(2,1)} %pad_maximum_fusion.refs_0_), channel_id=1, source_target_pairs={{0,4},{1,5},{2,3},{3,2},{4,0},{5,1},{6,7},{7,6},{8,12},{9,13},{10,... | collective-permute-start | bytes 6291464 | tf_op jit(solution)/shard_map/ppermute | solution.py:445
  62.2 44.2 %collective-permute-start.5 = (bf16[256,2048]{1,0:T(8,128)(2,1)}, bf16[256,2048]{1,0:T(8,128)(2,1)}, u32[]{:S(2)}, u32[]{:S(2)}) collective-permute-start(bf16[256,2048]{1,0:T(8,128)(2,1)} %get-tuple-element.204), channel_id=1, source_target_pairs={{0,1},{1,0},{2,6},{3,7},{4,5},{5,4},{6,2},{7,3},{8,9},{9,8},{10,14... | collective-permute-start | bytes 3145736 | tf_op jit(solution)/shard_map/ppermute | solution.py:445
  66.0 67.2 %collective-permute-start.2 = (bf16[512,2048]{1,0:T(8,128)(2,1)}, bf16[512,2048]{1,0:T(8,128)(2,1)}, u32[]{:S(2)}, u32[]{:S(2)}) collective-permute-start(bf16[512,2048]{1,0:T(8,128)(2,1)} %pad_maximum_fusion.refs_0_), channel_id=1, source_target_pairs={{0,2},{1,3},{2,0},{3,1},{4,6},{5,7},{6,4},{7,5},{8,10},{9,11},{10,... | collective-permute-start | bytes 6291464 | tf_op jit(solution)/shard_map/ppermute | solution.py:441
  112.8 208.4 %all-gather.8.cloned.1.call-start = ((), (), s32[]{:S(2)}) async-start(), calls=%async_computation.6 | async-start | bytes 7864320 | tf_op jit(solution)/shard_map/all_gather | solution.py:1262
  114.1 57.4 %collective-permute-start.11 = (bf16[512,2048]{1,0:T(8,128)(2,1)}, bf16[512,2048]{1,0:T(8,128)(2,1)}, u32[]{:S(2)}, u32[]{:S(2)}) collective-permute-start(bf16[512,2048]{1,0:T(8,128)(2,1)} %constant_dynamic-update-slice_fusion.refs_0_.refs_4_), channel_id=1, source_target_pairs={{0,4},{1,5},{2,3},{3,2},{4,0},{5,1},{6,7},{7,6},{8,12},{9,13},{10,... | collective-permute-start | bytes 6291464 | tf_op jit(solution)/shard_map/ppermute | solution.py:445
  130.9 42.3 %collective-permute-start.14 = (bf16[512,2048]{1,0:T(8,128)(2,1)}, bf16[512,2048]{1,0:T(8,128)(2,1)}, u32[]{:S(2)}, u32[]{:S(2)}) collective-permute-start(bf16[512,2048]{1,0:T(8,128)(2,1)} %constant_dynamic-update-slice_fusion.2.refs_2_.refs_0_), channel_id=1, source_target_pairs={{0,4},{1,5},{2,3},{3,2},{4,0},{5,1},{6,7},{7,6},{8,12},{9,13},{10,... | collective-permute-start | bytes 6291464 | tf_op jit(solution)/shard_map/ppermute | solution.py:445
  173.1 554.3 %reduce-scatter.5.cloned.1.call-start = ((), (), s32[]{:S(2)}) async-start(), calls=%async_computation.7 | async-start | bytes 7864320 | tf_op jit(solution)/shard_map/reduce_scatter | solution.py:1355
  183.0 40.6 %collective-permute-start.10 = (bf16[512,2048]{1,0:T(8,128)(2,1)}, bf16[512,2048]{1,0:T(8,128)(2,1)}, u32[]{:S(2)}, u32[]{:S(2)}) collective-permute-start(bf16[512,2048]{1,0:T(8,128)(2,1)} %add_convert_fusion.10), channel_id=1, source_target_pairs={{0,4},{1,5},{2,3},{3,2},{4,0},{5,1},{6,7},{7,6},{8,12},{9,13},{10,... | collective-permute-start | bytes 6291464 | tf_op jit(solution)/shard_map/ppermute | solution.py:445
  269.8 44.8 %collective-permute-start.19 = (bf16[512,2048]{1,0:T(8,128)(2,1)S(1)}, bf16[512,2048]{1,0:T(8,128)(2,1)S(1)}, u32[]{:S(2)}, u32[]{:S(2)}) collective-permute-start(bf16[512,2048]{1,0:T(8,128)(2,1)S(1)} %pad_maximum_fusion.1.refs_0_), channel_id=1, source_target_pairs={{0,4},{1,5},{2,3},{3,2},{4,0},{5,1},{6,7},{7,6},{8,12},{9,13},{10,... | collective-permute-start | bytes 6291464 | tf_op jit(solution)/shard_map/ppermute | solution.py:445
  380.6 46.4 %collective-permute-start.35 = (bf16[512,2048]{1,0:T(8,128)(2,1)S(1)}, bf16[512,2048]{1,0:T(8,128)(2,1)}, u32[]{:S(2)}, u32[]{:S(2)}) collective-permute-start(bf16[512,2048]{1,0:T(8,128)(2,1)S(1)} %pad_maximum_fusion.2.refs_0_.refs_4_), channel_id=1, source_target_pairs={{0,4},{1,5},{2,3},{3,2},{4,0},{5,1},{6,7},{7,6},{8,12},{9,13},{10,... | collective-permute-start | bytes 6291464 | tf_op jit(solution)/shard_map/ppermute | solution.py:445
  380.8 46.8 %collective-permute-start.37 = (bf16[512,2048]{1,0:T(8,128)(2,1)S(1)}, bf16[512,2048]{1,0:T(8,128)(2,1)}, u32[]{:S(2)}, u32[]{:S(2)}) collective-permute-start(bf16[512,2048]{1,0:T(8,128)(2,1)S(1)} %constant_dynamic-update-slice_fusion.4.refs_2_.refs_4_), channel_id=1, source_target_pairs={{0,2},{1,3},{2,0},{3,1},{4,6},{5,7},{6,4},{7,5},{8,10},{9,11},{10,... | collective-permute-start | bytes 6291464 | tf_op jit(solution)/shard_map/ppermute | solution.py:441
  380.8 46.8 %collective-permute-start.34 = (bf16[512,2048]{1,0:T(8,128)(2,1)S(1)}, bf16[512,2048]{1,0:T(8,128)(2,1)}, u32[]{:S(2)}, u32[]{:S(2)}) collective-permute-start(bf16[512,2048]{1,0:T(8,128)(2,1)S(1)} %pad_maximum_fusion.2.refs_0_.refs_4_), channel_id=1, source_target_pairs={{0,2},{1,3},{2,0},{3,1},{4,6},{5,7},{6,4},{7,5},{8,10},{9,11},{10,... | collective-permute-start | bytes 6291464 | tf_op jit(solution)/shard_map/ppermute | solution.py:441
  465.7 38.8 %collective-permute-start.44 = (bf16[256,2048]{1,0:T(8,128)(2,1)S(1)}, bf16[256,2048]{1,0:T(8,128)(2,1)S(1)}, u32[]{:S(2)}, u32[]{:S(2)}) collective-permute-start(bf16[256,2048]{1,0:T(8,128)(2,1)S(1)} %add_convert_fusion.19), channel_id=1, source_target_pairs={{0,1},{1,0},{2,6},{3,7},{4,5},{5,4},{6,2},{7,3},{8,9},{9,8},{10,14... | collective-permute-start | bytes 3145736 | tf_op jit(solution)/shard_map/ppermute | solution.py:445
  470.0 74.1 %collective-permute-start.40 = (bf16[512,2048]{1,0:T(8,128)(2,1)}, bf16[512,2048]{1,0:T(8,128)(2,1)}, u32[]{:S(2)}, u32[]{:S(2)}) collective-permute-start(bf16[512,2048]{1,0:T(8,128)(2,1)} %add_convert_fusion.6), channel_id=1, source_target_pairs={{0,4},{1,5},{2,3},{3,2},{4,0},{5,1},{6,7},{7,6},{8,12},{9,13},{10,... | collective-permute-start | bytes 6291464 | tf_op jit(solution)/shard_map/ppermute | solution.py:445
  544.0 256.4 %reduce-scatter.7.cloned.1.call-start = ((), (), s32[]{:S(2)}) async-start(), calls=%async_computation.8 | async-start | bytes 3932160 | tf_op jit(solution)/shard_map/reduce_scatter | solution.py:1355
  550.5 53.7 %collective-permute-start.50 = (bf16[512,2048]{1,0:T(8,128)(2,1)}, bf16[512,2048]{1,0:T(8,128)(2,1)}, u32[]{:S(2)}, u32[]{:S(2)}) collective-permute-start(bf16[512,2048]{1,0:T(8,128)(2,1)} %pad_maximum_fusion.3.refs_0_), channel_id=1, source_target_pairs={{0,4},{1,5},{2,3},{3,2},{4,0},{5,1},{6,7},{7,6},{8,12},{9,13},{10,... | collective-permute-start | bytes 6291464 | tf_op jit(solution)/shard_map/ppermute | solution.py:445
  604.2 67.7 %collective-permute-start.56 = (bf16[512,2048]{1,0:T(8,128)(2,1)}, bf16[512,2048]{1,0:T(8,128)(2,1)}, u32[]{:S(2)}, u32[]{:S(2)}) collective-permute-start(bf16[512,2048]{1,0:T(8,128)(2,1)} %get-tuple-element.323), channel_id=1, source_target_pairs={{0,2},{1,3},{2,0},{3,1},{4,6},{5,7},{6,4},{7,5},{8,10},{9,11},{10,... | collective-permute-start | bytes 6291464 | tf_op jit(solution)/shard_map/ppermute | solution.py:441
  604.7 67.3 %collective-permute-start.57 = (bf16[512,2048]{1,0:T(8,128)(2,1)}, bf16[512,2048]{1,0:T(8,128)(2,1)}, u32[]{:S(2)}, u32[]{:S(2)}) collective-permute-start(bf16[512,2048]{1,0:T(8,128)(2,1)} %get-tuple-element.324), channel_id=1, source_target_pairs={{0,2},{1,3},{2,0},{3,1},{4,6},{5,7},{6,4},{7,5},{8,10},{9,11},{10,... | collective-permute-start | bytes 6291464 | tf_op jit(solution)/shard_map/ppermute | solution.py:441
  611.2 56.0 %collective-permute-start.49 = (bf16[256,2048]{1,0:T(8,128)(2,1)S(1)}, bf16[256,2048]{1,0:T(8,128)(2,1)}, u32[]{:S(2)}, u32[]{:S(2)}) collective-permute-start(bf16[256,2048]{1,0:T(8,128)(2,1)S(1)} %get-tuple-element.430), channel_id=1, source_target_pairs={{0,1},{1,0},{2,6},{3,7},{4,5},{5,4},{6,2},{7,3},{8,9},{9,8},{10,14... | collective-permute-start | bytes 3145736 | tf_op jit(solution)/shard_map/ppermute | solution.py:445
  671.6 206.2 %reduce-scatter.11.cloned.1.call-start = ((), (), s32[]{:S(2)}) async-start(), calls=%async_computation.10 | async-start | bytes 1310720 | tf_op jit(solution)/shard_map/reduce_scatter | solution.py:1355
  671.9 41.8 %collective-permute-start.54 = (bf16[512,2048]{1,0:T(8,128)(2,1)}, bf16[512,2048]{1,0:T(8,128)(2,1)S(1)}, u32[]{:S(2)}, u32[]{:S(2)}) collective-permute-start(bf16[512,2048]{1,0:T(8,128)(2,1)} %pad_maximum_fusion.4.refs_4_.refs_0_), channel_id=1, source_target_pairs={{0,2},{1,3},{2,0},{3,1},{4,6},{5,7},{6,4},{7,5},{8,10},{9,11},{10,... | collective-permute-start | bytes 6291464 | tf_op jit(solution)/shard_map/ppermute | solution.py:441
  700.2 82.7 %collective-permute-start.60 = (bf16[512,2048]{1,0:T(8,128)(2,1)}, bf16[512,2048]{1,0:T(8,128)(2,1)}, u32[]{:S(2)}, u32[]{:S(2)}) collective-permute-start(bf16[512,2048]{1,0:T(8,128)(2,1)} %add_convert_fusion.4), channel_id=1, source_target_pairs={{0,4},{1,5},{2,3},{3,2},{4,0},{5,1},{6,7},{7,6},{8,12},{9,13},{10,... | collective-permute-start | bytes 6291464 | tf_op jit(solution)/shard_map/ppermute | solution.py:445
  709.1 73.7 %collective-permute-start.68 = (bf16[512,2048]{1,0:T(8,128)(2,1)}, bf16[512,2048]{1,0:T(8,128)(2,1)}, u32[]{:S(2)}, u32[]{:S(2)}) collective-permute-start(bf16[512,2048]{1,0:T(8,128)(2,1)} %add_convert_fusion.2), channel_id=1, source_target_pairs={{0,4},{1,5},{2,3},{3,2},{4,0},{5,1},{6,7},{7,6},{8,12},{9,13},{10,... | collective-permute-start | bytes 6291464 | tf_op jit(solution)/shard_map/ppermute | solution.py:445
  782.8 133.0 %reduce-scatter.9.cloned.1.call-start = ((), (), s32[]{:S(2)}) async-start(), calls=%async_computation.9 | async-start | bytes 3276800 | tf_op jit(solution)/shard_map/reduce_scatter | solution.py:1355
  824.9 54.6 %collective-permute-start.45 = (bf16[256,2048]{1,0:T(8,128)(2,1)}, bf16[256,2048]{1,0:T(8,128)(2,1)}, u32[]{:S(2)}, u32[]{:S(2)}) collective-permute-start(bf16[256,2048]{1,0:T(8,128)(2,1)} %add_convert_fusion.18), channel_id=1, source_target_pairs={{0,1},{1,0},{2,6},{3,7},{4,5},{5,4},{6,2},{7,3},{8,9},{9,8},{10,14... | collective-permute-start | bytes 3145736 | tf_op jit(solution)/shard_map/ppermute | solution.py:445
  825.6 63.9 %collective-permute-start.71 = (bf16[512,2048]{1,0:T(8,128)(2,1)}, bf16[512,2048]{1,0:T(8,128)(2,1)}, u32[]{:S(2)}, u32[]{:S(2)}) collective-permute-start(bf16[512,2048]{1,0:T(8,128)(2,1)} %add_convert_fusion), channel_id=1, source_target_pairs={{0,4},{1,5},{2,3},{3,2},{4,0},{5,1},{6,7},{7,6},{8,12},{9,13},{10,... | collective-permute-start | bytes 6291464 | tf_op jit(solution)/shard_map/ppermute | solution.py:445
  832.0 55.9 %collective-permute-start.72 = (bf16[256,2048]{1,0:T(8,128)(2,1)}, bf16[256,2048]{1,0:T(8,128)(2,1)S(1)}, u32[]{:S(2)}, u32[]{:S(2)}) collective-permute-start(bf16[256,2048]{1,0:T(8,128)(2,1)} %add_convert_fusion.14), channel_id=1, source_target_pairs={{0,1},{1,0},{2,6},{3,7},{4,5},{5,4},{6,2},{7,3},{8,9},{9,8},{10,14... | collective-permute-start | bytes 3145736 | tf_op jit(solution)/shard_map/ppermute | solution.py:445
  854.9 39.1 %collective-permute-start.65 = (bf16[768,128]{1,0:T(8,128)(2,1)}, bf16[768,128]{1,0:T(8,128)(2,1)S(1)}, u32[]{:S(2)}, u32[]{:S(2)}) collective-permute-start(bf16[768,128]{1,0:T(8,128)(2,1)} %get-tuple-element.464), channel_id=1, source_target_pairs={{0,2},{1,3},{2,0},{3,1},{4,6},{5,7},{6,4},{7,5},{8,10},{9,11},{10,... | collective-permute-start | bytes 589832 | tf_op jit(solution)/shard_map/ppermute | solution.py:441
  (139 other events, 2059.4 us)
Sparse Core Ops, SparseCore 0:
  28.2 73.5 all-gather.3
  112.9 63.8 all-gather.5
  178.9 113.9 all-gather.7
  544.1 110.9 reduce-scatter.4
  671.8 59.1 reduce-scatter.6
  782.9 26.7 reduce-scatter.10
  825.0 52.0 reduce-scatter.8

commit v4 on v3

--- a/solution.py
+++ b/solution.py
@@ -429,8 +429,8 @@
 TN = (((0,), (0,)), ((), ()))
 F32 = jnp.float32
 BF16 = jnp.bfloat16
-COST_SHARE = 0.4
-LATE_SHARE = 0.4
+COST_SHARE = 0.2
+LATE_SHARE = 0.1
 
 
 def dot(left, right, dims=NN):
@@ -488,6 +488,27 @@
         return far
 
 
+def add_pieces_kernel(*refs):
+    for k in range(2):
+        refs[4 + k][...] = (refs[k][...].astype(F32) + refs[2 + k][...].astype(F32)).astype(BF16)
+
+
+def add_pieces(near, far, near_came, far_came):
+    count, width = near.shape
+    block = pl.BlockSpec((count // 4, width), lambda i: (i, 0))
+    return pl.pallas_call(
+        add_pieces_kernel,
+        grid=(4,),
+        in_specs=[block] * 4,
+        out_specs=[block] * 2,
+        out_shape=[jax.ShapeDtypeStruct((count, width), BF16)] * 2,
+        cost_estimate=pl.CostEstimate(
+            flops=2 * count * width, bytes_accessed=12 * count * width, transcendentals=0
+        ),
+        name="add_pieces",
+    )(near, far, near_came, far_came)
+
+
 class Scatter:
     def __init__(self, order, near, far):
         self.order = order
@@ -495,22 +516,21 @@
 
     def add(self, near, far):
         near_came, far_came = self.order.pin(self.came)
-        far = (far.astype(F32) + far_came.astype(F32)).astype(BF16)
-        near = (near.astype(F32) + near_came.astype(F32)).astype(BF16)
-        return self.second(near, far)
-
-    def second(self, near, far):
-        self.kept = near
-        self.came = swap_mixed(far, BIT_Y, BIT_X)
-        return (near, far)
-
-    def third(self):
+        self.near, self.far = add_pieces(near, far, near_came, far_came)
+        return (self.near, self.far)
+
+    def send_far(self):
+        self.came = swap_mixed(self.order.pin(self.far), BIT_Y, BIT_X)
+
+    def take(self):
         came = self.order.pin(self.came)
         half = came.shape[0] // 2
-        sent = (self.kept[half:].astype(F32) + came[half:].astype(F32)).astype(BF16)
-        self.kept = self.kept[:half].astype(F32) + came[:half].astype(F32)
-        self.came = swap_mixed(sent, BIT_X, BIT_Y)
-        return sent
+        self.sent = (self.near[half:].astype(F32) + came[half:].astype(F32)).astype(BF16)
+        self.kept = self.near[:half].astype(F32) + came[:half].astype(F32)
+        return self.sent
+
+    def send_near(self):
+        self.came = swap_mixed(self.order.pin(self.sent), BIT_X, BIT_Y)
 
     def result(self):
         return self.kept + self.order.pin(self.came).astype(F32)
@@ -567,6 +587,31 @@
     near = jnp.where(slot < 2, pieces[0][...], pieces[1][...])
     far = jnp.where(slot < 6, pieces[2][...], pieces[3][...])
     return jnp.where(slot < 4, near, far)
+
+
+def walk_tiles(step, rows, live, add_tile):
+    pairs = step // 2
+    whole = jnp.minimum(pairs, live // (2 * rows))
+
+    def tile(index, carry):
+        add_tile(pl.multiple_of(index * 2 * rows, 2 * rows), 2 * rows, False)
+        return carry
+
+    lax.fori_loop(0, whole, tile, 0)
+    odd = step % 2 == 1
+    edge = pl.multiple_of(pairs * 2 * rows, 2 * rows)
+
+    @pl.when((whole < pairs) & (whole * 2 * rows < live))
+    def _():
+        add_tile(pl.multiple_of(whole * 2 * rows, 2 * rows), 2 * rows, True)
+
+    @pl.when(odd & (edge < live))
+    def _():
+        add_tile(edge, 2 * rows, True)
+
+    @pl.when(jnp.logical_not(odd) & (edge < live))
+    def _():
+        add_tile(edge, rows, True)
 
 
 def attend_forward_kernel(table, *refs):
@@ -588,37 +633,17 @@
     second, _, _ = norm_rope(proj[:, 128:256], q_gain[...], cos_b, sin_b)
     query = (jnp.concatenate([first, second], axis=0) * q_scale).astype(BF16)
 
-    def add_block(index, mask_of):
-        there = pl.multiple_of(index * rows, rows)
-        weight = jnp.exp(dot(query, keys[pl.ds(there, rows), :], NT))
-        if mask_of is not None:
-            weight = jnp.where(mask_of(there), weight, 0.0)
-        acc[...] += dot(weight.astype(BF16), values[pl.ds(there, rows), :])
-
-    def column():
-        return lax.broadcasted_iota(jnp.int32, (2 * rows, rows), 1)
-
-    def causal(there):
-        row = lax.broadcasted_iota(jnp.int32, (2 * rows, rows), 0)
-        return (column() <= jnp.where(row >= rows, row - rows, row)) & (column() + there < live)
+    def add_tile(there, count, masked):
+        weight = jnp.exp(dot(query, keys[pl.ds(there, count), :], NT))
+        if masked:
+            row = lax.broadcasted_iota(jnp.int32, (2 * rows, count), 0)
+            place = there + lax.broadcasted_iota(jnp.int32, (2 * rows, count), 1)
+            allowed = (place <= here + jnp.where(row >= rows, row - rows, row)) & (place < live)
+            weight = jnp.where(allowed, weight, 0.0)
+        acc[...] += dot(weight.astype(BF16), values[pl.ds(there, count), :])
 
     acc[...] = jnp.zeros_like(acc)
-    whole = jnp.minimum(step, live // rows)
-
-    def block(index, carry):
-        add_block(index, None)
-        return carry
-
-    lax.fori_loop(0, whole, block, 0)
-
-    @pl.when((whole < step) & (whole * rows < live))
-    def _():
-        add_block(whole, lambda there: column() + there < live)
-
-    @pl.when(here < live)
-    def _():
-        add_block(step, causal)
-
+    walk_tiles(step, rows, live, add_tile)
     total = acc[:, 128:129]
     out = acc[:, 0:128] / total
     log_total = jnp.log(total)
@@ -663,7 +688,7 @@
         key, _, _ = norm_rope(raw_key, k_gain[...], cos_b, sin_b)
         key = key.astype(BF16)
         keys[pl.ds(here, rows), :] = key
-        keys_t[step] = key.T
+        keys_t[:, pl.ds(here, rows)] = key.T
         values[pl.ds(here, rows), :] = proj[:, 384:512].astype(BF16)
         d_keys[pl.ds(here, rows), :] = jnp.zeros((rows, 128), F32)
         d_values[pl.ds(here, rows), :] = jnp.zeros((rows, 128), F32)
@@ -688,42 +713,22 @@
         log_total = jnp.concatenate([lse_t[0:1], lse_t[1:2]], axis=1)
         d_out = jnp.concatenate([do0, do1], axis=0)
 
-        def add_block(index, mask_of):
-            there = pl.multiple_of(index * rows, rows)
-            scores = dot(keys[pl.ds(there, rows), :], query, NT)
+        def add_tile(there, count, masked):
+            here_keys = pl.ds(there, count)
+            scores = dot(keys[here_keys, :], query, NT)
             probs = jnp.exp(scores - log_total)
-            if mask_of is not None:
-                probs = jnp.where(mask_of(there), probs, 0.0)
-            d_probs = dot(values[pl.ds(there, rows), :], d_out, NT)
+            if masked:
+                place = there + lax.broadcasted_iota(jnp.int32, (count, 2 * rows), 0)
+                q_col = lax.broadcasted_iota(jnp.int32, (count, 2 * rows), 1)
+                q_place = here + jnp.where(q_col >= rows, q_col - rows, q_col)
+                probs = jnp.where((place <= q_place) & (place < live), probs, 0.0)
+            d_probs = dot(values[here_keys, :], d_out, NT)
             d_scores = (probs * (d_probs - delta)).astype(BF16)
-            d_values[pl.ds(there, rows), :] += dot(probs.astype(BF16), d_out)
-            d_keys[pl.ds(there, rows), :] += dot(d_scores, query)
-            d_query[...] += dot(keys_t[index], d_scores)
-
-        def key_row():
-            return lax.broadcasted_iota(jnp.int32, (rows, 2 * rows), 0)
-
-        def causal(there):
-            q_col = lax.broadcasted_iota(jnp.int32, (rows, 2 * rows), 1)
-            q_col = jnp.where(q_col >= rows, q_col - rows, q_col)
-            return (key_row() <= q_col) & (key_row() + there < live)
-
-        whole = jnp.minimum(step, live // rows)
-
-        def block(index, carry):
-            add_block(index, None)
-            return carry
-
-        lax.fori_loop(0, whole, block, 0)
-
-        @pl.when((whole < step) & (whole * rows < live))
-        def _():
-            add_block(whole, lambda there: key_row() + there < live)
-
-        @pl.when(here < live)
-        def _():
-            add_block(step, causal)
-
+            d_values[here_keys, :] += dot(probs.astype(BF16), d_out)
+            d_keys[here_keys, :] += dot(d_scores, query)
+            d_query[...] += dot(keys_t[:, here_keys], d_scores)
+
+        walk_tiles(step, rows, live, add_tile)
         grads = d_query[...].T * q_scale
         raw0, part0 = norm_rope_back(grads[:rows], hat0, scale0, q_gain[...], cos_b, sin_b)
         raw1, part1 = norm_rope_back(grads[rows:], hat1, scale1, q_gain[...], cos_b, sin_b)
@@ -847,7 +852,7 @@
             ],
             scratch_shapes=[
                 pltpu.VMEM((seq_len, 128), BF16),
-                pltpu.VMEM((8, 128, rows), BF16),
+                pltpu.VMEM((128, seq_len), BF16),
                 pltpu.VMEM((seq_len, 128), BF16),
                 pltpu.VMEM((seq_len, 128), F32),
                 pltpu.VMEM((seq_len, 128), F32),
@@ -877,7 +882,6 @@
 
 def feed_forward_kernel(*refs):
     rows_near, rows_far, cot_near, cot_far, w_down_t, w_inner = refs[:6]
-    sums = refs[6:-6]
     hidden_out, d_pre_out, down_near, down_far, back_near, back_far = refs[-6:]
     near = pl.program_id(0) < 2
     units = hidden_out.shape[1]
@@ -893,8 +897,6 @@
     ).astype(BF16)
     back = dot(d_pre_out[...], w_inner[...], NT)
     down = dot(hidden_out[...], w_down_t[...], NT)
-    if sums:
-        back = back + jnp.where(near, sums[0][...], sums[1][...]).astype(F32)
 
     @pl.when(near)
     def _():
@@ -907,7 +909,7 @@
         down_far[...] = down.astype(BF16)
 
 
-def feed_forward_call(rows, cots, w_down_t, w_inner, backs=()):
+def feed_forward_call(rows, cots, w_down_t, w_inner):
     count, width = rows[0].shape
     units = w_down_t.shape[1]
     tile = count // 2
@@ -920,8 +922,7 @@
         feed_forward_kernel,
         grid=(4,),
         in_specs=[near, far, near, far]
-        + [pl.BlockSpec(w.shape, fixed, pipeline_mode=pl.Buffered(1)) for w in (w_down_t, w_inner)]
-        + [near, far] * (len(backs) // 2),
+        + [pl.BlockSpec(w.shape, fixed, pipeline_mode=pl.Buffered(1)) for w in (w_down_t, w_inner)],
         out_specs=[
             pl.BlockSpec((tile, units), by_row),
             pl.BlockSpec((tile, 2 * units), by_row),
@@ -943,11 +944,11 @@
         ),
         cost_estimate=cost(24 * count * width * units, 2 * width * (8 * count + 3 * units)),
         name="feed_forward",
-    )(*rows, *cots, w_down_t, w_inner, *backs)
+    )(*rows, *cots, w_down_t, w_inner)
     return (out[0], out[1], (out[2], out[3]), (out[4], out[5]))
 
 
-def weight_grad_call(n_parts, lefts, terms, weights=None):
+def weight_grad_call(n_parts, lefts, terms, weights=None, carried=None, final=True):
     n_pieces = len(lefts[0])
     rows, width = lefts[0][0].shape
     columns = [pieces[0][0].shape[1] for _, pieces in terms]
@@ -967,6 +968,8 @@
         rest = list(refs[len(left_refs) + len(arrays) :])
         if weights is not None:
             weights_ref = rest.pop(0)
+        if carried is not None:
+            carried_ref = rest.pop(0)
         out = rest.pop(0)
         if weights is not None:
             gain = rest.pop(0)
@@ -993,8 +996,10 @@
 
         for copy in copies(0, 0):
             copy.start()
+        if not final:
+            accs = [out]
         for acc in accs:
-            acc[...] = jnp.zeros_like(acc)
+            acc[...] = jnp.zeros_like(acc) if carried is None else carried_ref[...]
 
         def body(index, carry):
             slot = lax.rem(index, 2)
@@ -1014,6 +1019,8 @@
             return carry
 
         lax.fori_loop(0, n_pieces, body, 0)
+        if not final:
+            return
         part = width // n_parts
         for p in range(n_parts):
             for k in range(n_terms):
@@ -1026,6 +1033,8 @@
             gain[...] = jnp.broadcast_to(jnp.sum(scaled, axis=0, keepdims=True), gain.shape)
 
     out_shape = [jax.ShapeDtypeStruct((n_parts * total, width // n_parts), BF16)]
+    if not final:
+        out_shape = [jax.ShapeDtypeStruct((total, width), F32)]
     vmem = pl.BlockSpec(memory_space=pltpu.VMEM)
     operands = [piece for pieces in lefts for piece in pieces] + arrays
     in_specs = [pl.BlockSpec(memory_space=pl.ANY)] * len(operands)
@@ -1033,6 +1042,9 @@
         operands.append(weights)
         in_specs.append(vmem)
         out_shape.append(jax.ShapeDtypeStruct((8, width), F32))
+    if carried is not None:
+        operands.append(carried)
+        in_specs.append(vmem)
     return pl.pallas_call(
         kernel,
         in_specs=in_specs,
@@ -1040,7 +1052,7 @@
         out_shape=out_shape,
         scratch_shapes=[pltpu.VMEM((2, rows, width), BF16)] * n_left
         + [pltpu.VMEM((2, rows, c), BF16) for c in columns]
-        + [pltpu.VMEM((c, width), F32) for c in columns]
+        + [pltpu.VMEM((c, width), F32) for c in columns if final]
         + [pltpu.SemaphoreType.DMA((2, n_left + n_terms))],
         compiler_params=pltpu.CompilerParams(vmem_limit_bytes=56 << 20),
         cost_estimate=cost(
@@ -1251,17 +1263,19 @@
     attn_rows = jnp.concatenate(
         [pick(is_first, halves[0], attn_came), pick(is_first, attn_came, halves[0])], axis=0
     )
+    attn_rows = after(attn_rows, xn1[0].came)
     w_attn = lax.all_gather(attn_rows, "dp", axis=0, tiled=True)
-
-    quarters = pack_feed_forward(head_at, w_gate, w_up, w_down)
+    xn1[0].second()
+    xn1[0].third()
+
+    quarters = after(pack_feed_forward(head_at, w_gate, w_up, w_down), xn1[0].pieces[1])
     traded = [quarters[0]] + [swap(quarters[r], r * 2) for r in (1, 2, 3)]
-    near = xn1[0].second()
     parts = [[t[:, :units] for t in traded], [t[:, units:] for t in traded]]
     ffn_rows = [jnp.concatenate(reorder_by(part, head_idx), axis=0) for part in parts]
     ffn_rows = after(tuple(ffn_rows), attn_rows)
     w_ffn = [lax.all_gather(rows, "dp", axis=0, tiled=True) for rows in ffn_rows]
 
-    xn1[1] = Gather(order, after(xn1_own[1], traded[1]))
+    xn1[1] = Gather(order, after(xn1_own[1], xn1[0].pieces[1]))
     tables = [attend_table(plane_idx, core, count) for count in live]
     table_cos, table_sin = rope_tables(jnp.arange(seq_len, dtype=jnp.int32), 64)
     table_cos, table_sin = table_cos[:, 0, :], table_sin[:, 0, :]
@@ -1274,15 +1288,19 @@
         att[n] = order.run(
             lambda *pieces: attend_forward_call(tables[n], pieces, w_attn, *fixed), *xn1[n].pieces
         )
-        out_sum[n] = Scatter(order, att[n][6], att[n][7])
-
-    cot[0] = Gather(order, after(cot_own[0], xn1[1].second()))
-    order.need(xn1[0].third(), cot[0].second())
+
+    order.need(xn1[1].second())
+    cot[0] = Gather(order, after(cot_own[0], xn1[1].pieces[0]))
     attend(0)
-    order.need(xn1[1].third(), cot[0].third())
-    order.need(*out_sum[0].add(att[0][4], att[0][5]), w_ffn[0])
+    done = (xn1[1].third(), cot[0].second())
+    out_sum[0] = Scatter(order, *after((att[0][6], att[0][7]), *done))
+    order.need(*out_sum[0].add(att[0][4], att[0][5]), *done, w_ffn[0])
+    out_sum[0].send_far()
     attend(1)
-    order.need(out_sum[0].third())
+    done = (out_sum[0].take(), cot[0].third())
+    out_sum[0].send_near()
+    out_sum[1] = Scatter(order, *after((att[1][6], att[1][7]), *done))
+    order.need(*done)
 
     hidden1, scale2, normed2 = ([None] * micro_batches for _ in range(3))
 
@@ -1296,7 +1314,9 @@
 
     rows = middle(0)
     order.need(*out_sum[1].add(after(att[1][4], rows), att[1][5]))
-    order.need(xn2[0].second(), out_sum[1].third())
+    out_sum[1].send_far()
+    order.need(xn2[0].second(), out_sum[1].take())
+    out_sum[1].send_near()
     order.need(xn2[0].third(), middle(1))
     cot[1] = Gather(order, after(cot_own[1], xn2[0].pieces[1]))
 
@@ -1307,16 +1327,12 @@
         feed[n, 1] = order.run(
             lambda *v: feed_forward_call(v[0:2], v[2:4], *w_ffn), *xn2[n].pieces[2:], *cot[n].pieces[2:]
         )
-        back[n] = Scatter(order, *feed[n, 1][3])
 
     def feed_mine(n):
         feed[n, 0] = order.run(
-            lambda *v: feed_forward_call(v[0:2], v[2:4], *w_ffn, order.pin(back[n].came)),
-            *xn2[n].pieces[:2],
-            *cot[n].pieces[:2],
-        )
-        back[n].second(*feed[n, 0][3])
-        down[n] = Scatter(order, *after(feed[n, 1][2], feed[n, 0][0]))
+            lambda *v: feed_forward_call(v[0:2], v[2:4], *w_ffn), *xn2[n].pieces[:2], *cot[n].pieces[:2]
+        )
+        return back[n].add(*feed[n, 0][3])
 
     d_hidden1 = [None] * micro_batches
     gain_ffn = []
@@ -1339,14 +1355,14 @@
     def rows_of(gathers):
         return [piece for gather in gathers for piece in gather.pieces]
 
-    def grad_call(lefts, terms, weights=None):
+    def grad_call(lefts, terms, *more):
         count = [len(left) for left in lefts]
         return order.run(
             lambda *v: weight_grad_call(
                 n_dp,
                 [list(v[sum(count[:k]) : sum(count[: k + 1])]) for k in range(len(lefts))],
                 terms,
-                weights,
+                *more,
             ),
             *[piece for left in lefts for piece in left],
         )
@@ -1360,17 +1376,32 @@
         return [quarter(head_idx)] + [swap(quarter(head_idx ^ r), r * 2) for r in (1, 2, 3)]
 
     feed_other(0)
-    order.need(xn2[1].second(), cot[1].second())
-    feed_mine(0)
-    order.need(cot[1].third(), xn2[1].third())
+    done = (xn2[1].second(), cot[1].second())
+    back[0] = Scatter(order, *after(feed[0, 1][3], *done))
+    order.need(*done)
+    sums = feed_mine(0)
+    done = (xn2[1].third(), cot[1].third())
+    down[0] = Scatter(order, *after(feed[0, 1][2], *done, *sums))
+    back[0].send_far()
+    order.need(*sums, *done)
     feed_other(1)
-    order.need(back[0].third(), *down[0].add(*feed[0, 0][2]))
-    feed_mine(1)
-    order.need(turn(0))
-    grads_inner = sum_over_dp(grad_call([rows_of(xn2)], [(0, of_feed(1))])[0])
-    order.need(d_attn[0].second(), down[0].third())
-    grads_down = sum_over_dp(grad_call([rows_of(cot)], [(0, of_feed(0))])[0])
-    order.need(back[1].third(), d_attn[0].third(), turn(1))
+    done = (back[0].take(), *down[0].add(*feed[0, 0][2]))
+    back[0].send_near()
+    down[0].send_far()
+    back[1] = Scatter(order, *after(feed[1, 1][3], *done))
+    order.need(*done)
+    order.need(*feed_mine(1), turn(0), down[0].take())
+    back[1].send_far()
+    grad_inner = grad_call([rows_of(xn2)], [(0, of_feed(1))])[0]
+    done = (d_attn[0].second(), back[1].take())
+    back[1].send_near()
+    down[1] = Scatter(order, *after(feed[1, 1][2], *done))
+    order.need(*done)
+    grad_down = grad_call([rows_of(cot)], [(0, of_feed(0))])[0]
+    grads_inner = sum_over_dp(order.pin(grad_inner))
+    order.need(d_attn[0].third(), turn(1), *down[1].add(*feed[1, 0][2]))
+    down[0].send_near()
+    down[1].send_far()
 
     d_proj, gain_parts, rows_sum = ([None] * micro_batches for _ in range(3))
 
@@ -1383,7 +1414,6 @@
         )
         d_proj[n] = out[0]
         gain_parts[n] = (out[1][0], out[2][0])
-        rows_sum[n] = Scatter(order, out[5], out[6])
         return out
 
     def finish(n):
@@ -1392,41 +1422,54 @@
 
     outputs, input_grads = ([None] * micro_batches for _ in range(2))
     back_0 = attend_back(0)
-    order.need(d_attn[1].second(), *down[1].add(*feed[1, 0][2]))
-    order.need(*rows_sum[0].add(back_0[3], back_0[4]), d_attn[1].third())
+    grads_down = sum_over_dp(order.pin(grad_down))
+    done = (d_attn[1].second(), down[1].take())
+    outputs[0] = (hidden1[0] + down[0].result()).astype(BF16)
+    rows_sum[0] = Scatter(order, *after((back_0[5], back_0[6]), *done, outputs[0]))
+    order.need(*done, outputs[0], *rows_sum[0].add(back_0[3], back_0[4]))
+    grads_proj = grad_call([xn1[0].pieces], [(0, row_pieces(d_proj[0]))], None, None, False)[0]
+    order.need(d_attn[1].third())
     grads_out = sum_over_dp(
         grad_call(
             [rows_of(d_attn)], [(0, [p for n in both for p in row_pieces(att[n][3])])]
         )[0]
     )
-    inner_quarters = quarters_of(grads_inner)
+    rows_sum[0].send_far()
+    down[1].send_near()
+    inner_quarters = quarters_of(order.pin(grads_inner))
     order.need(grads_inner)
     back_1 = attend_back(1)
-    outputs[0] = (hidden1[0] + down[0].result()).astype(BF16)
-    order.need(rows_sum[0].third(), down[1].third(), *inner_quarters)
-    order.need(*rows_sum[1].add(back_1[3], back_1[4]))
-    down_quarters = quarters_of(grads_down)
-    order.need(grads_down)
+    done = (rows_sum[0].take(), *inner_quarters)
+    rows_sum[0].send_near()
+    rows_sum[1] = Scatter(order, *after((back_1[5], back_1[6]), *done))
+    down_quarters = quarters_of(order.pin(grads_down))
+    order.need(*done, grads_down)
     grads_proj, gain_rows = grad_call(
-        [rows_of(xn1)], [(0, [p for n in both for p in row_pieces(d_proj[n])])], w_attn
+        [xn1[1].pieces], [(0, row_pieces(d_proj[1]))], w_attn, grads_proj
     )
     grads_proj = sum_over_dp(grads_proj)
+    outputs[1] = (hidden1[1] + down[1].result()).astype(BF16)
     input_grads[0] = finish(0)
-    order.need(rows_sum[1].third(), *down_quarters)
+    order.need(*rows_sum[1].add(*after((back_1[3], back_1[4]), outputs[1], input_grads[0])))
+    rows_sum[1].send_far()
+    order.need(*down_quarters)
     grad_gate, grad_up, grad_down = order.run(
         lambda *v: unpack_feed_forward(head_at, v[:4], v[4:]), *inner_quarters, *down_quarters
     )
-    outputs[1] = (hidden1[1] + down[1].result()).astype(BF16)
+    rows_sum[1].take()
+    rows_sum[1].send_near()
     input_grads[1] = finish(1)
 
     gains = jnp.concatenate(
         [gain_rows[0] / attn_norm_gain, gain_ffn[0] + gain_ffn[1]]
         + [gain_parts[0][k] + gain_parts[1][k] for k in range(2)]
     ).reshape(-1, 128)
-    for bits in (BIT_C, BIT_X, BIT_Y):
-        gains = gains + swap(gains, bits)
+    gains = gains + swap(gains, BIT_C)
     for step in (1, 2):
         gains = gains + lax.ppermute(gains, "dp", [(i, i ^ step) for i in range(4)])
+    gains = after(gains, rows_sum[1].sent)
+    for bits in (BIT_X, BIT_Y):
+        gains = gains + swap(gains, bits)
     gains = gains.reshape(-1)
     sum_attn, sum_gain_ffn = gains[:model_width], gains[model_width : 2 * model_width]
     sum_query, sum_key = gains[-256:-128], gains[-128:]

time: 948 us -> 870 us (0.918)
  waiting for transfers between devices: 267 us -> 194 us
  Pallas kernels: 401 us -> 441 us
  other arithmetic: 114 us -> 87.8 us
  starting transfers between devices: 89.4 us -> 67.6 us
    ppermute x32, waiting for transfers between devices: 213 us -> 106 us  [swap_mixed(): lax.ppermute(values, PLANE, [(i, i ^ (core1 if i & BIT_C else core0)) for...]
    pallas_call x0 -> x8, Pallas kernels: none -> 47.3 us  [add_pieces(): pl.pallas_call(add_pieces_kernel, grid=(4,), in_specs=[block] * 4, out_sp...]
    convert_element_type x20 -> x11, other arithmetic: 50.1 us -> 26.4 us  [the longest x8 16.2 us: take(): (self.near[half:].astype(F32) + came[half:].astype(F32)).astype(BF16)]
    ppermute x47, starting transfers between devices: 44.8 us -> 22.5 us  [swap(): return lax.ppermute(values, PLANE, [(i, i ^ bits) for i in range(8)])]
    ppermute x47, waiting for transfers between devices: 52.7 us -> 64.4 us  [swap(): return lax.ppermute(values, PLANE, [(i, i ^ bits) for i in range(8)])]
    all_gather x2, waiting for transfers between devices: 0.01 us -> 11.1 us  [local_plane(): lax.all_gather(rows, 'dp', axis=0, tiled=True)]
    pallas_call x4 -> x5, Pallas kernels: 82.8 us -> 88.2 us  [weight_grad_call(): pl.pallas_call(kernel, in_specs=in_specs, out_specs=[vmem] * len(out_shap...]
    unnamed x171 -> x151, local copies, waits for them, and re-layouts: 23.2 us -> 23.7 us
  transfers between devices with their start and end apart: 88 -> 88, of which waited for: 23 -> 22; matrix products, arithmetic and copies ran while one was open for 14% -> 13% of each run, Pallas kernels for 39% -> 50%
where the time goes in v4:
time: 870 us; the launch traced here: 860 us
  Pallas kernels  441 us (51%)
  waiting for transfers between devices  194 us (22%)
  other arithmetic  87.8 us (10%)
  starting transfers between devices  67.6 us (8%)
  local copies, waits for them, and re-layouts  43.8 us (5%)
  between operations  25.8 us (3%)
    pallas_call x4, Pallas kernels, feed_forward_call(): pl.pallas_call(feed_forward_kernel, grid=(4,), in_specs=[near, far, near,...  121 us
    ppermute x32, waiting for transfers between devices, swap_mixed(): lax.ppermute(values, PLANE, [(i, i ^ (core1 if i & BIT_C else core0)) for...  106 us
    pallas_call x2, Pallas kernels, attend_backward_call(): pl.pallas_call(attend_backward_kernel, grid_spec=pltpu.PrefetchScalarGrid...  105 us
    pallas_call x5, Pallas kernels, weight_grad_call(): pl.pallas_call(kernel, in_specs=in_specs, out_specs=[vmem] * len(out_shap...  88.2 us
    pallas_call x2, Pallas kernels, attend_forward_call(): pl.pallas_call(attend_forward_kernel, grid_spec=pltpu.PrefetchScalarGridS...  66.7 us
    ppermute x47, waiting for transfers between devices, swap(): return lax.ppermute(values, PLANE, [(i, i ^ bits) for i in range(8)])  64.4 us
    pallas_call x8, Pallas kernels, add_pieces(): pl.pallas_call(add_pieces_kernel, grid=(4,), in_specs=[block] * 4, out_sp...  47.3 us
    ppermute x32, starting transfers between devices, swap_mixed(): lax.ppermute(values, PLANE, [(i, i ^ (core1 if i & BIT_C else core0)) for...  44 us
  transfers between devices with their start and end apart: 88, of which 22 were waited for; matrix products, arithmetic and copies ran while one was open for 13% of the time, Pallas kernels for 50%

profile of v4, /device:TPU:0, one launch (start us, length us, event | category | flops | bytes accessed | tf_op | source)
XLA Modules:
  0.0 860.1 jit_solution(18164162824285824843)
XLA Ops:
  18.0 18.4 %collective-permute-done.5 = bf16[256,896]{1,0:T(8,128)(2,1)S(1)} collective-permute-done((bf16[256,896]{1,0:T(8,128)(2,1)S(1)}, bf16[256,896]{1,0:T(8,128)(2,1)S(1)}, u32[]{:S(2)}, u32[]{:S(2)}) %collective-permute-start.5) | collective-permute-done | bytes 458784 | tf_op jit(solution)/shard_map/ppermute | solution.py:441
  56.8 11.1 %collective-permute-done.1.refs_1_ = bf16[512,2048]{1,0:T(8,128)(2,1)} collective-permute-done((bf16[512,2048]{1,0:T(8,128)(2,1)}, bf16[512,2048]{1,0:T(8,128)(2,1)}, u32[]{:S(2)}, u32[]{:S(2)}) %collective-permute-start.1) | collective-permute-done | bytes 2097184 | tf_op jit(solution)/shard_map/ppermute | solution.py:445
  86.4 11.8 %collective-permute-done.14 = bf16[128,2304]{1,0:T(8,128)(2,1)} collective-permute-done((bf16[128,2304]{1,0:T(8,128)(2,1)}, bf16[128,2304]{1,0:T(8,128)(2,1)}, u32[]{:S(2)}, u32[]{:S(2)}) %collective-permute-start.14) | collective-permute-done | bytes 589856 | tf_op jit(solution)/shard_map/ppermute | solution.py:441
  113.8 33.3 %attend_forward.2 = (f32[2048,640]{1,0:T(8,128)}, f32[2048,256]{1,0:T(8,128)}, f32[2048,128]{1,0:T(8,128)}, bf16[2048,256]{1,0:T(8,128)(2,1)}, bf16[512,2048]{1,...) custom-call(s32[49]{0:T(128)} %concatenate.48.table, ...), custom_call_target="tpu_custom_call" | custom-call | flops 49660559360 | bytes 128942080 | tf_op jit(solution)/shard_map/attend_forward/pallas_call | solution.py:771
  159.1 5.8 add_pieces.8
  166.4 11.1 %all-gather.6.cloned.1.call-done.refs_4_ = bf16[2048,768]{1,0:T(8,128)(2,1)} async-done(((bf16[512,768]{1,0:T(8,128)(2,1)}), bf16[2048,768]{1,0:T(8,128)(2,1)}) %all-gather.6.cloned.1.call-update) | async-done | bytes 3145744 | tf_op jit(solution)/shard_map/all_gather | solution.py:1276
  177.6 33.4 %attend_forward.3 = (f32[2048,640]{1,0:T(8,128)}, f32[2048,256]{1,0:T(8,128)}, f32[2048,128]{1,0:T(8,128)}, bf16[2048,256]{1,0:T(8,128)(2,1)}, bf16[512,2048]{1,...) custom-call(s32[49]{0:T(128)} %concatenate.55.table, ...), custom_call_target="tpu_custom_call" | custom-call | flops 49660559360 | bytes 128942080 | tf_op jit(solution)/shard_map/attend_forward/pallas_call | solution.py:771
  215.1 12.8 %collective-permute-done.16 = bf16[256,2048]{1,0:T(8,128)(2,1)S(1)} collective-permute-done((bf16[256,2048]{1,0:T(8,128)(2,1)S(1)}, bf16[256,2048]{1,0:T(8,128)(2,1)S(1)}, u32[]{:S(2)}, u32[]{:S(2)}) %collective-permute-start.16) | collective-permute-done | bytes 1048608 | tf_op jit(solution)/shard_map/ppermute | solution.py:445
  234.2 5.9 add_pieces.9
  241.9 12.0 %collective-permute-done.17 = bf16[256,2048]{1,0:T(8,128)(2,1)} collective-permute-done((bf16[256,2048]{1,0:T(8,128)(2,1)}, bf16[256,2048]{1,0:T(8,128)(2,1)}, u32[]{:S(2)}, u32[]{:S(2)}) %collective-permute-start.17) | collective-permute-done | bytes 1048608 | tf_op jit(solution)/shard_map/ppermute | solution.py:445
  258.5 9.9 %collective-permute-done.26 = bf16[512,2048]{1,0:T(8,128)(2,1)S(1)} collective-permute-done((bf16[512,2048]{1,0:T(8,128)(2,1)}, bf16[512,2048]{1,0:T(8,128)(2,1)S(1)}, u32[]{:S(2)}, u32[]{:S(2)}) %collective-permute-start.26) | collective-permute-done | bytes 2097184 | tf_op jit(solution)/shard_map/ppermute | solution.py:445
  272.8 29.2 %collective-permute-done.18.refs_1_ = bf16[512,2048]{1,0:T(8,128)(2,1)S(1)} collective-permute-done((bf16[512,2048]{1,0:T(8,128)(2,1)S(1)}, bf16[512,2048]{1,0:T(8,128)(2,1)S(1)}, u32[]{:S(2)}, u32[]{:S(2)}) %collective-permute-start.18) | collective-permute-done | bytes 2097184 | tf_op jit(solution)/shard_map/ppermute | solution.py:445
  311.9 30.1 %feed_forward.4 = (bf16[1024,768]{1,0:T(8,128)(2,1)S(1)}, bf16[1024,1536]{1,0:T(8,128)(2,1)}, bf16[512,2048]{1,0:T(8,128)(2,1)}, bf16[512,2048]{1,0:T(8,128)(2,1...) custom-call(bf16[512,2048]{1,0:T(8,128)(2,1)} %copy-done.68, ...), custom_call_target="tpu_custom_call" | custom-call | flops 96636764160 | bytes 131072000 | tf_op jit(solution)/shard_map/feed_forward/pallas_call | solution.py:921
  350.1 30.0 %feed_forward.5 = (bf16[1024,768]{1,0:T(8,128)(2,1)S(1)}, bf16[1024,1536]{1,0:T(8,128)(2,1)}, bf16[512,2048]{1,0:T(8,128)(2,1)}, bf16[512,2048]{1,0:T(8,128)(2,1...) custom-call(bf16[512,2048]{1,0:T(8,128)(2,1)} %copy-done.29, bf16[512,2048]{1,0:T(8,128)(2,1)} %copy-done.67, ...), custom_call_target="tpu_custom_call" | custom-call | flops 96636764160 | bytes 131072000 | tf_op jit(solution)/shard_map/feed_forward/pallas_call | solution.py:921
  381.7 12.2 %collective-permute-done.30.refs_1_.refs_5_ = bf16[512,2048]{1,0:T(8,128)(2,1)} collective-permute-done((bf16[512,2048]{1,0:T(8,128)(2,1)}, bf16[512,2048]{1,0:T(8,128)(2,1)}, u32[]{:S(2)}, u32[]{:S(2)}) %collective-permute-start.30) | collective-permute-done | bytes 2097184 | tf_op jit(solution)/shard_map/ppermute | solution.py:445
  403.4 30.2 %feed_forward.6 = (bf16[1024,768]{1,0:T(8,128)(2,1)S(1)}, bf16[1024,1536]{1,0:T(8,128)(2,1)}, bf16[512,2048]{1,0:T(8,128)(2,1)}, bf16[512,2048]{1,0:T(8,128)(2,1...) custom-call(bf16[512,2048]{1,0:T(8,128)(2,1)} %collective-permute-done.36.refs_0_.refs_6_, ...), custom_call_target="tpu_custom_call" | custom-call | flops 96636764160 | bytes 131072000 | tf_op jit(solution)/shard_map/feed_forward/pallas_call | solution.py:921
  445.7 30.5 %feed_forward.7 = (bf16[1024,768]{1,0:T(8,128)(2,1)S(1)}, bf16[1024,1536]{1,0:T(8,128)(2,1)}, bf16[512,2048]{1,0:T(8,128)(2,1)}, bf16[512,2048]{1,0:T(8,128)(2,1...) custom-call(bf16[512,2048]{1,0:T(8,128)(2,1)} %pad_maximum_fusion.2.refs_0_.refs_4_, ...), custom_call_target="tpu_custom_call" | custom-call | flops 96636764160 | bytes 131072000 | tf_op jit(solution)/shard_map/feed_forward/pallas_call | solution.py:921
  482.5 6.1 add_pieces.12
  492.1 33.1 %weight_grad.5 = bf16[6144,512]{1,0:T(8,128)(2,1)} custom-call(bf16[512,2048]{1,0:T(8,128)(2,1)} %copy-done.29, bf16[512,2048]{1,0:T(8,128)(2,1)} %copy-done.67, bf16[512,2048]{1,0:T(8,128)(2,1)} %copy-done.68, bf16[512,2048]{1,0:T(8,128)(2,1)} %collective-permute-done.21.refs_1_.refs_3_, bf16[512,2048]{1,0:T(8,128)(2,1)} %pad_maximum_fusion.2.refs_0_.refs_4_, ...), custom_call_target="tpu_custom_call" | custom-call | flops 257698037760 | bytes 356515840 | tf_op jit(solution)/shard_map/weight_grad/pallas_call | solution.py:1048
  533.5 18.5 %weight_grad.6 = bf16[3072,512]{1,0:T(8,128)(2,1)} custom-call(bf16[512,2048]{1,0:T(8,128)(2,1)} %constant_dynamic-update-slice_fusion.2.refs_2_.refs_0_, bf16[512,2048]{1,0:T(8,128)(2,1)} %collective-permute-done.19.refs_3_.refs_1_, bf16[512,2048]{1,0:T(8,128)(2,1)} %copy-done.65, bf16[512,2048]{1,0:T(8,128)(2,1)} %copy-done.66, ...), custom_call_target="tpu_custom_call" | custom-call | flops 128849018880 | bytes 262144000 | tf_op jit(solution)/shard_map/weight_grad/pallas_call | solution.py:1048
  552.0 14.2 %collective-permute-done.48.refs_1_ = bf16[512,2048]{1,0:T(8,128)(2,1)} collective-permute-done((bf16[512,2048]{1,0:T(8,128)(2,1)}, bf16[512,2048]{1,0:T(8,128)(2,1)}, u32[]{:S(2)}, u32[]{:S(2)}) %collective-permute-start.48) | collective-permute-done | bytes 2097184 | tf_op jit(solution)/shard_map/ppermute | solution.py:445
  576.2 5.9 add_pieces.13
  583.0 52.3 %attend_backward.2 = (bf16[2048,640]{1,0:T(8,128)(2,1)}, f32[8,128]{1,0:T(8,128)}, f32[8,128]{1,0:T(8,128)}, bf16[512,2048]{1,0:T(8,128)(2,1)}, bf16[512,2048]{1...) custom-call(s32[49]{0:T(128)} %concatenate.48.table, ...), custom_call_target="tpu_custom_call" | custom-call | flops 135559905280 | bytes 257884160 | tf_op jit(solution)/shard_map/attend_backward/pallas_call | solution.py:821
  648.9 6.0 collective-permute-done.58.refs_3_
  654.9 5.9 add_pieces.14
  660.8 10.6 %weight_grad.7.refs_6_ = f32[640,2048]{1,0:T(8,128)} custom-call(bf16[512,2048]{1,0:T(8,128)(2,1)} %pad_maximum_fusion.refs_0_, bf16[512,2048]{1,0:T(8,128)(2,1)} %collective-permute-done.1.refs_1_, bf16[512,2048]{1,0:T(8,128)(2,1)} %collective-permute-done.2.refs_2_, bf16[512,2048]{1,0:T(8,128)(2,1)} %collective-permute-done.3.refs_3_, ...), custom_call_target="tpu_custom_call" | custom-call | flops 53687091200 | bytes 136314880 | tf_op jit(solution)/shard_map/weight_grad/pallas_call | solution.py:1048
  676.0 11.8 %weight_grad.8 = bf16[1024,512]{1,0:T(8,128)(2,1)} custom-call(bf16[512,2048]{1,0:T(8,128)(2,1)} %pad_maximum_fusion.3.refs_0_, bf16[512,2048]{1,0:T(8,128)(2,1)} %collective-permute-done.48.refs_1_, bf16[512,2048]{1,0:T(8,128)(2,1)} %collective-permute-done.49.refs_2_, bf16[512,2048]{1,0:T(8,128)(2,1)} %collective-permute-done.50.refs_3_, ...), custom_call_target="tpu_custom_call" | custom-call | flops 42949672960 | bytes 199229440 | tf_op jit(solution)/shard_map/weight_grad/pallas_call | solution.py:1048
  695.3 52.6 %attend_backward.3 = (bf16[2048,640]{1,0:T(8,128)(2,1)}, f32[8,128]{1,0:T(8,128)}, f32[8,128]{1,0:T(8,128)}, bf16[512,2048]{1,0:T(8,128)(2,1)}, bf16[512,2048]{1...) custom-call(s32[49]{0:T(128)} %concatenate.55.table, bf16[512,2048]{1,0:T(8,128)(2,1)} %copy-done.33, ...), custom_call_target="tpu_custom_call" | custom-call | flops 135559905280 | bytes 257884160 | tf_op jit(solution)/shard_map/attend_backward/pallas_call | solution.py:821
  752.4 14.3 %weight_grad.9 = (bf16[2560,512]{1,0:T(8,128)(2,1)}, f32[8,2048]{1,0:T(8,128)}) custom-call(bf16[512,2048]{1,0:T(8,128)(2,1)} %constant_dynamic-update-slice_fusion.refs_0_, bf16[512,2048]{1,0:T(8,128)(2,1)} %collective-permute-done.6.refs_1_, bf16[512,2048]{1,0:T(8,128)(2,1)} %collective-permute-done.11.refs_2_, ...), custom_call_target="tpu_custom_call" | custom-call | flops 53687091200 | bytes 136314880 | tf_op jit(solution)/shard_map/weight_grad/pallas_call | solution.py:1048
  776.7 6.1 add_pieces.15
  792.2 7.1 collective-permute-done.76
  799.4 16.2 %collective-permute-done.71.refs_6_ = bf16[768,128]{1,0:T(8,128)(2,1)} collective-permute-done((bf16[768,128]{1,0:T(8,128)(2,1)S(1)}, bf16[768,128]{1,0:T(8,128)(2,1)}, u32[]{:S(2)}, u32[]{:S(2)}) %collective-permute-start.71) | collective-permute-done | bytes 196640 | tf_op jit(solution)/shard_map/ppermute | solution.py:441
  (408 shorter events, 246.0 us)
Async XLA Ops:
  7.2 106.6 %all-gather.4.cloned.1.call-start = ((), (), s32[]{:S(2)}) async-start(), calls=%async_computation.4 | async-start | bytes 4587520 | tf_op jit(solution)/shard_map/all_gather | solution.py:1267
  38.5 139.0 %all-gather.6.cloned.1.call-start = ((), (), s32[]{:S(2)}) async-start(), calls=%async_computation.5 | async-start | bytes 3932160 | tf_op jit(solution)/shard_map/all_gather | solution.py:1276
  103.0 208.9 %all-gather.8.cloned.1.call-start = ((), (), s32[]{:S(2)}) async-start(), calls=%async_computation.6 | async-start | bytes 7864320 | tf_op jit(solution)/shard_map/all_gather | solution.py:1276
  105.9 41.3 %collective-permute-start.6 = (bf16[512,2048]{1,0:T(8,128)(2,1)}, bf16[512,2048]{1,0:T(8,128)(2,1)}, u32[]{:S(2)}, u32[]{:S(2)}) collective-permute-start(bf16[512,2048]{1,0:T(8,128)(2,1)} %constant_dynamic-update-slice_fusion.refs_0_), channel_id=1, source_target_pairs={{0,4},{1,5},{2,3},{3,2},{4,0},{5,1},{6,7},{7,6},{8,12},{9,13},{10,... | collective-permute-start | bytes 6291464 | tf_op jit(solution)/shard_map/ppermute | solution.py:445
  105.9 41.3 %collective-permute-start.7 = (bf16[256,2048]{1,0:T(8,128)(2,1)}, bf16[256,2048]{1,0:T(8,128)(2,1)}, u32[]{:S(2)}, u32[]{:S(2)}) collective-permute-start(bf16[256,2048]{1,0:T(8,128)(2,1)} %get-tuple-element.270), channel_id=1, source_target_pairs={{0,1},{1,0},{2,6},{3,7},{4,5},{5,4},{6,2},{7,3},{8,9},{9,8},{10,14... | collective-permute-start | bytes 3145736 | tf_op jit(solution)/shard_map/ppermute | solution.py:445
  152.5 538.4 %reduce-scatter.5.cloned.1.call-start = ((), (), s32[]{:S(2)}) async-start(), calls=%async_computation.7 | async-start | bytes 7864320 | tf_op jit(solution)/shard_map/reduce_scatter | solution.py:1371
  152.5 62.0 %collective-permute-start.19 = (bf16[512,2048]{1,0:T(8,128)(2,1)}, bf16[512,2048]{1,0:T(8,128)(2,1)}, u32[]{:S(2)}, u32[]{:S(2)}) collective-permute-start(bf16[512,2048]{1,0:T(8,128)(2,1)} %constant_dynamic-update-slice_fusion.2.refs_2_.refs_0_), channel_id=1, source_target_pairs={{0,4},{1,5},{2,3},{3,2},{4,0},{5,1},{6,7},{7,6},{8,12},{9,13},{10,... | collective-permute-start | bytes 6291464 | tf_op jit(solution)/shard_map/ppermute | solution.py:445
  165.0 46.0 %collective-permute-start.10 = (bf16[512,2048]{1,0:T(8,128)(2,1)}, bf16[512,2048]{1,0:T(8,128)(2,1)}, u32[]{:S(2)}, u32[]{:S(2)}) collective-permute-start(bf16[512,2048]{1,0:T(8,128)(2,1)} %get-tuple-element.278), channel_id=1, source_target_pairs={{0,4},{1,5},{2,3},{3,2},{4,0},{5,1},{6,7},{7,6},{8,12},{9,13},{10,... | collective-permute-start | bytes 6291464 | tf_op jit(solution)/shard_map/ppermute | solution.py:445
  255.6 46.5 %collective-permute-start.18 = (bf16[512,2048]{1,0:T(8,128)(2,1)S(1)}, bf16[512,2048]{1,0:T(8,128)(2,1)S(1)}, u32[]{:S(2)}, u32[]{:S(2)}) collective-permute-start(bf16[512,2048]{1,0:T(8,128)(2,1)S(1)} %pad_maximum_fusion.1.refs_0_), channel_id=1, source_target_pairs={{0,4},{1,5},{2,3},{3,2},{4,0},{5,1},{6,7},{7,6},{8,12},{9,13},{10,... | collective-permute-start | bytes 6291464 | tf_op jit(solution)/shard_map/ppermute | solution.py:445
  346.8 54.8 %collective-permute-start.38 = (bf16[512,2048]{1,0:T(8,128)(2,1)}, bf16[512,2048]{1,0:T(8,128)(2,1)}, u32[]{:S(2)}, u32[]{:S(2)}) collective-permute-start(bf16[512,2048]{1,0:T(8,128)(2,1)} %constant_dynamic-update-slice_fusion.4.refs_2_.refs_4_), channel_id=1, source_target_pairs={{0,2},{1,3},{2,0},{3,1},{4,6},{5,7},{6,4},{7,5},{8,10},{9,11},{10,... | collective-permute-start | bytes 6291464 | tf_op jit(solution)/shard_map/ppermute | solution.py:441
  348.3 45.5 %collective-permute-start.30 = (bf16[512,2048]{1,0:T(8,128)(2,1)}, bf16[512,2048]{1,0:T(8,128)(2,1)}, u32[]{:S(2)}, u32[]{:S(2)}) collective-permute-start(bf16[512,2048]{1,0:T(8,128)(2,1)} %pad_maximum_fusion.2.refs_0_.refs_4_), channel_id=1, source_target_pairs={{0,4},{1,5},{2,3},{3,2},{4,0},{5,1},{6,7},{7,6},{8,12},{9,13},{10,... | collective-permute-start | bytes 6291464 | tf_op jit(solution)/shard_map/ppermute | solution.py:445
  349.0 44.8 %collective-permute-start.32 = (bf16[512,2048]{1,0:T(8,128)(2,1)S(1)}, bf16[512,2048]{1,0:T(8,128)(2,1)S(1)}, u32[]{:S(2)}, u32[]{:S(2)}) collective-permute-start(bf16[512,2048]{1,0:T(8,128)(2,1)S(1)} %copy-done.70), channel_id=1, source_target_pairs={{0,2},{1,3},{2,0},{3,1},{4,6},{5,7},{6,4},{7,5},{8,10},{9,11},{10,... | collective-permute-start | bytes 6291464 | tf_op jit(solution)/shard_map/ppermute | solution.py:441
  350.0 44.3 %collective-permute-start.33 = (bf16[512,2048]{1,0:T(8,128)(2,1)S(1)}, bf16[512,2048]{1,0:T(8,128)(2,1)}, u32[]{:S(2)}, u32[]{:S(2)}) collective-permute-start(bf16[512,2048]{1,0:T(8,128)(2,1)S(1)} %copy-done.69), channel_id=1, source_target_pairs={{0,2},{1,3},{2,0},{3,1},{4,6},{5,7},{6,4},{7,5},{8,10},{9,11},{10,... | collective-permute-start | bytes 6291464 | tf_op jit(solution)/shard_map/ppermute | solution.py:441
  443.3 39.1 %collective-permute-start.42 = (bf16[512,2048]{1,0:T(8,128)(2,1)}, bf16[512,2048]{1,0:T(8,128)(2,1)}, u32[]{:S(2)}, u32[]{:S(2)}) collective-permute-start(bf16[512,2048]{1,0:T(8,128)(2,1)} %get-tuple-element.361), channel_id=1, source_target_pairs={{0,2},{1,3},{2,0},{3,1},{4,6},{5,7},{6,4},{7,5},{8,10},{9,11},{10,... | collective-permute-start | bytes 6291464 | tf_op jit(solution)/shard_map/ppermute | solution.py:441
  443.4 39.1 %collective-permute-start.43 = (bf16[512,2048]{1,0:T(8,128)(2,1)}, bf16[512,2048]{1,0:T(8,128)(2,1)}, u32[]{:S(2)}, u32[]{:S(2)}) collective-permute-start(bf16[512,2048]{1,0:T(8,128)(2,1)} %get-tuple-element.362), channel_id=1, source_target_pairs={{0,2},{1,3},{2,0},{3,1},{4,6},{5,7},{6,4},{7,5},{8,10},{9,11},{10,... | collective-permute-start | bytes 6291464 | tf_op jit(solution)/shard_map/ppermute | solution.py:441
  443.9 45.5 %collective-permute-start.40 = (bf16[512,2048]{1,0:T(8,128)(2,1)}, bf16[512,2048]{1,0:T(8,128)(2,1)}, u32[]{:S(2)}, u32[]{:S(2)}) collective-permute-start(bf16[512,2048]{1,0:T(8,128)(2,1)} %get-tuple-element.348), channel_id=1, source_target_pairs={{0,4},{1,5},{2,3},{3,2},{4,0},{5,1},{6,7},{7,6},{8,12},{9,13},{10,... | collective-permute-start | bytes 6291464 | tf_op jit(solution)/shard_map/ppermute | solution.py:445
  481.0 44.1 %collective-permute-start.45 = (bf16[256,2048]{1,0:T(8,128)(2,1)}, bf16[256,2048]{1,0:T(8,128)(2,1)}, u32[]{:S(2)}, u32[]{:S(2)}) collective-permute-start(bf16[256,2048]{1,0:T(8,128)(2,1)} %get-tuple-element.538), channel_id=1, source_target_pairs={{0,1},{1,0},{2,6},{3,7},{4,5},{5,4},{6,2},{7,3},{8,9},{9,8},{10,14... | collective-permute-start | bytes 3145736 | tf_op jit(solution)/shard_map/ppermute | solution.py:445
  488.6 41.2 %collective-permute-start.46 = (bf16[512,2048]{1,0:T(8,128)(2,1)}, bf16[512,2048]{1,0:T(8,128)(2,1)}, u32[]{:S(2)}, u32[]{:S(2)}) collective-permute-start(bf16[512,2048]{1,0:T(8,128)(2,1)} %get-tuple-element.382), channel_id=1, source_target_pairs={{0,4},{1,5},{2,3},{3,2},{4,0},{5,1},{6,7},{7,6},{8,12},{9,13},{10,... | collective-permute-start | bytes 6291464 | tf_op jit(solution)/shard_map/ppermute | solution.py:445
  529.8 52.3 %collective-permute-start.49 = (bf16[512,2048]{1,0:T(8,128)(2,1)}, bf16[512,2048]{1,0:T(8,128)(2,1)}, u32[]{:S(2)}, u32[]{:S(2)}) collective-permute-start(bf16[512,2048]{1,0:T(8,128)(2,1)} %pad_maximum_fusion.3.refs_0_), channel_id=1, source_target_pairs={{0,2},{1,3},{2,0},{3,1},{4,6},{5,7},{6,4},{7,5},{8,10},{9,11},{10,... | collective-permute-start | bytes 6291464 | tf_op jit(solution)/shard_map/ppermute | solution.py:441
  533.0 42.1 %collective-permute-start.52 = (bf16[512,2048]{1,0:T(8,128)(2,1)}, bf16[512,2048]{1,0:T(8,128)(2,1)}, u32[]{:S(2)}, u32[]{:S(2)}) collective-permute-start(bf16[512,2048]{1,0:T(8,128)(2,1)} %get-tuple-element.400), channel_id=1, source_target_pairs={{0,2},{1,3},{2,0},{3,1},{4,6},{5,7},{6,4},{7,5},{8,10},{9,11},{10,... | collective-permute-start | bytes 6291464 | tf_op jit(solution)/shard_map/ppermute | solution.py:441
  533.5 42.7 %collective-permute-start.53 = (bf16[512,2048]{1,0:T(8,128)(2,1)}, bf16[512,2048]{1,0:T(8,128)(2,1)}, u32[]{:S(2)}, u32[]{:S(2)}) collective-permute-start(bf16[512,2048]{1,0:T(8,128)(2,1)} %get-tuple-element.401), channel_id=1, source_target_pairs={{0,2},{1,3},{2,0},{3,1},{4,6},{5,7},{6,4},{7,5},{8,10},{9,11},{10,... | collective-permute-start | bytes 6291464 | tf_op jit(solution)/shard_map/ppermute | solution.py:441
  566.3 185.3 %reduce-scatter.7.cloned.1.call-start = ((), (), s32[]{:S(2)}) async-start(), calls=%async_computation.8 | async-start | bytes 3932160 | tf_op jit(solution)/shard_map/reduce_scatter | solution.py:1371
  566.5 68.7 %collective-permute-start.47 = (bf16[256,2048]{1,0:T(8,128)(2,1)}, bf16[256,2048]{1,0:T(8,128)(2,1)}, u32[]{:S(2)}, u32[]{:S(2)}) collective-permute-start(bf16[256,2048]{1,0:T(8,128)(2,1)} %add_convert_fusion.6), channel_id=1, source_target_pairs={{0,1},{1,0},{2,6},{3,7},{4,5},{5,4},{6,2},{7,3},{8,9},{9,8},{10,14... | collective-permute-start | bytes 3145736 | tf_op jit(solution)/shard_map/ppermute | solution.py:445
  575.1 60.2 %collective-permute-start.55 = (bf16[256,2048]{1,0:T(8,128)(2,1)}, bf16[256,2048]{1,0:T(8,128)(2,1)S(1)}, u32[]{:S(2)}, u32[]{:S(2)}) collective-permute-start(bf16[256,2048]{1,0:T(8,128)(2,1)} %get-tuple-element.536), channel_id=1, source_target_pairs={{0,1},{1,0},{2,6},{3,7},{4,5},{5,4},{6,2},{7,3},{8,9},{9,8},{10,14... | collective-permute-start | bytes 3145736 | tf_op jit(solution)/shard_map/ppermute | solution.py:445
  582.1 59.8 %collective-permute-start.54 = (bf16[512,2048]{1,0:T(8,128)(2,1)}, bf16[512,2048]{1,0:T(8,128)(2,1)}, u32[]{:S(2)}, u32[]{:S(2)}) collective-permute-start(bf16[512,2048]{1,0:T(8,128)(2,1)} %get-tuple-element.414), channel_id=1, source_target_pairs={{0,4},{1,5},{2,3},{3,2},{4,0},{5,1},{6,7},{7,6},{8,12},{9,13},{10,... | collective-permute-start | bytes 6291464 | tf_op jit(solution)/shard_map/ppermute | solution.py:445
  646.6 179.1 %reduce-scatter.11.cloned.1.call-start = ((), (), s32[]{:S(2)}) async-start(), calls=%async_computation.10 | async-start | bytes 1310720 | tf_op jit(solution)/shard_map/reduce_scatter | solution.py:1371
  687.8 60.1 %collective-permute-start.62 = (bf16[512,2048]{1,0:T(8,128)(2,1)}, bf16[512,2048]{1,0:T(8,128)(2,1)}, u32[]{:S(2)}, u32[]{:S(2)}) collective-permute-start(bf16[512,2048]{1,0:T(8,128)(2,1)} %get-tuple-element.451), channel_id=1, source_target_pairs={{0,4},{1,5},{2,3},{3,2},{4,0},{5,1},{6,7},{7,6},{8,12},{9,13},{10,... | collective-permute-start | bytes 6291464 | tf_op jit(solution)/shard_map/ppermute | solution.py:445
  689.5 144.8 %reduce-scatter.9.cloned.1.call-start = ((), (), s32[]{:S(2)}) async-start(), calls=%async_computation.9 | async-start | bytes 3276800 | tf_op jit(solution)/shard_map/reduce_scatter | solution.py:1371
  689.6 77.2 %collective-permute-start.61 = (bf16[256,2048]{1,0:T(8,128)(2,1)}, bf16[256,2048]{1,0:T(8,128)(2,1)}, u32[]{:S(2)}, u32[]{:S(2)}) collective-permute-start(bf16[256,2048]{1,0:T(8,128)(2,1)} %add_convert_fusion.3), channel_id=1, source_target_pairs={{0,1},{1,0},{2,6},{3,7},{4,5},{5,4},{6,2},{7,3},{8,9},{9,8},{10,14... | collective-permute-start | bytes 3145736 | tf_op jit(solution)/shard_map/ppermute | solution.py:445
  693.4 58.2 %collective-permute-start.63 = (bf16[1536,128]{1,0:T(8,128)(2,1)}, bf16[1536,128]{1,0:T(8,128)(2,1)S(1)}, u32[]{:S(2)}, u32[]{:S(2)}) collective-permute-start(bf16[1536,128]{1,0:T(8,128)(2,1)} %get-tuple-element.562), channel_id=1, source_target_pairs={{0,2},{1,3},{2,0},{3,1},{4,6},{5,7},{6,4},{7,5},{8,10},{9,11},{10,... | collective-permute-start | bytes 1179656 | tf_op jit(solution)/shard_map/ppermute | solution.py:441
  693.4 58.2 %collective-permute-start.64 = (bf16[1536,128]{1,0:T(8,128)(2,1)}, bf16[1536,128]{1,0:T(8,128)(2,1)S(1)}, u32[]{:S(2)}, u32[]{:S(2)}) collective-permute-start(bf16[1536,128]{1,0:T(8,128)(2,1)} %get-tuple-element.561), channel_id=1, source_target_pairs={{0,4},{1,5},{2,6},{3,7},{4,0},{5,1},{6,2},{7,3},{8,12},{9,13},{10,... | collective-permute-start | bytes 1179656 | tf_op jit(solution)/shard_map/ppermute | solution.py:441
  693.8 57.8 %collective-permute-start.65 = (bf16[1536,128]{1,0:T(8,128)(2,1)}, bf16[1536,128]{1,0:T(8,128)(2,1)}, u32[]{:S(2)}, u32[]{:S(2)}) collective-permute-start(bf16[1536,128]{1,0:T(8,128)(2,1)} %get-tuple-element.560), channel_id=1, source_target_pairs={{0,6},{1,7},{2,4},{3,5},{4,2},{5,3},{6,0},{7,1},{8,14},{9,15},{10,... | collective-permute-start | bytes 1179656 | tf_op jit(solution)/shard_map/ppermute | solution.py:441
  (129 other events, 1873.4 us)
Sparse Core Ops, SparseCore 0:
  38.7 75.1 all-gather.3
  115.4 62.1 all-gather.5
  179.7 113.9 all-gather.7
  566.4 108.4 reduce-scatter.4
  677.0 60.7 reduce-scatter.6
  740.0 27.1 reduce-scatter.10
  769.6 51.6 reduce-scatter.8

commit v5 on v4

--- a/solution.py
+++ b/solution.py
@@ -488,25 +488,24 @@
         return far
 
 
-def add_pieces_kernel(*refs):
-    for k in range(2):
-        refs[4 + k][...] = (refs[k][...].astype(F32) + refs[2 + k][...].astype(F32)).astype(BF16)
-
-
-def add_pieces(near, far, near_came, far_came):
-    count, width = near.shape
+def add_pieces_kernel(first, second, out):
+    out[...] = (first[...].astype(F32) + second[...].astype(F32)).astype(BF16)
+
+
+def add_pieces(first, second):
+    count, width = first.shape
     block = pl.BlockSpec((count // 4, width), lambda i: (i, 0))
     return pl.pallas_call(
         add_pieces_kernel,
         grid=(4,),
-        in_specs=[block] * 4,
-        out_specs=[block] * 2,
-        out_shape=[jax.ShapeDtypeStruct((count, width), BF16)] * 2,
+        in_specs=[block] * 2,
+        out_specs=block,
+        out_shape=jax.ShapeDtypeStruct((count, width), BF16),
         cost_estimate=pl.CostEstimate(
-            flops=2 * count * width, bytes_accessed=12 * count * width, transcendentals=0
+            flops=count * width, bytes_accessed=6 * count * width, transcendentals=0
         ),
         name="add_pieces",
-    )(near, far, near_came, far_came)
+    )(first, second)
 
 
 class Scatter:
@@ -516,17 +515,19 @@
 
     def add(self, near, far):
         near_came, far_came = self.order.pin(self.came)
-        self.near, self.far = add_pieces(near, far, near_came, far_came)
-        return (self.near, self.far)
+        self.near = (near, near_came)
+        self.far = add_pieces(far, far_came)
+        return (self.far,)
 
     def send_far(self):
         self.came = swap_mixed(self.order.pin(self.far), BIT_Y, BIT_X)
 
     def take(self):
-        came = self.order.pin(self.came)
-        half = came.shape[0] // 2
-        self.sent = (self.near[half:].astype(F32) + came[half:].astype(F32)).astype(BF16)
-        self.kept = self.near[:half].astype(F32) + came[:half].astype(F32)
+        terms = (*self.near, self.order.pin(self.came))
+        half = terms[0].shape[0] // 2
+        low, high = [sum(t[part].astype(F32) for t in terms) for part in (slice(0, half), slice(half, None))]
+        self.kept = low
+        self.sent = high.astype(BF16)
         return self.sent
 
     def send_near(self):
@@ -948,12 +949,13 @@
     return (out[0], out[1], (out[2], out[3]), (out[4], out[5]))
 
 
-def weight_grad_call(n_parts, lefts, terms, weights=None, carried=None, final=True):
+def weight_grad_call(n_parts, lefts, terms, weights=None, carried=None, final=True, keep=None):
     n_pieces = len(lefts[0])
     rows, width = lefts[0][0].shape
     columns = [pieces[0][0].shape[1] for _, pieces in terms]
-    starts = [sum(columns[:k]) for k in range(len(terms))]
-    total = sum(columns)
+    kept = [keep or c for c in columns]
+    starts = [sum(kept[:k]) for k in range(len(terms))]
+    total = sum(kept)
     arrays, place = ([], {})
     for _, pieces in terms:
         for array, _ in pieces:
@@ -1025,9 +1027,8 @@
         for p in range(n_parts):
             for k in range(n_terms):
                 start = p * total + starts[k]
-                out[start : start + columns[k], :] = accs[k][:, p * part : (p + 1) * part].astype(
-                    BF16
-                )
+                some = accs[k][: kept[k], p * part : (p + 1) * part]
+                out[start : start + kept[k], :] = some.astype(BF16)
         if weights is not None:
             scaled = accs[0][...] * weights_ref[:, : columns[0]].T.astype(F32)
             gain[...] = jnp.broadcast_to(jnp.sum(scaled, axis=0, keepdims=True), gain.shape)
@@ -1113,7 +1114,7 @@
         query[:, 256 * k : 256 * k + 256] = part[0:256].T
         key[:, 128 * k : 128 * k + 128] = part[256:384].T
         value[:, 128 * k : 128 * k + 128] = part[384:512].T
-        headgate[:, 2 * k : 2 * k + 2] = part[512:640].T[:, 0:2]
+        headgate[:, 2 * k : 2 * k + 2] = part[512:528].T[:, 0:2]
     for k, part in enumerate(ordered(out_kept, out_came)):
         out[256 * k : 256 * k + 256, :] = part
 
@@ -1258,12 +1259,11 @@
     ]
     cot_own = [c.astype(BF16) for c in cot_live]
     xn1, xn2, cot, d_attn = ([None] * micro_batches for _ in range(4))
-    xn1[0] = Gather(order, xn1_own[0])
+    xn1[0] = Gather(order, after(xn1_own[0], attn_came))
     is_first = mp_idx == 0
     attn_rows = jnp.concatenate(
         [pick(is_first, halves[0], attn_came), pick(is_first, attn_came, halves[0])], axis=0
     )
-    attn_rows = after(attn_rows, xn1[0].came)
     w_attn = lax.all_gather(attn_rows, "dp", axis=0, tiled=True)
     xn1[0].second()
     xn1[0].third()
@@ -1442,23 +1442,22 @@
     done = (rows_sum[0].take(), *inner_quarters)
     rows_sum[0].send_near()
     rows_sum[1] = Scatter(order, *after((back_1[5], back_1[6]), *done))
-    down_quarters = quarters_of(order.pin(grads_down))
     order.need(*done, grads_down)
     grads_proj, gain_rows = grad_call(
-        [xn1[1].pieces], [(0, row_pieces(d_proj[1]))], w_attn, grads_proj
+        [xn1[1].pieces], [(0, row_pieces(d_proj[1]))], w_attn, grads_proj, True, 528
     )
     grads_proj = sum_over_dp(grads_proj)
     outputs[1] = (hidden1[1] + down[1].result()).astype(BF16)
     input_grads[0] = finish(0)
     order.need(*rows_sum[1].add(*after((back_1[3], back_1[4]), outputs[1], input_grads[0])))
     rows_sum[1].send_far()
-    order.need(*down_quarters)
+    down_quarters = quarters_of(after(grads_down, rows_sum[1].take()))
+    rows_sum[1].send_near()
+    input_grads[1] = finish(1)
+    order.need(input_grads[1])
     grad_gate, grad_up, grad_down = order.run(
         lambda *v: unpack_feed_forward(head_at, v[:4], v[4:]), *inner_quarters, *down_quarters
     )
-    rows_sum[1].take()
-    rows_sum[1].send_near()
-    input_grads[1] = finish(1)
 
     gains = jnp.concatenate(
         [gain_rows[0] / attn_norm_gain, gain_ffn[0] + gain_ffn[1]]
@@ -1467,7 +1466,7 @@
     gains = gains + swap(gains, BIT_C)
     for step in (1, 2):
         gains = gains + lax.ppermute(gains, "dp", [(i, i ^ step) for i in range(4)])
-    gains = after(gains, rows_sum[1].sent)
+    gains = after(gains, input_grads[1])
     for bits in (BIT_X, BIT_Y):
         gains = gains + swap(gains, bits)
     gains = gains.reshape(-1)
@@ -1478,8 +1477,8 @@
         left, right = values[:, :row_count], values[:, row_count:]
         return pick(is_first, left, right), swap(pick(is_first, right, left), BIT_X)
 
-    grad_query, grad_key, grad_value, grad_headgate, grad_out = unpack_attention(
-        mp_at, *halves_of(grads_proj), *halves_of(grads_out)
+    grad_query, grad_key, grad_value, grad_headgate, grad_out = order.run(
+        lambda *v: unpack_attention(mp_at, *v), *halves_of(grads_proj), *halves_of(grads_out)
     )
     return (
         jnp.stack(outputs),

time: 870 us -> 862 us (level)
  other arithmetic: 87.8 us -> 104 us
  Pallas kernels: 441 us -> 428 us
  waiting for transfers between devices: 194 us -> 185 us
    ppermute x32, waiting for transfers between devices: 106 us -> 144 us  [swap_mixed(): lax.ppermute(values, PLANE, [(i, i ^ (core1 if i & BIT_C else core0)) for...]
    ppermute x47, waiting for transfers between devices: 64.4 us -> 39.4 us  [swap(): return lax.ppermute(values, PLANE, [(i, i ^ bits) for i in range(8)])]
    pallas_call x8, Pallas kernels: 47.3 us -> 35.4 us  [add_pieces(): pl.pallas_call(add_pieces_kernel, grid=(4,), in_specs=[block] * 2, out_sp...]
    all_gather x2, waiting for transfers between devices: 11.1 us -> 0.01 us  [local_plane(): lax.all_gather(rows, 'dp', axis=0, tiled=True)]
    ppermute x32, starting transfers between devices: 44 us -> 34.2 us  [swap_mixed(): lax.ppermute(values, PLANE, [(i, i ^ (core1 if i & BIT_C else core0)) for...]
    unnamed x151 -> x152, local copies, waits for them, and re-layouts: 23.7 us -> 22.1 us
  transfers between devices with their start and end apart: 88 -> 88, of which waited for: 22 -> 22; matrix products, arithmetic and copies ran while one was open for 13% -> 15% of each run, Pallas kernels for 50% -> 49%
where the time goes in v5:
time: 862 us; the launch traced here: 853 us
  Pallas kernels  428 us (50%)
  waiting for transfers between devices  185 us (21%)
  other arithmetic  104 us (12%)
  starting transfers between devices  68.3 us (8%)
  local copies, waits for them, and re-layouts  42.2 us (5%)
  between operations  25.9 us (3%)
    ppermute x32, waiting for transfers between devices, swap_mixed(): lax.ppermute(values, PLANE, [(i, i ^ (core1 if i & BIT_C else core0)) for...  144 us
    pallas_call x4, Pallas kernels, feed_forward_call(): pl.pallas_call(feed_forward_kernel, grid=(4,), in_specs=[near, far, near,...  121 us
    pallas_call x2, Pallas kernels, attend_backward_call(): pl.pallas_call(attend_backward_kernel, grid_spec=pltpu.PrefetchScalarGrid...  104 us
    pallas_call x5, Pallas kernels, weight_grad_call(): pl.pallas_call(kernel, in_specs=in_specs, out_specs=[vmem] * len(out_shap...  88.3 us
    pallas_call x2, Pallas kernels, attend_forward_call(): pl.pallas_call(attend_forward_kernel, grid_spec=pltpu.PrefetchScalarGridS...  66.1 us
    ppermute x47, waiting for transfers between devices, swap(): return lax.ppermute(values, PLANE, [(i, i ^ bits) for i in range(8)])  39.4 us
    pallas_call x8, Pallas kernels, add_pieces(): pl.pallas_call(add_pieces_kernel, grid=(4,), in_specs=[block] * 2, out_sp...  35.4 us
    ppermute x32, starting transfers between devices, swap_mixed(): lax.ppermute(values, PLANE, [(i, i ^ (core1 if i & BIT_C else core0)) for...  34.2 us
  transfers between devices with their start and end apart: 88, of which 22 were waited for; matrix products, arithmetic and copies ran while one was open for 15% of the time, Pallas kernels for 49%

profile of v5, /device:TPU:0, one launch (start us, length us, event | category | flops | bytes accessed | tf_op | source)
XLA Modules:
  0.0 852.7 jit_solution(682814493748056075)
XLA Ops:
  17.1 8.6 %collective-permute-done = bf16[256,896]{1,0:T(8,128)(2,1)S(1)} collective-permute-done((bf16[256,896]{1,0:T(8,128)(2,1)S(1)}, bf16[256,896]{1,0:T(8,128)(2,1)S(1)}, u32[]{:S(2)}, u32[]{:S(2)}) %collective-permute-start) | collective-permute-done | bytes 458784 | tf_op jit(solution)/shard_map/ppermute | solution.py:441
  31.7 9.6 %collective-permute-done.1 = bf16[256,2048]{1,0:T(8,128)(2,1)S(1)} collective-permute-done((bf16[256,2048]{1,0:T(8,128)(2,1)S(1)}, bf16[256,2048]{1,0:T(8,128)(2,1)S(1)}, u32[]{:S(2)}, u32[]{:S(2)}) %collective-permute-start.1) | collective-permute-done | bytes 1048608 | tf_op jit(solution)/shard_map/ppermute | solution.py:445
  57.3 11.4 %collective-permute-done.2.refs_1_ = bf16[512,2048]{1,0:T(8,128)(2,1)} collective-permute-done((bf16[512,2048]{1,0:T(8,128)(2,1)}, bf16[512,2048]{1,0:T(8,128)(2,1)}, u32[]{:S(2)}, u32[]{:S(2)}) %collective-permute-start.2) | collective-permute-done | bytes 2097184 | tf_op jit(solution)/shard_map/ppermute | solution.py:445
  87.6 11.2 %collective-permute-done.14 = bf16[128,2304]{1,0:T(8,128)(2,1)} collective-permute-done((bf16[128,2304]{1,0:T(8,128)(2,1)}, bf16[128,2304]{1,0:T(8,128)(2,1)}, u32[]{:S(2)}, u32[]{:S(2)}) %collective-permute-start.14) | collective-permute-done | bytes 589856 | tf_op jit(solution)/shard_map/ppermute | solution.py:441
  110.3 32.8 %attend_forward.2 = (f32[2048,640]{1,0:T(8,128)}, f32[2048,256]{1,0:T(8,128)}, f32[2048,128]{1,0:T(8,128)}, bf16[2048,256]{1,0:T(8,128)(2,1)}, bf16[512,2048]{1,...) custom-call(s32[49]{0:T(128)} %concatenate.48.table, ...), custom_call_target="tpu_custom_call" | custom-call | flops 49660559360 | bytes 128942080 | tf_op jit(solution)/shard_map/attend_forward/pallas_call | solution.py:772
  145.4 5.8 collective-permute-start.8
  167.8 33.3 %attend_forward.3 = (f32[2048,640]{1,0:T(8,128)}, f32[2048,256]{1,0:T(8,128)}, f32[2048,128]{1,0:T(8,128)}, bf16[2048,256]{1,0:T(8,128)(2,1)}, bf16[512,2048]{1,...) custom-call(s32[49]{0:T(128)} %concatenate.55.table, ...), custom_call_target="tpu_custom_call" | custom-call | flops 49660559360 | bytes 128942080 | tf_op jit(solution)/shard_map/attend_forward/pallas_call | solution.py:772
  205.5 13.9 %collective-permute-done.16 = bf16[256,2048]{1,0:T(8,128)(2,1)S(1)} collective-permute-done((bf16[256,2048]{1,0:T(8,128)(2,1)S(1)}, bf16[256,2048]{1,0:T(8,128)(2,1)S(1)}, u32[]{:S(2)}, u32[]{:S(2)}) %collective-permute-start.16) | collective-permute-done | bytes 1048608 | tf_op jit(solution)/shard_map/ppermute | solution.py:445
  224.8 4.4 add_pieces.9
  230.9 16.7 %collective-permute-done.17 = bf16[256,2048]{1,0:T(8,128)(2,1)} collective-permute-done((bf16[256,2048]{1,0:T(8,128)(2,1)}, bf16[256,2048]{1,0:T(8,128)(2,1)}, u32[]{:S(2)}, u32[]{:S(2)}) %collective-permute-start.17) | collective-permute-done | bytes 1048608 | tf_op jit(solution)/shard_map/ppermute | solution.py:445
  250.6 9.3 %collective-permute-done.26 = bf16[512,2048]{1,0:T(8,128)(2,1)S(1)} collective-permute-done((bf16[512,2048]{1,0:T(8,128)(2,1)}, bf16[512,2048]{1,0:T(8,128)(2,1)S(1)}, u32[]{:S(2)}, u32[]{:S(2)}) %collective-permute-start.26) | collective-permute-done | bytes 2097184 | tf_op jit(solution)/shard_map/ppermute | solution.py:445
  265.2 28.3 %collective-permute-done.18.refs_1_ = bf16[512,2048]{1,0:T(8,128)(2,1)S(1)} collective-permute-done((bf16[512,2048]{1,0:T(8,128)(2,1)S(1)}, bf16[512,2048]{1,0:T(8,128)(2,1)S(1)}, u32[]{:S(2)}, u32[]{:S(2)}) %collective-permute-start.18) | collective-permute-done | bytes 2097184 | tf_op jit(solution)/shard_map/ppermute | solution.py:445
  305.0 30.3 %feed_forward.4 = (bf16[1024,768]{1,0:T(8,128)(2,1)S(1)}, bf16[1024,1536]{1,0:T(8,128)(2,1)}, bf16[512,2048]{1,0:T(8,128)(2,1)}, bf16[512,2048]{1,0:T(8,128)(2,1...) custom-call(bf16[512,2048]{1,0:T(8,128)(2,1)} %copy-done.67, ...), custom_call_target="tpu_custom_call" | custom-call | flops 96636764160 | bytes 131072000 | tf_op jit(solution)/shard_map/feed_forward/pallas_call | solution.py:922
  342.4 30.0 %feed_forward.5 = (bf16[1024,768]{1,0:T(8,128)(2,1)S(1)}, bf16[1024,1536]{1,0:T(8,128)(2,1)}, bf16[512,2048]{1,0:T(8,128)(2,1)}, bf16[512,2048]{1,0:T(8,128)(2,1...) custom-call(bf16[512,2048]{1,0:T(8,128)(2,1)} %copy-done.34, bf16[512,2048]{1,0:T(8,128)(2,1)} %copy-done.66, ...), custom_call_target="tpu_custom_call" | custom-call | flops 96636764160 | bytes 131072000 | tf_op jit(solution)/shard_map/feed_forward/pallas_call | solution.py:922
  373.9 13.1 %collective-permute-done.30.refs_1_.refs_5_ = bf16[512,2048]{1,0:T(8,128)(2,1)} collective-permute-done((bf16[512,2048]{1,0:T(8,128)(2,1)}, bf16[512,2048]{1,0:T(8,128)(2,1)}, u32[]{:S(2)}, u32[]{:S(2)}) %collective-permute-start.30) | collective-permute-done | bytes 2097184 | tf_op jit(solution)/shard_map/ppermute | solution.py:445
  387.5 4.3 add_pieces.10
  394.5 30.2 %feed_forward.6 = (bf16[1024,768]{1,0:T(8,128)(2,1)S(1)}, bf16[1024,1536]{1,0:T(8,128)(2,1)}, bf16[512,2048]{1,0:T(8,128)(2,1)}, bf16[512,2048]{1,0:T(8,128)(2,1...) custom-call(bf16[512,2048]{1,0:T(8,128)(2,1)} %collective-permute-done.36.refs_0_.refs_6_, ...), custom_call_target="tpu_custom_call" | custom-call | flops 96636764160 | bytes 131072000 | tf_op jit(solution)/shard_map/feed_forward/pallas_call | solution.py:922
  435.0 30.5 %feed_forward.7 = (bf16[1024,768]{1,0:T(8,128)(2,1)S(1)}, bf16[1024,1536]{1,0:T(8,128)(2,1)}, bf16[512,2048]{1,0:T(8,128)(2,1)}, bf16[512,2048]{1,0:T(8,128)(2,1...) custom-call(bf16[512,2048]{1,0:T(8,128)(2,1)} %pad_maximum_fusion.1.refs_0_.refs_4_, ...), custom_call_target="tpu_custom_call" | custom-call | flops 96636764160 | bytes 131072000 | tf_op jit(solution)/shard_map/feed_forward/pallas_call | solution.py:922
  473.9 4.5 add_pieces.12
  482.5 33.1 %weight_grad.5 = bf16[6144,512]{1,0:T(8,128)(2,1)} custom-call(bf16[512,2048]{1,0:T(8,128)(2,1)} %copy-done.34, bf16[512,2048]{1,0:T(8,128)(2,1)} %copy-done.66, bf16[512,2048]{1,0:T(8,128)(2,1)} %copy-done.67, bf16[512,2048]{1,0:T(8,128)(2,1)} %collective-permute-done.21.refs_1_.refs_3_, bf16[512,2048]{1,0:T(8,128)(2,1)} %pad_maximum_fusion.1.refs_0_.refs_4_, ...), custom_call_target="tpu_custom_call" | custom-call | flops 257698037760 | bytes 356515840 | tf_op jit(solution)/shard_map/weight_grad/pallas_call | solution.py:1049
  524.6 18.5 %weight_grad.6 = bf16[3072,512]{1,0:T(8,128)(2,1)} custom-call(bf16[512,2048]{1,0:T(8,128)(2,1)} %constant_dynamic-update-slice_fusion.4.refs_2_.refs_0_, bf16[512,2048]{1,0:T(8,128)(2,1)} %collective-permute-done.19.refs_3_.refs_1_, bf16[512,2048]{1,0:T(8,128)(2,1)} %copy-done.64, bf16[512,2048]{1,0:T(8,128)(2,1)} %copy-done.65, ...), custom_call_target="tpu_custom_call" | custom-call | flops 128849018880 | bytes 262144000 | tf_op jit(solution)/shard_map/weight_grad/pallas_call | solution.py:1049
  543.1 13.3 %collective-permute-done.48.refs_1_ = bf16[512,2048]{1,0:T(8,128)(2,1)} collective-permute-done((bf16[512,2048]{1,0:T(8,128)(2,1)}, bf16[512,2048]{1,0:T(8,128)(2,1)}, u32[]{:S(2)}, u32[]{:S(2)}) %collective-permute-start.48) | collective-permute-done | bytes 2097184 | tf_op jit(solution)/shard_map/ppermute | solution.py:445
  561.1 4.4 fusion.30
  572.6 51.2 %attend_backward.2 = (bf16[2048,640]{1,0:T(8,128)(2,1)}, f32[8,128]{1,0:T(8,128)}, f32[8,128]{1,0:T(8,128)}, bf16[512,2048]{1,0:T(8,128)(2,1)}, bf16[512,2048]{1...) custom-call(s32[49]{0:T(128)} %concatenate.48.table, ...), custom_call_target="tpu_custom_call" | custom-call | flops 135559905280 | bytes 257884160 | tf_op jit(solution)/shard_map/attend_backward/pallas_call | solution.py:822
  635.5 5.6 collective-permute-done.57
  641.2 4.9 add_pieces.14
  646.1 10.6 %weight_grad.7.refs_6_ = f32[640,2048]{1,0:T(8,128)} custom-call(bf16[512,2048]{1,0:T(8,128)(2,1)} %constant_dynamic-update-slice_fusion.refs_0_, bf16[512,2048]{1,0:T(8,128)(2,1)} %collective-permute-done.2.refs_1_, bf16[512,2048]{1,0:T(8,128)(2,1)} %collective-permute-done.3.refs_2_, bf16[512,2048]{1,0:T(8,128)(2,1)} %collective-permute-done.4.refs_3_, ...), custom_call_target="tpu_custom_call" | custom-call | flops 53687091200 | bytes 136314880 | tf_op jit(solution)/shard_map/weight_grad/pallas_call | solution.py:1049
  660.6 4.4 collective-permute-done.60.refs_7_.refs_3_
  666.2 11.8 %weight_grad.8 = bf16[1024,512]{1,0:T(8,128)(2,1)} custom-call(bf16[512,2048]{1,0:T(8,128)(2,1)} %pad_maximum_fusion.2.refs_0_, bf16[512,2048]{1,0:T(8,128)(2,1)} %collective-permute-done.48.refs_1_, bf16[512,2048]{1,0:T(8,128)(2,1)} %collective-permute-done.49.refs_2_, bf16[512,2048]{1,0:T(8,128)(2,1)} %collective-permute-done.50.refs_3_, ...), custom_call_target="tpu_custom_call" | custom-call | flops 42949672960 | bytes 199229440 | tf_op jit(solution)/shard_map/weight_grad/pallas_call | solution.py:1049
  684.2 52.4 %attend_backward.3 = (bf16[2048,640]{1,0:T(8,128)(2,1)}, f32[8,128]{1,0:T(8,128)}, f32[8,128]{1,0:T(8,128)}, bf16[512,2048]{1,0:T(8,128)(2,1)}, bf16[512,2048]{1...) custom-call(s32[49]{0:T(128)} %concatenate.55.table, ...), custom_call_target="tpu_custom_call" | custom-call | flops 135559905280 | bytes 257884160 | tf_op jit(solution)/shard_map/attend_backward/pallas_call | solution.py:822
  742.7 14.4 %weight_grad.9 = (bf16[2112,512]{1,0:T(8,128)(2,1)}, f32[8,2048]{1,0:T(8,128)}) custom-call(bf16[512,2048]{1,0:T(8,128)(2,1)} %constant_dynamic-update-slice_fusion.2.refs_0_, bf16[512,2048]{1,0:T(8,128)(2,1)} %collective-permute-done.6.refs_1_, bf16[512,2048]{1,0:T(8,128)(2,1)} %collective-permute-done.11.refs_2_, ...), custom_call_target="tpu_custom_call" | custom-call | flops 44291850240 | bytes 127139840 | tf_op jit(solution)/shard_map/weight_grad/pallas_call | solution.py:1049
  775.6 22.5 %collective-permute-done.69 = bf16[512,2048]{1,0:T(8,128)(2,1)} collective-permute-done((bf16[512,2048]{1,0:T(8,128)(2,1)}, bf16[512,2048]{1,0:T(8,128)(2,1)}, u32[]{:S(2)}, u32[]{:S(2)}) %collective-permute-start.69) | collective-permute-done | bytes 2097184 | tf_op jit(solution)/shard_map/ppermute | solution.py:445
  (409 shorter events, 251.5 us)
Async XLA Ops:
  7.2 103.1 %all-gather.4.cloned.1.call-start = ((), (), s32[]{:S(2)}) async-start(), calls=%async_computation.4 | async-start | bytes 4587520 | tf_op jit(solution)/shard_map/all_gather | solution.py:1267
  30.5 137.3 %all-gather.6.cloned.1.call-start = ((), (), s32[]{:S(2)}) async-start(), calls=%async_computation.5 | async-start | bytes 3932160 | tf_op jit(solution)/shard_map/all_gather | solution.py:1276
  103.6 201.4 %all-gather.8.cloned.1.call-start = ((), (), s32[]{:S(2)}) async-start(), calls=%async_computation.6 | async-start | bytes 7864320 | tf_op jit(solution)/shard_map/all_gather | solution.py:1276
  106.4 39.0 %collective-permute-start.6 = (bf16[512,2048]{1,0:T(8,128)(2,1)}, bf16[512,2048]{1,0:T(8,128)(2,1)}, u32[]{:S(2)}, u32[]{:S(2)}) collective-permute-start(bf16[512,2048]{1,0:T(8,128)(2,1)} %constant_dynamic-update-slice_fusion.2.refs_0_), channel_id=1, source_target_pairs={{0,4},{1,5},{2,3},{3,2},{4,0},{5,1},{6,7},{7,6},{8,12},{9,13},{10,... | collective-permute-start | bytes 6291464 | tf_op jit(solution)/shard_map/ppermute | solution.py:445
  153.0 526.8 %reduce-scatter.5.cloned.1.call-start = ((), (), s32[]{:S(2)}) async-start(), calls=%async_computation.7 | async-start | bytes 7864320 | tf_op jit(solution)/shard_map/reduce_scatter | solution.py:1371
  153.1 51.9 %collective-permute-start.19 = (bf16[512,2048]{1,0:T(8,128)(2,1)}, bf16[512,2048]{1,0:T(8,128)(2,1)}, u32[]{:S(2)}, u32[]{:S(2)}) collective-permute-start(bf16[512,2048]{1,0:T(8,128)(2,1)} %constant_dynamic-update-slice_fusion.4.refs_2_.refs_0_), channel_id=1, source_target_pairs={{0,4},{1,5},{2,3},{3,2},{4,0},{5,1},{6,7},{7,6},{8,12},{9,13},{10,... | collective-permute-start | bytes 6291464 | tf_op jit(solution)/shard_map/ppermute | solution.py:445
  249.4 44.1 %collective-permute-start.18 = (bf16[512,2048]{1,0:T(8,128)(2,1)S(1)}, bf16[512,2048]{1,0:T(8,128)(2,1)S(1)}, u32[]{:S(2)}, u32[]{:S(2)}) collective-permute-start(bf16[512,2048]{1,0:T(8,128)(2,1)S(1)} %pad_maximum_fusion.refs_0_), channel_id=1, source_target_pairs={{0,4},{1,5},{2,3},{3,2},{4,0},{5,1},{6,7},{7,6},{8,12},{9,13},{10,... | collective-permute-start | bytes 6291464 | tf_op jit(solution)/shard_map/ppermute | solution.py:445
  296.5 38.8 %collective-permute-start.29 = (bf16[256,2048]{1,0:T(8,128)(2,1)S(1)}, bf16[256,2048]{1,0:T(8,128)(2,1)}, u32[]{:S(2)}, u32[]{:S(2)}) collective-permute-start(bf16[256,2048]{1,0:T(8,128)(2,1)S(1)} %get-tuple-element.298), channel_id=1, source_target_pairs={{0,1},{1,0},{2,6},{3,7},{4,5},{5,4},{6,2},{7,3},{8,9},{9,8},{10,14... | collective-permute-start | bytes 3145736 | tf_op jit(solution)/shard_map/ppermute | solution.py:445
  300.6 38.6 %collective-permute-start.28 = (bf16[256,2048]{1,0:T(8,128)(2,1)S(1)}, bf16[256,2048]{1,0:T(8,128)(2,1)S(1)}, u32[]{:S(2)}, u32[]{:S(2)}) collective-permute-start(bf16[256,2048]{1,0:T(8,128)(2,1)S(1)} %multiply_convert_fusion), channel_id=1, source_target_pairs={{0,1},{1,0},{2,6},{3,7},{4,5},{5,4},{6,2},{7,3},{8,9},{9,8},{10,14... | collective-permute-start | bytes 3145736 | tf_op jit(solution)/shard_map/ppermute | solution.py:445
  339.2 52.7 %collective-permute-start.38 = (bf16[512,2048]{1,0:T(8,128)(2,1)}, bf16[512,2048]{1,0:T(8,128)(2,1)}, u32[]{:S(2)}, u32[]{:S(2)}) collective-permute-start(bf16[512,2048]{1,0:T(8,128)(2,1)} %constant_dynamic-update-slice_fusion.6.refs_2_.refs_4_), channel_id=1, source_target_pairs={{0,2},{1,3},{2,0},{3,1},{4,6},{5,7},{6,4},{7,5},{8,10},{9,11},{10,... | collective-permute-start | bytes 6291464 | tf_op jit(solution)/shard_map/ppermute | solution.py:441
  340.8 46.2 %collective-permute-start.30 = (bf16[512,2048]{1,0:T(8,128)(2,1)}, bf16[512,2048]{1,0:T(8,128)(2,1)}, u32[]{:S(2)}, u32[]{:S(2)}) collective-permute-start(bf16[512,2048]{1,0:T(8,128)(2,1)} %pad_maximum_fusion.1.refs_0_.refs_4_), channel_id=1, source_target_pairs={{0,4},{1,5},{2,3},{3,2},{4,0},{5,1},{6,7},{7,6},{8,12},{9,13},{10,... | collective-permute-start | bytes 6291464 | tf_op jit(solution)/shard_map/ppermute | solution.py:445
  341.8 45.2 %collective-permute-start.32 = (bf16[512,2048]{1,0:T(8,128)(2,1)S(1)}, bf16[512,2048]{1,0:T(8,128)(2,1)S(1)}, u32[]{:S(2)}, u32[]{:S(2)}) collective-permute-start(bf16[512,2048]{1,0:T(8,128)(2,1)S(1)} %copy-done.70), channel_id=1, source_target_pairs={{0,2},{1,3},{2,0},{3,1},{4,6},{5,7},{6,4},{7,5},{8,10},{9,11},{10,... | collective-permute-start | bytes 6291464 | tf_op jit(solution)/shard_map/ppermute | solution.py:441
  342.2 45.3 %collective-permute-start.33 = (bf16[512,2048]{1,0:T(8,128)(2,1)S(1)}, bf16[512,2048]{1,0:T(8,128)(2,1)}, u32[]{:S(2)}, u32[]{:S(2)}) collective-permute-start(bf16[512,2048]{1,0:T(8,128)(2,1)S(1)} %copy-done.69), channel_id=1, source_target_pairs={{0,2},{1,3},{2,0},{3,1},{4,6},{5,7},{6,4},{7,5},{8,10},{9,11},{10,... | collective-permute-start | bytes 6291464 | tf_op jit(solution)/shard_map/ppermute | solution.py:441
  432.3 41.6 %collective-permute-start.42 = (bf16[512,2048]{1,0:T(8,128)(2,1)}, bf16[512,2048]{1,0:T(8,128)(2,1)}, u32[]{:S(2)}, u32[]{:S(2)}) collective-permute-start(bf16[512,2048]{1,0:T(8,128)(2,1)} %get-tuple-element.340), channel_id=1, source_target_pairs={{0,2},{1,3},{2,0},{3,1},{4,6},{5,7},{6,4},{7,5},{8,10},{9,11},{10,... | collective-permute-start | bytes 6291464 | tf_op jit(solution)/shard_map/ppermute | solution.py:441
  432.5 41.4 %collective-permute-start.43 = (bf16[512,2048]{1,0:T(8,128)(2,1)}, bf16[512,2048]{1,0:T(8,128)(2,1)}, u32[]{:S(2)}, u32[]{:S(2)}) collective-permute-start(bf16[512,2048]{1,0:T(8,128)(2,1)} %get-tuple-element.341), channel_id=1, source_target_pairs={{0,2},{1,3},{2,0},{3,1},{4,6},{5,7},{6,4},{7,5},{8,10},{9,11},{10,... | collective-permute-start | bytes 6291464 | tf_op jit(solution)/shard_map/ppermute | solution.py:441
  432.9 46.5 %collective-permute-start.40 = (bf16[512,2048]{1,0:T(8,128)(2,1)}, bf16[512,2048]{1,0:T(8,128)(2,1)}, u32[]{:S(2)}, u32[]{:S(2)}) collective-permute-start(bf16[512,2048]{1,0:T(8,128)(2,1)} %add_pieces.11), channel_id=1, source_target_pairs={{0,4},{1,5},{2,3},{3,2},{4,0},{5,1},{6,7},{7,6},{8,12},{9,13},{10,... | collective-permute-start | bytes 6291464 | tf_op jit(solution)/shard_map/ppermute | solution.py:445
  472.9 42.6 %collective-permute-start.45 = (bf16[256,2048]{1,0:T(8,128)(2,1)}, bf16[256,2048]{1,0:T(8,128)(2,1)}, u32[]{:S(2)}, u32[]{:S(2)}) collective-permute-start(bf16[256,2048]{1,0:T(8,128)(2,1)} %get-tuple-element.514), channel_id=1, source_target_pairs={{0,1},{1,0},{2,6},{3,7},{4,5},{5,4},{6,2},{7,3},{8,9},{9,8},{10,14... | collective-permute-start | bytes 3145736 | tf_op jit(solution)/shard_map/ppermute | solution.py:445
  478.4 41.5 %collective-permute-start.46 = (bf16[512,2048]{1,0:T(8,128)(2,1)}, bf16[512,2048]{1,0:T(8,128)(2,1)}, u32[]{:S(2)}, u32[]{:S(2)}) collective-permute-start(bf16[512,2048]{1,0:T(8,128)(2,1)} %add_pieces.12), channel_id=1, source_target_pairs={{0,4},{1,5},{2,3},{3,2},{4,0},{5,1},{6,7},{7,6},{8,12},{9,13},{10,... | collective-permute-start | bytes 6291464 | tf_op jit(solution)/shard_map/ppermute | solution.py:445
  519.9 52.7 %collective-permute-start.49 = (bf16[512,2048]{1,0:T(8,128)(2,1)}, bf16[512,2048]{1,0:T(8,128)(2,1)}, u32[]{:S(2)}, u32[]{:S(2)}) collective-permute-start(bf16[512,2048]{1,0:T(8,128)(2,1)} %pad_maximum_fusion.2.refs_0_), channel_id=1, source_target_pairs={{0,2},{1,3},{2,0},{3,1},{4,6},{5,7},{6,4},{7,5},{8,10},{9,11},{10,... | collective-permute-start | bytes 6291464 | tf_op jit(solution)/shard_map/ppermute | solution.py:441
  524.1 41.4 %collective-permute-start.52 = (bf16[512,2048]{1,0:T(8,128)(2,1)}, bf16[512,2048]{1,0:T(8,128)(2,1)}, u32[]{:S(2)}, u32[]{:S(2)}) collective-permute-start(bf16[512,2048]{1,0:T(8,128)(2,1)} %get-tuple-element.377), channel_id=1, source_target_pairs={{0,2},{1,3},{2,0},{3,1},{4,6},{5,7},{6,4},{7,5},{8,10},{9,11},{10,... | collective-permute-start | bytes 6291464 | tf_op jit(solution)/shard_map/ppermute | solution.py:441
  524.2 42.7 %collective-permute-start.53 = (bf16[512,2048]{1,0:T(8,128)(2,1)}, bf16[512,2048]{1,0:T(8,128)(2,1)}, u32[]{:S(2)}, u32[]{:S(2)}) collective-permute-start(bf16[512,2048]{1,0:T(8,128)(2,1)} %get-tuple-element.378), channel_id=1, source_target_pairs={{0,2},{1,3},{2,0},{3,1},{4,6},{5,7},{6,4},{7,5},{8,10},{9,11},{10,... | collective-permute-start | bytes 6291464 | tf_op jit(solution)/shard_map/ppermute | solution.py:441
  556.5 186.2 %reduce-scatter.7.cloned.1.call-start = ((), (), s32[]{:S(2)}) async-start(), calls=%async_computation.8 | async-start | bytes 3932160 | tf_op jit(solution)/shard_map/reduce_scatter | solution.py:1371
  556.7 67.1 %collective-permute-start.47 = (bf16[256,2048]{1,0:T(8,128)(2,1)}, bf16[256,2048]{1,0:T(8,128)(2,1)}, u32[]{:S(2)}, u32[]{:S(2)}) collective-permute-start(bf16[256,2048]{1,0:T(8,128)(2,1)} %add_convert_fusion.6), channel_id=1, source_target_pairs={{0,1},{1,0},{2,6},{3,7},{4,5},{5,4},{6,2},{7,3},{8,9},{9,8},{10,14... | collective-permute-start | bytes 3145736 | tf_op jit(solution)/shard_map/ppermute | solution.py:445
  565.5 58.3 %collective-permute-start.55 = (bf16[256,2048]{1,0:T(8,128)(2,1)}, bf16[256,2048]{1,0:T(8,128)(2,1)S(1)}, u32[]{:S(2)}, u32[]{:S(2)}) collective-permute-start(bf16[256,2048]{1,0:T(8,128)(2,1)} %get-tuple-element.512), channel_id=1, source_target_pairs={{0,1},{1,0},{2,6},{3,7},{4,5},{5,4},{6,2},{7,3},{8,9},{9,8},{10,14... | collective-permute-start | bytes 3145736 | tf_op jit(solution)/shard_map/ppermute | solution.py:445
  571.2 59.5 %collective-permute-start.54 = (bf16[512,2048]{1,0:T(8,128)(2,1)}, bf16[512,2048]{1,0:T(8,128)(2,1)}, u32[]{:S(2)}, u32[]{:S(2)}) collective-permute-start(bf16[512,2048]{1,0:T(8,128)(2,1)} %add_pieces.13), channel_id=1, source_target_pairs={{0,4},{1,5},{2,3},{3,2},{4,0},{5,1},{6,7},{7,6},{8,12},{9,13},{10,... | collective-permute-start | bytes 6291464 | tf_op jit(solution)/shard_map/ppermute | solution.py:445
  635.2 167.3 %reduce-scatter.11.cloned.1.call-start = ((), (), s32[]{:S(2)}) async-start(), calls=%async_computation.10 | async-start | bytes 1310720 | tf_op jit(solution)/shard_map/reduce_scatter | solution.py:1371
  678.0 58.5 %collective-permute-start.62 = (bf16[512,2048]{1,0:T(8,128)(2,1)}, bf16[512,2048]{1,0:T(8,128)(2,1)}, u32[]{:S(2)}, u32[]{:S(2)}) collective-permute-start(bf16[512,2048]{1,0:T(8,128)(2,1)} %add_pieces.14), channel_id=1, source_target_pairs={{0,4},{1,5},{2,3},{3,2},{4,0},{5,1},{6,7},{7,6},{8,12},{9,13},{10,... | collective-permute-start | bytes 6291464 | tf_op jit(solution)/shard_map/ppermute | solution.py:445
  679.0 78.1 %collective-permute-start.61 = (bf16[256,2048]{1,0:T(8,128)(2,1)}, bf16[256,2048]{1,0:T(8,128)(2,1)}, u32[]{:S(2)}, u32[]{:S(2)}) collective-permute-start(bf16[256,2048]{1,0:T(8,128)(2,1)} %add_convert_fusion.3), channel_id=1, source_target_pairs={{0,1},{1,0},{2,6},{3,7},{4,5},{5,4},{6,2},{7,3},{8,9},{9,8},{10,14... | collective-permute-start | bytes 3145736 | tf_op jit(solution)/shard_map/ppermute | solution.py:445
  679.7 146.0 %reduce-scatter.9.cloned.1.call-start = ((), (), s32[]{:S(2)}) async-start(), calls=%async_computation.9 | async-start | bytes 2703360 | tf_op jit(solution)/shard_map/reduce_scatter | solution.py:1371
  682.3 59.0 %collective-permute-start.63 = (bf16[1536,128]{1,0:T(8,128)(2,1)}, bf16[1536,128]{1,0:T(8,128)(2,1)S(1)}, u32[]{:S(2)}, u32[]{:S(2)}) collective-permute-start(bf16[1536,128]{1,0:T(8,128)(2,1)} %get-tuple-element.538), channel_id=1, source_target_pairs={{0,2},{1,3},{2,0},{3,1},{4,6},{5,7},{6,4},{7,5},{8,10},{9,11},{10,... | collective-permute-start | bytes 1179656 | tf_op jit(solution)/shard_map/ppermute | solution.py:441
  682.3 59.0 %collective-permute-start.64 = (bf16[1536,128]{1,0:T(8,128)(2,1)}, bf16[1536,128]{1,0:T(8,128)(2,1)S(1)}, u32[]{:S(2)}, u32[]{:S(2)}) collective-permute-start(bf16[1536,128]{1,0:T(8,128)(2,1)} %get-tuple-element.537), channel_id=1, source_target_pairs={{0,4},{1,5},{2,6},{3,7},{4,0},{5,1},{6,2},{7,3},{8,12},{9,13},{10,... | collective-permute-start | bytes 1179656 | tf_op jit(solution)/shard_map/ppermute | solution.py:441
  683.5 57.9 %collective-permute-start.65 = (bf16[1536,128]{1,0:T(8,128)(2,1)}, bf16[1536,128]{1,0:T(8,128)(2,1)}, u32[]{:S(2)}, u32[]{:S(2)}) collective-permute-start(bf16[1536,128]{1,0:T(8,128)(2,1)} %get-tuple-element.536), channel_id=1, source_target_pairs={{0,6},{1,7},{2,4},{3,5},{4,2},{5,3},{6,0},{7,1},{8,14},{9,15},{10,... | collective-permute-start | bytes 1179656 | tf_op jit(solution)/shard_map/ppermute | solution.py:441
  (129 other events, 1832.0 us)
Sparse Core Ops, SparseCore 0:
  30.6 72.4 all-gather.3
  104.7 62.8 all-gather.5
  169.7 113.9 all-gather.7
  556.6 111.7 reduce-scatter.4
  670.5 60.7 reduce-scatter.6
  733.5 27.1 reduce-scatter.10
  773.3 46.5 reduce-scatter.8

commit v6 on v5

--- a/solution.py
+++ b/solution.py
@@ -523,7 +523,8 @@
         self.came = swap_mixed(self.order.pin(self.far), BIT_Y, BIT_X)
 
     def take(self):
-        terms = (*self.near, self.order.pin(self.came))
+        self.second_came = self.order.pin(self.came)
+        terms = (*self.near, self.second_came)
         half = terms[0].shape[0] // 2
         low, high = [sum(t[part].astype(F32) for t in terms) for part in (slice(0, half), slice(half, None))]
         self.kept = low
@@ -535,6 +536,9 @@
 
     def result(self):
         return self.kept + self.order.pin(self.came).astype(F32)
+
+    def terms(self):
+        return (*self.near, self.second_came, self.order.pin(self.came))
 
 
 def norm_rope(raw, gain, cosine, sine):
@@ -1196,6 +1200,58 @@
     )(index, *inners, *downs)
 
 
+def row_sum(refs):
+    return sum(ref[...].astype(F32) for ref in refs)
+
+
+def middle_kernel(rows, t0, t1, t2, t3, gain, hidden, normed_rows):
+    total = rows[...].astype(F32) + row_sum((t0, t1, t2, t3))
+    hidden[...] = total
+    normed_rows[...] = (total * rms_scale(total) * gain[...]).astype(BF16)
+
+
+def turn_kernel(hidden, cot, t0, t1, t2, t3, gain, grad, grad_rows, gain_sum):
+    values = hidden[...]
+    scale = rms_scale(values)
+    normed = values * scale
+    d_rows = row_sum((t0, t1, t2, t3))
+    total = cot[...].astype(F32) + norm_back(d_rows, normed, scale, gain[...])
+    grad[...] = total
+    grad_rows[...] = total.astype(BF16)
+
+    @pl.when(pl.program_id(0) == 0)
+    def _():
+        gain_sum[...] = jnp.zeros_like(gain_sum)
+
+    gain_sum[0:1, :] += jnp.sum(d_rows * normed, axis=0, keepdims=True)
+
+
+def finish_kernel(rows, grad, t0, t1, t2, t3, gain, out):
+    values = rows[...].astype(F32)
+    scale = rms_scale(values)
+    back = norm_back(row_sum((t0, t1, t2, t3)), values * scale, scale, gain[...])
+    out[...] = (grad[...] + back).astype(BF16)
+
+
+def on_rows(kernel, rows, gain, out_types, with_sum, name):
+    count, width = rows[0].shape
+    block = pl.BlockSpec((count // 4, width), lambda i: (i, 0))
+    fixed = lambda size: pl.BlockSpec((size, width), lambda i: (0, 0))
+    extra = int(with_sum)
+    return pl.pallas_call(
+        kernel,
+        grid=(4,),
+        in_specs=[block] * len(rows) + [fixed(1)],
+        out_specs=[block] * len(out_types) + [fixed(8)] * extra,
+        out_shape=[jax.ShapeDtypeStruct((count, width), t) for t in out_types]
+        + [jax.ShapeDtypeStruct((8, width), F32)] * extra,
+        cost_estimate=pl.CostEstimate(
+            flops=20 * count * width, bytes_accessed=18 * count * width, transcendentals=0
+        ),
+        name=name,
+    )(*rows, gain[None, :])
+
+
 def pick(flag, first, second):
     return jnp.where(flag, first, second)
 
@@ -1305,10 +1361,9 @@
     hidden1, scale2, normed2 = ([None] * micro_batches for _ in range(3))
 
     def middle(n):
-        hidden1[n] = x_float[n] + out_sum[n].result()
-        scale2[n] = rms_scale(hidden1[n])
-        normed2[n] = hidden1[n] * scale2[n]
-        rows = (normed2[n] * ffn_norm_gain).astype(BF16)
+        hidden1[n], rows = on_rows(
+            middle_kernel, (inputs[n], *out_sum[n].terms()), ffn_norm_gain, (F32, BF16), False, "middle"
+        )
         xn2[n] = Gather(order, rows)
         return rows
 
@@ -1338,10 +1393,15 @@
     gain_ffn = []
 
     def turn(n):
-        d_xn2 = back[n].result()
-        gain_ffn.append(jnp.sum(d_xn2 * normed2[n], axis=0))
-        d_hidden1[n] = cot_live[n] + norm_back(d_xn2, normed2[n], scale2[n], ffn_norm_gain)
-        rows = d_hidden1[n].astype(BF16)
+        d_hidden1[n], rows, part = on_rows(
+            turn_kernel,
+            (hidden1[n], cot_own[n], *back[n].terms()),
+            ffn_norm_gain,
+            (F32, BF16),
+            True,
+            "turn",
+        )
+        gain_ffn.append(part[0])
         d_attn[n] = Gather(order, rows)
         return rows
 
@@ -1417,8 +1477,14 @@
         return out
 
     def finish(n):
-        d_xn1 = rows_sum[n].result()
-        return (d_hidden1[n] + norm_back(d_xn1, normed1[n], scale1[n], attn_norm_gain)).astype(BF16)
+        return on_rows(
+            finish_kernel,
+            (inputs[n], d_hidden1[n], *rows_sum[n].terms()),
+            attn_norm_gain,
+            (BF16,),
+            False,
+            "finish",
+        )[0]
 
     outputs, input_grads = ([None] * micro_batches for _ in range(2))
     back_0 = attend_back(0)

time: 862 us -> 895 us (1.038)
  other arithmetic: 104 us -> 60.3 us
  Pallas kernels: 428 us -> 462 us
  waiting for transfers between devices: 185 us -> 214 us
  local copies, waits for them, and re-layouts: 42.2 us -> 60.5 us
    pallas_call x0 -> x6, Pallas kernels: none -> 33.1 us  [on_rows(): pl.pallas_call(kernel, grid=(4,), in_specs=[block] * len(rows) + [fixed(1...]
    convert_element_type x6 -> x0, other arithmetic: 17.8 us -> none  [the longest x2 8.4 us: turn(): rows = d_hidden1[n].astype(BF16)]
    reduce_sum x4 -> x0, other arithmetic: 12.1 us -> none  [the longest x2 7.08 us: turn(): gain_ffn.append(jnp.sum(d_xn2 * normed2[n], axis=0))]
    ppermute x47, waiting for transfers between devices: 39.4 us -> 50.9 us  [swap(): return lax.ppermute(values, PLANE, [(i, i ^ bits) for i in range(8)])]
    ppermute x32, waiting for transfers between devices: 144 us -> 155 us  [swap_mixed(): lax.ppermute(values, PLANE, [(i, i ^ (core1 if i & BIT_C else core0)) for...]
    unnamed x152 -> x112, local copies, waits for them, and re-layouts: 22.1 us -> 32.1 us
    concatenate x4 -> x0, other arithmetic: 9.63 us -> none  [second(): near = jnp.concatenate([self.rows, came], axis=0)]
  transfers between devices with their start and end apart: 88 -> 88, of which waited for: 22 -> 28; matrix products, arithmetic and copies ran while one was open for 15% -> 11% of each run, Pallas kernels for 49% -> 51%
where the time goes in v6:
time: 895 us; the launch traced here: 887 us
  Pallas kernels  462 us (52%)
  waiting for transfers between devices  214 us (24%)
  starting transfers between devices  64.8 us (7%)
  local copies, waits for them, and re-layouts  60.5 us (7%)
  other arithmetic  60.3 us (7%)
  between operations  25.5 us (3%)
    ppermute x32, waiting for transfers between devices, swap_mixed(): lax.ppermute(values, PLANE, [(i, i ^ (core1 if i & BIT_C else core0)) for...  155 us
    pallas_call x4, Pallas kernels, feed_forward_call(): pl.pallas_call(feed_forward_kernel, grid=(4,), in_specs=[near, far, near,...  121 us
    pallas_call x2, Pallas kernels, attend_backward_call(): pl.pallas_call(attend_backward_kernel, grid_spec=pltpu.PrefetchScalarGrid...  104 us
    pallas_call x5, Pallas kernels, weight_grad_call(): pl.pallas_call(kernel, in_specs=in_specs, out_specs=[vmem] * len(out_shap...  87.9 us
    pallas_call x2, Pallas kernels, attend_forward_call(): pl.pallas_call(attend_forward_kernel, grid_spec=pltpu.PrefetchScalarGridS...  66.2 us
    ppermute x47, waiting for transfers between devices, swap(): return lax.ppermute(values, PLANE, [(i, i ^ bits) for i in range(8)])  50.9 us
    ppermute x32, starting transfers between devices, swap_mixed(): lax.ppermute(values, PLANE, [(i, i ^ (core1 if i & BIT_C else core0)) for...  38.1 us
    pallas_call x8, Pallas kernels, add_pieces(): pl.pallas_call(add_pieces_kernel, grid=(4,), in_specs=[block] * 2, out_sp...  36.8 us
  transfers between devices with their start and end apart: 88, of which 28 were waited for; matrix products, arithmetic and copies ran while one was open for 11% of the time, Pallas kernels for 51%

profile of v6, /device:TPU:0, one launch (start us, length us, event | category | flops | bytes accessed | tf_op | source)
XLA Modules:
  0.0 886.5 jit_solution(4382070293387201345)
XLA Ops:
  17.1 8.6 collective-permute-done
  31.7 9.6 %collective-permute-done.1 = bf16[256,2048]{1,0:T(8,128)(2,1)S(1)} collective-permute-done((bf16[256,2048]{1,0:T(8,128)(2,1)S(1)}, bf16[256,2048]{1,0:T(8,128)(2,1)S(1)}, u32[]{:S(2)}, u32[]{:S(2)}) %collective-permute-start.1) | collective-permute-done | bytes 1048608 | tf_op jit(solution)/shard_map/ppermute | solution.py:445
  57.3 11.4 %collective-permute-done.2.refs_1_ = bf16[512,2048]{1,0:T(8,128)(2,1)} collective-permute-done((bf16[512,2048]{1,0:T(8,128)(2,1)}, bf16[512,2048]{1,0:T(8,128)(2,1)}, u32[]{:S(2)}, u32[]{:S(2)}) %collective-permute-start.2) | collective-permute-done | bytes 2097184 | tf_op jit(solution)/shard_map/ppermute | solution.py:445
  88.3 10.2 %collective-permute-done.13 = bf16[128,2304]{1,0:T(8,128)(2,1)} collective-permute-done((bf16[128,2304]{1,0:T(8,128)(2,1)}, bf16[128,2304]{1,0:T(8,128)(2,1)}, u32[]{:S(2)}, u32[]{:S(2)}) %collective-permute-start.13) | collective-permute-done | bytes 589856 | tf_op jit(solution)/shard_map/ppermute | solution.py:441
  110.2 33.9 %attend_forward.2 = (f32[2048,640]{1,0:T(8,128)}, f32[2048,256]{1,0:T(8,128)}, f32[2048,128]{1,0:T(8,128)}, bf16[2048,256]{1,0:T(8,128)(2,1)}, bf16[512,2048]{1,...) custom-call(s32[49]{0:T(128)} %concatenate.48.table, ...), custom_call_target="tpu_custom_call" | custom-call | flops 49660559360 | bytes 128942080 | tf_op jit(solution)/shard_map/attend_forward/pallas_call | solution.py:776
  162.7 6.1 all-gather.6.cloned.1.call-done.refs_4_
  168.8 32.3 %attend_forward.3 = (f32[2048,640]{1,0:T(8,128)}, f32[2048,256]{1,0:T(8,128)}, f32[2048,128]{1,0:T(8,128)}, bf16[2048,256]{1,0:T(8,128)(2,1)}, bf16[512,2048]{1,...) custom-call(s32[49]{0:T(128)} %concatenate.55.table, ...), custom_call_target="tpu_custom_call" | custom-call | flops 49660559360 | bytes 128942080 | tf_op jit(solution)/shard_map/attend_forward/pallas_call | solution.py:776
  207.3 11.3 %collective-permute-done.16.t3 = bf16[256,2048]{1,0:T(8,128)(2,1)S(1)} collective-permute-done((bf16[256,2048]{1,0:T(8,128)(2,1)S(1)}, bf16[256,2048]{1,0:T(8,128)(2,1)S(1)}, u32[]{:S(2)}, u32[]{:S(2)}) %collective-permute-start.16) | collective-permute-done | bytes 1048608 | tf_op jit(solution)/shard_map/ppermute | solution.py:445
  228.4 11.2 %collective-permute-done.17 = bf16[256,2048]{1,0:T(8,128)(2,1)S(1)} collective-permute-done((bf16[256,2048]{1,0:T(8,128)(2,1)}, bf16[256,2048]{1,0:T(8,128)(2,1)S(1)}, u32[]{:S(2)}, u32[]{:S(2)}) %collective-permute-start.17) | collective-permute-done | bytes 1048608 | tf_op jit(solution)/shard_map/ppermute | solution.py:445
  247.5 19.5 %collective-permute-done.18.refs_1_ = bf16[512,2048]{1,0:T(8,128)(2,1)} collective-permute-done((bf16[512,2048]{1,0:T(8,128)(2,1)}, bf16[512,2048]{1,0:T(8,128)(2,1)}, u32[]{:S(2)}, u32[]{:S(2)}) %collective-permute-start.18) | collective-permute-done | bytes 2097184 | tf_op jit(solution)/shard_map/ppermute | solution.py:445
  267.0 22.4 %collective-permute-done.26.t2 = bf16[512,2048]{1,0:T(8,128)(2,1)S(1)} collective-permute-done((bf16[512,2048]{1,0:T(8,128)(2,1)}, bf16[512,2048]{1,0:T(8,128)(2,1)S(1)}, u32[]{:S(2)}, u32[]{:S(2)}) %collective-permute-start.26) | collective-permute-done | bytes 2097184 | tf_op jit(solution)/shard_map/ppermute | solution.py:445
  294.8 12.2 %collective-permute-done.27.t3 = bf16[256,2048]{1,0:T(8,128)(2,1)S(1)} collective-permute-done((bf16[256,2048]{1,0:T(8,128)(2,1)S(1)}, bf16[256,2048]{1,0:T(8,128)(2,1)S(1)}, u32[]{:S(2)}, u32[]{:S(2)}) %collective-permute-start.27) | collective-permute-done | bytes 1048608 | tf_op jit(solution)/shard_map/ppermute | solution.py:445
  317.0 30.6 %feed_forward.4 = (bf16[1024,768]{1,0:T(8,128)(2,1)S(1)}, bf16[1024,1536]{1,0:T(8,128)(2,1)}, bf16[512,2048]{1,0:T(8,128)(2,1)}, bf16[512,2048]{1,0:T(8,128)(2,1...) custom-call(bf16[512,2048]{1,0:T(8,128)(2,1)} %collective-permute-done.20.refs_0_.refs_2_, ...), custom_call_target="tpu_custom_call" | custom-call | flops 96636764160 | bytes 131072000 | tf_op jit(solution)/shard_map/feed_forward/pallas_call | solution.py:926
  356.1 30.0 %feed_forward.5 = (bf16[1024,768]{1,0:T(8,128)(2,1)S(1)}, bf16[1024,1536]{1,0:T(8,128)(2,1)}, bf16[512,2048]{1,0:T(8,128)(2,1)}, bf16[512,2048]{1,0:T(8,128)(2,1...) custom-call(bf16[512,2048]{1,0:T(8,128)(2,1)} %constant_dynamic-update-slice_fusion.6.refs_0_, ...), custom_call_target="tpu_custom_call" | custom-call | flops 96636764160 | bytes 131072000 | tf_op jit(solution)/shard_map/feed_forward/pallas_call | solution.py:926
  387.7 11.7 %collective-permute-done.30.refs_1_.refs_5_ = bf16[512,2048]{1,0:T(8,128)(2,1)} collective-permute-done((bf16[512,2048]{1,0:T(8,128)(2,1)}, bf16[512,2048]{1,0:T(8,128)(2,1)}, u32[]{:S(2)}, u32[]{:S(2)}) %collective-permute-start.30) | collective-permute-done | bytes 2097184 | tf_op jit(solution)/shard_map/ppermute | solution.py:445
  406.9 30.2 %feed_forward.6 = (bf16[1024,768]{1,0:T(8,128)(2,1)S(1)}, bf16[1024,1536]{1,0:T(8,128)(2,1)}, bf16[512,2048]{1,0:T(8,128)(2,1)}, bf16[512,2048]{1,0:T(8,128)(2,1...) custom-call(bf16[512,2048]{1,0:T(8,128)(2,1)} %collective-permute-done.36.refs_0_.refs_6_, ...), custom_call_target="tpu_custom_call" | custom-call | flops 96636764160 | bytes 131072000 | tf_op jit(solution)/shard_map/feed_forward/pallas_call | solution.py:926
  447.7 30.0 %feed_forward.7 = (bf16[1024,768]{1,0:T(8,128)(2,1)S(1)}, bf16[1024,1536]{1,0:T(8,128)(2,1)}, bf16[512,2048]{1,0:T(8,128)(2,1)}, bf16[512,2048]{1,0:T(8,128)(2,1...) custom-call(bf16[512,2048]{1,0:T(8,128)(2,1)} %constant_dynamic-update-slice_fusion.8.refs_0_.refs_4_, ...), custom_call_target="tpu_custom_call" | custom-call | flops 96636764160 | bytes 131072000 | tf_op jit(solution)/shard_map/feed_forward/pallas_call | solution.py:926
  479.9 6.0 turn.2
  498.5 33.1 %weight_grad.5 = bf16[6144,512]{1,0:T(8,128)(2,1)} custom-call(bf16[512,2048]{1,0:T(8,128)(2,1)} %constant_dynamic-update-slice_fusion.6.refs_0_, bf16[512,2048]{1,0:T(8,128)(2,1)} %collective-permute-done.18.refs_1_, bf16[512,2048]{1,0:T(8,128)(2,1)} %collective-permute-done.20.refs_0_.refs_2_, bf16[512,2048]{1,0:T(8,128)(2,1)} %collective-permute-done.21.refs_1_.refs_3_, ...), custom_call_target="tpu_custom_call" | custom-call | flops 257698037760 | bytes 356515840 | tf_op jit(solution)/shard_map/weight_grad/pallas_call | solution.py:1053
  538.4 18.5 %weight_grad.6 = bf16[3072,512]{1,0:T(8,128)(2,1)} custom-call(bf16[512,2048]{1,0:T(8,128)(2,1)} %constant_dynamic-update-slice_fusion.4.refs_2_.refs_0_, bf16[512,2048]{1,0:T(8,128)(2,1)} %collective-permute-done.19.refs_3_.refs_1_, bf16[512,2048]{1,0:T(8,128)(2,1)} %collective-permute-done.22.refs_2_, bf16[512,2048]{1,0:T(8,128)(2,1)} %collective-permute-done.23.refs_3_, ...), custom_call_target="tpu_custom_call" | custom-call | flops 128849018880 | bytes 262144000 | tf_op jit(solution)/shard_map/weight_grad/pallas_call | solution.py:1053
  561.5 13.9 %collective-permute-done.51.t3 = bf16[256,2048]{1,0:T(8,128)(2,1)} collective-permute-done((bf16[256,2048]{1,0:T(8,128)(2,1)S(1)}, bf16[256,2048]{1,0:T(8,128)(2,1)}, u32[]{:S(2)}, u32[]{:S(2)}) %collective-permute-start.51) | collective-permute-done | bytes 1048608 | tf_op jit(solution)/shard_map/ppermute | solution.py:445
  576.3 6.4 turn.3
  593.5 52.5 %attend_backward.2 = (bf16[2048,640]{1,0:T(8,128)(2,1)}, f32[8,128]{1,0:T(8,128)}, f32[8,128]{1,0:T(8,128)}, bf16[512,2048]{1,0:T(8,128)(2,1)}, bf16[512,2048]{1...) custom-call(s32[49]{0:T(128)} %concatenate.48.table, ...), custom_call_target="tpu_custom_call" | custom-call | flops 135559905280 | bytes 257884160 | tf_op jit(solution)/shard_map/attend_backward/pallas_call | solution.py:826
  656.8 5.9 collective-permute-done.57.t1
  667.9 10.5 %weight_grad.7.refs_6_ = f32[640,2048]{1,0:T(8,128)} custom-call(bf16[512,2048]{1,0:T(8,128)(2,1)} %constant_dynamic-update-slice_fusion.refs_0_, bf16[512,2048]{1,0:T(8,128)(2,1)} %collective-permute-done.2.refs_1_, bf16[512,2048]{1,0:T(8,128)(2,1)} %collective-permute-done.3.refs_2_, bf16[512,2048]{1,0:T(8,128)(2,1)} %collective-permute-done.4.refs_3_, ...), custom_call_target="tpu_custom_call" | custom-call | flops 53687091200 | bytes 136314880 | tf_op jit(solution)/shard_map/weight_grad/pallas_call | solution.py:1053
  687.9 11.8 %weight_grad.8 = bf16[1024,512]{1,0:T(8,128)(2,1)} custom-call(bf16[512,2048]{1,0:T(8,128)(2,1)} %constant_dynamic-update-slice_fusion.12.refs_0_, bf16[512,2048]{1,0:T(8,128)(2,1)} %collective-permute-done.48.refs_1_, bf16[512,2048]{1,0:T(8,128)(2,1)} %collective-permute-done.49.refs_2_, bf16[512,2048]{1,0:T(8,128)(2,1)} %collective-permute-done.50.refs_3_, ...), custom_call_target="tpu_custom_call" | custom-call | flops 42949672960 | bytes 199229440 | tf_op jit(solution)/shard_map/weight_grad/pallas_call | solution.py:1053
  701.6 51.5 %attend_backward.3 = (bf16[2048,640]{1,0:T(8,128)(2,1)}, f32[8,128]{1,0:T(8,128)}, f32[8,128]{1,0:T(8,128)}, bf16[512,2048]{1,0:T(8,128)(2,1)}, bf16[512,2048]{1...) custom-call(s32[49]{0:T(128)} %concatenate.55.table, ...), custom_call_target="tpu_custom_call" | custom-call | flops 135559905280 | bytes 257884160 | tf_op jit(solution)/shard_map/attend_backward/pallas_call | solution.py:826
  760.3 6.0 collective-permute-done.64.refs_2_
  766.4 7.9 collective-permute-done.65.refs_3_
  775.0 14.0 %weight_grad.9 = (bf16[2112,512]{1,0:T(8,128)(2,1)}, f32[8,2048]{1,0:T(8,128)}) custom-call(bf16[512,2048]{1,0:T(8,128)(2,1)} %constant_dynamic-update-slice_fusion.2.refs_0_, bf16[512,2048]{1,0:T(8,128)(2,1)} %collective-permute-done.6.refs_1_, bf16[512,2048]{1,0:T(8,128)(2,1)} %collective-permute-done.11.refs_2_, ...), custom_call_target="tpu_custom_call" | custom-call | flops 44291850240 | bytes 127139840 | tf_op jit(solution)/shard_map/weight_grad/pallas_call | solution.py:1053
  810.5 21.4 %collective-permute-done.69.t2 = bf16[512,2048]{1,0:T(8,128)(2,1)S(1)} collective-permute-done((bf16[512,2048]{1,0:T(8,128)(2,1)}, bf16[512,2048]{1,0:T(8,128)(2,1)S(1)}, u32[]{:S(2)}, u32[]{:S(2)}) %collective-permute-start.69) | collective-permute-done | bytes 2097184 | tf_op jit(solution)/shard_map/ppermute | solution.py:445
  852.8 5.4 finish.3
  (358 shorter events, 275.1 us)
Async XLA Ops:
  7.2 103.0 %all-gather.4.cloned.1.call-start = ((), (), s32[]{:S(2)}) async-start(), calls=%async_computation.4 | async-start | bytes 4587520 | tf_op jit(solution)/shard_map/all_gather | solution.py:1323
  30.5 138.3 %all-gather.6.cloned.1.call-start = ((), (), s32[]{:S(2)}) async-start(), calls=%async_computation.5 | async-start | bytes 3932160 | tf_op jit(solution)/shard_map/all_gather | solution.py:1332
  103.2 213.7 %all-gather.8.cloned.1.call-start = ((), (), s32[]{:S(2)}) async-start(), calls=%async_computation.6 | async-start | bytes 7864320 | tf_op jit(solution)/shard_map/all_gather | solution.py:1332
  105.8 40.6 %collective-permute-start.6 = (bf16[512,2048]{1,0:T(8,128)(2,1)}, bf16[512,2048]{1,0:T(8,128)(2,1)}, u32[]{:S(2)}, u32[]{:S(2)}) collective-permute-start(bf16[512,2048]{1,0:T(8,128)(2,1)} %constant_dynamic-update-slice_fusion.2.refs_0_), channel_id=1, source_target_pairs={{0,4},{1,5},{2,3},{3,2},{4,0},{5,1},{6,7},{7,6},{8,12},{9,13},{10,... | collective-permute-start | bytes 6291464 | tf_op jit(solution)/shard_map/ppermute | solution.py:445
  151.4 550.2 %reduce-scatter.5.cloned.1.call-start = ((), (), s32[]{:S(2)}) async-start(), calls=%async_computation.7 | async-start | bytes 7864320 | tf_op jit(solution)/shard_map/reduce_scatter | solution.py:1431
  151.4 53.9 %collective-permute-start.19 = (bf16[512,2048]{1,0:T(8,128)(2,1)}, bf16[512,2048]{1,0:T(8,128)(2,1)}, u32[]{:S(2)}, u32[]{:S(2)}) collective-permute-start(bf16[512,2048]{1,0:T(8,128)(2,1)} %constant_dynamic-update-slice_fusion.4.refs_2_.refs_0_), channel_id=1, source_target_pairs={{0,4},{1,5},{2,3},{3,2},{4,0},{5,1},{6,7},{7,6},{8,12},{9,13},{10,... | collective-permute-start | bytes 6291464 | tf_op jit(solution)/shard_map/ppermute | solution.py:445
  161.0 40.1 %collective-permute-start.10 = (bf16[512,2048]{1,0:T(8,128)(2,1)}, bf16[512,2048]{1,0:T(8,128)(2,1)}, u32[]{:S(2)}, u32[]{:S(2)}) collective-permute-start(bf16[512,2048]{1,0:T(8,128)(2,1)} %add_pieces.8), channel_id=1, source_target_pairs={{0,4},{1,5},{2,3},{3,2},{4,0},{5,1},{6,7},{7,6},{8,12},{9,13},{10,... | collective-permute-start | bytes 6291464 | tf_op jit(solution)/shard_map/ppermute | solution.py:445
  246.8 42.6 %collective-permute-start.26 = (bf16[512,2048]{1,0:T(8,128)(2,1)}, bf16[512,2048]{1,0:T(8,128)(2,1)S(1)}, u32[]{:S(2)}, u32[]{:S(2)}) collective-permute-start(bf16[512,2048]{1,0:T(8,128)(2,1)} %add_pieces.9), channel_id=1, source_target_pairs={{0,4},{1,5},{2,3},{3,2},{4,0},{5,1},{6,7},{7,6},{8,12},{9,13},{10,... | collective-permute-start | bytes 6291464 | tf_op jit(solution)/shard_map/ppermute | solution.py:445
  247.0 69.0 %collective-permute-start.22 = (bf16[512,2048]{1,0:T(8,128)(2,1)}, bf16[512,2048]{1,0:T(8,128)(2,1)}, u32[]{:S(2)}, u32[]{:S(2)}) collective-permute-start(bf16[512,2048]{1,0:T(8,128)(2,1)} %constant_dynamic-update-slice_fusion.4.refs_2_.refs_0_), channel_id=1, source_target_pairs={{0,2},{1,3},{2,0},{3,1},{4,6},{5,7},{6,4},{7,5},{8,10},{9,11},{10,... | collective-permute-start | bytes 6291464 | tf_op jit(solution)/shard_map/ppermute | solution.py:441
  247.0 69.9 %collective-permute-start.23 = (bf16[512,2048]{1,0:T(8,128)(2,1)}, bf16[512,2048]{1,0:T(8,128)(2,1)}, u32[]{:S(2)}, u32[]{:S(2)}) collective-permute-start(bf16[512,2048]{1,0:T(8,128)(2,1)} %collective-permute-done.19.refs_3_.refs_1_), channel_id=1, source_target_pairs={{0,2},{1,3},{2,0},{3,1},{4,6},{5,7},{6,4},{7,5},{8,10},{9,11},{10,... | collective-permute-start | bytes 6291464 | tf_op jit(solution)/shard_map/ppermute | solution.py:441
  247.5 69.4 %collective-permute-start.20 = (bf16[512,2048]{1,0:T(8,128)(2,1)}, bf16[512,2048]{1,0:T(8,128)(2,1)}, u32[]{:S(2)}, u32[]{:S(2)}) collective-permute-start(bf16[512,2048]{1,0:T(8,128)(2,1)} %constant_dynamic-update-slice_fusion.6.refs_0_), channel_id=1, source_target_pairs={{0,2},{1,3},{2,0},{3,1},{4,6},{5,7},{6,4},{7,5},{8,10},{9,11},{10,... | collective-permute-start | bytes 6291464 | tf_op jit(solution)/shard_map/ppermute | solution.py:441
  267.0 49.9 %collective-permute-start.21 = (bf16[512,2048]{1,0:T(8,128)(2,1)}, bf16[512,2048]{1,0:T(8,128)(2,1)}, u32[]{:S(2)}, u32[]{:S(2)}) collective-permute-start(bf16[512,2048]{1,0:T(8,128)(2,1)} %collective-permute-done.18.refs_1_), channel_id=1, source_target_pairs={{0,2},{1,3},{2,0},{3,1},{4,6},{5,7},{6,4},{7,5},{8,10},{9,11},{10,... | collective-permute-start | bytes 6291464 | tf_op jit(solution)/shard_map/ppermute | solution.py:441
  307.0 40.5 %collective-permute-start.29 = (bf16[256,2048]{1,0:T(8,128)(2,1)S(1)}, bf16[256,2048]{1,0:T(8,128)(2,1)}, u32[]{:S(2)}, u32[]{:S(2)}) collective-permute-start(bf16[256,2048]{1,0:T(8,128)(2,1)S(1)} %get-tuple-element.311.cot), channel_id=1, source_target_pairs={{0,1},{1,0},{2,6},{3,7},{4,5},{5,4},{6,2},{7,3},{8,9},{9,8},{10,14... | collective-permute-start | bytes 3145736 | tf_op jit(solution)/shard_map/ppermute | solution.py:445
  352.4 53.9 %collective-permute-start.38 = (bf16[512,2048]{1,0:T(8,128)(2,1)}, bf16[512,2048]{1,0:T(8,128)(2,1)}, u32[]{:S(2)}, u32[]{:S(2)}) collective-permute-start(bf16[512,2048]{1,0:T(8,128)(2,1)} %constant_dynamic-update-slice_fusion.10.refs_2_.refs_4_), channel_id=1, source_target_pairs={{0,2},{1,3},{2,0},{3,1},{4,6},{5,7},{6,4},{7,5},{8,10},{9,11},{10,... | collective-permute-start | bytes 6291464 | tf_op jit(solution)/shard_map/ppermute | solution.py:441
  354.7 44.7 %collective-permute-start.30 = (bf16[512,2048]{1,0:T(8,128)(2,1)}, bf16[512,2048]{1,0:T(8,128)(2,1)}, u32[]{:S(2)}, u32[]{:S(2)}) collective-permute-start(bf16[512,2048]{1,0:T(8,128)(2,1)} %constant_dynamic-update-slice_fusion.8.refs_0_.refs_4_), channel_id=1, source_target_pairs={{0,4},{1,5},{2,3},{3,2},{4,0},{5,1},{6,7},{7,6},{8,12},{9,13},{10,... | collective-permute-start | bytes 6291464 | tf_op jit(solution)/shard_map/ppermute | solution.py:445
  354.9 44.5 %collective-permute-start.32 = (bf16[512,2048]{1,0:T(8,128)(2,1)S(1)}, bf16[512,2048]{1,0:T(8,128)(2,1)S(1)}, u32[]{:S(2)}, u32[]{:S(2)}) collective-permute-start(bf16[512,2048]{1,0:T(8,128)(2,1)S(1)} %copy-done.48), channel_id=1, source_target_pairs={{0,2},{1,3},{2,0},{3,1},{4,6},{5,7},{6,4},{7,5},{8,10},{9,11},{10,... | collective-permute-start | bytes 6291464 | tf_op jit(solution)/shard_map/ppermute | solution.py:441
  356.0 43.9 %collective-permute-start.33 = (bf16[512,2048]{1,0:T(8,128)(2,1)S(1)}, bf16[512,2048]{1,0:T(8,128)(2,1)}, u32[]{:S(2)}, u32[]{:S(2)}) collective-permute-start(bf16[512,2048]{1,0:T(8,128)(2,1)S(1)} %copy-done.47), channel_id=1, source_target_pairs={{0,2},{1,3},{2,0},{3,1},{4,6},{5,7},{6,4},{7,5},{8,10},{9,11},{10,... | collective-permute-start | bytes 6291464 | tf_op jit(solution)/shard_map/ppermute | solution.py:441
  445.4 43.9 %collective-permute-start.42 = (bf16[512,2048]{1,0:T(8,128)(2,1)}, bf16[512,2048]{1,0:T(8,128)(2,1)S(1)}, u32[]{:S(2)}, u32[]{:S(2)}) collective-permute-start(bf16[512,2048]{1,0:T(8,128)(2,1)} %get-tuple-element.353), channel_id=1, source_target_pairs={{0,2},{1,3},{2,0},{3,1},{4,6},{5,7},{6,4},{7,5},{8,10},{9,11},{10,... | collective-permute-start | bytes 6291464 | tf_op jit(solution)/shard_map/ppermute | solution.py:441
  445.9 43.3 %collective-permute-start.43 = (bf16[512,2048]{1,0:T(8,128)(2,1)}, bf16[512,2048]{1,0:T(8,128)(2,1)}, u32[]{:S(2)}, u32[]{:S(2)}) collective-permute-start(bf16[512,2048]{1,0:T(8,128)(2,1)} %get-tuple-element.354), channel_id=1, source_target_pairs={{0,2},{1,3},{2,0},{3,1},{4,6},{5,7},{6,4},{7,5},{8,10},{9,11},{10,... | collective-permute-start | bytes 6291464 | tf_op jit(solution)/shard_map/ppermute | solution.py:441
  446.0 43.3 %collective-permute-start.40 = (bf16[512,2048]{1,0:T(8,128)(2,1)}, bf16[512,2048]{1,0:T(8,128)(2,1)}, u32[]{:S(2)}, u32[]{:S(2)}) collective-permute-start(bf16[512,2048]{1,0:T(8,128)(2,1)} %add_pieces.11), channel_id=1, source_target_pairs={{0,4},{1,5},{2,3},{3,2},{4,0},{5,1},{6,7},{7,6},{8,12},{9,13},{10,... | collective-permute-start | bytes 6291464 | tf_op jit(solution)/shard_map/ppermute | solution.py:445
  485.9 45.7 %collective-permute-start.45 = (bf16[256,2048]{1,0:T(8,128)(2,1)}, bf16[256,2048]{1,0:T(8,128)(2,1)}, u32[]{:S(2)}, u32[]{:S(2)}) collective-permute-start(bf16[256,2048]{1,0:T(8,128)(2,1)} %get-tuple-element.358), channel_id=1, source_target_pairs={{0,1},{1,0},{2,6},{3,7},{4,5},{5,4},{6,2},{7,3},{8,9},{9,8},{10,14... | collective-permute-start | bytes 3145736 | tf_op jit(solution)/shard_map/ppermute | solution.py:445
  535.7 57.8 %collective-permute-start.49 = (bf16[512,2048]{1,0:T(8,128)(2,1)}, bf16[512,2048]{1,0:T(8,128)(2,1)}, u32[]{:S(2)}, u32[]{:S(2)}) collective-permute-start(bf16[512,2048]{1,0:T(8,128)(2,1)} %constant_dynamic-update-slice_fusion.12.refs_0_), channel_id=1, source_target_pairs={{0,2},{1,3},{2,0},{3,1},{4,6},{5,7},{6,4},{7,5},{8,10},{9,11},{10,... | collective-permute-start | bytes 6291464 | tf_op jit(solution)/shard_map/ppermute | solution.py:441
  537.8 47.3 %collective-permute-start.52 = (bf16[512,2048]{1,0:T(8,128)(2,1)}, bf16[512,2048]{1,0:T(8,128)(2,1)}, u32[]{:S(2)}, u32[]{:S(2)}) collective-permute-start(bf16[512,2048]{1,0:T(8,128)(2,1)} %get-tuple-element.393), channel_id=1, source_target_pairs={{0,2},{1,3},{2,0},{3,1},{4,6},{5,7},{6,4},{7,5},{8,10},{9,11},{10,... | collective-permute-start | bytes 6291464 | tf_op jit(solution)/shard_map/ppermute | solution.py:441
  538.4 47.8 %collective-permute-start.53 = (bf16[512,2048]{1,0:T(8,128)(2,1)}, bf16[512,2048]{1,0:T(8,128)(2,1)S(1)}, u32[]{:S(2)}, u32[]{:S(2)}) collective-permute-start(bf16[512,2048]{1,0:T(8,128)(2,1)} %get-tuple-element.394), channel_id=1, source_target_pairs={{0,2},{1,3},{2,0},{3,1},{4,6},{5,7},{6,4},{7,5},{8,10},{9,11},{10,... | collective-permute-start | bytes 6291464 | tf_op jit(solution)/shard_map/ppermute | solution.py:441
  561.4 198.9 %reduce-scatter.7.cloned.1.call-start = ((), (), s32[]{:S(2)}) async-start(), calls=%async_computation.8 | async-start | bytes 3932160 | tf_op jit(solution)/shard_map/reduce_scatter | solution.py:1431
  575.3 70.7 %collective-permute-start.47 = (bf16[256,2048]{1,0:T(8,128)(2,1)}, bf16[256,2048]{1,0:T(8,128)(2,1)S(1)}, u32[]{:S(2)}, u32[]{:S(2)}) collective-permute-start(bf16[256,2048]{1,0:T(8,128)(2,1)} %add_convert_fusion.6), channel_id=1, source_target_pairs={{0,1},{1,0},{2,6},{3,7},{4,5},{5,4},{6,2},{7,3},{8,9},{9,8},{10,14... | collective-permute-start | bytes 3145736 | tf_op jit(solution)/shard_map/ppermute | solution.py:445
  585.1 60.9 %collective-permute-start.55 = (bf16[256,2048]{1,0:T(8,128)(2,1)}, bf16[256,2048]{1,0:T(8,128)(2,1)}, u32[]{:S(2)}, u32[]{:S(2)}) collective-permute-start(bf16[256,2048]{1,0:T(8,128)(2,1)} %get-tuple-element.389), channel_id=1, source_target_pairs={{0,1},{1,0},{2,6},{3,7},{4,5},{5,4},{6,2},{7,3},{8,9},{9,8},{10,14... | collective-permute-start | bytes 3145736 | tf_op jit(solution)/shard_map/ppermute | solution.py:445
  591.9 60.5 %collective-permute-start.54 = (bf16[512,2048]{1,0:T(8,128)(2,1)}, bf16[512,2048]{1,0:T(8,128)(2,1)}, u32[]{:S(2)}, u32[]{:S(2)}) collective-permute-start(bf16[512,2048]{1,0:T(8,128)(2,1)} %add_pieces.13), channel_id=1, source_target_pairs={{0,4},{1,5},{2,3},{3,2},{4,0},{5,1},{6,7},{7,6},{8,12},{9,13},{10,... | collective-permute-start | bytes 6291464 | tf_op jit(solution)/shard_map/ppermute | solution.py:445
  656.8 179.7 %reduce-scatter.11.cloned.1.call-start = ((), (), s32[]{:S(2)}) async-start(), calls=%async_computation.10 | async-start | bytes 1310720 | tf_op jit(solution)/shard_map/reduce_scatter | solution.py:1431
  699.8 89.3 %collective-permute-start.61 = (bf16[256,2048]{1,0:T(8,128)(2,1)}, bf16[256,2048]{1,0:T(8,128)(2,1)}, u32[]{:S(2)}, u32[]{:S(2)}) collective-permute-start(bf16[256,2048]{1,0:T(8,128)(2,1)} %add_convert_fusion.3), channel_id=1, source_target_pairs={{0,1},{1,0},{2,6},{3,7},{4,5},{5,4},{6,2},{7,3},{8,9},{9,8},{10,14... | collective-permute-start | bytes 3145736 | tf_op jit(solution)/shard_map/ppermute | solution.py:445
  701.0 52.1 %collective-permute-start.62 = (bf16[512,2048]{1,0:T(8,128)(2,1)}, bf16[512,2048]{1,0:T(8,128)(2,1)}, u32[]{:S(2)}, u32[]{:S(2)}) collective-permute-start(bf16[512,2048]{1,0:T(8,128)(2,1)} %add_pieces.14), channel_id=1, source_target_pairs={{0,4},{1,5},{2,3},{3,2},{4,0},{5,1},{6,7},{7,6},{8,12},{9,13},{10,... | collective-permute-start | bytes 6291464 | tf_op jit(solution)/shard_map/ppermute | solution.py:445
  701.5 157.6 %reduce-scatter.9.cloned.1.call-start = ((), (), s32[]{:S(2)}) async-start(), calls=%async_computation.9 | async-start | bytes 2703360 | tf_op jit(solution)/shard_map/reduce_scatter | solution.py:1431
  (107 other events, 1813.8 us)
Sparse Core Ops, SparseCore 0:
  30.6 72.4 all-gather.3
  105.2 63.5 all-gather.5
  171.0 113.9 all-gather.7
  561.5 110.0 reduce-scatter.4
  673.8 60.7 reduce-scatter.6
  736.7 27.1 reduce-scatter.10
  789.2 44.3 reduce-scatter.8
